TPU v7x, 32 devices: a whole 2x2x4 slice. The times are simulated.
32 devices in a mesh: grp: 2 (over x), ctx: 16 (over z, y, core).
Axes of the slice: x: 2, y: 2, z: 4, core: 2. Of those that a mesh axis runs over, the one named last changes fastest.
Arguments:
- tokens: bfloat16 [2, 2048, 2048], P('grp', 'ctx'), may hold values from -6 to 6
- segments: int32 [2, 2048], P('grp'), may hold values from 0 to 65, as said below
- output_cotangent_rows: bfloat16 [2, 2048, 2048], P('grp', 'ctx'), may hold values from -6 to 6
- attention_norm_gain: bfloat16 [2048], P('ctx'), may hold values from -0.5 to 0.5
- query_key_value_matrix: bfloat16 [2048, 2560], P('ctx'), may hold values from -0.125 to 0.125
- query_key_value_adapter_first: bfloat16 [2048, 256], P('ctx'), may hold values from -0.125 to 0.125
- query_key_value_adapter_second: bfloat16 [256, 2560], P('ctx'), may hold values from -0.1875 to 0.1875
- output_matrix: bfloat16 [2048, 2048], P('ctx'), may hold values from -0.75 to 0.75
- output_adapter_first: bfloat16 [2048, 256], P('ctx'), may hold values from -0.75 to 0.75
- output_adapter_second: bfloat16 [256, 2048], P('ctx'), may hold values from -0.1875 to 0.1875
- feed_norm_gain: bfloat16 [2048], P('ctx'), may hold values from -0.5 to 0.5
- gate_up_matrix: bfloat16 [2048, 32768], P('ctx'), may hold values from -0.125 to 0.125
- gate_up_adapter_first: bfloat16 [2048, 256], P('ctx'), may hold values from -0.125 to 0.125
- gate_up_adapter_second: bfloat16 [256, 32768], P('ctx'), may hold values from -0.1875 to 0.1875
- down_matrix: bfloat16 [16384, 2048], P('ctx'), may hold values from -0.046875 to 0.046875
- down_adapter_first: bfloat16 [16384, 256], P('ctx'), may hold values from -0.046875 to 0.046875
- down_adapter_second: bfloat16 [256, 2048], P('ctx'), may hold values from -0.1875 to 0.1875
Outputs:
- output: bfloat16 [2, 2048, 2048], P('grp', 'ctx')
- grad_input: bfloat16 [2, 2048, 2048], P('grp', 'ctx')
- g_attn_gain: float32 [2048], P('ctx')
- g_qkv_weight: float32 [2048, 2560], P('ctx')
- g_qkv_lora_a: float32 [2048, 256], P('ctx')
- g_qkv_lora_b: float32 [256, 2560], P('ctx')
- g_out_weight: float32 [2048, 2048], P('ctx')
- g_out_lora_a: float32 [2048, 256], P('ctx')
- g_out_lora_b: float32 [256, 2048], P('ctx')
- g_ffn_gain: float32 [2048], P('ctx')
- g_gate_up_weight: float32 [2048, 32768], P('ctx')
- g_gate_up_lora_a: float32 [2048, 256], P('ctx')
- g_gate_up_lora_b: float32 [256, 32768], P('ctx')
- g_down_weight: float32 [16384, 2048], P('ctx')
- g_down_lora_a: float32 [16384, 256], P('ctx')
- g_down_lora_b: float32 [256, 2048], P('ctx')
Inputs may be any that keep to these rules, and one draw needn't show every extreme that they name: `segments`: along a sequence's positions the document numbers never fall; the last document starts at or before position 960 and runs to the end.
All inputs are finite; a program needn't handle non-finite values.
Results may differ from a plain program's by a relative error of at most 0.019.
Values may be sent and summed in bfloat16 or wider, within the bound.
No kernel may reach another device: no remote copies, remote signals or barrier semaphores. Data moves between devices by JAX's collectives and lax.ppermute only.
A program may use at most 960 MiB of HBM per device.

v0:
```python
import jax
import jax.numpy as jnp
from jax import lax
from jax.sharding import PartitionSpec as P

MODEL_WIDTH = 2048
HEADS = 8
HD = 256


norm_eps = 1e-06
rope_base = 10000.0


def product(left_arg, right_arg):
    return jnp.dot(left_arg, right_arg, preferred_element_type=jnp.float32)


def transposed_left(left_arg, right_arg):
    return lax.dot_general(
        left_arg, right_arg, (((0,), (0,)), ((), ())), preferred_element_type=jnp.float32
    )


def transposed_right(left_arg, right_arg):
    return lax.dot_general(
        left_arg, right_arg, (((1,), (1,)), ((), ())), preferred_element_type=jnp.float32
    )


def positions(row_count, per_device, device_count):
    row_index = jnp.arange(row_count, dtype=jnp.int32)
    device = row_index // per_device
    within = row_index % per_device
    half_len = per_device // 2
    block_id = jnp.where(within < half_len, device, 2 * device_count - 1 - device)
    return block_id * half_len + within % half_len


def angles(pos_rows):
    frequency = rope_base ** (-2.0 * jnp.arange(HD // 2, dtype=jnp.float32) / HD)
    angle_rows = pos_rows.astype(jnp.float32)[:, None] * frequency[None, :]
    return (jnp.cos(angle_rows), jnp.sin(angle_rows))


def rotate(vectors, cosine, sine_rows):
    front_half, back_half = jnp.split(vectors, 2, axis=-1)
    return jnp.concatenate(
        [front_half * cosine - back_half * sine_rows, back_half * cosine + front_half * sine_rows],
        axis=-1,
    )


def rms_norm(values, gain_vec):
    inv_rms = lax.rsqrt(jnp.mean(values * values, axis=-1, keepdims=True) + norm_eps)
    return values * inv_rms * (1.0 + gain_vec)


def gated_gelu(gate_up_output):
    gate_part, up_part = jnp.split(gate_up_output, 2, axis=-1)
    return jax.nn.gelu(gate_part, approximate=True) * up_part


def body(
    tokens,
    segments,
    output_cotangent_rows,
    attention_norm_gain,
    query_key_value_matrix,
    query_key_value_adapter_first,
    query_key_value_adapter_second,
    output_matrix,
    output_adapter_first,
    output_adapter_second,
    feed_norm_gain,
    gate_up_matrix,
    gate_up_adapter_first,
    gate_up_adapter_second,
    down_matrix,
    down_adapter_first,
    down_adapter_second,
):
    ctx_size = lax.axis_size("ctx")
    ctx_rank = lax.axis_index("ctx")
    rows_dev = tokens.shape[1]
    seq_len = rows_dev * ctx_size
    score_scale = HD ** (-0.5)
    key_pos = positions(seq_len, rows_dev, ctx_size)
    local_pos = lax.dynamic_slice_in_dim(key_pos, ctx_rank * rows_dev, rows_dev)
    key_seg = jnp.take(segments[0], key_pos)
    local_seg = jnp.take(segments[0], local_pos)
    allowed = (local_seg[:, None] == key_seg[None, :]) & (key_pos[None, :] <= local_pos[:, None])
    cosine, sine_rows = angles(local_pos)
    residual_stream = tokens[0].astype(jnp.float32)
    cotangent = output_cotangent_rows[0]

    def fetch_attention():
        return (
            lax.all_gather(attention_norm_gain, "ctx", axis=0, tiled=True),
            lax.all_gather(query_key_value_matrix, "ctx", axis=0, tiled=True),
            lax.all_gather(query_key_value_adapter_first, "ctx", axis=0, tiled=True),
            lax.all_gather(query_key_value_adapter_second, "ctx", axis=0, tiled=True),
            lax.all_gather(output_matrix, "ctx", axis=0, tiled=True),
            lax.all_gather(output_adapter_first, "ctx", axis=0, tiled=True),
            lax.all_gather(output_adapter_second, "ctx", axis=0, tiled=True),
        )

    def fetch_gate():
        return (
            lax.all_gather(feed_norm_gain, "ctx", axis=0, tiled=True),
            lax.all_gather(gate_up_matrix, "ctx", axis=0, tiled=True),
            lax.all_gather(gate_up_adapter_first, "ctx", axis=0, tiled=True),
            lax.all_gather(gate_up_adapter_second, "ctx", axis=0, tiled=True),
        )

    def fetch_down():
        return (
            lax.all_gather(down_matrix, "ctx", axis=0, tiled=True),
            lax.all_gather(down_adapter_first, "ctx", axis=0, tiled=True),
            lax.all_gather(down_adapter_second, "ctx", axis=0, tiled=True),
        )

    attn_full = fetch_attention()
    first_normed, norm_one_pull = jax.vjp(
        rms_norm, residual_stream, attn_full[0].astype(jnp.float32)
    )
    norm_one_low = first_normed.astype(jnp.bfloat16)
    inner_qkv = product(norm_one_low, attn_full[2]).astype(jnp.bfloat16)
    query_key_value_rows = product(norm_one_low, attn_full[1]) + product(inner_qkv, attn_full[3])
    queries = rotate(
        query_key_value_rows[:, :MODEL_WIDTH].reshape(rows_dev, HEADS, HD),
        cosine[:, None, :],
        sine_rows[:, None, :],
    ).astype(jnp.bfloat16)
    flat_queries = queries.reshape(rows_dev * HEADS, HD)
    key_mine = rotate(
        query_key_value_rows[:, MODEL_WIDTH : MODEL_WIDTH + HD], cosine, sine_rows
    ).astype(jnp.bfloat16)
    value_mine = query_key_value_rows[:, MODEL_WIDTH + HD :].astype(jnp.bfloat16)
    key_all, value_all = (
        lax.all_gather(key_mine, "ctx", axis=0, tiled=True),
        lax.all_gather(value_mine, "ctx", axis=0, tiled=True),
    )

    def masked_scores():
        raw_scores = (
            transposed_right(flat_queries, key_all).reshape(rows_dev, HEADS, seq_len) * score_scale
        )
        return jnp.where(allowed[:, None, :], raw_scores, -jnp.inf)

    scores = masked_scores()
    row_peak = jnp.max(scores, axis=-1, keepdims=True)
    unnormed = jnp.exp(scores - row_peak)
    row_total = jnp.sum(unnormed, axis=-1, keepdims=True)
    probs_low = (unnormed / row_total).astype(jnp.bfloat16)
    log_total = row_peak + jnp.log(row_total)
    attention_result = (
        product(probs_low.reshape(rows_dev * HEADS, seq_len), value_all)
        .reshape(rows_dev, MODEL_WIDTH)
        .astype(jnp.bfloat16)
    )
    inner_out = product(attention_result, attn_full[5]).astype(jnp.bfloat16)
    middle_residual = (
        residual_stream + product(attention_result, attn_full[4]) + product(inner_out, attn_full[6])
    )
    gate_side = fetch_gate()
    second_normed, norm_two_pull = jax.vjp(
        rms_norm, middle_residual, gate_side[0].astype(jnp.float32)
    )
    norm_two_low = second_normed.astype(jnp.bfloat16)
    inner_gate_up = product(norm_two_low, gate_side[2]).astype(jnp.bfloat16)
    gate_up_output = product(norm_two_low, gate_side[1]) + product(inner_gate_up, gate_side[3])
    activated, gelu_pull = jax.vjp(gated_gelu, gate_up_output)
    hidden_activation = activated.astype(jnp.bfloat16)
    down_side = fetch_down()
    inner_down = product(hidden_activation, down_side[1]).astype(jnp.bfloat16)
    output = (
        middle_residual
        + product(hidden_activation, down_side[0])
        + product(inner_down, down_side[2])
    ).astype(jnp.bfloat16)
    down_again = fetch_down()
    g_down_weight = lax.psum_scatter(
        transposed_left(hidden_activation, cotangent), "ctx", scatter_dimension=0, tiled=True
    )
    grad_inner_down = transposed_right(cotangent, down_again[2]).astype(jnp.bfloat16)
    grad_hidden = transposed_right(cotangent, down_again[0]) + transposed_right(
        grad_inner_down, down_again[1]
    )
    grad_gate_up = gelu_pull(grad_hidden)[0].astype(jnp.bfloat16)
    gate_again = fetch_gate()
    g_gate_up_weight = lax.psum_scatter(
        transposed_left(norm_two_low, grad_gate_up), "ctx", scatter_dimension=0, tiled=True
    )
    grad_inner_gate_up = transposed_right(grad_gate_up, gate_again[3]).astype(jnp.bfloat16)
    grad_norm_two = transposed_right(grad_gate_up, gate_again[1]) + transposed_right(
        grad_inner_gate_up, gate_again[2]
    )
    grad_mid_part, gain_two_term = norm_two_pull(grad_norm_two)
    ffn_small = (
        lax.psum_scatter(gain_two_term, "ctx", scatter_dimension=0, tiled=True),
        lax.psum_scatter(
            transposed_left(norm_two_low, grad_inner_gate_up),
            "ctx",
            scatter_dimension=0,
            tiled=True,
        ),
        lax.psum_scatter(
            transposed_left(inner_gate_up, grad_gate_up), "ctx", scatter_dimension=0, tiled=True
        ),
        lax.psum_scatter(
            transposed_left(hidden_activation, grad_inner_down),
            "ctx",
            scatter_dimension=0,
            tiled=True,
        ),
        lax.psum_scatter(
            transposed_left(inner_down, cotangent), "ctx", scatter_dimension=0, tiled=True
        ),
    )
    ffn_sums = (
        ffn_small[0],
        g_gate_up_weight,
        ffn_small[1],
        ffn_small[2],
        g_down_weight,
        ffn_small[3],
        ffn_small[4],
    )
    grad_mid = cotangent.astype(jnp.float32) + grad_mid_part
    grad_branch = grad_mid.astype(jnp.bfloat16)
    attn_back = fetch_attention()
    grad_inner_out = transposed_right(grad_branch, attn_back[6]).astype(jnp.bfloat16)
    grad_attended = (
        transposed_right(grad_branch, attn_back[4]) + transposed_right(grad_inner_out, attn_back[5])
    ).astype(jnp.bfloat16)
    grad_flat = grad_attended.reshape(rows_dev * HEADS, HD)
    attn_probs = jnp.exp(masked_scores() - log_total)
    grad_probs = transposed_right(grad_flat, value_all).reshape(rows_dev, HEADS, seq_len)
    delta_rows = jnp.sum(attn_probs * grad_probs, axis=-1, keepdims=True)
    grad_scores = (
        (attn_probs * (grad_probs - delta_rows))
        .astype(jnp.bfloat16)
        .reshape(rows_dev * HEADS, seq_len)
    )
    probs_again = attn_probs.astype(jnp.bfloat16).reshape(rows_dev * HEADS, seq_len)
    grad_queries = product(grad_scores, key_all) * score_scale
    grad_key_all = transposed_left(grad_scores, flat_queries) * score_scale
    grad_value_all = transposed_left(probs_again, grad_flat)
    grad_key_mine, grad_value_mine = (
        lax.psum_scatter(grad_key_all, "ctx", scatter_dimension=0, tiled=True),
        lax.psum_scatter(grad_value_all, "ctx", scatter_dimension=0, tiled=True),
    )
    grad_query_rows = rotate(
        grad_queries.reshape(rows_dev, HEADS, HD), cosine[:, None, :], -sine_rows[:, None, :]
    ).reshape(rows_dev, MODEL_WIDTH)
    grad_key_rows = rotate(grad_key_mine, cosine, -sine_rows)
    grad_qkv = jnp.concatenate([grad_query_rows, grad_key_rows, grad_value_mine], axis=1).astype(
        jnp.bfloat16
    )
    grad_inner_qkv = transposed_right(grad_qkv, attn_back[3]).astype(jnp.bfloat16)
    grad_norm_one = transposed_right(grad_qkv, attn_back[1]) + transposed_right(
        grad_inner_qkv, attn_back[2]
    )
    grad_input_part, gain_one_term = norm_one_pull(grad_norm_one)
    grad_input = (grad_mid + grad_input_part).astype(jnp.bfloat16)
    attn_grads = (
        lax.psum_scatter(gain_one_term, "ctx", scatter_dimension=0, tiled=True),
        lax.psum_scatter(
            transposed_left(norm_one_low, grad_qkv), "ctx", scatter_dimension=0, tiled=True
        ),
        lax.psum_scatter(
            transposed_left(norm_one_low, grad_inner_qkv), "ctx", scatter_dimension=0, tiled=True
        ),
        lax.psum_scatter(
            transposed_left(inner_qkv, grad_qkv), "ctx", scatter_dimension=0, tiled=True
        ),
        lax.psum_scatter(
            transposed_left(attention_result, grad_branch), "ctx", scatter_dimension=0, tiled=True
        ),
        lax.psum_scatter(
            transposed_left(attention_result, grad_inner_out),
            "ctx",
            scatter_dimension=0,
            tiled=True,
        ),
        lax.psum_scatter(
            transposed_left(inner_out, grad_branch), "ctx", scatter_dimension=0, tiled=True
        ),
    )
    total_sums = (
        lax.psum(attn_grads[0].astype(jnp.bfloat16), "grp").astype(jnp.float32),
        lax.psum(attn_grads[1].astype(jnp.bfloat16), "grp").astype(jnp.float32),
        lax.psum(attn_grads[2].astype(jnp.bfloat16), "grp").astype(jnp.float32),
        lax.psum(attn_grads[3].astype(jnp.bfloat16), "grp").astype(jnp.float32),
        lax.psum(attn_grads[4].astype(jnp.bfloat16), "grp").astype(jnp.float32),
        lax.psum(attn_grads[5].astype(jnp.bfloat16), "grp").astype(jnp.float32),
        lax.psum(attn_grads[6].astype(jnp.bfloat16), "grp").astype(jnp.float32),
        lax.psum(ffn_sums[0].astype(jnp.bfloat16), "grp").astype(jnp.float32),
        lax.psum(ffn_sums[1].astype(jnp.bfloat16), "grp").astype(jnp.float32),
        lax.psum(ffn_sums[2].astype(jnp.bfloat16), "grp").astype(jnp.float32),
        lax.psum(ffn_sums[3].astype(jnp.bfloat16), "grp").astype(jnp.float32),
        lax.psum(ffn_sums[4].astype(jnp.bfloat16), "grp").astype(jnp.float32),
        lax.psum(ffn_sums[5].astype(jnp.bfloat16), "grp").astype(jnp.float32),
        lax.psum(ffn_sums[6].astype(jnp.bfloat16), "grp").astype(jnp.float32),
    )
    attn_sums = total_sums[:7]
    ffn_sums = total_sums[7:]
    return (
        output[None],
        grad_input[None],
        attn_sums[0],
        attn_sums[1],
        attn_sums[2],
        attn_sums[3],
        attn_sums[4],
        attn_sums[5],
        attn_sums[6],
        ffn_sums[0],
        ffn_sums[1],
        ffn_sums[2],
        ffn_sums[3],
        ffn_sums[4],
        ffn_sums[5],
        ffn_sums[6],
    )


def solution(mesh):
    return jax.shard_map(
        body,
        mesh=mesh,
        in_specs=(
            P("grp", "ctx", None),
            P("grp", None),
            P("grp", "ctx", None),
            P("ctx"),
            P("ctx", None),
            P("ctx", None),
            P("ctx", None),
            P("ctx", None),
            P("ctx", None),
            P("ctx", None),
            P("ctx"),
            P("ctx", None),
            P("ctx", None),
            P("ctx", None),
            P("ctx", None),
            P("ctx", None),
            P("ctx", None),
        ),
        out_specs=(
            P("grp", "ctx", None),
            P("grp", "ctx", None),
            P("ctx"),
            P("ctx", None),
            P("ctx", None),
            P("ctx", None),
            P("ctx", None),
            P("ctx", None),
            P("ctx", None),
            P("ctx"),
            P("ctx", None),
            P("ctx", None),
            P("ctx", None),
            P("ctx", None),
            P("ctx", None),
            P("ctx", None),
        ),
        check_vma=False,
    )
```

profile of v0, /device:TPU:0, one launch (start us, length us, event | category | flops | bytes accessed | tf_op | source)
XLA Modules:
  0.0 7320.1 jit_solution(11056863090045913158)
XLA Ops:
  11.8 23.1 all-gather
  35.0 15.8 all-gather.19.cloned.1.call-done
  52.6 87.3 %all-gather.17.cloned.1.call-done = bf16[2048,2560]{1,0:T(8,128)(2,1)} async-done(((bf16[128,2560]{1,0:T(8,128)(2,1)}), bf16[2048,2560]{1,0:T(8,128)(2,1)}) %all-gather.17.cloned.1.call-update) | async-done | bytes 10485776 | tf_op jit(solution)/shard_map/all_gather | solution.py:100
  145.7 33.5 all-gather.21.cloned.1.call-done
  190.1 19.3 all-gather.1
  209.4 11.8 gather_fusion.1
  224.1 33.5 all-gather.23.cloned.1.call-done
  267.0 30.0 all-gather.25.cloned.1.call-done
  302.2 33.9 all-gather.29.cloned.1.call-done
  337.6 74.4 %all-gather.27.cloned.1.call-done = bf16[2048,2048]{1,0:T(8,128)(2,1)} async-done(((bf16[128,2048]{1,0:T(8,128)(2,1)}), bf16[2048,2048]{1,0:T(8,128)(2,1)}) %all-gather.27.cloned.1.call-update) | async-done | bytes 8388624 | tf_op jit(solution)/shard_map/all_gather | solution.py:103
  416.8 33.7 all-gather.31.cloned.1.call-done
  453.9 35.5 all-gather.35.cloned.1.call-done
  490.9 325.1 %all-gather.39.cloned.1.call-done = bf16[16384,2048]{1,0:T(8,128)(2,1)} async-done(((bf16[1024,2048]{1,0:T(8,128)(2,1)}), bf16[16384,2048]{1,0:T(8,128)(2,1)}) %all-gather.39.cloned.1.call-update) | async-done | bytes 67108880 | tf_op jit(solution)/shard_map/all_gather | solution.py:118
  816.0 34.8 fusion.51
  850.9 608.9 %all-gather.33.cloned.1.call-done = bf16[2048,32768]{1,0:T(8,128)(2,1)} async-done(((bf16[128,32768]{1,0:T(8,128)(2,1)}), bf16[2048,32768]{1,0:T(8,128)(2,1)}) %all-gather.33.cloned.1.call-update) | async-done | bytes 134217744 | tf_op jit(solution)/shard_map/all_gather | solution.py:111
  1459.7 50.5 fusion.103
  1510.2 78.6 %all-gather.37.cloned.1.call-done = bf16[256,32768]{1,0:T(8,128)(2,1)} async-done(((bf16[16,32768]{1,0:T(8,128)(2,1)}), bf16[256,32768]{1,0:T(8,128)(2,1)}) %all-gather.37.cloned.1.call-update) | async-done | bytes 16777232 | tf_op jit(solution)/shard_map/all_gather | solution.py:113
  1588.8 20.3 convolution_add_fusion
  1609.1 54.8 all-gather.41.cloned.1.call-done
  1663.9 20.3 fusion.6
  1684.2 53.0 fusion.88
  1737.3 10.6 convolution_convert_fusion.2
  1751.9 6.4 fusion.104
  1770.0 6.5 fusion.9
  1782.1 6.2 convolution_convert_fusion.7
  1795.9 33.5 reduce-scatter.17.cloned.1.call-done
  1830.8 63.9 reduce-scatter.19.cloned.1.call-done
  1902.3 8.5 fusion.105
  1910.9 10.4 fusion.109
  1921.4 9.7 fusion.91
  1932.0 19.3 fusion.86
  1951.6 47.1 fusion.48
  1999.7 91.9 %fusion.87 = f32[2048,32768]{1,0:T(8,128)} fusion(bf16[128,2048]{1,0:T(8,128)(2,1)S(1)} %copy-done.14, bf16[128,16384]{1,0:T(8,128)(2,1)} %get-tuple-element.39, bf16[128,16384]{1,0:T(8,128)(2,1)} %get-tuple-element.38), kind=kOutput, calls=%fused_computation.170 | convolution fusion | flops 17196646400 | bytes 277348352 | tf_op jit(solution)/shard_map/dot_general | solution.py:20
  2096.3 56.1 reduce-scatter.41.cloned.1.call-done
  2154.0 63.3 reduce-scatter.23.cloned.1.call-done
  2218.9 66.2 reduce-scatter.25.cloned.1.call-done
  2286.6 181.3 %reduce-scatter.27.cloned.1.call-done = f32[128,2048]{1,0:T(8,128)} async-done(((f32[2048,2048]{1,0:T(8,128)}), f32[128,2048]{1,0:T(8,128)}) %reduce-scatter.27.cloned.1.call-update) | async-done | bytes 1048592 | tf_op jit(solution)/shard_map/reduce_scatter | solution.py:278
  2469.9 180.1 %reduce-scatter.39.cloned.1.call-done = f32[1024,256]{1,0:T(8,128)} async-done(((f32[16384,256]{1,0:T(8,128)}), f32[1024,256]{1,0:T(8,128)}) %reduce-scatter.39.cloned.1.call-update) | async-done | bytes 1048592 | tf_op jit(solution)/shard_map/reduce_scatter | solution.py:211
  2652.1 212.5 %reduce-scatter.21.cloned.1.call-done = f32[128,2560]{1,0:T(8,128)} async-done(((f32[2048,2560]{1,0:T(8,128)}), f32[128,2560]{1,0:T(8,128)}) %reduce-scatter.21.cloned.1.call-update) | async-done | bytes 1310736 | tf_op jit(solution)/shard_map/reduce_scatter | solution.py:269
  2866.8 334.4 %reduce-scatter.37.cloned.1.call-done = f32[16,32768]{1,0:T(8,128)} async-done(((f32[256,32768]{1,0:T(8,128)}), f32[16,32768]{1,0:T(8,128)}) %reduce-scatter.37.cloned.1.call-update) | async-done | bytes 2097168 | tf_op jit(solution)/shard_map/reduce_scatter | solution.py:208
  3203.9 1237.3 %reduce-scatter.43.cloned.1.call-done = f32[1024,2048]{1,0:T(8,128)} async-done(((f32[16384,2048]{1,0:T(8,128)}), f32[1024,2048]{1,0:T(8,128)}) %reduce-scatter.43.cloned.1.call-update) | async-done | bytes 8388624
  4447.2 2458.0 %reduce-scatter.33.cloned.1.call-done = f32[128,32768]{1,0:T(8,128)} async-done(((f32[2048,32768]{1,0:T(8,128)}), f32[128,32768]{1,0:T(8,128)}) %reduce-scatter.33.cloned.1.call-update) | async-done | bytes 16777232 | tf_op jit(solution)/shard_map/reduce_scatter | solution.py:192
  6905.2 8.9 convert_element_type.211
  6916.0 25.4 convolution_add_fusion.9
  6944.1 7.8 fusion.98
  6953.4 57.6 all-reduce.3
  7019.9 259.3 %all-reduce.8.cloned.1.call-done = (bf16[128,2560]{1,0:T(8,128)(2,1)}, bf16[128,256]{1,0:T(8,128)(2,1)}, bf16[16,2560]{1,0:T(8,128)(2,1)}, bf16[128,2048]{1,0:T(...) async-done(((bf16[128,2560]{1,0:T(8,128)(2,1)}, ...) | async-done | bytes 15745040 | tf_op jit(solution)/shard_map/psum | solution.py:293
  7302.1 11.3 convert_element_type.212
  (309 shorter events, 152.0 us)
Async XLA Ops:
  7.2 181.7 %copy-start = (s32[1,2048]{1,0:T(1,128)S(1)}, s32[1,2048]{1,0:T(1,128)}, u32[]{:S(2)}) copy-start(s32[1,2048]{1,0:T(1,128)} %param.18) | copy-start | bytes 24580
  7.2 43.7 all-gather.19.cloned.1.call-start
  7.9 132.0 %all-gather.17.cloned.1.call-start = ((), (), s32[]{:S(2)}) async-start(), calls=%async_computation.14 | async-start | bytes 11141120 | tf_op jit(solution)/shard_map/all_gather | solution.py:100
  8.7 170.6 %all-gather.21.cloned.1.call-start = ((), (), s32[]{:S(2)}) async-start(), calls=%async_computation.16 | async-start | bytes 1392640 | tf_op jit(solution)/shard_map/all_gather | solution.py:102
  9.4 212.2 %all-gather.43.cloned.1.call-start = ((), (), s32[]{:S(2)}) async-start(), calls=%async_computation.27 | async-start | bytes 1114112 | tf_op jit(solution)/shard_map/all_gather | solution.py:120
  10.0 247.6 %all-gather.23.cloned.1.call-start = ((), (), s32[]{:S(2)}) async-start(), calls=%async_computation.17 | async-start | bytes 1114112 | tf_op jit(solution)/shard_map/all_gather | solution.py:141
  11.3 134.4 %copy-start.55 = (f32[128]{0:T(128)}, f32[128]{0:T(128)S(1)}, u32[]{:S(2)}) copy-start(f32[128]{0:T(128)S(1)} %fusion.82) | copy-start | bytes 1540
  11.3 169.6 %copy-start.65 = (f32[128]{0:T(128)}, f32[128]{0:T(128)S(1)}, u32[]{:S(2)}) copy-start(f32[128]{0:T(128)S(1)} %multiply_power_fusion) | copy-start | bytes 1540
  35.0 146.0 %copy-start.61 = (f32[128]{0:T(128)}, f32[128]{0:T(128)S(1)}, u32[]{:S(2)}) copy-start(f32[128]{0:T(128)S(1)} %get-tuple-element.36) | copy-start | bytes 1540
  35.0 110.7 %copy-start.34 = (f32[16,1,128]{2,1,0:T(1,128)}, f32[16,1,128]{2,1,0:T(1,128)S(1)}, u32[]{:S(2)}) copy-start(f32[16,1,128]{2,1,0:T(1,128)S(1)} %convert_add_fusion.1) | copy-start | bytes 24580
  52.6 126.7 %copy-start.41 = (bf16[128,256]{1,0:T(8,128)(2,1)}, bf16[128,256]{1,0:T(8,128)(2,1)S(1)}, u32[]{:S(2)}) copy-start(bf16[128,256]{1,0:T(8,128)(2,1)S(1)} %convolution_convert_fusion.6) | copy-start | bytes 196612
  182.6 114.4 %all-gather.25.cloned.1.call-start = ((), (), s32[]{:S(2)}) async-start(), calls=%async_computation.18 | async-start | bytes 1114112 | tf_op jit(solution)/shard_map/all_gather | solution.py:142
  183.3 152.8 %all-gather.29.cloned.1.call-start = ((), (), s32[]{:S(2)}) async-start(), calls=%async_computation.20 | async-start | bytes 1114112 | tf_op jit(solution)/shard_map/all_gather | solution.py:104
  184.1 228.0 %all-gather.27.cloned.1.call-start = ((), (), s32[]{:S(2)}) async-start(), calls=%async_computation.19 | async-start | bytes 8912896 | tf_op jit(solution)/shard_map/all_gather | solution.py:103
  184.8 265.6 %all-gather.31.cloned.1.call-start = ((), (), s32[]{:S(2)}) async-start(), calls=%async_computation.21 | async-start | bytes 1114112 | tf_op jit(solution)/shard_map/all_gather | solution.py:105
  185.6 303.8 %all-gather.35.cloned.1.call-start = ((), (), s32[]{:S(2)}) async-start(), calls=%async_computation.23 | async-start | bytes 1114112 | tf_op jit(solution)/shard_map/all_gather | solution.py:112
  186.2 629.9 %all-gather.39.cloned.1.call-start = ((), (), s32[]{:S(2)}) async-start(), calls=%async_computation.25 | async-start | bytes 71303168 | tf_op jit(solution)/shard_map/all_gather | solution.py:118
  186.9 1272.8 %all-gather.33.cloned.1.call-start = ((), (), s32[]{:S(2)}) async-start(), calls=%async_computation.22 | async-start | bytes 142606336 | tf_op jit(solution)/shard_map/all_gather | solution.py:111
  187.5 1401.3 %all-gather.37.cloned.1.call-start = ((), (), s32[]{:S(2)}) async-start(), calls=%async_computation.24 | async-start | bytes 17825792 | tf_op jit(solution)/shard_map/all_gather | solution.py:113
  188.2 1475.7 %all-gather.41.cloned.1.call-start = ((), (), s32[]{:S(2)}) async-start(), calls=%async_computation.26 | async-start | bytes 8912896 | tf_op jit(solution)/shard_map/all_gather | solution.py:119
  188.8 1640.7 %reduce-scatter.17.cloned.1.call-start = ((), (), s32[]{:S(2)}) async-start(), calls=%async_computation.28 | async-start | bytes 2228224 | tf_op jit(solution)/shard_map/reduce_scatter | solution.py:251
  209.4 242.7 %copy-start.50 = (f32[16,1,128]{2,1,0:T(1,128)}, f32[16,1,128]{2,1,0:T(1,128)S(1)}, u32[]{:S(2)}) copy-start(f32[16,1,128]{2,1,0:T(1,128)S(1)} %convert_add_fusion) | copy-start | bytes 24580
  267.0 145.1 %copy-start.6 = (bf16[1,128,2048]{2,1,0:T(8,128)(2,1)S(1)}, bf16[1,128,2048]{2,1,0:T(8,128)(2,1)}, u32[]{:S(2)}) copy-start(bf16[1,128,2048]{2,1,0:T(8,128)(2,1)} %param.17) | copy-start | bytes 1572868
  302.2 114.6 %copy-start.11 = (bf16[128,2048]{1,0:T(8,128)(2,1)}, bf16[128,2048]{1,0:T(8,128)(2,1)S(1)}, u32[]{:S(2)}) copy-start(bf16[128,2048]{1,0:T(8,128)(2,1)S(1)} %convert_element_type.177) | copy-start | bytes 1572868
  337.6 114.5 %copy-start.28 = (bf16[128,256]{1,0:T(8,128)(2,1)}, bf16[128,256]{1,0:T(8,128)(2,1)S(1)}, u32[]{:S(2)}) copy-start(bf16[128,256]{1,0:T(8,128)(2,1)S(1)} %convolution_convert_fusion.5) | copy-start | bytes 196612
  452.1 398.7 %copy-start.70 = (f32[128]{0:T(128)}, f32[128]{0:T(128)S(1)}, u32[]{:S(2)}) copy-start(f32[128]{0:T(128)S(1)} %get-tuple-element.62) | copy-start | bytes 1540
  452.1 398.7 %copy-start.58 = (f32[128]{0:T(128)}, f32[128]{0:T(128)S(1)}, u32[]{:S(2)}) copy-start(f32[128]{0:T(128)S(1)} %fusion.83) | copy-start | bytes 1540
  453.2 1327.0 %copy-start.13 = (bf16[128,2048]{1,0:T(8,128)(2,1)}, bf16[128,2048]{1,0:T(8,128)(2,1)S(1)}, u32[]{:S(2)}) copy-start(bf16[128,2048]{1,0:T(8,128)(2,1)S(1)} %multiply_convert_fusion.3) | copy-start | bytes 1572868
  490.9 1097.9 %copy-start.32 = (bf16[128,256]{1,0:T(8,128)(2,1)}, bf16[128,256]{1,0:T(8,128)(2,1)S(1)}, u32[]{:S(2)}) copy-start(bf16[128,256]{1,0:T(8,128)(2,1)S(1)} %convolution_convert_fusion.4) | copy-start | bytes 196612
  1769.5 125.2 %reduce-scatter.19.cloned.1.call-start = ((), (), s32[]{:S(2)}) async-start(), calls=%async_computation.29 | async-start | bytes 2228224 | tf_op jit(solution)/shard_map/reduce_scatter | solution.py:252
  1776.5 315.2 %reduce-scatter.29.cloned.1.call-start = ((), (), s32[]{:S(2)}) async-start(), calls=%async_computation.34 | async-start | bytes 2228224 | tf_op jit(solution)/shard_map/reduce_scatter | solution.py:281
  1778.4 314.9 %reduce-scatter.31.cloned.1.call-start = ((), (), s32[]{:S(2)}) async-start(), calls=%async_computation.35 | async-start | bytes 2228224 | tf_op jit(solution)/shard_map/reduce_scatter | solution.py:287
  1780.2 314.6 %reduce-scatter.35.cloned.1.call-start = ((), (), s32[]{:S(2)}) async-start(), calls=%async_computation.37 | async-start | bytes 2228224 | tf_op jit(solution)/shard_map/reduce_scatter | solution.py:202
  1782.1 370.4 %reduce-scatter.41.cloned.1.call-start = ((), (), s32[]{:S(2)}) async-start(), calls=%async_computation.40 | async-start | bytes 2228224 | tf_op jit(solution)/shard_map/reduce_scatter | solution.py:217
  1790.2 107.6 %copy-start.7 = (bf16[1,128,2048]{2,1,0:T(8,128)(2,1)S(1)}, bf16[1,128,2048]{2,1,0:T(8,128)(2,1)}, u32[]{:S(2)}) copy-start(bf16[1,128,2048]{2,1,0:T(8,128)(2,1)} %param.17) | copy-start | bytes 1572868
  1790.2 107.6 %copy-start.35 = (f32[16,1,128]{2,1,0:T(1,128)S(1)}, f32[16,1,128]{2,1,0:T(1,128)}, u32[]{:S(2)}) copy-start(f32[16,1,128]{2,1,0:T(1,128)} %copy-done.34) | copy-start | bytes 24580
  1790.2 107.6 %copy-start.56 = (f32[128]{0:T(128)S(1)}, f32[128]{0:T(128)}, u32[]{:S(2)}) copy-start(f32[128]{0:T(128)} %copy-done.55) | copy-start | bytes 1540
  1790.2 427.1 %reduce-scatter.23.cloned.1.call-start = ((), (), s32[]{:S(2)}) async-start(), calls=%async_computation.31 | async-start | bytes 2228224 | tf_op jit(solution)/shard_map/reduce_scatter | solution.py:272
  1795.2 104.5 %copy-start.42 = (bf16[128,256]{1,0:T(8,128)(2,1)S(1)}, bf16[128,256]{1,0:T(8,128)(2,1)}, u32[]{:S(2)}) copy-start(bf16[128,256]{1,0:T(8,128)(2,1)} %copy-done.41) | copy-start | bytes 196612
  1795.9 125.5 %copy-start.17 = (bf16[128,8,256]{0,2,1:T(8,128)(2,1)}, bf16[128,8,256]{0,2,1:T(8,128)(2,1)S(1)}, u32[]{:S(2)}) copy-start(bf16[128,8,256]{0,2,1:T(8,128)(2,1)S(1)} %copy.57) | copy-start | bytes 1572868
  1899.7 385.3 %reduce-scatter.25.cloned.1.call-start = ((), (), s32[]{:S(2)}) async-start(), calls=%async_computation.32 | async-start | bytes 2785280 | tf_op jit(solution)/shard_map/reduce_scatter | solution.py:275
  1901.8 566.0 %reduce-scatter.27.cloned.1.call-start = ((), (), s32[]{:S(2)}) async-start(), calls=%async_computation.33 | async-start | bytes 17825792 | tf_op jit(solution)/shard_map/reduce_scatter | solution.py:278
  1910.8 739.2 %reduce-scatter.39.cloned.1.call-start = ((), (), s32[]{:S(2)}) async-start(), calls=%async_computation.39 | async-start | bytes 17825792 | tf_op jit(solution)/shard_map/reduce_scatter | solution.py:211
  1921.4 943.2 %reduce-scatter.21.cloned.1.call-start = ((), (), s32[]{:S(2)}) async-start(), calls=%async_computation.30 | async-start | bytes 22282240 | tf_op jit(solution)/shard_map/reduce_scatter | solution.py:269
  1931.2 1270.0 %reduce-scatter.37.cloned.1.call-start = ((), (), s32[]{:S(2)}) async-start(), calls=%async_computation.38 | async-start | bytes 35651584 | tf_op jit(solution)/shard_map/reduce_scatter | solution.py:208
  1951.4 2489.8 %reduce-scatter.43.cloned.1.call-start = ((), (), s32[]{:S(2)}) async-start(), calls=%async_computation.41 | async-start | bytes 142606336
  1998.7 4906.5 %reduce-scatter.33.cloned.1.call-start = ((), (), s32[]{:S(2)}) async-start(), calls=%async_computation.36 | async-start | bytes 285212672 | tf_op jit(solution)/shard_map/reduce_scatter | solution.py:192
  2091.6 5187.6 %all-reduce.8.cloned.1.call-start = ((), (), s32[]{:S(2)}) async-start(), calls=%async_computation.42 | async-start | bytes 31490048 | tf_op jit(solution)/shard_map/psum | solution.py:293
  (56 other events, 1191.3 us)
Sparse Core Ops, SparseCore 0:
  10.2 40.6 all-gather.18
  53.1 86.7 all-gather.16
  142.3 36.9 all-gather.20
  181.3 36.7 all-gather.42
  220.7 36.8 all-gather.22
  260.1 36.8 all-gather.24
  299.2 36.8 all-gather.28
  338.2 73.7 all-gather.26
  414.3 36.1 all-gather.30
  452.5 36.8 all-gather.34
  491.0 325.0 all-gather.38
  817.5 642.1 all-gather.32
  1461.9 126.8 all-gather.36
  1590.8 73.0 all-gather.40
  1769.6 59.7 reduce-scatter.16
  1834.1 60.5 reduce-scatter.18
  1898.3 60.5 reduce-scatter.28
  1962.9 60.5 reduce-scatter.30
  2027.3 60.4 reduce-scatter.34
  2091.9 60.5 reduce-scatter.40
  2156.8 60.4 reduce-scatter.22
  2222.1 62.8 reduce-scatter.24
  2290.3 177.5 reduce-scatter.26
  2472.4 177.5 reduce-scatter.38
  2654.7 209.8 reduce-scatter.20
  2869.3 331.8 reduce-scatter.36
  3205.9 1235.2 reduce-scatter.42
  4446.0 2459.1 reduce-scatter.32
  6914.2 365.0 all-reduce.7
where the time goes:
time: 7330 us; the launch traced here: 7320 us
  waiting for transfers between devices  6600 us (90%)
  matrix products  487 us (7%)
  blocking collectives  105 us (1%)
  other arithmetic  85.8 us (1%)
    reduce_scatter x1, waiting for transfers between devices, body(): lax.psum_scatter(transposed_left(norm_two_low, grad_gate_up), 'ctx', scat...  2460 us
    unnamed x30, waiting for transfers between devices  1250 us
    all_gather x1, waiting for transfers between devices, fetch_gate(): lax.all_gather(gate_up_matrix, 'ctx', axis=0, tiled=True)  609 us
    reduce_scatter x1, waiting for transfers between devices, body(): lax.psum_scatter(transposed_left(inner_gate_up, grad_gate_up), 'ctx', sca...  334 us
    all_gather x1, waiting for transfers between devices, fetch_down(): lax.all_gather(down_matrix, 'ctx', axis=0, tiled=True)  325 us
    psum x1, waiting for transfers between devices, body(): lax.psum(attn_grads[1].astype(jnp.bfloat16), 'grp').astype(jnp.float32)  259 us
    reduce_scatter x1, waiting for transfers between devices, body(): lax.psum_scatter(transposed_left(norm_one_low, grad_qkv), 'ctx', scatter_...  212 us
    dot_general x14, matrix products, transposed_left(): lax.dot_general(left_arg, right_arg, (((0,), (0,)), ((), ())), preferred_...  207 us
  transfers between devices with their start and end apart: 29, of which 25 were waited for; matrix products, arithmetic and copies ran while one was open for 6% of the time, Pallas kernels for 0%

commit v1 on v0

v1 whole, which is shorter than its diff:
```python
import functools

import jax
import jax.numpy as jnp
from jax import lax
from jax.experimental import pallas as pl
from jax.experimental.pallas import tpu as pltpu
from jax.sharding import PartitionSpec as P

HEADS = 8
HD = 256
norm_eps = 1e-06
rope_base = 10000.0
BF = jnp.bfloat16
F32 = jnp.float32


def mm(a, b, ca=1, cb=0):
    return lax.dot_general(a, b, (((ca,), (cb,)), ((), ())), preferred_element_type=F32)


def rotate(vectors, cosine, sine_rows):
    front, back = jnp.split(vectors, 2, axis=-1)
    return jnp.concatenate(
        [front * cosine - back * sine_rows, back * cosine + front * sine_rows], axis=-1
    )


def inv_rms(values):
    return lax.rsqrt(jnp.mean(values * values, axis=-1, keepdims=True) + norm_eps)


def norm_back(values, inv, gain, grad):
    weighted = grad * (1.0 + gain)
    inner = jnp.mean(weighted * values, axis=-1, keepdims=True)
    return inv * weighted - values * (inv * inv * inv) * inner


def after(value, *others):
    return lax.optimization_barrier((value,) + others)[0]


def deal_kernel(plane_ref, *refs):
    out_ref = refs[-1]
    each = out_ref.shape[0]
    for k in range(each):
        w_ref, b_ref = refs[k], refs[each + k]
        w_rows = w_ref.shape[0]
        out_ref[k, :w_rows] = w_ref[...]
        out_ref[k, w_rows:] = b_ref[...]


def deal_out(part, plane, matrix, second, n):
    w_rows, r_rows = matrix.shape[0], second.shape[0]
    cols = matrix.shape[1] // (4 * n)
    each = 4

    def column(k, s, plane_ref):
        return (0, (part * n + s * each + k) * 2 + plane_ref[0])

    maps = [functools.partial(column, k) for k in range(each)]
    return pl.pallas_call(
        deal_kernel,
        out_shape=jax.ShapeDtypeStruct((n, w_rows + r_rows, cols), BF),
        grid_spec=pltpu.PrefetchScalarGridSpec(
            num_scalar_prefetch=1,
            grid=(n // each,),
            in_specs=[pl.BlockSpec((w_rows, cols), m) for m in maps]
            + [pl.BlockSpec((r_rows, cols), m) for m in maps],
            out_specs=pl.BlockSpec((each, w_rows + r_rows, cols), lambda s, p: (s, 0, 0)),
        ),
        cost_estimate=pl.CostEstimate(
            flops=0, transcendentals=0, bytes_accessed=4 * n * (w_rows + r_rows) * cols
        ),
    )(plane, *([matrix] * each), *([second] * each))


def fold_kernel(gate_ref, up_ref, b_gate_ref, b_up_ref, a_ref, *refs):
    out_ref = refs[-1]
    each, w_rows = gate_ref.shape[0], a_ref.shape[0] // gate_ref.shape[0]
    cols = b_gate_ref.shape[1]
    gate = mm(a_ref[...], b_gate_ref[...])
    up = mm(a_ref[...], b_up_ref[...])
    for k in range(each):
        part = slice(k * w_rows, (k + 1) * w_rows)
        out_ref[part, :cols] = (gate_ref[k, :w_rows].astype(F32) + gate[part]).astype(BF)
        out_ref[part, cols:] = (up_ref[k, :w_rows].astype(F32) + up[part]).astype(BF)


def fold(gate, up, first, place, given):
    n, ext, cols = gate.shape
    width, rank = first.shape
    w_rows = width // n
    each = max(1, min(4, 512 // w_rows))
    seconds = [x[:, w_rows:].reshape(rank, cols) for x in (gate, up)]
    piece = pl.BlockSpec((each, ext, cols), lambda s: (s, 0, 0))
    whole = pl.BlockSpec((rank, cols), lambda s: (0, 0))
    held = [] if given is None else [given]
    return pl.pallas_call(
        fold_kernel,
        out_shape=jax.ShapeDtypeStruct((width, 4 * cols), BF),
        grid=(n // each,),
        in_specs=[piece, piece, whole, whole]
        + [pl.BlockSpec((each * w_rows, rank), lambda s: (s, 0))]
        + [pl.BlockSpec(memory_space=pl.ANY)] * len(held),
        out_specs=pl.BlockSpec((each * w_rows, 2 * cols), lambda s: (s, place)),
        input_output_aliases={5: 0} if held else {},
        cost_estimate=pl.CostEstimate(
            flops=4 * width * rank * cols, transcendentals=0, bytes_accessed=8 * width * cols
        ),
    )(gate, up, *seconds, first, *held), seconds


def forward_kernel(x_ref, w_ref, hidden_ref, act_ref, slope_ref):
    h = hidden_ref.shape[1] // 2
    c = 0.7978845608028654
    for k in (0, 1):
        both = mm(x_ref[...], w_ref[:, 2 * k * h : 2 * (k + 1) * h])
        gate, up = both[:, :h], both[:, h:]
        square = gate * gate
        t = jnp.tanh(c * gate * (1.0 + 0.044715 * square))
        half_up = 0.5 * (1.0 + t)
        act = gate * half_up
        slope = half_up + 0.5 * gate * (1.0 - t * t) * (c * (1.0 + 3 * 0.044715 * square))
        part = slice(k * h, (k + 1) * h)
        hidden_ref[:, part] = (act * up).astype(BF)
        act_ref[:, part] = act.astype(BF)
        slope_ref[:, part] = (slope * up).astype(BF)


def forward(x, w):
    t, d = x.shape
    f = w.shape[1] // 2
    tile = 256
    out = pl.BlockSpec((tile, f), lambda i: (i, 0))
    return pl.pallas_call(
        forward_kernel,
        out_shape=(jax.ShapeDtypeStruct((t, f), BF),) * 3,
        grid=(t // tile,),
        in_specs=[
            pl.BlockSpec((tile, d), lambda i: (i, 0)),
            pl.BlockSpec((d, 2 * f), lambda i: (0, 0)),
        ],
        out_specs=(out,) * 3,
        compiler_params=pltpu.CompilerParams(vmem_limit_bytes=44 * 2**20),
        cost_estimate=pl.CostEstimate(
            flops=4 * t * d * f, transcendentals=t * f, bytes_accessed=2 * (t * d + 2 * d * f + 3 * t * f)
        ),
    )(x, w)


def backward_kernel(dy_ref, w_ref, act_ref, slope_ref, out_ref):
    h = act_ref.shape[1] // 2
    for k in (0, 1):
        part = slice(k * h, (k + 1) * h)
        grad = mm(dy_ref[...], w_ref[part, :], 1, 1)
        out_ref[:, 2 * k * h : (2 * k + 1) * h] = (grad * slope_ref[:, part].astype(F32)).astype(BF)
        out_ref[:, (2 * k + 1) * h : 2 * (k + 1) * h] = (
            grad * act_ref[:, part].astype(F32)
        ).astype(BF)


def backward(dy, w, act, slope):
    t, d = dy.shape
    f = w.shape[0]
    tile = 256
    given = pl.BlockSpec((tile, f), lambda i: (i, 0))
    return pl.pallas_call(
        backward_kernel,
        out_shape=jax.ShapeDtypeStruct((t, 2 * f), BF),
        grid=(t // tile,),
        in_specs=[
            pl.BlockSpec((tile, d), lambda i: (i, 0)),
            pl.BlockSpec((f, d), lambda i: (0, 0)),
            given,
            given,
        ],
        out_specs=pl.BlockSpec((tile, 2 * f), lambda i: (i, 0)),
        compiler_params=pltpu.CompilerParams(vmem_limit_bytes=44 * 2**20),
        cost_estimate=pl.CostEstimate(
            flops=2 * t * d * f, transcendentals=0, bytes_accessed=2 * (t * d + d * f + 4 * t * f)
        ),
    )(dy, w, act, slope)


def collect_kernel(plane_ref, mine, other, *refs):
    w_ref, b_ref = refs[-2:]
    w_rows = w_ref.shape[0]
    each, _, cols = mine.shape
    for plane in (0, 1):

        @pl.when(plane_ref[0] == plane)
        def _():
            for k in range(each):
                for ref, h in ((mine, plane), (other, 1 - plane)):
                    at = slice((2 * k + h) * cols, (2 * k + h + 1) * cols)
                    w_ref[:, at] = ref[k, :w_rows].astype(F32)
                    b_ref[:, at] = ref[k, w_rows:].astype(F32)


def collect(plane, mine, other, w_rows, part, given):
    n, ext, cols = mine.shape
    each = 4
    piece = pl.BlockSpec((each, ext, cols), lambda s, _: (s, 0, 0))
    held = [] if given is None else list(given)
    steps = n // each
    return pl.pallas_call(
        collect_kernel,
        out_shape=(
            jax.ShapeDtypeStruct((w_rows, 4 * n * cols), F32),
            jax.ShapeDtypeStruct((ext - w_rows, 4 * n * cols), F32),
        ),
        grid_spec=pltpu.PrefetchScalarGridSpec(
            num_scalar_prefetch=1,
            grid=(steps,),
            in_specs=[piece, piece] + [pl.BlockSpec(memory_space=pl.ANY)] * len(held),
            out_specs=(
                pl.BlockSpec((w_rows, 2 * cols * each), lambda s, _: (0, part * steps + s)),
                pl.BlockSpec((ext - w_rows, 2 * cols * each), lambda s, _: (0, part * steps + s)),
            ),
        ),
        input_output_aliases={3: 0, 4: 1} if held else {},
        cost_estimate=pl.CostEstimate(
            flops=0, transcendentals=0, bytes_accessed=12 * n * ext * cols
        ),
    )(plane, mine, other, *held)


def stack_kernel(plane_ref, mine, other, w_ref, a_ref):
    width = w_ref.shape[1]
    own = pl.program_id(0) == plane_ref[0]

    @pl.when(own)
    def _():
        w_ref[...] = mine[:, :width].astype(F32)
        a_ref[...] = mine[:, width:].astype(F32)

    @pl.when(jnp.logical_not(own))
    def _():
        w_ref[...] = other[:, :width].astype(F32)
        a_ref[...] = other[:, width:].astype(F32)


def stack(plane, mine, other, width):
    half, cols = mine.shape
    tile = min(half, 128)
    tiles = half // tile
    given = pl.BlockSpec((tile, cols), lambda h, t, _: (t, 0))
    return pl.pallas_call(
        stack_kernel,
        out_shape=(
            jax.ShapeDtypeStruct((2 * half, width), F32),
            jax.ShapeDtypeStruct((2 * half, cols - width), F32),
        ),
        grid_spec=pltpu.PrefetchScalarGridSpec(
            num_scalar_prefetch=1,
            grid=(2, tiles),
            in_specs=[given, given],
            out_specs=(
                pl.BlockSpec((tile, width), lambda h, t, _: (h * tiles + t, 0)),
                pl.BlockSpec((tile, cols - width), lambda h, t, _: (h * tiles + t, 0)),
            ),
        ),
        cost_estimate=pl.CostEstimate(
            flops=0, transcendentals=0, bytes_accessed=16 * half * cols
        ),
    )(plane, mine, other)


def body(
    tokens,
    segments,
    output_cotangent_rows,
    attention_norm_gain,
    query_key_value_matrix,
    query_key_value_adapter_first,
    query_key_value_adapter_second,
    output_matrix,
    output_adapter_first,
    output_adapter_second,
    feed_norm_gain,
    gate_up_matrix,
    gate_up_adapter_first,
    gate_up_adapter_second,
    down_matrix,
    down_adapter_first,
    down_adapter_second,
):
    n = lax.axis_size("ctx")
    me = lax.axis_index("ctx")
    plane = lax.axis_index("grp")
    lines = n // 4
    rows = tokens.shape[1]
    width = tokens.shape[2]
    seq = rows * n
    rank = query_key_value_adapter_first.shape[1]
    qkv_cols = query_key_value_matrix.shape[1]
    feed_dev = down_matrix.shape[0]
    feed_half = feed_dev // 2
    w_rows = width // n
    r_rows = rank // n
    score_scale = HD ** (-0.5)

    def hop(x, k):
        return lax.ppermute(x, "ctx", [(i, i ^ k) for i in range(n)])

    def swap(x):
        return lax.ppermute(x, "grp", [(0, 1), (1, 0)])

    def swap_pieces(x, count):
        each = x.shape[0] // count
        return [swap(x[k * each : (k + 1) * each]) for k in range(count)]

    rel = jnp.arange(n, dtype=jnp.int32)
    rel = me ^ (rel // (2 * lines) + 2 * (rel // lines % 2) + 4 * (rel % lines))

    def reorder(x):
        r = x.shape[0] // n
        order = [4 * k + 2 * j + i for i in (0, 1) for j in (0, 1) for k in range(lines)]
        return jnp.concatenate(
            [lax.dynamic_slice_in_dim(x, (me ^ k) * r, r) for k in order], axis=0
        )

    def lines_of(x):
        return [x] + [hop(x, 4 * k) for k in range(1, lines)]

    def gather_lines(along):
        near = jnp.concatenate(along + [hop(b, 2) for b in along], axis=0)
        return jnp.concatenate([near, hop(near, 1)], axis=0)

    def gather(x):
        return gather_lines(lines_of(x))

    def scatter_halves(near, far):
        arrived = hop(far, 1)
        r = near.shape[0] // (2 * lines)
        mine = [None] * (2 * lines)
        for k in range(2 * lines):
            part = slice(k * r, (k + 1) * r)
            mine[k] = near[part].astype(F32) + arrived[part].astype(F32)
        total = None
        for k in list(range(1, lines)) + [0]:
            side = hop(mine[lines + k].astype(near.dtype), 2)
            here = mine[k] + side.astype(F32)
            if k:
                here = hop(here.astype(near.dtype), 4 * k).astype(F32)
            total = here if total is None else total + here
        return total

    def scatter(partial):
        kind = partial.dtype
        half = partial.shape[0] // 2
        mine = partial[:half].astype(F32) + hop(partial[half:], 1).astype(F32)
        half = half // 2
        mine = mine[:half] + hop(mine[half:].astype(kind), 2).astype(F32)
        r = half // lines
        total = mine[:r]
        for k in range(1, lines):
            total = total + hop(mine[k * r : (k + 1) * r].astype(kind), 4 * k).astype(F32)
        return total

    x = tokens[0].astype(F32)
    dy = output_cotangent_rows[0]
    plane_id = plane.astype(jnp.int32).reshape(1)
    ext = w_rows + r_rows

    def beside(second):
        return second.reshape(w_rows, second.shape[1] * r_rows // w_rows)

    def apart(columns):
        return columns.reshape(rank, columns.shape[1] * w_rows // r_rows)

    q_second = qkv_cols * r_rows // w_rows
    o_second = width * r_rows // w_rows
    at_q = qkv_cols + rank
    pad = -(at_q + q_second) % 128
    gains = jnp.concatenate(
        [
            attention_norm_gain[:, None],
            feed_norm_gain[:, None],
            jnp.zeros((w_rows, pad - 2), BF),
        ],
        axis=1,
    )
    qkv_ext = jnp.concatenate(
        [
            query_key_value_matrix,
            query_key_value_adapter_first,
            beside(query_key_value_adapter_second),
            gains,
        ],
        axis=1,
    )
    qkv_got = lax.all_gather(qkv_ext, "ctx", axis=0, tiled=True)
    out_ext = jnp.concatenate(
        [
            output_matrix,
            output_adapter_first,
            gate_up_adapter_first,
            beside(output_adapter_second),
            beside(down_adapter_second),
        ],
        axis=1,
    )
    out_got = lax.all_gather(out_ext, "ctx", axis=0, tiled=True)
    qkv_full = qkv_got[:, :at_q]
    qkv_second = apart(qkv_got[:, at_q : at_q + q_second])
    gains_full = qkv_got[:, at_q + q_second : at_q + q_second + 2].astype(F32).T
    attn_gain, feed_gain = gains_full[:1], gains_full[1:]
    out_full = out_got[:, : width + rank]
    gate_up_first = out_got[:, width + rank : width + 2 * rank]
    out_second = apart(out_got[:, width + 2 * rank : width + 2 * rank + o_second])
    down_second = apart(out_got[:, width + 2 * rank + o_second :])

    def exchange(pieces):
        flat = pieces.reshape(n * ext, feed_half)
        return lax.all_to_all(flat, "ctx", 0, 0, tiled=True).reshape(n, ext, feed_half)

    gate_mine = exchange(deal_out(0, plane_id, gate_up_matrix, gate_up_adapter_second, n))
    up_sent = deal_out(1, plane_id, gate_up_matrix, gate_up_adapter_second, n)

    def own_first(x):
        pair = x.reshape(2, feed_half, x.shape[1])
        a = lax.dynamic_index_in_dim(pair, plane, 0, False)
        b = lax.dynamic_index_in_dim(pair, 1 - plane, 0, False)
        return jnp.concatenate([a, b], axis=0)

    down_first = own_first(down_adapter_first)
    down_eff = (own_first(down_matrix).astype(F32) + mm(down_first, down_second)).astype(BF)

    def positions(device):
        within = jnp.arange(rows, dtype=jnp.int32)
        half = rows // 2
        block = jnp.where(within < half, device[:, None], 2 * n - 1 - device[:, None])
        return block * half + within % half

    local_pos = positions(me[None])[0]
    key_pos = positions(rel).reshape(seq)
    half = rows // 2
    local_seg = jnp.concatenate(
        [
            lax.dynamic_slice_in_dim(segments[0], me * half, half),
            lax.dynamic_slice_in_dim(segments[0], (2 * n - 1 - me) * half, half),
        ]
    )
    doc_start = jnp.sum(
        (segments[0][None, :] < local_seg[:, None]).astype(jnp.int32), axis=1
    )
    allowed = (key_pos[None, :] >= doc_start[:, None]) & (key_pos[None, :] <= local_pos[:, None])
    frequency = rope_base ** (-2.0 * jnp.arange(HD // 2, dtype=F32) / HD)
    angle_rows = local_pos.astype(F32)[:, None] * frequency[None, :]
    cosine, sine_rows = jnp.cos(angle_rows), jnp.sin(angle_rows)

    inv_one = inv_rms(x)
    norm_one = (x * inv_one * (1.0 + attn_gain)).astype(BF)
    norm_one = after(norm_one, gate_mine, up_sent)
    qkv_base = mm(norm_one, qkv_full)
    inner_qkv = qkv_base[:, qkv_cols:].astype(BF)
    qkv = qkv_base[:, :qkv_cols] + mm(inner_qkv, qkv_second)
    q = rotate(
        qkv[:, :width].reshape(rows, HEADS, HD), cosine[:, None, :], sine_rows[:, None, :]
    ).astype(BF)
    q_flat = q.reshape(rows * HEADS, HD)
    k_mine = rotate(qkv[:, width : width + HD], cosine, sine_rows).astype(BF)
    kv_mine = jnp.concatenate([k_mine, qkv[:, width + HD :].astype(BF)], axis=1)
    kv_all = gather(kv_mine)
    dy_got = lax.all_gather(after(dy, kv_mine), "ctx", axis=0, tiled=True)
    up_mine = exchange(after(up_sent, kv_all))
    gate_pieces = swap_pieces(gate_mine, 2)
    kv_all = after(kv_all, gate_pieces[0])
    k_all, v_all = kv_all[:, :HD], kv_all[:, HD:]
    raw = mm(q_flat, k_all, 1, 1).reshape(rows, HEADS, seq) * score_scale
    scores = jnp.where(allowed[:, None, :], raw, -jnp.inf)
    peak = jnp.max(scores, axis=-1, keepdims=True)
    unnormed = jnp.exp(scores - peak)
    total = jnp.sum(unnormed, axis=-1, keepdims=True)
    probs = (unnormed / total).astype(BF).reshape(rows * HEADS, seq)
    attended_f = mm(after(probs, gate_pieces[1]), v_all)
    gate_other = jnp.concatenate(gate_pieces, axis=0)
    attended = attended_f.reshape(rows, width).astype(BF)
    attended = after(attended, up_mine)
    up_pieces = swap_pieces(up_mine, 2)
    out_base = mm(attended, out_full)
    inner_out = out_base[:, width:].astype(BF)
    mid = x + out_base[:, :width] + mm(inner_out, out_second)

    inv_two = inv_rms(mid)
    norm_two = (mid * inv_two * (1.0 + feed_gain)).astype(BF)
    all_rows = gather(norm_two)
    all_dy = reorder(dy_got)
    up_other = jnp.concatenate(up_pieces, axis=0)
    w_eff, (gate_b, up_b) = fold(gate_mine, up_mine, gate_up_first, 0, None)
    w_eff, _ = fold(gate_other, up_other, gate_up_first, 1, w_eff)
    hidden, act, slope = forward(all_rows, w_eff)
    h = feed_half
    half_seq = seq // 2
    down_part = mm(hidden[:, h:], all_dy, 0, 0).astype(BF)
    grads = backward(after(all_dy, down_part), down_eff, act, slope)
    down_pieces = swap_pieces(down_part, 4)
    grads = after(grads, down_pieces[0])
    far_part = mm(grads[half_seq:], w_eff, 1, 1).astype(BF)
    near_part = mm(after(grads[:half_seq], far_part, down_pieces[1]), w_eff, 1, 1).astype(BF)
    grad_norm_two = scatter_halves(near_part, far_part)

    late_rows, late_grads = lax.optimization_barrier(
        (all_rows, grads, near_part, down_pieces[2])
    )[:2]
    other_part = mm(late_rows, late_grads[:, 2 * h :], 0, 0).astype(BF)
    gate_pieces, up_pieces = swap_pieces(other_part[:, :h], 4), swap_pieces(other_part[:, h:], 4)
    out_part = mm(after(hidden, other_part, down_pieces[3]), down_eff).astype(BF)
    down_part = jnp.concatenate(down_pieces, axis=0)
    down_half = (
        mm(after(hidden, out_part, gate_pieces[0])[:, :h], all_dy, 0, 0) + down_part.astype(F32)
    ).astype(BF)
    g_down_first = mm(down_half, down_second, 1, 1).astype(BF)
    down_rows = jnp.concatenate([down_half, g_down_first], axis=1)

    pieces = jnp.concatenate(
        [
            norm_one.reshape(rows, n, w_rows),
            inner_qkv.reshape(rows, n, r_rows),
            attended.reshape(rows, n, w_rows),
            inner_out.reshape(rows, n, r_rows),
        ],
        axis=2,
    ).transpose(1, 0, 2)
    pieces = after(pieces, all_rows)
    inputs = lax.all_to_all(pieces.reshape(seq, 2 * ext), "ctx", 0, 0, tiled=True)

    grad_norm_two = after(grad_norm_two, down_rows, inputs, *gate_pieces[:2])
    feed_gain_rows = jnp.sum(grad_norm_two * mid * inv_two, axis=0, keepdims=True)
    grad_mid = dy.astype(F32) + norm_back(mid, inv_two, feed_gain, grad_norm_two)
    grad_branch = grad_mid.astype(BF)
    branch_all = lax.all_gather(grad_branch, "ctx", axis=0, tiled=True)
    grad_inner_out = mm(grad_branch, out_second, 1, 1).astype(BF)
    grad_attended = mm(
        jnp.concatenate([grad_branch, grad_inner_out], axis=1), out_full, 1, 1
    )
    delta = jnp.sum(
        (grad_attended * attended.astype(F32)).reshape(rows * HEADS, HD), axis=1, keepdims=True
    )
    grad_flat = grad_attended.astype(BF).reshape(rows * HEADS, HD)
    gate_part = jnp.concatenate(gate_pieces, axis=0)
    gate_half = (
        mm(after(all_rows, grad_flat), grads[:, :h], 0, 0) + gate_part.astype(F32)
    ).astype(BF)
    gate_second = mm(gate_up_first, gate_half, 0, 0).astype(BF)
    gate_ext = jnp.concatenate(
        [gate_half.reshape(n, w_rows, h), gate_second.reshape(n, r_rows, h)], axis=1
    )
    gate_got = exchange(gate_ext)
    grad_flat = after(grad_flat, gate_ext, up_pieces[0])
    grad_probs = mm(grad_flat, v_all, 1, 1)
    grad_scores = (probs.astype(F32) * (grad_probs - delta)).astype(BF)
    grad_scores = after(grad_scores, up_pieces[1])
    grad_k = mm(grad_scores, q_flat, 0, 0) * score_scale
    grad_v = mm(probs, grad_flat, 0, 0)
    kv_part = jnp.concatenate([grad_k, grad_v], axis=1).astype(BF)
    grad_kv = scatter(kv_part)
    grad_q = mm(after(grad_scores, kv_part, up_pieces[2]), k_all) * score_scale
    grad_q_rows = (
        rotate(grad_q.reshape(rows, HEADS, HD), cosine[:, None, :], -sine_rows[:, None, :])
        .reshape(rows, width)
        .astype(BF)
    )
    q_all = lax.all_gather(grad_q_rows, "ctx", axis=0, tiled=True)
    up_part = jnp.concatenate(up_pieces, axis=0)
    up_half = (
        mm(after(all_rows, grad_q_rows), grads[:, h : 2 * h], 0, 0) + up_part.astype(F32)
    ).astype(BF)
    down_back = swap(after(down_rows, up_half))
    grad_kv = after(grad_kv, up_half, grad_q_rows)
    grad_k_rows = rotate(grad_kv[:, :HD], cosine, -sine_rows)
    grad_kv_rows = jnp.concatenate([grad_k_rows, grad_kv[:, HD:]], axis=1).astype(BF)
    kv_all_grads = gather(grad_kv_rows)
    up_second = mm(gate_up_first, after(up_half, grad_kv_rows), 0, 0).astype(BF)
    up_ext = jnp.concatenate(
        [up_half.reshape(n, w_rows, h), up_second.reshape(n, r_rows, h)], axis=1
    )
    up_ext = after(up_ext, gate_got)
    up_got = exchange(up_ext)
    grad_qkv = jnp.concatenate([grad_q_rows, grad_kv_rows], axis=1)
    grad_qkv = after(grad_qkv, up_ext)
    grad_inner_qkv = mm(grad_qkv, qkv_second, 1, 1).astype(BF)
    grad_norm_one = mm(
        jnp.concatenate([grad_qkv, grad_inner_qkv], axis=1), qkv_full, 1, 1
    )
    attn_gain_rows = jnp.sum(grad_norm_one * x * inv_one, axis=0, keepdims=True)
    grad_input = (grad_mid + norm_back(x, inv_one, attn_gain, grad_norm_one)).astype(BF)
    gate_back = swap_pieces(gate_got, 2)

    def both_planes(own):
        own = own.astype(BF)
        return own.astype(F32) + swap(own).astype(F32)

    g_out = mm(inputs[:, ext:], after(branch_all, grad_input), 0, 0).astype(BF)

    small = jnp.concatenate(
        [
            (mm(gate_half, gate_b, 1, 1) + mm(up_half, up_b, 1, 1))
            .astype(BF)
            .reshape(n, w_rows, rank),
            mm(down_first[:h], after(down_half, g_out), 0, 0)
            .astype(BF)
            .reshape(n, w_rows, width * r_rows // w_rows),
        ],
        axis=2,
    )
    small = after(small, g_out)
    small = scatter(reorder(small.reshape(n * w_rows, small.shape[2])))
    gain_rows = jnp.concatenate([attn_gain_rows, feed_gain_rows], axis=0)
    gain_rows = gain_rows.reshape(2, n, w_rows).transpose(1, 0, 2).reshape(2 * n, w_rows)
    gain_rows = scatter(reorder(gain_rows))

    down_grads = stack(plane_id, down_rows, after(down_back, small), width)
    output = (mid + scatter(after(out_part, kv_all_grads, gate_back[0]))).astype(BF)
    gate_got_other = jnp.concatenate(gate_back, axis=0)
    gate_up_grads = collect(
        plane_id, gate_got, after(gate_got_other, down_grads[0]), w_rows, 0, None
    )
    up_got_other = jnp.concatenate(swap_pieces(up_got, 2), axis=0)
    gate_up_grads = collect(plane_id, up_got, up_got_other, w_rows, 1, gate_up_grads)

    g_q = mm(inputs[:, :ext], q_all, 0, 0)
    inputs_rel = reorder(inputs[:, :ext])
    g_kv = mm(inputs_rel, kv_all_grads, 0, 0)
    g_qkv = jnp.concatenate([g_q, g_kv], axis=1).astype(BF)
    g_out = both_planes(g_out)
    small = both_planes(small)
    g_qkv = both_planes(g_qkv)
    gain_rows = gain_rows + swap(gain_rows)
    g_gu_first = small[:, :rank]
    g_down_second = small[:, rank:].reshape(r_rows, width)
    g_out_first = mm(g_out[:w_rows].astype(BF), out_second, 1, 1)
    g_qkv_first = mm(g_qkv[:w_rows].astype(BF), qkv_second, 1, 1)

    return (
        output[None],
        grad_input[None],
        gain_rows[0],
        g_qkv[:w_rows],
        g_qkv_first,
        g_qkv[w_rows:],
        g_out[:w_rows],
        g_out_first,
        g_out[w_rows:],
        gain_rows[1],
        gate_up_grads[0],
        g_gu_first,
        gate_up_grads[1],
        down_grads[0],
        down_grads[1],
        g_down_second,
    )


def solution(mesh):
    rows = P("grp", "ctx", None)
    vector, matrix = P("ctx"), P("ctx", None)
    return jax.shard_map(
        body,
        mesh=mesh,
        in_specs=(rows, P("grp", None), rows, vector)
        + (matrix,) * 6
        + (vector,)
        + (matrix,) * 6,
        out_specs=(rows, rows, vector) + (matrix,) * 6 + (vector,) + (matrix,) * 6,
        check_vma=False,
    )
```

time: 7330 us -> 1280 us (0.17)
  waiting for transfers between devices: 6600 us -> 647 us
  matrix products: 487 us -> 163 us
  local copies, waits for them, and re-layouts: 25.1 us -> 161 us
  starting transfers between devices: 1.92 us -> 122 us
  blocking collectives: 105 us -> 0 us
  Pallas kernels: 0 us -> 83.4 us
    reduce_scatter x13 -> x0, waiting for transfers between devices: 3650 us -> none  [the longest x1 2460 us: body(): lax.psum_scatter(transposed_left(norm_two_low, grad_gate_up), 'ctx', scat...]
    unnamed x30 -> x5, waiting for transfers between devices: 1250 us -> 0.08 us
    all_gather x14 -> x5, waiting for transfers between devices: 1450 us -> 216 us  [the longest x1 127 us: body(): qkv_got = lax.all_gather(qkv_ext, 'ctx', axis=0, tiled=True)]
    ppermute x0 -> x77, waiting for transfers between devices: none -> 431 us  [the longest x52 272 us: hop(): return lax.ppermute(x, 'ctx', [(i, i ^ k) for i in range(n)])]
    dot_general x42 -> x34, matrix products: 487 us -> 163 us  [mm(): lax.dot_general(a, b, (((ca,), (cb,)), ((), ())), preferred_element_type=...]
    psum x1 -> x0, waiting for transfers between devices: 259 us -> none  [body(): lax.psum(attn_grads[1].astype(jnp.bfloat16), 'grp').astype(jnp.float32)]
    ppermute x0 -> x77, starting transfers between devices: none -> 87.9 us  [the longest x52 61.9 us: hop(): return lax.ppermute(x, 'ctx', [(i, i ^ k) for i in range(n)])]
    pallas_call x0 -> x9, Pallas kernels: none -> 83.4 us  [the longest x1 25.3 us: forward(): pl.pallas_call(forward_kernel, out_shape=(jax.ShapeDtypeStruct((t, f), BF...]
  transfers between devices with their start and end apart: 29 -> 87, of which waited for: 25 -> 32; matrix products, arithmetic and copies ran while one was open for 6% -> 27% of each run, Pallas kernels for 0% -> 7%
where the time goes in v1:
time: 1280 us; the launch traced here: 1260 us
  waiting for transfers between devices  647 us (51%)
  matrix products  163 us (13%)
  local copies, waits for them, and re-layouts  161 us (13%)
  starting transfers between devices  122 us (10%)
  Pallas kernels  83.4 us (7%)
  other arithmetic  70.8 us (6%)
  between operations  16.2 us (1%)
    ppermute x52, waiting for transfers between devices, hop(): return lax.ppermute(x, 'ctx', [(i, i ^ k) for i in range(n)])  272 us
    dot_general x34, matrix products, mm(): lax.dot_general(a, b, (((ca,), (cb,)), ((), ())), preferred_element_type=...  163 us
    ppermute x25, waiting for transfers between devices, swap(): return lax.ppermute(x, 'grp', [(0, 1), (1, 0)])  159 us
    all_gather x1, waiting for transfers between devices, body(): qkv_got = lax.all_gather(qkv_ext, 'ctx', axis=0, tiled=True)  127 us
    all_gather x1, waiting for transfers between devices, body(): out_got = lax.all_gather(out_ext, 'ctx', axis=0, tiled=True)  88.7 us
    unnamed x267, local copies, waits for them, and re-layouts  64.5 us
    ppermute x52, starting transfers between devices, hop(): return lax.ppermute(x, 'ctx', [(i, i ^ k) for i in range(n)])  61.9 us
    all_to_all x4, starting transfers between devices, exchange(): lax.all_to_all(flat, 'ctx', 0, 0, tiled=True).reshape(n, ext, feed_half)  29.8 us
  transfers between devices with their start and end apart: 87, of which 32 were waited for; matrix products, arithmetic and copies ran while one was open for 27% of the time, Pallas kernels for 7%

profile of v1, /device:TPU:0, one launch (start us, length us, event | category | flops | bytes accessed | tf_op | source)
XLA Modules:
  0.0 1263.8 jit_solution(15447620286151222119)
XLA Ops:
  19.7 7.4 all-to-all-start
  32.9 127.4 %all-gather.6.cloned.1.call-done = bf16[2048,3200]{1,0:T(8,128)(2,1)} async-done(((bf16[128,3200]{1,0:T(8,128)(2,1)}), bf16[2048,3200]{1,0:T(8,128)(2,1)}) %all-gather.6.cloned.1.call-update) | async-done | bytes 13107216 | tf_op jit(solution)/shard_map/all_gather | solution.py:394
  169.1 6.8 fusion.3
  184.1 5.9 collective-permute-done.2
  190.6 13.7 %collective-permute-done.1 = bf16[128,512]{1,0:T(8,128)(2,1)S(1)} collective-permute-done((bf16[128,512]{1,0:T(8,128)(2,1)S(1)}, bf16[128,512]{1,0:T(8,128)(2,1)S(1)}, u32[]{:S(2)}, u32[]{:S(2)}) %collective-permute-start.1) | collective-permute-done | bytes 131104 | tf_op jit(solution)/shard_map/ppermute | solution.py:305
  228.8 88.7 %all-gather.8.cloned.1.call-done = bf16[2048,3072]{1,0:T(8,128)(2,1)} async-done(((bf16[128,3072]{1,0:T(8,128)(2,1)}), bf16[2048,3072]{1,0:T(8,128)(2,1)}) %all-gather.8.cloned.1.call-update) | async-done | bytes 12582928 | tf_op jit(solution)/shard_map/all_gather | solution.py:405
  326.5 5.9 fusion.131
  343.6 5.3 fusion.7
  356.8 21.5 %collective-permute-done.12 = bf16[128,2048]{1,0:T(8,128)(2,1)S(1)} collective-permute-done((bf16[128,2048]{1,0:T(8,128)(2,1)S(1)}, bf16[128,2048]{1,0:T(8,128)(2,1)S(1)}, u32[]{:S(2)}, u32[]{:S(2)}) %collective-permute-start.12) | collective-permute-done | bytes 524320 | tf_op jit(solution)/shard_map/ppermute | solution.py:305
  379.8 48.8 %collective-permute-done.11 = bf16[128,2048]{1,0:T(8,128)(2,1)S(1)} collective-permute-done((bf16[128,2048]{1,0:T(8,128)(2,1)S(1)}, bf16[128,2048]{1,0:T(8,128)(2,1)S(1)}, u32[]{:S(2)}, u32[]{:S(2)}) %collective-permute-start.11) | collective-permute-done | bytes 524320 | tf_op jit(solution)/shard_map/ppermute | solution.py:305
  434.3 18.0 %collective-permute-done.14 = bf16[128,2048]{1,0:T(8,128)(2,1)S(1)} collective-permute-done((bf16[128,2048]{1,0:T(8,128)(2,1)S(1)}, bf16[128,2048]{1,0:T(8,128)(2,1)S(1)}, u32[]{:S(2)}, u32[]{:S(2)}) %collective-permute-start.14) | collective-permute-done | bytes 524320 | tf_op jit(solution)/shard_map/ppermute | solution.py:305
  490.8 5.9 add_convert_fusion.w_ref
  498.4 6.7 shard_map.290.refs_0_
  506.4 15.6 %collective-permute-done.19 = bf16[8,144,512]{2,1,0:T(8,128)(2,1)} collective-permute-done((bf16[8,144,512]{2,1,0:T(8,128)(2,1)}, bf16[8,144,512]{2,1,0:T(8,128)(2,1)}, u32[]{:S(2)}, u32[]{:S(2)}) %collective-permute-start.19) | collective-permute-done | bytes 1179680 | tf_op jit(solution)/shard_map/ppermute | solution.py:308
  525.0 6.2 shard_map.291.w_ref
  531.2 25.3 %shard_map.292 = (bf16[2048,1024]{1,0:T(8,128)(2,1)S(1)}, bf16[2048,1024]{1,0:T(8,128)(2,1)S(1)}, bf16[2048,1024]{1,0:T(8,128)(2,1)}) custom-call(bf16[2048,2048]{1,0:T(8,128)(2,1)} %constant_dynamic-update-slice_fusion.30.x_ref, bf16[2048,2048]{1,0:T(8,128)(2,1)} %shard_map.291.w_ref), custom_call_target="tpu_custom_call" | custom-call | flops 17179869184 | bytes 29360128 | tf_op jit(solution)/shard_map/pallas_call | solution.py:136
  584.4 14.7 %shard_map.293 = bf16[2048,2048]{1,0:T(8,128)(2,1)} custom-call(bf16[2048,2048]{1,0:T(8,128)(2,1)} %copy-done.75, bf16[1024,2048]{1,0:T(8,128)(2,1)S(1)} %copy-done, bf16[2048,1024]{1,0:T(8,128)(2,1)S(1)} %copy-done.2, bf16[2048,1024]{1,0:T(8,128)(2,1)} %get-tuple-element.65.slope_ref), custom_call_target="tpu_custom_call" | custom-call | flops 8589934592 | bytes 29360128 | tf_op jit(solution)/shard_map/pallas_call | solution.py:168
  599.1 28.6 %collective-permute-done.20 = bf16[128,2048]{1,0:T(8,128)(2,1)} collective-permute-done((bf16[128,2048]{1,0:T(8,128)(2,1)S(1)}, bf16[128,2048]{1,0:T(8,128)(2,1)}, u32[]{:S(2)}, u32[]{:S(2)}) %collective-permute-start.20) | collective-permute-done | bytes 524320 | tf_op jit(solution)/shard_map/ppermute | solution.py:308
  627.7 13.9 %fusion.17 = bf16[1024,2048]{1,0:T(8,128)(2,1)} fusion(bf16[2048,2048]{1,0:T(8,128)(2,1)} %shard_map.291.w_ref, bf16[2048,2048]{1,0:T(8,128)(2,1)} %shard_map.293), kind=kOutput, calls=%fused_computation.30 | convolution fusion | flops 8592031744 | bytes 16777216 | tf_op jit(solution)/shard_map/dot_general | solution.py:19
  643.8 10.5 convolution_convert_fusion.1
  654.3 12.7 %fusion.20 = bf16[2048,1024]{1,0:T(8,128)(2,1)S(1)} fusion(bf16[2048,2048]{1,0:T(8,128)(2,1)} %constant_dynamic-update-slice_fusion.30.x_ref, bf16[2048,2048]{1,0:T(8,128)(2,1)} %shard_map.293), kind=kOutput, calls=%fused_computation.31 | convolution fusion | flops 8592031744 | bytes 16777216 | tf_op jit(solution)/shard_map/dot_general | solution.py:19
  673.5 10.8 convolution_convert_fusion
  690.3 5.9 add_convert_fusion.3
  696.8 6.3 collective-permute-done.29
  703.2 11.2 collective-permute-done.27
  722.9 22.7 %collective-permute-done.28 = bf16[128,2048]{1,0:T(8,128)(2,1)S(1)} collective-permute-done((bf16[128,2048]{1,0:T(8,128)(2,1)S(1)}, bf16[128,2048]{1,0:T(8,128)(2,1)S(1)}, u32[]{:S(2)}, u32[]{:S(2)}) %collective-permute-start.28) | collective-permute-done | bytes 524320 | tf_op jit(solution)/shard_map/ppermute | solution.py:305
  756.5 8.0 convert_multiply_fusion.5
  765.6 23.0 %collective-permute-done.35 = bf16[512,512]{1,0:T(8,128)(2,1)} collective-permute-done((bf16[512,512]{1,0:T(8,128)(2,1)}, bf16[512,512]{1,0:T(8,128)(2,1)}, u32[]{:S(2)}, u32[]{:S(2)}) %collective-permute-start.35) | collective-permute-done | bytes 524320 | tf_op jit(solution)/shard_map/ppermute | solution.py:308
  788.5 10.2 collective-permute-done.34
  798.7 9.2 add_convert_fusion.2
  816.1 6.2 multiply_convert_fusion
  832.6 13.1 %all-to-all-start.3 = ((bf16[16,144,512]{2,1,0:T(8,128)(2,1)}), bf16[16,144,512]{2,1,0:T(8,128)(2,1)S(1)}, u32[]{:S(2)}, u32[]{:S(2)}) async-start(bf16[16,144,512]{2,1,0:T(8,128)(2,1)} %pad_maximum_fusion.2), calls=%async_computation.3 | async-start | bytes 4718592 | tf_op jit(solution)/shard_map/all_to_all | solution.py:417
  858.9 23.7 %collective-permute-done.39 = bf16[512,512]{1,0:T(8,128)(2,1)} collective-permute-done((bf16[512,512]{1,0:T(8,128)(2,1)}, bf16[512,512]{1,0:T(8,128)(2,1)}, u32[]{:S(2)}, u32[]{:S(2)}) %collective-permute-start.39) | collective-permute-done | bytes 524320 | tf_op jit(solution)/shard_map/ppermute | solution.py:305
  884.2 10.9 collective-permute-start.40
  896.6 10.4 add_convert_fusion.1
  910.1 34.0 %collective-permute-done.41 = bf16[128,512]{1,0:T(8,128)(2,1)S(1)} collective-permute-done((bf16[128,512]{1,0:T(8,128)(2,1)S(1)}, bf16[128,512]{1,0:T(8,128)(2,1)S(1)}, u32[]{:S(2)}, u32[]{:S(2)}) %collective-permute-start.41) | collective-permute-done | bytes 131104 | tf_op jit(solution)/shard_map/ppermute | solution.py:305
  957.9 10.9 collective-permute-done.46
  983.9 25.1 %collective-permute-done.53 = bf16[8,144,512]{2,1,0:T(8,128)(2,1)} collective-permute-done((bf16[8,144,512]{2,1,0:T(8,128)(2,1)}, bf16[8,144,512]{2,1,0:T(8,128)(2,1)}, u32[]{:S(2)}, u32[]{:S(2)}) %collective-permute-start.53) | collective-permute-done | bytes 1179680 | tf_op jit(solution)/shard_map/ppermute | solution.py:308
  1038.0 9.9 fusion.39
  1057.9 5.4 convert_add_fusion
  1083.4 48.1 %collective-permute-done.64 = f32[2,128]{1,0:T(2,128)S(1)} collective-permute-done((f32[2,128]{1,0:T(2,128)S(1)}, f32[2,128]{1,0:T(2,128)S(1)}, u32[]{:S(2)}, u32[]{:S(2)}) %collective-permute-start.64) | collective-permute-done | bytes 1056 | tf_op jit(solution)/shard_map/ppermute | solution.py:308
  1147.4 5.7 convolution_convert_fusion.5
  1164.5 7.4 collective-permute-done.58
  1171.9 20.6 %collective-permute-done.57 = bf16[128,2048]{1,0:T(8,128)(2,1)} collective-permute-done((bf16[128,2048]{1,0:T(8,128)(2,1)}, bf16[128,2048]{1,0:T(8,128)(2,1)}, u32[]{:S(2)}, u32[]{:S(2)}) %collective-permute-start.57) | collective-permute-done | bytes 524320 | tf_op jit(solution)/shard_map/ppermute | solution.py:305
  1197.0 6.3 convolution_convert_fusion.6
  1233.0 9.5 shard_map.294
  1242.5 6.5 shard_map.295
  1248.9 6.5 shard_map.296
  (587 shorter events, 390.8 us)
Async XLA Ops:
  7.2 153.1 %all-gather.6.cloned.1.call-start = ((), (), s32[]{:S(2)}) async-start(), calls=%async_computation.5 | async-start | bytes 13926400 | tf_op jit(solution)/shard_map/all_gather | solution.py:394
  11.8 305.7 %all-gather.8.cloned.1.call-start = ((), (), s32[]{:S(2)}) async-start(), calls=%async_computation.6 | async-start | bytes 13369344 | tf_op jit(solution)/shard_map/all_gather | solution.py:405
  19.7 149.3 %all-to-all-start = ((bf16[16,144,512]{2,1,0:T(8,128)(2,1)}), bf16[16,144,512]{2,1,0:T(8,128)(2,1)S(1)}, u32[]{:S(2)}, u32[]{:S(2)}) async-start(bf16[16,144,512]{2,1,0:T(8,128)(2,1)} %shard_map.288), calls=%async_computation | async-start | bytes 4718592 | tf_op jit(solution)/shard_map/all_to_all | solution.py:417
  219.1 124.4 %all-to-all-start.1 = ((bf16[16,144,512]{2,1,0:T(8,128)(2,1)}), bf16[16,144,512]{2,1,0:T(8,128)(2,1)}, u32[]{:S(2)}, u32[]{:S(2)}) async-start(bf16[16,144,512]{2,1,0:T(8,128)(2,1)} %shard_map.289), calls=%async_computation.1 | async-start | bytes 4718592 | tf_op jit(solution)/shard_map/all_to_all | solution.py:417
  224.1 337.6 %all-gather.10.cloned.1.call-start = ((), (), s32[]{:S(2)}) async-start(), calls=%async_computation.7 | async-start | bytes 8912896 | tf_op jit(solution)/shard_map/all_gather | solution.py:467
  225.8 99.4 %collective-permute-start.8 = (bf16[8,144,512]{2,1,0:T(8,128)(2,1)}, bf16[8,144,512]{2,1,0:T(8,128)(2,1)}, u32[]{:S(2)}, u32[]{:S(2)}) collective-permute-start(bf16[8,144,512]{2,1,0:T(8,128)(2,1)} %get-tuple-element.140), channel_id=1, source_target_pairs={{0,16},{16,0},{1,17},{17,1},{2,18},{18,2},{3,19},{19,3},{4,20},{20... | collective-permute-start | bytes 3538952 | tf_op jit(solution)/shard_map/ppermute | solution.py:308
  228.3 111.1 %collective-permute-start.9 = (bf16[8,144,512]{2,1,0:T(8,128)(2,1)}, bf16[8,144,512]{2,1,0:T(8,128)(2,1)}, u32[]{:S(2)}, u32[]{:S(2)}) collective-permute-start(bf16[8,144,512]{2,1,0:T(8,128)(2,1)} %get-tuple-element.139), channel_id=1, source_target_pairs={{0,16},{16,0},{1,17},{17,1},{2,18},{18,2},{3,19},{19,3},{4,20},{20... | collective-permute-start | bytes 3538952 | tf_op jit(solution)/shard_map/ppermute | solution.py:308
  351.0 27.4 %collective-permute-start.12 = (bf16[128,2048]{1,0:T(8,128)(2,1)S(1)}, bf16[128,2048]{1,0:T(8,128)(2,1)S(1)}, u32[]{:S(2)}, u32[]{:S(2)}) collective-permute-start(bf16[128,2048]{1,0:T(8,128)(2,1)S(1)} %get-tuple-element.111), channel_id=1, source_target_pairs={{0,12},{1,13},{2,14},{3,15},{4,8},{5,9},{6,10},{7,11},{8,4},{9,5},... | collective-permute-start | bytes 1572872 | tf_op jit(solution)/shard_map/ppermute | solution.py:305
  352.5 76.1 %collective-permute-start.11 = (bf16[128,2048]{1,0:T(8,128)(2,1)S(1)}, bf16[128,2048]{1,0:T(8,128)(2,1)S(1)}, u32[]{:S(2)}, u32[]{:S(2)}) collective-permute-start(bf16[128,2048]{1,0:T(8,128)(2,1)S(1)} %get-tuple-element.111), channel_id=1, source_target_pairs={{0,8},{1,9},{2,10},{3,11},{4,12},{5,13},{6,14},{7,15},{8,0},{9,1},... | collective-permute-start | bytes 1572872 | tf_op jit(solution)/shard_map/ppermute | solution.py:305
  352.5 77.9 %collective-permute-start.10 = (bf16[128,2048]{1,0:T(8,128)(2,1)S(1)}, bf16[128,2048]{1,0:T(8,128)(2,1)S(1)}, u32[]{:S(2)}, u32[]{:S(2)}) collective-permute-start(bf16[128,2048]{1,0:T(8,128)(2,1)S(1)} %get-tuple-element.111), channel_id=1, source_target_pairs={{0,4},{1,5},{2,6},{3,7},{4,0},{5,1},{6,2},{7,3},{8,12},{9,13},{10,... | collective-permute-start | bytes 1572872 | tf_op jit(solution)/shard_map/ppermute | solution.py:305
  355.3 78.1 %collective-permute-start.13 = (bf16[128,2048]{1,0:T(8,128)(2,1)S(1)}, bf16[128,2048]{1,0:T(8,128)(2,1)S(1)}, u32[]{:S(2)}, u32[]{:S(2)}) collective-permute-start(bf16[128,2048]{1,0:T(8,128)(2,1)S(1)} %get-tuple-element.111), channel_id=1, source_target_pairs={{0,2},{1,3},{2,0},{3,1},{4,6},{5,7},{6,4},{7,5},{8,10},{9,11},{10,... | collective-permute-start | bytes 1572872 | tf_op jit(solution)/shard_map/ppermute | solution.py:305
  378.3 75.8 %collective-permute-start.16 = (bf16[128,2048]{1,0:T(8,128)(2,1)S(1)}, bf16[128,2048]{1,0:T(8,128)(2,1)S(1)}, u32[]{:S(2)}, u32[]{:S(2)}) collective-permute-start(bf16[128,2048]{1,0:T(8,128)(2,1)S(1)} %collective-permute-done.12), channel_id=1, source_target_pairs={{0,2},{1,3},{2,0},{3,1},{4,6},{5,7},{6,4},{7,5},{8,10},{9,11},{10,... | collective-permute-start | bytes 1572872 | tf_op jit(solution)/shard_map/ppermute | solution.py:305
  468.1 37.0 %collective-permute-start.18 = (bf16[8,144,512]{2,1,0:T(8,128)(2,1)}, bf16[8,144,512]{2,1,0:T(8,128)(2,1)}, u32[]{:S(2)}, u32[]{:S(2)}) collective-permute-start(bf16[8,144,512]{2,1,0:T(8,128)(2,1)} %get-tuple-element.138), channel_id=1, source_target_pairs={{0,16},{16,0},{1,17},{17,1},{2,18},{18,2},{3,19},{19,3},{4,20},{20... | collective-permute-start | bytes 3538952 | tf_op jit(solution)/shard_map/ppermute | solution.py:308
  471.0 51.1 %collective-permute-start.19 = (bf16[8,144,512]{2,1,0:T(8,128)(2,1)}, bf16[8,144,512]{2,1,0:T(8,128)(2,1)}, u32[]{:S(2)}, u32[]{:S(2)}) collective-permute-start(bf16[8,144,512]{2,1,0:T(8,128)(2,1)} %get-tuple-element.137), channel_id=1, source_target_pairs={{0,16},{16,0},{1,17},{17,1},{2,18},{18,2},{3,19},{19,3},{4,20},{20... | collective-permute-start | bytes 3538952 | tf_op jit(solution)/shard_map/ppermute | solution.py:308
  487.0 73.5 %all-to-all-start.2 = ((bf16[16,128,288]{1,2,0:T(8,128)(2,1)}), bf16[16,128,288]{1,2,0:T(8,128)(2,1)S(1)}, u32[]{:S(2)}, u32[]{:S(2)}) async-start(bf16[16,128,288]{1,2,0:T(8,128)(2,1)} %maximum_bitcast_fusion), calls=%async_computation.2 | async-start | bytes 2359296 | tf_op jit(solution)/shard_map/all_to_all | solution.py:528
  490.7 656.6 %all-gather.14.cloned.1.call-start = ((), (), s32[]{:S(2)}) async-start(), calls=%async_computation.9 | async-start | bytes 8912896 | tf_op jit(solution)/shard_map/all_gather | solution.py:534
  580.2 86.8 %collective-permute-start.23 = (bf16[128,2048]{1,0:T(8,128)(2,1)S(1)}, bf16[128,2048]{1,0:T(8,128)(2,1)S(1)}, u32[]{:S(2)}, u32[]{:S(2)}) collective-permute-start(bf16[128,2048]{1,0:T(8,128)(2,1)S(1)} %get-tuple-element.160), channel_id=1, source_target_pairs={{0,16},{16,0},{1,17},{17,1},{2,18},{18,2},{3,19},{19,3},{4,20},{20... | collective-permute-start | bytes 1572872 | tf_op jit(solution)/shard_map/ppermute | solution.py:308
  581.8 72.5 %collective-permute-start.22 = (bf16[128,2048]{1,0:T(8,128)(2,1)S(1)}, bf16[128,2048]{1,0:T(8,128)(2,1)S(1)}, u32[]{:S(2)}, u32[]{:S(2)}) collective-permute-start(bf16[128,2048]{1,0:T(8,128)(2,1)S(1)} %get-tuple-element.161), channel_id=1, source_target_pairs={{0,16},{16,0},{1,17},{17,1},{2,18},{18,2},{3,19},{19,3},{4,20},{20... | collective-permute-start | bytes 1572872 | tf_op jit(solution)/shard_map/ppermute | solution.py:308
  582.3 59.3 %collective-permute-start.21 = (bf16[128,2048]{1,0:T(8,128)(2,1)S(1)}, bf16[128,2048]{1,0:T(8,128)(2,1)S(1)}, u32[]{:S(2)}, u32[]{:S(2)}) collective-permute-start(bf16[128,2048]{1,0:T(8,128)(2,1)S(1)} %get-tuple-element.162), channel_id=1, source_target_pairs={{0,16},{16,0},{1,17},{17,1},{2,18},{18,2},{3,19},{19,3},{4,20},{20... | collective-permute-start | bytes 1572872 | tf_op jit(solution)/shard_map/ppermute | solution.py:308
  583.9 43.8 %collective-permute-start.20 = (bf16[128,2048]{1,0:T(8,128)(2,1)S(1)}, bf16[128,2048]{1,0:T(8,128)(2,1)}, u32[]{:S(2)}, u32[]{:S(2)}) collective-permute-start(bf16[128,2048]{1,0:T(8,128)(2,1)S(1)} %get-tuple-element.163), channel_id=1, source_target_pairs={{0,16},{16,0},{1,17},{17,1},{2,18},{18,2},{3,19},{19,3},{4,20},{20... | collective-permute-start | bytes 1572872 | tf_op jit(solution)/shard_map/ppermute | solution.py:308
  641.6 28.7 %collective-permute-start.24 = (bf16[1024,2048]{1,0:T(8,128)(2,1)}, bf16[1024,2048]{1,0:T(8,128)(2,1)}, u32[]{:S(2)}, u32[]{:S(2)}) collective-permute-start(bf16[1024,2048]{1,0:T(8,128)(2,1)} %fusion.17), channel_id=1, source_target_pairs={{0,1},{1,0},{2,3},{3,2},{4,5},{5,4},{6,7},{7,6},{8,9},{9,8},{10,11... | collective-permute-start | bytes 12582920 | tf_op jit(solution)/shard_map/ppermute | solution.py:305
  684.3 62.9 %collective-permute-start.33 = (bf16[512,512]{1,0:T(8,128)(2,1)S(1)}, bf16[512,512]{1,0:T(8,128)(2,1)S(1)}, u32[]{:S(2)}, u32[]{:S(2)}) collective-permute-start(bf16[512,512]{1,0:T(8,128)(2,1)S(1)} %get-tuple-element.129), channel_id=1, source_target_pairs={{0,16},{16,0},{1,17},{17,1},{2,18},{18,2},{3,19},{19,3},{4,20},{20... | collective-permute-start | bytes 1572872 | tf_op jit(solution)/shard_map/ppermute | solution.py:308
  696.4 26.5 %collective-permute-start.31 = (bf16[128,2048]{1,0:T(8,128)(2,1)S(1)}, bf16[128,2048]{1,0:T(8,128)(2,1)S(1)}, u32[]{:S(2)}, u32[]{:S(2)}) collective-permute-start(bf16[128,2048]{1,0:T(8,128)(2,1)S(1)} %get-tuple-element.118), channel_id=1, source_target_pairs={{0,2},{1,3},{2,0},{3,1},{4,6},{5,7},{6,4},{7,5},{8,10},{9,11},{10,... | collective-permute-start | bytes 1572872 | tf_op jit(solution)/shard_map/ppermute | solution.py:305
  716.1 29.5 %collective-permute-start.28 = (bf16[128,2048]{1,0:T(8,128)(2,1)S(1)}, bf16[128,2048]{1,0:T(8,128)(2,1)S(1)}, u32[]{:S(2)}, u32[]{:S(2)}) collective-permute-start(bf16[128,2048]{1,0:T(8,128)(2,1)S(1)} %get-tuple-element.121), channel_id=1, source_target_pairs={{0,8},{1,9},{2,10},{3,11},{4,12},{5,13},{6,14},{7,15},{8,0},{9,1},... | collective-permute-start | bytes 1572872 | tf_op jit(solution)/shard_map/ppermute | solution.py:305
  716.2 29.4 %collective-permute-start.30 = (bf16[128,2048]{1,0:T(8,128)(2,1)S(1)}, bf16[128,2048]{1,0:T(8,128)(2,1)S(1)}, u32[]{:S(2)}, u32[]{:S(2)}) collective-permute-start(bf16[128,2048]{1,0:T(8,128)(2,1)S(1)} %get-tuple-element.122), channel_id=1, source_target_pairs={{0,12},{1,13},{2,14},{3,15},{4,8},{5,9},{6,10},{7,11},{8,4},{9,5},... | collective-permute-start | bytes 1572872 | tf_op jit(solution)/shard_map/ppermute | solution.py:305
  750.9 71.3 %collective-permute-start.37 = (bf16[512,512]{1,0:T(8,128)(2,1)}, bf16[512,512]{1,0:T(8,128)(2,1)}, u32[]{:S(2)}, u32[]{:S(2)}) collective-permute-start(bf16[512,512]{1,0:T(8,128)(2,1)} %get-tuple-element.125), channel_id=1, source_target_pairs={{0,16},{16,0},{1,17},{17,1},{2,18},{18,2},{3,19},{19,3},{4,20},{20... | collective-permute-start | bytes 1572872 | tf_op jit(solution)/shard_map/ppermute | solution.py:308
  751.5 63.1 %collective-permute-start.36 = (bf16[512,512]{1,0:T(8,128)(2,1)}, bf16[512,512]{1,0:T(8,128)(2,1)}, u32[]{:S(2)}, u32[]{:S(2)}) collective-permute-start(bf16[512,512]{1,0:T(8,128)(2,1)} %get-tuple-element.126), channel_id=1, source_target_pairs={{0,16},{16,0},{1,17},{17,1},{2,18},{18,2},{3,19},{19,3},{4,20},{20... | collective-permute-start | bytes 1572872 | tf_op jit(solution)/shard_map/ppermute | solution.py:308
  753.0 35.6 %collective-permute-start.35 = (bf16[512,512]{1,0:T(8,128)(2,1)}, bf16[512,512]{1,0:T(8,128)(2,1)}, u32[]{:S(2)}, u32[]{:S(2)}) collective-permute-start(bf16[512,512]{1,0:T(8,128)(2,1)} %get-tuple-element.127), channel_id=1, source_target_pairs={{0,16},{16,0},{1,17},{17,1},{2,18},{18,2},{3,19},{19,3},{4,20},{20... | collective-permute-start | bytes 1572872 | tf_op jit(solution)/shard_map/ppermute | solution.py:308
  753.5 45.2 %collective-permute-start.34 = (bf16[512,512]{1,0:T(8,128)(2,1)}, bf16[512,512]{1,0:T(8,128)(2,1)}, u32[]{:S(2)}, u32[]{:S(2)}) collective-permute-start(bf16[512,512]{1,0:T(8,128)(2,1)} %get-tuple-element.128), channel_id=1, source_target_pairs={{0,16},{16,0},{1,17},{17,1},{2,18},{18,2},{3,19},{19,3},{4,20},{20... | collective-permute-start | bytes 1572872 | tf_op jit(solution)/shard_map/ppermute | solution.py:308
  830.7 65.9 %collective-permute-start.44 = (bf16[512,512]{1,0:T(8,128)(2,1)}, bf16[512,512]{1,0:T(8,128)(2,1)}, u32[]{:S(2)}, u32[]{:S(2)}) collective-permute-start(bf16[512,512]{1,0:T(8,128)(2,1)} %get-tuple-element.123), channel_id=1, source_target_pairs={{0,16},{16,0},{1,17},{17,1},{2,18},{18,2},{3,19},{19,3},{4,20},{20... | collective-permute-start | bytes 1572872 | tf_op jit(solution)/shard_map/ppermute | solution.py:308
  832.6 145.9 %all-to-all-start.3 = ((bf16[16,144,512]{2,1,0:T(8,128)(2,1)}), bf16[16,144,512]{2,1,0:T(8,128)(2,1)S(1)}, u32[]{:S(2)}, u32[]{:S(2)}) async-start(bf16[16,144,512]{2,1,0:T(8,128)(2,1)} %pad_maximum_fusion.2), calls=%async_computation.3 | async-start | bytes 4718592 | tf_op jit(solution)/shard_map/all_to_all | solution.py:417
  845.8 351.3 %all-gather.12.cloned.1.call-start = ((), (), s32[]{:S(2)}) async-start(), calls=%async_computation.8 | async-start | bytes 8912896 | tf_op jit(solution)/shard_map/all_gather | solution.py:566
  853.7 28.8 %collective-permute-start.39 = (bf16[512,512]{1,0:T(8,128)(2,1)}, bf16[512,512]{1,0:T(8,128)(2,1)}, u32[]{:S(2)}, u32[]{:S(2)}) collective-permute-start(bf16[512,512]{1,0:T(8,128)(2,1)} %slice.678), channel_id=1, source_target_pairs={{0,2},{1,3},{2,0},{3,1},{4,6},{5,7},{6,4},{7,5},{8,10},{9,11},{10,... | collective-permute-start | bytes 1572872 | tf_op jit(solution)/shard_map/ppermute | solution.py:305
  884.2 26.0 %collective-permute-start.40 = (bf16[128,512]{1,0:T(8,128)(2,1)S(1)}, bf16[128,512]{1,0:T(8,128)(2,1)S(1)}, u32[]{:S(2)}, u32[]{:S(2)}) collective-permute-start(bf16[128,512]{1,0:T(8,128)(2,1)S(1)} %get-tuple-element.179), channel_id=1, source_target_pairs={{0,4},{1,5},{2,6},{3,7},{4,0},{5,1},{6,2},{7,3},{8,12},{9,13},{10,... | collective-permute-start | bytes 393224 | tf_op jit(solution)/shard_map/ppermute | solution.py:305
  895.1 49.0 %collective-permute-start.41 = (bf16[128,512]{1,0:T(8,128)(2,1)S(1)}, bf16[128,512]{1,0:T(8,128)(2,1)S(1)}, u32[]{:S(2)}, u32[]{:S(2)}) collective-permute-start(bf16[128,512]{1,0:T(8,128)(2,1)S(1)} %get-tuple-element.181), channel_id=1, source_target_pairs={{0,8},{1,9},{2,10},{3,11},{4,12},{5,13},{6,14},{7,15},{8,0},{9,1},... | collective-permute-start | bytes 393224 | tf_op jit(solution)/shard_map/ppermute | solution.py:305
  980.3 28.7 %collective-permute-start.53 = (bf16[8,144,512]{2,1,0:T(8,128)(2,1)}, bf16[8,144,512]{2,1,0:T(8,128)(2,1)}, u32[]{:S(2)}, u32[]{:S(2)}) collective-permute-start(bf16[8,144,512]{2,1,0:T(8,128)(2,1)} %get-tuple-element.134), channel_id=1, source_target_pairs={{0,16},{16,0},{1,17},{17,1},{2,18},{18,2},{3,19},{19,3},{4,20},{20... | collective-permute-start | bytes 3538952 | tf_op jit(solution)/shard_map/ppermute | solution.py:308
  1013.7 44.2 %collective-permute-start.54 = (bf16[1024,2048]{1,0:T(8,128)(2,1)}, bf16[1024,2048]{1,0:T(8,128)(2,1)}, u32[]{:S(2)}, u32[]{:S(2)}) collective-permute-start(bf16[1024,2048]{1,0:T(8,128)(2,1)} %slice.439), channel_id=1, source_target_pairs={{0,1},{1,0},{2,3},{3,2},{4,5},{5,4},{6,7},{7,6},{8,9},{9,8},{10,11... | collective-permute-start | bytes 12582920 | tf_op jit(solution)/shard_map/ppermute | solution.py:305
  1018.3 55.0 %all-to-all-start.4 = ((bf16[16,144,512]{2,1,0:T(8,128)(2,1)}), bf16[16,144,512]{2,1,0:T(8,128)(2,1)S(1)}, u32[]{:S(2)}, u32[]{:S(2)}) async-start(bf16[16,144,512]{2,1,0:T(8,128)(2,1)} %pad_maximum_fusion.3), calls=%async_computation.4 | async-start | bytes 4718592 | tf_op jit(solution)/shard_map/all_to_all | solution.py:417
  1052.5 79.7 %collective-permute-start.69 = (bf16[8,144,512]{2,1,0:T(8,128)(2,1)}, bf16[8,144,512]{2,1,0:T(8,128)(2,1)}, u32[]{:S(2)}, u32[]{:S(2)}) collective-permute-start(bf16[8,144,512]{2,1,0:T(8,128)(2,1)} %get-tuple-element.133), channel_id=1, source_target_pairs={{0,16},{16,0},{1,17},{17,1},{2,18},{18,2},{3,19},{19,3},{4,20},{20... | collective-permute-start | bytes 3538952 | tf_op jit(solution)/shard_map/ppermute | solution.py:308
  1068.3 69.0 %collective-permute-start.55 = (bf16[512,2048]{1,0:T(8,128)(2,1)}, bf16[512,2048]{1,0:T(8,128)(2,1)}, u32[]{:S(2)}, u32[]{:S(2)}) collective-permute-start(bf16[512,2048]{1,0:T(8,128)(2,1)} %slice.676), channel_id=1, source_target_pairs={{0,2},{1,3},{2,0},{3,1},{4,6},{5,7},{6,4},{7,5},{8,10},{9,11},{10,... | collective-permute-start | bytes 6291464 | tf_op jit(solution)/shard_map/ppermute | solution.py:305
  1073.6 62.1 %collective-permute-start.67 = (bf16[8,144,512]{2,1,0:T(8,128)(2,1)S(1)}, bf16[8,144,512]{2,1,0:T(8,128)(2,1)S(1)}, u32[]{:S(2)}, u32[]{:S(2)}) collective-permute-start(bf16[8,144,512]{2,1,0:T(8,128)(2,1)S(1)} %get-tuple-element.135), channel_id=1, source_target_pairs={{0,16},{16,0},{1,17},{17,1},{2,18},{18,2},{3,19},{19,3},{4,20},{20... | collective-permute-start | bytes 3538952 | tf_op jit(solution)/shard_map/ppermute | solution.py:308
  1076.6 59.1 %collective-permute-start.68 = (bf16[8,144,512]{2,1,0:T(8,128)(2,1)S(1)}, bf16[8,144,512]{2,1,0:T(8,128)(2,1)S(1)}, u32[]{:S(2)}, u32[]{:S(2)}) collective-permute-start(bf16[8,144,512]{2,1,0:T(8,128)(2,1)S(1)} %get-tuple-element.136), channel_id=1, source_target_pairs={{0,16},{16,0},{1,17},{17,1},{2,18},{18,2},{3,19},{19,3},{4,20},{20... | collective-permute-start | bytes 3538952 | tf_op jit(solution)/shard_map/ppermute | solution.py:308
  1079.7 51.7 %collective-permute-start.64 = (f32[2,128]{1,0:T(2,128)S(1)}, f32[2,128]{1,0:T(2,128)S(1)}, u32[]{:S(2)}, u32[]{:S(2)}) collective-permute-start(f32[2,128]{1,0:T(2,128)S(1)} %add_add_fusion.1), channel_id=1, source_target_pairs={{0,16},{16,0},{1,17},{17,1},{2,18},{18,2},{3,19},{19,3},{4,20},{20... | collective-permute-start | bytes 3080 | tf_op jit(solution)/shard_map/ppermute | solution.py:308
  1131.4 101.6 %collective-permute-start.70 = (bf16[512,2304]{1,0:T(8,128)(2,1)}, bf16[512,2304]{1,0:T(8,128)(2,1)}, u32[]{:S(2)}, u32[]{:S(2)}) collective-permute-start(bf16[512,2304]{1,0:T(8,128)(2,1)} %pad_maximum_fusion.1.mine), channel_id=1, source_target_pairs={{0,16},{16,0},{1,17},{17,1},{2,18},{18,2},{3,19},{19,3},{4,20},{20... | collective-permute-start | bytes 7077896 | tf_op jit(solution)/shard_map/ppermute | solution.py:308
  1145.0 26.8 %collective-permute-start.58 = (bf16[128,2048]{1,0:T(8,128)(2,1)}, bf16[128,2048]{1,0:T(8,128)(2,1)}, u32[]{:S(2)}, u32[]{:S(2)}) collective-permute-start(bf16[128,2048]{1,0:T(8,128)(2,1)} %get-tuple-element.158), channel_id=1, source_target_pairs={{0,12},{1,13},{2,14},{3,15},{4,8},{5,9},{6,10},{7,11},{8,4},{9,5},... | collective-permute-start | bytes 1572872 | tf_op jit(solution)/shard_map/ppermute | solution.py:305
  1147.4 45.1 %collective-permute-start.57 = (bf16[128,2048]{1,0:T(8,128)(2,1)}, bf16[128,2048]{1,0:T(8,128)(2,1)}, u32[]{:S(2)}, u32[]{:S(2)}) collective-permute-start(bf16[128,2048]{1,0:T(8,128)(2,1)} %get-tuple-element.159), channel_id=1, source_target_pairs={{0,8},{1,9},{2,10},{3,11},{4,12},{5,13},{6,14},{7,15},{8,0},{9,1},... | collective-permute-start | bytes 1572872 | tf_op jit(solution)/shard_map/ppermute | solution.py:305
  1164.5 39.3 %collective-permute-start.71 = (bf16[1024,512]{1,0:T(8,128)(2,1)}, bf16[1024,512]{1,0:T(8,128)(2,1)}, u32[]{:S(2)}, u32[]{:S(2)}) collective-permute-start(bf16[1024,512]{1,0:T(8,128)(2,1)} %get-tuple-element.142), channel_id=1, source_target_pairs={{0,1},{1,0},{2,3},{3,2},{4,5},{5,4},{6,7},{7,6},{8,9},{9,8},{10,11... | collective-permute-start | bytes 3145736 | tf_op jit(solution)/shard_map/ppermute | solution.py:305
  1229.5 25.9 %collective-permute-start.76 = (bf16[128,512]{1,0:T(8,128)(2,1)S(1)}, bf16[128,512]{1,0:T(8,128)(2,1)S(1)}, u32[]{:S(2)}, u32[]{:S(2)}) collective-permute-start(bf16[128,512]{1,0:T(8,128)(2,1)S(1)} %fusion.76), channel_id=1, source_target_pairs={{0,16},{16,0},{1,17},{17,1},{2,18},{18,2},{3,19},{19,3},{4,20},{20... | collective-permute-start | bytes 393224 | tf_op jit(solution)/shard_map/ppermute | solution.py:308
  (142 other events, 2781.9 us)
Sparse Core Ops, SparseCore 0:
  12.0 148.2 all-gather.5
  163.1 154.3 all-gather.7
  319.7 110.5 all-gather.9
  750.0 83.9 all-gather.13
  859.0 117.8 all-gather.11

commit v2 on v1

--- a/solution.py
+++ b/solution.py
@@ -324,40 +324,37 @@
     def lines_of(x):
         return [x] + [hop(x, 4 * k) for k in range(1, lines)]
 
-    def gather_lines(along):
-        near = jnp.concatenate(along + [hop(b, 2) for b in along], axis=0)
+    def gather_near(x):
+        along = lines_of(x)
+        return jnp.concatenate(along + [hop(b, 2) for b in along], axis=0)
+
+    def gather(x):
+        near = gather_near(x)
         return jnp.concatenate([near, hop(near, 1)], axis=0)
 
-    def gather(x):
-        return gather_lines(lines_of(x))
-
-    def scatter_halves(near, far):
-        arrived = hop(far, 1)
+    def fold_core(near, arrived):
         r = near.shape[0] // (2 * lines)
-        mine = [None] * (2 * lines)
-        for k in range(2 * lines):
-            part = slice(k * r, (k + 1) * r)
-            mine[k] = near[part].astype(F32) + arrived[part].astype(F32)
-        total = None
-        for k in list(range(1, lines)) + [0]:
-            side = hop(mine[lines + k].astype(near.dtype), 2)
-            here = mine[k] + side.astype(F32)
-            if k:
-                here = hop(here.astype(near.dtype), 4 * k).astype(F32)
-            total = here if total is None else total + here
-        return total
-
-    def scatter(partial):
-        kind = partial.dtype
-        half = partial.shape[0] // 2
-        mine = partial[:half].astype(F32) + hop(partial[half:], 1).astype(F32)
-        half = half // 2
+        parts = [slice(k * r, (k + 1) * r) for k in range(2 * lines)]
+        both = [near[p].astype(F32) + arrived[p].astype(F32) for p in parts]
+        return both[:lines], [x.astype(near.dtype) for x in both[lines:]]
+
+    def all_after(values, *others):
+        return lax.optimization_barrier((*values, *others))[: len(values)]
+
+    def scatter(near, far):
+        kind = near.dtype
+        mine = near.astype(F32) + hop(far, 1).astype(F32)
+        half = near.shape[0] // 2
         mine = mine[:half] + hop(mine[half:].astype(kind), 2).astype(F32)
         r = half // lines
         total = mine[:r]
         for k in range(1, lines):
             total = total + hop(mine[k * r : (k + 1) * r].astype(kind), 4 * k).astype(F32)
         return total
+
+    def scatter_whole(partial):
+        half = partial.shape[0] // 2
+        return scatter(partial[:half], partial[half:])
 
     x = tokens[0].astype(F32)
     dy = output_cotangent_rows[0]
@@ -407,10 +404,6 @@
     qkv_second = apart(qkv_got[:, at_q : at_q + q_second])
     gains_full = qkv_got[:, at_q + q_second : at_q + q_second + 2].astype(F32).T
     attn_gain, feed_gain = gains_full[:1], gains_full[1:]
-    out_full = out_got[:, : width + rank]
-    gate_up_first = out_got[:, width + rank : width + 2 * rank]
-    out_second = apart(out_got[:, width + 2 * rank : width + 2 * rank + o_second])
-    down_second = apart(out_got[:, width + 2 * rank + o_second :])
 
     def exchange(pieces):
         flat = pieces.reshape(n * ext, feed_half)
@@ -425,8 +418,7 @@
         b = lax.dynamic_index_in_dim(pair, 1 - plane, 0, False)
         return jnp.concatenate([a, b], axis=0)
 
-    down_first = own_first(down_adapter_first)
-    down_eff = (own_first(down_matrix).astype(F32) + mm(down_first, down_second)).astype(BF)
+    down_first, down_rows = own_first(down_adapter_first), own_first(down_matrix)
 
     def positions(device):
         within = jnp.arange(rows, dtype=jnp.int32)
@@ -475,6 +467,12 @@
     unnormed = jnp.exp(scores - peak)
     total = jnp.sum(unnormed, axis=-1, keepdims=True)
     probs = (unnormed / total).astype(BF).reshape(rows * HEADS, seq)
+    out_got = after(out_got, probs)
+    out_full = out_got[:, : width + rank]
+    gate_up_first = out_got[:, width + rank : width + 2 * rank]
+    out_second = apart(out_got[:, width + 2 * rank : width + 2 * rank + o_second])
+    down_second = apart(out_got[:, width + 2 * rank + o_second :])
+    down_eff = (down_rows.astype(F32) + mm(down_first, down_second)).astype(BF)
     attended_f = mm(after(probs, gate_pieces[1]), v_all)
     gate_other = jnp.concatenate(gate_pieces, axis=0)
     attended = attended_f.reshape(rows, width).astype(BF)
@@ -486,34 +484,44 @@
 
     inv_two = inv_rms(mid)
     norm_two = (mid * inv_two * (1.0 + feed_gain)).astype(BF)
-    all_rows = gather(norm_two)
+    near_rows = gather_near(norm_two)
     all_dy = reorder(dy_got)
     up_other = jnp.concatenate(up_pieces, axis=0)
     w_eff, (gate_b, up_b) = fold(gate_mine, up_mine, gate_up_first, 0, None)
     w_eff, _ = fold(gate_other, up_other, gate_up_first, 1, w_eff)
-    hidden, act, slope = forward(all_rows, w_eff)
+    near_rows = after(near_rows, w_eff, down_eff)
+    all_rows = jnp.concatenate([near_rows, hop(near_rows, 1)], axis=0)
+    hidden, act, slope = forward(after(all_rows, all_dy), w_eff)
     h = feed_half
     half_seq = seq // 2
     down_part = mm(hidden[:, h:], all_dy, 0, 0).astype(BF)
     grads = backward(after(all_dy, down_part), down_eff, act, slope)
-    down_pieces = swap_pieces(down_part, 4)
-    grads = after(grads, down_pieces[0])
+    down_part = swap(down_part)
     far_part = mm(grads[half_seq:], w_eff, 1, 1).astype(BF)
-    near_part = mm(after(grads[:half_seq], far_part, down_pieces[1]), w_eff, 1, 1).astype(BF)
-    grad_norm_two = scatter_halves(near_part, far_part)
+    near_part = mm(after(grads, far_part)[:half_seq], w_eff, 1, 1).astype(BF)
+    here, there = fold_core(near_part, hop(far_part, 1))
+    sides = [hop(part, 2) for part in there]
 
     late_rows, late_grads = lax.optimization_barrier(
-        (all_rows, grads, near_part, down_pieces[2])
+        (all_rows, grads, near_part, *there)
     )[:2]
     other_part = mm(late_rows, late_grads[:, 2 * h :], 0, 0).astype(BF)
-    gate_pieces, up_pieces = swap_pieces(other_part[:, :h], 4), swap_pieces(other_part[:, h:], 4)
-    out_part = mm(after(hidden, other_part, down_pieces[3]), down_eff).astype(BF)
-    down_part = jnp.concatenate(down_pieces, axis=0)
+    gate_part, up_part = swap(other_part[:, :h]), swap(other_part[:, h:])
+    sides = all_after(sides, other_part)
+    sums = [a + b.astype(F32) for a, b in zip(here, sides)]
+    line_sums = [part.astype(BF) for part in sums[1:]]
+    arrivals = [hop(part, 4 * (k + 1)) for k, part in enumerate(line_sums)]
+    late_hidden = after(hidden, other_part)
+    out_far = mm(late_hidden[half_seq:], down_eff).astype(BF)
+    out_near = mm(late_hidden[:half_seq], down_eff).astype(BF)
     down_half = (
-        mm(after(hidden, out_part, gate_pieces[0])[:, :h], all_dy, 0, 0) + down_part.astype(F32)
+        mm(after(hidden, other_part)[:, :h], all_dy, 0, 0) + down_part.astype(F32)
     ).astype(BF)
     g_down_first = mm(down_half, down_second, 1, 1).astype(BF)
     down_rows = jnp.concatenate([down_half, g_down_first], axis=1)
+
+    late_rows = after(all_rows, down_rows, out_near, out_far, *line_sums)
+    gate_half = (mm(late_rows, grads[:, :h], 0, 0) + gate_part.astype(F32)).astype(BF)
 
     pieces = jnp.concatenate(
         [
@@ -527,7 +535,8 @@
     pieces = after(pieces, all_rows)
     inputs = lax.all_to_all(pieces.reshape(seq, 2 * ext), "ctx", 0, 0, tiled=True)
 
-    grad_norm_two = after(grad_norm_two, down_rows, inputs, *gate_pieces[:2])
+    arrivals = all_after(arrivals, gate_half, inputs)
+    grad_norm_two = sums[0] + sum(part.astype(F32) for part in arrivals)
     feed_gain_rows = jnp.sum(grad_norm_two * mid * inv_two, axis=0, keepdims=True)
     grad_mid = dy.astype(F32) + norm_back(mid, inv_two, feed_gain, grad_norm_two)
     grad_branch = grad_mid.astype(BF)
@@ -540,36 +549,32 @@
         (grad_attended * attended.astype(F32)).reshape(rows * HEADS, HD), axis=1, keepdims=True
     )
     grad_flat = grad_attended.astype(BF).reshape(rows * HEADS, HD)
-    gate_part = jnp.concatenate(gate_pieces, axis=0)
-    gate_half = (
-        mm(after(all_rows, grad_flat), grads[:, :h], 0, 0) + gate_part.astype(F32)
-    ).astype(BF)
     gate_second = mm(gate_up_first, gate_half, 0, 0).astype(BF)
     gate_ext = jnp.concatenate(
         [gate_half.reshape(n, w_rows, h), gate_second.reshape(n, r_rows, h)], axis=1
     )
     gate_got = exchange(gate_ext)
-    grad_flat = after(grad_flat, gate_ext, up_pieces[0])
+    grad_flat = after(grad_flat, gate_ext)
     grad_probs = mm(grad_flat, v_all, 1, 1)
     grad_scores = (probs.astype(F32) * (grad_probs - delta)).astype(BF)
-    grad_scores = after(grad_scores, up_pieces[1])
+    grad_scores = after(grad_scores, up_part)
     grad_k = mm(grad_scores, q_flat, 0, 0) * score_scale
     grad_v = mm(probs, grad_flat, 0, 0)
     kv_part = jnp.concatenate([grad_k, grad_v], axis=1).astype(BF)
-    grad_kv = scatter(kv_part)
-    grad_q = mm(after(grad_scores, kv_part, up_pieces[2]), k_all) * score_scale
+    grad_kv = scatter_whole(kv_part)
+    grad_q = mm(after(grad_scores, kv_part), k_all) * score_scale
     grad_q_rows = (
         rotate(grad_q.reshape(rows, HEADS, HD), cosine[:, None, :], -sine_rows[:, None, :])
         .reshape(rows, width)
         .astype(BF)
     )
     q_all = lax.all_gather(grad_q_rows, "ctx", axis=0, tiled=True)
-    up_part = jnp.concatenate(up_pieces, axis=0)
     up_half = (
-        mm(after(all_rows, grad_q_rows), grads[:, h : 2 * h], 0, 0) + up_part.astype(F32)
+        mm(after(all_rows, grad_q_rows, gate_got), grads[:, h : 2 * h], 0, 0)
+        + up_part.astype(F32)
     ).astype(BF)
-    down_back = swap(after(down_rows, up_half))
-    grad_kv = after(grad_kv, up_half, grad_q_rows)
+    down_back = swap(after(down_rows, up_part))
+    grad_kv = after(grad_kv, up_half, down_back)
     grad_k_rows = rotate(grad_kv[:, :HD], cosine, -sine_rows)
     grad_kv_rows = jnp.concatenate([grad_k_rows, grad_kv[:, HD:]], axis=1).astype(BF)
     kv_all_grads = gather(grad_kv_rows)
@@ -587,7 +592,8 @@
     )
     attn_gain_rows = jnp.sum(grad_norm_one * x * inv_one, axis=0, keepdims=True)
     grad_input = (grad_mid + norm_back(x, inv_one, attn_gain, grad_norm_one)).astype(BF)
-    gate_back = swap_pieces(gate_got, 2)
+    gate_back = swap(after(gate_got, down_back))
+    output = (mid + scatter(out_near, after(out_far, kv_all_grads))).astype(BF)
 
     def both_planes(own):
         own = own.astype(BF)
@@ -607,28 +613,26 @@
         axis=2,
     )
     small = after(small, g_out)
-    small = scatter(reorder(small.reshape(n * w_rows, small.shape[2])))
+    small = scatter_whole(reorder(small.reshape(n * w_rows, small.shape[2])))
     gain_rows = jnp.concatenate([attn_gain_rows, feed_gain_rows], axis=0)
     gain_rows = gain_rows.reshape(2, n, w_rows).transpose(1, 0, 2).reshape(2 * n, w_rows)
-    gain_rows = scatter(reorder(gain_rows))
+    gain_rows = scatter_whole(reorder(gain_rows))
 
     down_grads = stack(plane_id, down_rows, after(down_back, small), width)
-    output = (mid + scatter(after(out_part, kv_all_grads, gate_back[0]))).astype(BF)
-    gate_got_other = jnp.concatenate(gate_back, axis=0)
     gate_up_grads = collect(
-        plane_id, gate_got, after(gate_got_other, down_grads[0]), w_rows, 0, None
-    )
-    up_got_other = jnp.concatenate(swap_pieces(up_got, 2), axis=0)
+        plane_id, gate_got, after(gate_back, down_grads[0]), w_rows, 0, None
+    )
+    up_got_other = swap(after(up_got, gate_back))
     gate_up_grads = collect(plane_id, up_got, up_got_other, w_rows, 1, gate_up_grads)
 
     g_q = mm(inputs[:, :ext], q_all, 0, 0)
     inputs_rel = reorder(inputs[:, :ext])
     g_kv = mm(inputs_rel, kv_all_grads, 0, 0)
     g_qkv = jnp.concatenate([g_q, g_kv], axis=1).astype(BF)
-    g_out = both_planes(g_out)
-    small = both_planes(small)
+    g_out = both_planes(after(g_out, gate_back))
+    small = both_planes(after(small, gate_back))
     g_qkv = both_planes(g_qkv)
-    gain_rows = gain_rows + swap(gain_rows)
+    gain_rows = gain_rows + swap(after(gain_rows, up_got_other))
     g_gu_first = small[:, :rank]
     g_down_second = small[:, rank:].reshape(r_rows, width)
     g_out_first = mm(g_out[:w_rows].astype(BF), out_second, 1, 1)

time: 1280 us -> 1140 us (0.89)
  waiting for transfers between devices: 647 us -> 541 us
  starting transfers between devices: 122 us -> 106 us
    all_gather x1, waiting for transfers between devices: 88.7 us -> 21.7 us  [body(): out_got = lax.all_gather(out_ext, 'ctx', axis=0, tiled=True)]
    ppermute x25 -> x14, waiting for transfers between devices: 159 us -> 118 us  [swap(): return lax.ppermute(x, 'grp', [(0, 1), (1, 0)])]
    unnamed x267 -> x233, local copies, waits for them, and re-layouts: 64.5 us -> 76.3 us
    ppermute x25 -> x14, starting transfers between devices: 26 us -> 16.4 us  [swap(): return lax.ppermute(x, 'grp', [(0, 1), (1, 0)])]
    dot_general x34 -> x35, matrix products: 163 us -> 170 us  [mm(): lax.dot_general(a, b, (((ca,), (cb,)), ((), ())), preferred_element_type=...]
  transfers between devices with their start and end apart: 87 -> 76, of which waited for: 32 -> 36; matrix products, arithmetic and copies ran while one was open for 27% -> 32% of each run, Pallas kernels for 7% -> 7%
where the time goes in v2:
time: 1140 us; the launch traced here: 1130 us
  waiting for transfers between devices  541 us (47%)
  matrix products  170 us (15%)
  local copies, waits for them, and re-layouts  154 us (14%)
  starting transfers between devices  106 us (9%)
  Pallas kernels  83.4 us (7%)
  other arithmetic  63 us (6%)
  between operations  15.8 us (1%)
    ppermute x52, waiting for transfers between devices, hop(): return lax.ppermute(x, 'ctx', [(i, i ^ k) for i in range(n)])  275 us
    dot_general x35, matrix products, mm(): lax.dot_general(a, b, (((ca,), (cb,)), ((), ())), preferred_element_type=...  170 us
    all_gather x1, waiting for transfers between devices, body(): qkv_got = lax.all_gather(qkv_ext, 'ctx', axis=0, tiled=True)  126 us
    ppermute x14, waiting for transfers between devices, swap(): return lax.ppermute(x, 'grp', [(0, 1), (1, 0)])  118 us
    unnamed x233, local copies, waits for them, and re-layouts  76.3 us
    ppermute x52, starting transfers between devices, hop(): return lax.ppermute(x, 'ctx', [(i, i ^ k) for i in range(n)])  61.6 us
    pallas_call x1, Pallas kernels, forward(): pl.pallas_call(forward_kernel, out_shape=(jax.ShapeDtypeStruct((t, f), BF...  25.8 us
    all_to_all x4, starting transfers between devices, exchange(): lax.all_to_all(flat, 'ctx', 0, 0, tiled=True).reshape(n, ext, feed_half)  24.4 us
  transfers between devices with their start and end apart: 76, of which 36 were waited for; matrix products, arithmetic and copies ran while one was open for 32% of the time, Pallas kernels for 7%

profile of v2, /device:TPU:0, one launch (start us, length us, event | category | flops | bytes accessed | tf_op | source)
XLA Modules:
  0.0 1133.3 jit_solution(1237344903306977114)
XLA Ops:
  19.7 7.4 all-to-all-start
  34.3 126.0 %all-gather.6.cloned.1.call-done = bf16[2048,3200]{1,0:T(8,128)(2,1)} async-done(((bf16[128,3200]{1,0:T(8,128)(2,1)}), bf16[2048,3200]{1,0:T(8,128)(2,1)}) %all-gather.6.cloned.1.call-update) | async-done | bytes 13107216 | tf_op jit(solution)/shard_map/all_gather | solution.py:391
  170.7 6.4 fusion.3
  191.9 14.4 %collective-permute-done.1 = bf16[128,512]{1,0:T(8,128)(2,1)S(1)} collective-permute-done((bf16[128,512]{1,0:T(8,128)(2,1)S(1)}, bf16[128,512]{1,0:T(8,128)(2,1)S(1)}, u32[]{:S(2)}, u32[]{:S(2)}) %collective-permute-start.1) | collective-permute-done | bytes 131104 | tf_op jit(solution)/shard_map/ppermute | solution.py:305
  223.9 5.7 all-to-all-start.1
  235.9 10.6 collective-permute-done.8
  247.9 23.5 %collective-permute-done.9 = bf16[8,144,512]{2,1,0:T(8,128)(2,1)} collective-permute-done((bf16[8,144,512]{2,1,0:T(8,128)(2,1)}, bf16[8,144,512]{2,1,0:T(8,128)(2,1)}, u32[]{:S(2)}, u32[]{:S(2)}) %collective-permute-start.9) | collective-permute-done | bytes 1179680 | tf_op jit(solution)/shard_map/ppermute | solution.py:308
  276.7 5.7 fusion.138
  293.5 21.7 %all-gather.8.cloned.1.call-done = bf16[2048,3072]{1,0:T(8,128)(2,1)} async-done(((bf16[128,3072]{1,0:T(8,128)(2,1)}), bf16[2048,3072]{1,0:T(8,128)(2,1)}) %all-gather.8.cloned.1.call-update) | async-done | bytes 12582928 | tf_op jit(solution)/shard_map/all_gather | solution.py:402
  324.2 5.7 fusion.7
  348.1 6.2 shard_map.290.refs_0_
  358.5 64.7 %collective-permute-done.11 = bf16[128,2048]{1,0:T(8,128)(2,1)} collective-permute-done((bf16[128,2048]{1,0:T(8,128)(2,1)S(1)}, bf16[128,2048]{1,0:T(8,128)(2,1)}, u32[]{:S(2)}, u32[]{:S(2)}) %collective-permute-start.11) | collective-permute-done | bytes 524320 | tf_op jit(solution)/shard_map/ppermute | solution.py:305
  430.0 8.1 collective-permute-done.14
  438.9 10.4 collective-permute-done.15
  450.1 7.2 collective-permute-done.16
  461.1 6.3 shard_map.291.w_ref
  507.1 25.8 %shard_map.292 = (bf16[2048,1024]{1,0:T(8,128)(2,1)S(1)}, bf16[2048,1024]{1,0:T(8,128)(2,1)S(1)}, bf16[2048,1024]{1,0:T(8,128)(2,1)}) custom-call(bf16[2048,2048]{1,0:T(8,128)(2,1)} %constant_dynamic-update-slice_fusion.34.x_ref, bf16[2048,2048]{1,0:T(8,128)(2,1)} %shard_map.291.w_ref), custom_call_target="tpu_custom_call" | custom-call | flops 17179869184 | bytes 29360128 | tf_op jit(solution)/shard_map/pallas_call | solution.py:136
  532.9 9.7 convolution_convert_fusion.2
  542.7 14.7 %shard_map.293 = bf16[2048,2048]{1,0:T(8,128)(2,1)} custom-call(bf16[2048,2048]{1,0:T(8,128)(2,1)} %dynamic-slice_dynamic-update-slice_fusion.dy_ref, bf16[1024,2048]{1,0:T(8,128)(2,1)S(1)} %copy-done, bf16[2048,1024]{1,0:T(8,128)(2,1)S(1)} %get-tuple-element.79.act_ref, bf16[2048,1024]{1,0:T(8,128)(2,1)} %get-tuple-element.80.slope_ref), custom_call_target="tpu_custom_call" | custom-call | flops 8589934592 | bytes 29360128 | tf_op jit(solution)/shard_map/pallas_call | solution.py:168
  557.4 12.0 %fusion.25 = bf16[1024,2048]{1,0:T(8,128)(2,1)} fusion(bf16[2048,2048]{1,0:T(8,128)(2,1)S(1)} %bitcast.124, bf16[2048,2048]{1,0:T(8,128)(2,1)} %shard_map.293), kind=kOutput, calls=%fused_computation.33 | convolution fusion | flops 8592031744 | bytes 16777216 | tf_op jit(solution)/shard_map/dot_general | solution.py:19
  571.8 12.7 %fusion.19 = bf16[1024,2048]{1,0:T(8,128)(2,1)S(1)} fusion(bf16[2048,2048]{1,0:T(8,128)(2,1)} %shard_map.291.w_ref, bf16[2048,2048]{1,0:T(8,128)(2,1)} %shard_map.293), kind=kOutput, calls=%fused_computation.31 | convolution fusion | flops 8592031744 | bytes 16777216 | tf_op jit(solution)/shard_map/dot_general | solution.py:19
  591.0 12.7 %fusion.22 = bf16[2048,1024]{1,0:T(8,128)(2,1)S(1)} fusion(bf16[2048,2048]{1,0:T(8,128)(2,1)} %constant_dynamic-update-slice_fusion.34.x_ref, bf16[2048,2048]{1,0:T(8,128)(2,1)} %shard_map.293), kind=kOutput, calls=%fused_computation.32 | convolution fusion | flops 8592031744 | bytes 16777216 | tf_op jit(solution)/shard_map/dot_general | solution.py:19
  607.9 6.1 convolution_convert_fusion
  619.5 8.2 add_convert_fusion.3
  627.7 6.5 convolution_convert_fusion.1
  643.3 22.1 %collective-permute-done.29 = bf16[2048,512]{1,0:T(8,128)(2,1)S(1)} collective-permute-done((bf16[2048,512]{1,0:T(8,128)(2,1)S(1)}, bf16[2048,512]{1,0:T(8,128)(2,1)S(1)}, u32[]{:S(2)}, u32[]{:S(2)}) %collective-permute-start.29) | collective-permute-done | bytes 2097184 | tf_op jit(solution)/shard_map/ppermute | solution.py:308
  665.4 10.0 add_convert_fusion.2
  675.4 11.5 %collective-permute-done.26 = bf16[128,2048]{1,0:T(8,128)(2,1)S(1)} collective-permute-done((bf16[128,2048]{1,0:T(8,128)(2,1)S(1)}, bf16[128,2048]{1,0:T(8,128)(2,1)S(1)}, u32[]{:S(2)}, u32[]{:S(2)}) %collective-permute-start.26) | collective-permute-done | bytes 524320 | tf_op jit(solution)/shard_map/ppermute | solution.py:305
  695.1 8.6 convert_multiply_fusion.5
  716.7 5.5 multiply_convert_fusion
  722.2 15.2 %collective-permute-done.30 = bf16[2048,512]{1,0:T(8,128)(2,1)} collective-permute-done((bf16[2048,512]{1,0:T(8,128)(2,1)}, bf16[2048,512]{1,0:T(8,128)(2,1)}, u32[]{:S(2)}, u32[]{:S(2)}) %collective-permute-start.30) | collective-permute-done | bytes 2097184 | tf_op jit(solution)/shard_map/ppermute | solution.py:308
  748.7 24.3 %collective-permute-done.32 = bf16[512,512]{1,0:T(8,128)(2,1)S(1)} collective-permute-done((bf16[512,512]{1,0:T(8,128)(2,1)S(1)}, bf16[512,512]{1,0:T(8,128)(2,1)S(1)}, u32[]{:S(2)}, u32[]{:S(2)}) %collective-permute-start.32) | collective-permute-done | bytes 524320 | tf_op jit(solution)/shard_map/ppermute | solution.py:305
  781.9 10.0 collective-permute-done.33
  796.0 20.0 %collective-permute-done.34 = bf16[128,512]{1,0:T(8,128)(2,1)} collective-permute-done((bf16[128,512]{1,0:T(8,128)(2,1)}, bf16[128,512]{1,0:T(8,128)(2,1)}, u32[]{:S(2)}, u32[]{:S(2)}) %collective-permute-start.34) | collective-permute-done | bytes 131104 | tf_op jit(solution)/shard_map/ppermute | solution.py:305
  817.1 9.6 add_convert_fusion.1
  840.6 10.2 collective-permute-done.38
  863.5 6.8 all-to-all-start.4
  889.9 9.9 fusion.49
  900.7 34.7 %collective-permute-done.55.other = bf16[16,144,512]{2,1,0:T(8,128)(2,1)} collective-permute-done((bf16[16,144,512]{2,1,0:T(8,128)(2,1)}, bf16[16,144,512]{2,1,0:T(8,128)(2,1)}, u32[]{:S(2)}, u32[]{:S(2)}) %collective-permute-start.55) | collective-permute-done | bytes 2359328 | tf_op jit(solution)/shard_map/ppermute | solution.py:308
  936.8 5.4 convert_add_fusion
  955.7 41.3 %collective-permute-done.51 = f32[8,128]{1,0:T(8,128)S(1)} collective-permute-done((f32[8,128]{1,0:T(8,128)S(1)}, f32[8,128]{1,0:T(8,128)S(1)}, u32[]{:S(2)}, u32[]{:S(2)}) %collective-permute-start.51) | collective-permute-done | bytes 4128 | tf_op jit(solution)/shard_map/ppermute | solution.py:305
  997.0 6.9 collective-permute-start.52
  1023.3 5.9 convolution_convert_fusion.5
  1046.5 18.7 %collective-permute-done.48 = bf16[128,2048]{1,0:T(8,128)(2,1)} collective-permute-done((bf16[128,2048]{1,0:T(8,128)(2,1)}, bf16[128,2048]{1,0:T(8,128)(2,1)}, u32[]{:S(2)}, u32[]{:S(2)}) %collective-permute-start.48) | collective-permute-done | bytes 524320 | tf_op jit(solution)/shard_map/ppermute | solution.py:305
  1069.4 6.5 convolution_convert_fusion.6
  1102.6 9.5 shard_map.294
  1112.0 6.5 shard_map.295
  1118.5 6.5 shard_map.296
  (522 shorter events, 373.4 us)
Async XLA Ops:
  7.2 153.1 %all-gather.6.cloned.1.call-start = ((), (), s32[]{:S(2)}) async-start(), calls=%async_computation.5 | async-start | bytes 13926400 | tf_op jit(solution)/shard_map/all_gather | solution.py:391
  11.8 303.3 %all-gather.8.cloned.1.call-start = ((), (), s32[]{:S(2)}) async-start(), calls=%async_computation.6 | async-start | bytes 13369344 | tf_op jit(solution)/shard_map/all_gather | solution.py:402
  19.7 151.0 %all-to-all-start = ((bf16[16,144,512]{2,1,0:T(8,128)(2,1)}), bf16[16,144,512]{2,1,0:T(8,128)(2,1)S(1)}, u32[]{:S(2)}, u32[]{:S(2)}) async-start(bf16[16,144,512]{2,1,0:T(8,128)(2,1)} %shard_map.288), calls=%async_computation | async-start | bytes 4718592 | tf_op jit(solution)/shard_map/all_to_all | solution.py:410
  27.1 457.3 %all-gather.10.cloned.1.call-start = ((), (), s32[]{:S(2)}) async-start(), calls=%async_computation.7 | async-start | bytes 8912896 | tf_op jit(solution)/shard_map/all_gather | solution.py:459
  183.0 23.4 %collective-permute-start.1 = (bf16[128,512]{1,0:T(8,128)(2,1)S(1)}, bf16[128,512]{1,0:T(8,128)(2,1)S(1)}, u32[]{:S(2)}, u32[]{:S(2)}) collective-permute-start(bf16[128,512]{1,0:T(8,128)(2,1)S(1)} %get-tuple-element.233), channel_id=1, source_target_pairs={{0,8},{1,9},{2,10},{3,11},{4,12},{5,13},{6,14},{7,15},{8,0},{9,1},... | collective-permute-start | bytes 393224 | tf_op jit(solution)/shard_map/ppermute | solution.py:305
  183.0 24.5 %collective-permute-start = (bf16[128,512]{1,0:T(8,128)(2,1)S(1)}, bf16[128,512]{1,0:T(8,128)(2,1)S(1)}, u32[]{:S(2)}, u32[]{:S(2)}) collective-permute-start(bf16[128,512]{1,0:T(8,128)(2,1)S(1)} %get-tuple-element.233), channel_id=1, source_target_pairs={{0,4},{1,5},{2,6},{3,7},{4,0},{5,1},{6,2},{7,3},{8,12},{9,13},{10,... | collective-permute-start | bytes 393224 | tf_op jit(solution)/shard_map/ppermute | solution.py:305
  185.9 24.7 %collective-permute-start.3 = (bf16[128,512]{1,0:T(8,128)(2,1)S(1)}, bf16[128,512]{1,0:T(8,128)(2,1)S(1)}, u32[]{:S(2)}, u32[]{:S(2)}) collective-permute-start(bf16[128,512]{1,0:T(8,128)(2,1)S(1)} %get-tuple-element.233), channel_id=1, source_target_pairs={{0,2},{1,3},{2,0},{3,1},{4,6},{5,7},{6,4},{7,5},{8,10},{9,11},{10,... | collective-permute-start | bytes 393224 | tf_op jit(solution)/shard_map/ppermute | solution.py:305
  191.4 23.6 %collective-permute-start.6 = (bf16[128,512]{1,0:T(8,128)(2,1)S(1)}, bf16[128,512]{1,0:T(8,128)(2,1)S(1)}, u32[]{:S(2)}, u32[]{:S(2)}) collective-permute-start(bf16[128,512]{1,0:T(8,128)(2,1)S(1)} %collective-permute-done.2), channel_id=1, source_target_pairs={{0,2},{1,3},{2,0},{3,1},{4,6},{5,7},{6,4},{7,5},{8,10},{9,11},{10,... | collective-permute-start | bytes 393224 | tf_op jit(solution)/shard_map/ppermute | solution.py:305
  217.4 29.1 %collective-permute-start.8 = (bf16[8,144,512]{2,1,0:T(8,128)(2,1)}, bf16[8,144,512]{2,1,0:T(8,128)(2,1)}, u32[]{:S(2)}, u32[]{:S(2)}) collective-permute-start(bf16[8,144,512]{2,1,0:T(8,128)(2,1)} %get-tuple-element.156), channel_id=1, source_target_pairs={{0,16},{16,0},{1,17},{17,1},{2,18},{18,2},{3,19},{19,3},{4,20},{20... | collective-permute-start | bytes 3538952 | tf_op jit(solution)/shard_map/ppermute | solution.py:308
  220.6 50.7 %collective-permute-start.9 = (bf16[8,144,512]{2,1,0:T(8,128)(2,1)}, bf16[8,144,512]{2,1,0:T(8,128)(2,1)}, u32[]{:S(2)}, u32[]{:S(2)}) collective-permute-start(bf16[8,144,512]{2,1,0:T(8,128)(2,1)} %get-tuple-element.155), channel_id=1, source_target_pairs={{0,16},{16,0},{1,17},{17,1},{2,18},{18,2},{3,19},{19,3},{4,20},{20... | collective-permute-start | bytes 3538952 | tf_op jit(solution)/shard_map/ppermute | solution.py:308
  223.9 100.3 %all-to-all-start.1 = ((bf16[16,144,512]{2,1,0:T(8,128)(2,1)}), bf16[16,144,512]{2,1,0:T(8,128)(2,1)}, u32[]{:S(2)}, u32[]{:S(2)}) async-start(bf16[16,144,512]{2,1,0:T(8,128)(2,1)} %shard_map.289), calls=%async_computation.1 | async-start | bytes 4718592 | tf_op jit(solution)/shard_map/all_to_all | solution.py:410
  332.4 23.7 %collective-permute-start.10 = (bf16[128,2048]{1,0:T(8,128)(2,1)S(1)}, bf16[128,2048]{1,0:T(8,128)(2,1)S(1)}, u32[]{:S(2)}, u32[]{:S(2)}) collective-permute-start(bf16[128,2048]{1,0:T(8,128)(2,1)S(1)} %get-tuple-element.136), channel_id=1, source_target_pairs={{0,4},{1,5},{2,6},{3,7},{4,0},{5,1},{6,2},{7,3},{8,12},{9,13},{10,... | collective-permute-start | bytes 1572872 | tf_op jit(solution)/shard_map/ppermute | solution.py:305
  337.9 90.2 %collective-permute-start.13 = (bf16[128,2048]{1,0:T(8,128)(2,1)S(1)}, bf16[128,2048]{1,0:T(8,128)(2,1)}, u32[]{:S(2)}, u32[]{:S(2)}) collective-permute-start(bf16[128,2048]{1,0:T(8,128)(2,1)S(1)} %get-tuple-element.136), channel_id=1, source_target_pairs={{0,2},{1,3},{2,0},{3,1},{4,6},{5,7},{6,4},{7,5},{8,10},{9,11},{10,... | collective-permute-start | bytes 1572872 | tf_op jit(solution)/shard_map/ppermute | solution.py:305
  339.4 85.7 %collective-permute-start.12 = (bf16[128,2048]{1,0:T(8,128)(2,1)S(1)}, bf16[128,2048]{1,0:T(8,128)(2,1)S(1)}, u32[]{:S(2)}, u32[]{:S(2)}) collective-permute-start(bf16[128,2048]{1,0:T(8,128)(2,1)S(1)} %get-tuple-element.136), channel_id=1, source_target_pairs={{0,12},{1,13},{2,14},{3,15},{4,8},{5,9},{6,10},{7,11},{8,4},{9,5},... | collective-permute-start | bytes 1572872 | tf_op jit(solution)/shard_map/ppermute | solution.py:305
  341.7 81.5 %collective-permute-start.11 = (bf16[128,2048]{1,0:T(8,128)(2,1)S(1)}, bf16[128,2048]{1,0:T(8,128)(2,1)}, u32[]{:S(2)}, u32[]{:S(2)}) collective-permute-start(bf16[128,2048]{1,0:T(8,128)(2,1)S(1)} %get-tuple-element.136), channel_id=1, source_target_pairs={{0,8},{1,9},{2,10},{3,11},{4,12},{5,13},{6,14},{7,15},{8,0},{9,1},... | collective-permute-start | bytes 1572872 | tf_op jit(solution)/shard_map/ppermute | solution.py:305
  344.9 113.3 %collective-permute-start.18 = (bf16[8,144,512]{2,1,0:T(8,128)(2,1)}, bf16[8,144,512]{2,1,0:T(8,128)(2,1)}, u32[]{:S(2)}, u32[]{:S(2)}) collective-permute-start(bf16[8,144,512]{2,1,0:T(8,128)(2,1)} %get-tuple-element.153), channel_id=1, source_target_pairs={{0,16},{16,0},{1,17},{17,1},{2,18},{18,2},{3,19},{19,3},{4,20},{20... | collective-permute-start | bytes 3538952 | tf_op jit(solution)/shard_map/ppermute | solution.py:308
  356.2 102.0 %collective-permute-start.17 = (bf16[8,144,512]{2,1,0:T(8,128)(2,1)S(1)}, bf16[8,144,512]{2,1,0:T(8,128)(2,1)S(1)}, u32[]{:S(2)}, u32[]{:S(2)}) collective-permute-start(bf16[8,144,512]{2,1,0:T(8,128)(2,1)S(1)} %get-tuple-element.154), channel_id=1, source_target_pairs={{0,16},{16,0},{1,17},{17,1},{2,18},{18,2},{3,19},{19,3},{4,20},{20... | collective-permute-start | bytes 3538952 | tf_op jit(solution)/shard_map/ppermute | solution.py:308
  425.1 24.2 %collective-permute-start.15 = (bf16[128,2048]{1,0:T(8,128)(2,1)}, bf16[128,2048]{1,0:T(8,128)(2,1)S(1)}, u32[]{:S(2)}, u32[]{:S(2)}) collective-permute-start(bf16[128,2048]{1,0:T(8,128)(2,1)} %collective-permute-done.11), channel_id=1, source_target_pairs={{0,2},{1,3},{2,0},{3,1},{4,6},{5,7},{6,4},{7,5},{8,10},{9,11},{10,... | collective-permute-start | bytes 1572872 | tf_op jit(solution)/shard_map/ppermute | solution.py:305
  428.1 29.2 %collective-permute-start.16 = (bf16[128,2048]{1,0:T(8,128)(2,1)S(1)}, bf16[128,2048]{1,0:T(8,128)(2,1)S(1)}, u32[]{:S(2)}, u32[]{:S(2)}) collective-permute-start(bf16[128,2048]{1,0:T(8,128)(2,1)S(1)} %collective-permute-done.12), channel_id=1, source_target_pairs={{0,2},{1,3},{2,0},{3,1},{4,6},{5,7},{6,4},{7,5},{8,10},{9,11},{10,... | collective-permute-start | bytes 1572872 | tf_op jit(solution)/shard_map/ppermute | solution.py:305
  480.7 89.1 %all-to-all-start.2 = ((bf16[16,128,288]{1,2,0:T(8,128)(2,1)}), bf16[16,128,288]{1,2,0:T(8,128)(2,1)S(1)}, u32[]{:S(2)}, u32[]{:S(2)}) async-start(bf16[16,128,288]{1,2,0:T(8,128)(2,1)} %maximum_bitcast_fusion), calls=%async_computation.2 | async-start | bytes 2359296 | tf_op jit(solution)/shard_map/all_to_all | solution.py:536
  484.4 539.0 %all-gather.14.cloned.1.call-start = ((), (), s32[]{:S(2)}) async-start(), calls=%async_computation.9 | async-start | bytes 8912896 | tf_op jit(solution)/shard_map/all_gather | solution.py:543
  570.9 47.6 %collective-permute-start.28 = (bf16[512,2048]{1,0:T(8,128)(2,1)S(1)}, bf16[512,2048]{1,0:T(8,128)(2,1)S(1)}, u32[]{:S(2)}, u32[]{:S(2)}) collective-permute-start(bf16[512,2048]{1,0:T(8,128)(2,1)S(1)} %convolution_convert_fusion.2), channel_id=1, source_target_pairs={{0,16},{16,0},{1,17},{17,1},{2,18},{18,2},{3,19},{19,3},{4,20},{20... | collective-permute-start | bytes 6291464 | tf_op jit(solution)/shard_map/ppermute | solution.py:308
  586.9 49.7 %collective-permute-start.24 = (bf16[128,2048]{1,0:T(8,128)(2,1)S(1)}, bf16[128,2048]{1,0:T(8,128)(2,1)S(1)}, u32[]{:S(2)}, u32[]{:S(2)}) collective-permute-start(bf16[128,2048]{1,0:T(8,128)(2,1)S(1)} %get-tuple-element.145), channel_id=1, source_target_pairs={{0,2},{1,3},{2,0},{3,1},{4,6},{5,7},{6,4},{7,5},{8,10},{9,11},{10,... | collective-permute-start | bytes 1572872 | tf_op jit(solution)/shard_map/ppermute | solution.py:305
  588.5 48.1 %collective-permute-start.23 = (bf16[128,2048]{1,0:T(8,128)(2,1)S(1)}, bf16[128,2048]{1,0:T(8,128)(2,1)S(1)}, u32[]{:S(2)}, u32[]{:S(2)}) collective-permute-start(bf16[128,2048]{1,0:T(8,128)(2,1)S(1)} %get-tuple-element.146), channel_id=1, source_target_pairs={{0,2},{1,3},{2,0},{3,1},{4,6},{5,7},{6,4},{7,5},{8,10},{9,11},{10,... | collective-permute-start | bytes 1572872 | tf_op jit(solution)/shard_map/ppermute | solution.py:305
  589.0 47.6 %collective-permute-start.22 = (bf16[128,2048]{1,0:T(8,128)(2,1)S(1)}, bf16[128,2048]{1,0:T(8,128)(2,1)S(1)}, u32[]{:S(2)}, u32[]{:S(2)}) collective-permute-start(bf16[128,2048]{1,0:T(8,128)(2,1)S(1)} %get-tuple-element.147), channel_id=1, source_target_pairs={{0,2},{1,3},{2,0},{3,1},{4,6},{5,7},{6,4},{7,5},{8,10},{9,11},{10,... | collective-permute-start | bytes 1572872 | tf_op jit(solution)/shard_map/ppermute | solution.py:305
  590.6 46.0 %collective-permute-start.21 = (bf16[128,2048]{1,0:T(8,128)(2,1)S(1)}, bf16[128,2048]{1,0:T(8,128)(2,1)S(1)}, u32[]{:S(2)}, u32[]{:S(2)}) collective-permute-start(bf16[128,2048]{1,0:T(8,128)(2,1)S(1)} %get-tuple-element.148), channel_id=1, source_target_pairs={{0,2},{1,3},{2,0},{3,1},{4,6},{5,7},{6,4},{7,5},{8,10},{9,11},{10,... | collective-permute-start | bytes 1572872 | tf_op jit(solution)/shard_map/ppermute | solution.py:305
  618.6 46.8 %collective-permute-start.29 = (bf16[2048,512]{1,0:T(8,128)(2,1)S(1)}, bf16[2048,512]{1,0:T(8,128)(2,1)S(1)}, u32[]{:S(2)}, u32[]{:S(2)}) collective-permute-start(bf16[2048,512]{1,0:T(8,128)(2,1)S(1)} %get-tuple-element.150), channel_id=1, source_target_pairs={{0,16},{16,0},{1,17},{17,1},{2,18},{18,2},{3,19},{19,3},{4,20},{20... | collective-permute-start | bytes 6291464 | tf_op jit(solution)/shard_map/ppermute | solution.py:308
  638.8 36.6 %collective-permute-start.27 = (bf16[128,2048]{1,0:T(8,128)(2,1)S(1)}, bf16[128,2048]{1,0:T(8,128)(2,1)S(1)}, u32[]{:S(2)}, u32[]{:S(2)}) collective-permute-start(bf16[128,2048]{1,0:T(8,128)(2,1)S(1)} %get-tuple-element.142), channel_id=1, source_target_pairs={{0,12},{1,13},{2,14},{3,15},{4,8},{5,9},{6,10},{7,11},{8,4},{9,5},... | collective-permute-start | bytes 1572872 | tf_op jit(solution)/shard_map/ppermute | solution.py:305
  642.5 44.4 %collective-permute-start.26 = (bf16[128,2048]{1,0:T(8,128)(2,1)S(1)}, bf16[128,2048]{1,0:T(8,128)(2,1)S(1)}, u32[]{:S(2)}, u32[]{:S(2)}) collective-permute-start(bf16[128,2048]{1,0:T(8,128)(2,1)S(1)} %get-tuple-element.143), channel_id=1, source_target_pairs={{0,8},{1,9},{2,10},{3,11},{4,12},{5,13},{6,14},{7,15},{8,0},{9,1},... | collective-permute-start | bytes 1572872 | tf_op jit(solution)/shard_map/ppermute | solution.py:305
  642.5 44.4 %collective-permute-start.25 = (bf16[128,2048]{1,0:T(8,128)(2,1)S(1)}, bf16[128,2048]{1,0:T(8,128)(2,1)S(1)}, u32[]{:S(2)}, u32[]{:S(2)}) collective-permute-start(bf16[128,2048]{1,0:T(8,128)(2,1)S(1)} %get-tuple-element.144), channel_id=1, source_target_pairs={{0,4},{1,5},{2,6},{3,7},{4,0},{5,1},{6,2},{7,3},{8,12},{9,13},{10,... | collective-permute-start | bytes 1572872 | tf_op jit(solution)/shard_map/ppermute | solution.py:305
  690.3 47.2 %collective-permute-start.30 = (bf16[2048,512]{1,0:T(8,128)(2,1)}, bf16[2048,512]{1,0:T(8,128)(2,1)}, u32[]{:S(2)}, u32[]{:S(2)}) collective-permute-start(bf16[2048,512]{1,0:T(8,128)(2,1)} %get-tuple-element.149), channel_id=1, source_target_pairs={{0,16},{16,0},{1,17},{17,1},{2,18},{18,2},{3,19},{19,3},{4,20},{20... | collective-permute-start | bytes 6291464 | tf_op jit(solution)/shard_map/ppermute | solution.py:308
  711.8 105.4 %all-to-all-start.3 = ((bf16[16,144,512]{2,1,0:T(8,128)(2,1)}), bf16[16,144,512]{2,1,0:T(8,128)(2,1)}, u32[]{:S(2)}, u32[]{:S(2)}) async-start(bf16[16,144,512]{2,1,0:T(8,128)(2,1)} %pad_maximum_fusion.2), calls=%async_computation.3 | async-start | bytes 4718592 | tf_op jit(solution)/shard_map/all_to_all | solution.py:410
  716.3 353.1 %all-gather.12.cloned.1.call-start = ((), (), s32[]{:S(2)}) async-start(), calls=%async_computation.8 | async-start | bytes 8912896 | tf_op jit(solution)/shard_map/all_gather | solution.py:571
  742.9 83.8 %collective-permute-start.36 = (bf16[512,2304]{1,0:T(8,128)(2,1)}, bf16[512,2304]{1,0:T(8,128)(2,1)}, u32[]{:S(2)}, u32[]{:S(2)}) collective-permute-start(bf16[512,2304]{1,0:T(8,128)(2,1)} %pad_maximum_fusion.1.mine), channel_id=1, source_target_pairs={{0,16},{16,0},{1,17},{17,1},{2,18},{18,2},{3,19},{19,3},{4,20},{20... | collective-permute-start | bytes 7077896 | tf_op jit(solution)/shard_map/ppermute | solution.py:308
  746.0 27.1 %collective-permute-start.32 = (bf16[512,512]{1,0:T(8,128)(2,1)S(1)}, bf16[512,512]{1,0:T(8,128)(2,1)S(1)}, u32[]{:S(2)}, u32[]{:S(2)}) collective-permute-start(bf16[512,512]{1,0:T(8,128)(2,1)S(1)} %slice.598), channel_id=1, source_target_pairs={{0,2},{1,3},{2,0},{3,1},{4,6},{5,7},{6,4},{7,5},{8,10},{9,11},{10,... | collective-permute-start | bytes 1572872 | tf_op jit(solution)/shard_map/ppermute | solution.py:305
  780.0 35.9 %collective-permute-start.34 = (bf16[128,512]{1,0:T(8,128)(2,1)}, bf16[128,512]{1,0:T(8,128)(2,1)}, u32[]{:S(2)}, u32[]{:S(2)}) collective-permute-start(bf16[128,512]{1,0:T(8,128)(2,1)} %get-tuple-element.193), channel_id=1, source_target_pairs={{0,8},{1,9},{2,10},{3,11},{4,12},{5,13},{6,14},{7,15},{8,0},{9,1},... | collective-permute-start | bytes 393224 | tf_op jit(solution)/shard_map/ppermute | solution.py:305
  829.9 22.5 %collective-permute-start.37 = (bf16[128,512]{1,0:T(8,128)(2,1)S(1)}, bf16[128,512]{1,0:T(8,128)(2,1)S(1)}, u32[]{:S(2)}, u32[]{:S(2)}) collective-permute-start(bf16[128,512]{1,0:T(8,128)(2,1)S(1)} %get-tuple-element.216), channel_id=1, source_target_pairs={{0,4},{1,5},{2,6},{3,7},{4,0},{5,1},{6,2},{7,3},{8,12},{9,13},{10,... | collective-permute-start | bytes 393224 | tf_op jit(solution)/shard_map/ppermute | solution.py:305
  863.5 71.9 %all-to-all-start.4 = ((bf16[16,144,512]{2,1,0:T(8,128)(2,1)}), bf16[16,144,512]{2,1,0:T(8,128)(2,1)}, u32[]{:S(2)}, u32[]{:S(2)}) async-start(bf16[16,144,512]{2,1,0:T(8,128)(2,1)} %pad_maximum_fusion.3), calls=%async_computation.4 | async-start | bytes 4718592 | tf_op jit(solution)/shard_map/all_to_all | solution.py:410
  872.8 64.0 %collective-permute-start.45 = (bf16[1024,2048]{1,0:T(8,128)(2,1)}, bf16[1024,2048]{1,0:T(8,128)(2,1)}, u32[]{:S(2)}, u32[]{:S(2)}) collective-permute-start(bf16[1024,2048]{1,0:T(8,128)(2,1)} %convolution_convert_fusion), channel_id=1, source_target_pairs={{0,1},{1,0},{2,3},{3,2},{4,5},{5,4},{6,7},{7,6},{8,9},{9,8},{10,11... | collective-permute-start | bytes 12582920 | tf_op jit(solution)/shard_map/ppermute | solution.py:305
  881.8 53.7 %collective-permute-start.55 = (bf16[16,144,512]{2,1,0:T(8,128)(2,1)}, bf16[16,144,512]{2,1,0:T(8,128)(2,1)}, u32[]{:S(2)}, u32[]{:S(2)}) collective-permute-start(bf16[16,144,512]{2,1,0:T(8,128)(2,1)} %all-to-all-done.3.mine), channel_id=1, source_target_pairs={{0,16},{16,0},{1,17},{17,1},{2,18},{18,2},{3,19},{19,3},{4,20},{20... | collective-permute-start | bytes 7077896 | tf_op jit(solution)/shard_map/ppermute | solution.py:308
  900.0 52.3 %collective-permute-start.50 = (f32[16,128]{1,0:T(8,128)S(1)}, f32[16,128]{1,0:T(8,128)S(1)}, u32[]{:S(2)}, u32[]{:S(2)}) collective-permute-start(f32[16,128]{1,0:T(8,128)S(1)} %concatenate.162), channel_id=1, source_target_pairs={{0,1},{1,0},{2,3},{3,2},{4,5},{5,4},{6,7},{7,6},{8,9},{9,8},{10,11... | collective-permute-start | bytes 24584 | tf_op jit(solution)/shard_map/ppermute | solution.py:305
  935.5 74.6 %collective-permute-start.56 = (bf16[16,144,512]{2,1,0:T(8,128)(2,1)}, bf16[16,144,512]{2,1,0:T(8,128)(2,1)}, u32[]{:S(2)}, u32[]{:S(2)}) collective-permute-start(bf16[16,144,512]{2,1,0:T(8,128)(2,1)} %all-to-all-done.4.mine), channel_id=1, source_target_pairs={{0,16},{16,0},{1,17},{17,1},{2,18},{18,2},{3,19},{19,3},{4,20},{20... | collective-permute-start | bytes 7077896 | tf_op jit(solution)/shard_map/ppermute | solution.py:308
  947.3 66.9 %collective-permute-start.46 = (bf16[512,2048]{1,0:T(8,128)(2,1)}, bf16[512,2048]{1,0:T(8,128)(2,1)}, u32[]{:S(2)}, u32[]{:S(2)}) collective-permute-start(bf16[512,2048]{1,0:T(8,128)(2,1)} %slice.596), channel_id=1, source_target_pairs={{0,2},{1,3},{2,0},{3,1},{4,6},{5,7},{6,4},{7,5},{8,10},{9,11},{10,... | collective-permute-start | bytes 6291464 | tf_op jit(solution)/shard_map/ppermute | solution.py:305
  952.3 44.6 %collective-permute-start.51 = (f32[8,128]{1,0:T(8,128)S(1)}, f32[8,128]{1,0:T(8,128)S(1)}, u32[]{:S(2)}, u32[]{:S(2)}) collective-permute-start(f32[8,128]{1,0:T(8,128)S(1)} %slice.455), channel_id=1, source_target_pairs={{0,2},{1,3},{2,0},{3,1},{4,6},{5,7},{6,4},{7,5},{8,10},{9,11},{10,... | collective-permute-start | bytes 12296 | tf_op jit(solution)/shard_map/ppermute | solution.py:305
  1019.9 26.7 %collective-permute-start.49 = (bf16[128,2048]{1,0:T(8,128)(2,1)}, bf16[128,2048]{1,0:T(8,128)(2,1)}, u32[]{:S(2)}, u32[]{:S(2)}) collective-permute-start(bf16[128,2048]{1,0:T(8,128)(2,1)} %get-tuple-element.174), channel_id=1, source_target_pairs={{0,12},{1,13},{2,14},{3,15},{4,8},{5,9},{6,10},{7,11},{8,4},{9,5},... | collective-permute-start | bytes 1572872 | tf_op jit(solution)/shard_map/ppermute | solution.py:305
  1022.1 43.2 %collective-permute-start.48 = (bf16[128,2048]{1,0:T(8,128)(2,1)}, bf16[128,2048]{1,0:T(8,128)(2,1)}, u32[]{:S(2)}, u32[]{:S(2)}) collective-permute-start(bf16[128,2048]{1,0:T(8,128)(2,1)} %get-tuple-element.175), channel_id=1, source_target_pairs={{0,8},{1,9},{2,10},{3,11},{4,12},{5,13},{6,14},{7,15},{8,0},{9,1},... | collective-permute-start | bytes 1572872 | tf_op jit(solution)/shard_map/ppermute | solution.py:305
  1041.6 35.1 %collective-permute-start.60 = (bf16[1024,512]{1,0:T(8,128)(2,1)}, bf16[1024,512]{1,0:T(8,128)(2,1)}, u32[]{:S(2)}, u32[]{:S(2)}) collective-permute-start(bf16[1024,512]{1,0:T(8,128)(2,1)} %get-tuple-element.158), channel_id=1, source_target_pairs={{0,1},{1,0},{2,3},{3,2},{4,5},{5,4},{6,7},{7,6},{8,9},{9,8},{10,11... | collective-permute-start | bytes 3145736 | tf_op jit(solution)/shard_map/ppermute | solution.py:305
  1098.9 26.1 %collective-permute-start.65 = (bf16[128,512]{1,0:T(8,128)(2,1)S(1)}, bf16[128,512]{1,0:T(8,128)(2,1)S(1)}, u32[]{:S(2)}, u32[]{:S(2)}) collective-permute-start(bf16[128,512]{1,0:T(8,128)(2,1)S(1)} %fusion.86), channel_id=1, source_target_pairs={{0,16},{16,0},{1,17},{17,1},{2,18},{18,2},{3,19},{19,3},{4,20},{20... | collective-permute-start | bytes 393224 | tf_op jit(solution)/shard_map/ppermute | solution.py:308
  (114 other events, 2215.4 us)
Sparse Core Ops, SparseCore 0:
  12.0 148.2 all-gather.5
  163.1 152.0 all-gather.7
  317.3 111.4 all-gather.9
  690.4 114.3 all-gather.13
  806.8 126.2 all-gather.11

commit v3 on v2

--- a/solution.py
+++ b/solution.py
@@ -324,19 +324,32 @@
     def lines_of(x):
         return [x] + [hop(x, 4 * k) for k in range(1, lines)]
 
-    def gather_near(x):
+    def gather(x):
         along = lines_of(x)
-        return jnp.concatenate(along + [hop(b, 2) for b in along], axis=0)
-
-    def gather(x):
-        near = gather_near(x)
+        near = jnp.concatenate(along + [hop(b, 2) for b in along], axis=0)
         return jnp.concatenate([near, hop(near, 1)], axis=0)
+
+    chip, core = me // 2, me % 2
+
+    def gather_chips(x):
+        along = lines_of(x)
+        blocks = [(2 * k, b) for k, b in enumerate(along)]
+        blocks = blocks + [(k + 1, hop(b, 2)) for k, b in blocks]
+        near = jnp.zeros((x.shape[0] * n // 2, x.shape[1]), x.dtype)
+        for k, b in blocks:
+            near = lax.dynamic_update_slice_in_dim(near, b, (chip ^ k) * x.shape[0], 0)
+        return near
 
     def fold_core(near, arrived):
         r = near.shape[0] // (2 * lines)
-        parts = [slice(k * r, (k + 1) * r) for k in range(2 * lines)]
-        both = [near[p].astype(F32) + arrived[p].astype(F32) for p in parts]
-        return both[:lines], [x.astype(near.dtype) for x in both[lines:]]
+
+        def block(k):
+            at = (chip ^ k) * r
+            a = lax.dynamic_slice_in_dim(near, at, r).astype(F32)
+            return a + lax.dynamic_slice_in_dim(arrived, at, r).astype(F32)
+
+        here = [block(2 * k) for k in range(lines)]
+        return here, [block(2 * k + 1).astype(near.dtype) for k in range(lines)]
 
     def all_after(values, *others):
         return lax.optimization_barrier((*values, *others))[: len(values)]
@@ -484,8 +497,15 @@
 
     inv_two = inv_rms(mid)
     norm_two = (mid * inv_two * (1.0 + feed_gain)).astype(BF)
-    near_rows = gather_near(norm_two)
-    all_dy = reorder(dy_got)
+    near_rows = gather_chips(norm_two)
+    dy_pair = dy_got.reshape(n // 2, 2, rows, width)
+    all_dy = jnp.concatenate(
+        [
+            lax.dynamic_index_in_dim(dy_pair, c, 1, False).reshape(n // 2 * rows, width)
+            for c in (core, 1 - core)
+        ],
+        axis=0,
+    )
     up_other = jnp.concatenate(up_pieces, axis=0)
     w_eff, (gate_b, up_b) = fold(gate_mine, up_mine, gate_up_first, 0, None)
     w_eff, _ = fold(gate_other, up_other, gate_up_first, 1, w_eff)
@@ -540,7 +560,6 @@
     feed_gain_rows = jnp.sum(grad_norm_two * mid * inv_two, axis=0, keepdims=True)
     grad_mid = dy.astype(F32) + norm_back(mid, inv_two, feed_gain, grad_norm_two)
     grad_branch = grad_mid.astype(BF)
-    branch_all = lax.all_gather(grad_branch, "ctx", axis=0, tiled=True)
     grad_inner_out = mm(grad_branch, out_second, 1, 1).astype(BF)
     grad_attended = mm(
         jnp.concatenate([grad_branch, grad_inner_out], axis=1), out_full, 1, 1
@@ -574,6 +593,9 @@
         + up_part.astype(F32)
     ).astype(BF)
     down_back = swap(after(down_rows, up_part))
+    out_here, out_there = fold_core(out_near, hop(after(out_far, grad_kv), 1))
+    out_side = hop(jnp.concatenate(out_there, axis=0), 2)
+    branch_all = lax.all_gather(after(grad_branch, grad_kv), "ctx", axis=0, tiled=True)
     grad_kv = after(grad_kv, up_half, down_back)
     grad_k_rows = rotate(grad_kv[:, :HD], cosine, -sine_rows)
     grad_kv_rows = jnp.concatenate([grad_k_rows, grad_kv[:, HD:]], axis=1).astype(BF)
@@ -588,48 +610,51 @@
     grad_qkv = after(grad_qkv, up_ext)
     grad_inner_qkv = mm(grad_qkv, qkv_second, 1, 1).astype(BF)
     grad_norm_one = mm(
-        jnp.concatenate([grad_qkv, grad_inner_qkv], axis=1), qkv_full, 1, 1
+        after(jnp.concatenate([grad_qkv, grad_inner_qkv], axis=1), out_side), qkv_full, 1, 1
     )
     attn_gain_rows = jnp.sum(grad_norm_one * x * inv_one, axis=0, keepdims=True)
     grad_input = (grad_mid + norm_back(x, inv_one, attn_gain, grad_norm_one)).astype(BF)
     gate_back = swap(after(gate_got, down_back))
-    output = (mid + scatter(out_near, after(out_far, kv_all_grads))).astype(BF)
+    output = mid + out_here[0] + out_side[:rows].astype(F32)
+    for k in range(1, lines):
+        part = out_here[k] + out_side[k * rows : (k + 1) * rows].astype(F32)
+        output = output + hop(part.astype(BF), 4 * k).astype(F32)
+    output = output.astype(BF)
 
     def both_planes(own):
         own = own.astype(BF)
         return own.astype(F32) + swap(own).astype(F32)
 
-    g_out = mm(inputs[:, ext:], after(branch_all, grad_input), 0, 0).astype(BF)
 
     small = jnp.concatenate(
         [
             (mm(gate_half, gate_b, 1, 1) + mm(up_half, up_b, 1, 1))
             .astype(BF)
             .reshape(n, w_rows, rank),
-            mm(down_first[:h], after(down_half, g_out), 0, 0)
+            mm(down_first[:h], after(down_half, grad_input), 0, 0)
             .astype(BF)
             .reshape(n, w_rows, width * r_rows // w_rows),
         ],
         axis=2,
     )
-    small = after(small, g_out)
     small = scatter_whole(reorder(small.reshape(n * w_rows, small.shape[2])))
     gain_rows = jnp.concatenate([attn_gain_rows, feed_gain_rows], axis=0)
     gain_rows = gain_rows.reshape(2, n, w_rows).transpose(1, 0, 2).reshape(2 * n, w_rows)
     gain_rows = scatter_whole(reorder(gain_rows))
 
-    down_grads = stack(plane_id, down_rows, after(down_back, small), width)
+    down_grads = stack(plane_id, down_rows, after(down_back, grad_input), width)
     gate_up_grads = collect(
-        plane_id, gate_got, after(gate_back, down_grads[0]), w_rows, 0, None
+        plane_id, gate_got, after(gate_back, grad_input), w_rows, 0, None
     )
     up_got_other = swap(after(up_got, gate_back))
     gate_up_grads = collect(plane_id, up_got, up_got_other, w_rows, 1, gate_up_grads)
 
-    g_q = mm(inputs[:, :ext], q_all, 0, 0)
+    g_q = mm(inputs[:, :ext], after(q_all, down_grads[0]), 0, 0)
+    g_out = mm(inputs[:, ext:], after(branch_all, g_q), 0, 0).astype(BF)
     inputs_rel = reorder(inputs[:, :ext])
     g_kv = mm(inputs_rel, kv_all_grads, 0, 0)
     g_qkv = jnp.concatenate([g_q, g_kv], axis=1).astype(BF)
-    g_out = both_planes(after(g_out, gate_back))
+    g_out = g_out.astype(F32) + after(swap(g_out), gate_up_grads[0]).astype(F32)
     small = both_planes(after(small, gate_back))
     g_qkv = both_planes(g_qkv)
     gain_rows = gain_rows + swap(after(gain_rows, up_got_other))

time: 1140 us -> 1160 us (1.018)
  waiting for transfers between devices: 541 us -> 566 us
  local copies, waits for them, and re-layouts: 154 us -> 142 us
    unnamed x233 -> x232, local copies, waits for them, and re-layouts: 76.3 us -> 53.1 us
    ppermute x52, waiting for transfers between devices: 275 us -> 296 us  [hop(): return lax.ppermute(x, 'ctx', [(i, i ^ k) for i in range(n)])]
    ppermute x52, starting transfers between devices: 61.6 us -> 73.3 us  [hop(): return lax.ppermute(x, 'ctx', [(i, i ^ k) for i in range(n)])]
  transfers between devices with their start and end apart: 76 -> 76, of which waited for: 36 -> 28; matrix products, arithmetic and copies ran while one was open for 32% -> 30% of each run, Pallas kernels for 7% -> 7%
where the time goes in v3:
time: 1160 us; the launch traced here: 1150 us
  waiting for transfers between devices  566 us (49%)
  matrix products  164 us (14%)
  local copies, waits for them, and re-layouts  142 us (12%)
  starting transfers between devices  113 us (10%)
  Pallas kernels  84 us (7%)
  other arithmetic  68.4 us (6%)
  between operations  16 us (1%)
    ppermute x52, waiting for transfers between devices, hop(): return lax.ppermute(x, 'ctx', [(i, i ^ k) for i in range(n)])  296 us
    dot_general x35, matrix products, mm(): lax.dot_general(a, b, (((ca,), (cb,)), ((), ())), preferred_element_type=...  164 us
    all_gather x1, waiting for transfers between devices, body(): qkv_got = lax.all_gather(qkv_ext, 'ctx', axis=0, tiled=True)  129 us
    ppermute x14, waiting for transfers between devices, swap(): return lax.ppermute(x, 'grp', [(0, 1), (1, 0)])  115 us
    ppermute x52, starting transfers between devices, hop(): return lax.ppermute(x, 'ctx', [(i, i ^ k) for i in range(n)])  73.3 us
    unnamed x232, local copies, waits for them, and re-layouts  53.1 us
    all_gather x1, waiting for transfers between devices, body(): out_got = lax.all_gather(out_ext, 'ctx', axis=0, tiled=True)  25.7 us
    pallas_call x1, Pallas kernels, forward(): pl.pallas_call(forward_kernel, out_shape=(jax.ShapeDtypeStruct((t, f), BF...  25.5 us
  transfers between devices with their start and end apart: 76, of which 28 were waited for; matrix products, arithmetic and copies ran while one was open for 30% of the time, Pallas kernels for 7%

profile of v3, /device:TPU:0, one launch (start us, length us, event | category | flops | bytes accessed | tf_op | source)
XLA Modules:
  0.0 1152.9 jit_solution(17195261599061113365)
XLA Ops:
  17.1 7.4 all-to-all-start
  31.7 128.7 %all-gather.6.cloned.1.call-done = bf16[2048,3200]{1,0:T(8,128)(2,1)} async-done(((bf16[128,3200]{1,0:T(8,128)(2,1)}), bf16[2048,3200]{1,0:T(8,128)(2,1)}) %all-gather.6.cloned.1.call-update) | async-done | bytes 13107216 | tf_op jit(solution)/shard_map/all_gather | solution.py:404
  169.2 6.6 fusion.3
  191.0 13.5 %collective-permute-done.1 = bf16[128,512]{1,0:T(8,128)(2,1)} collective-permute-done((bf16[128,512]{1,0:T(8,128)(2,1)}, bf16[128,512]{1,0:T(8,128)(2,1)}, u32[]{:S(2)}, u32[]{:S(2)}) %collective-permute-start.1) | collective-permute-done | bytes 131104 | tf_op jit(solution)/shard_map/ppermute | solution.py:305
  225.4 5.6 all-to-all-start.1
  238.5 8.9 collective-permute-done.8
  248.7 23.5 %collective-permute-done.9 = bf16[8,144,512]{2,1,0:T(8,128)(2,1)} collective-permute-done((bf16[8,144,512]{2,1,0:T(8,128)(2,1)}, bf16[8,144,512]{2,1,0:T(8,128)(2,1)}, u32[]{:S(2)}, u32[]{:S(2)}) %collective-permute-start.9) | collective-permute-done | bytes 1179680 | tf_op jit(solution)/shard_map/ppermute | solution.py:308
  289.4 25.7 %all-gather.8.cloned.1.call-done = bf16[2048,3072]{1,0:T(8,128)(2,1)} async-done(((bf16[128,3072]{1,0:T(8,128)(2,1)}), bf16[2048,3072]{1,0:T(8,128)(2,1)}) %all-gather.8.cloned.1.call-update) | async-done | bytes 12582928 | tf_op jit(solution)/shard_map/all_gather | solution.py:415
  326.7 5.6 fusion.7
  352.2 6.8 shard_map.290.refs_0_
  359.9 62.1 %collective-permute-done.11 = bf16[128,2048]{1,0:T(8,128)(2,1)S(1)} collective-permute-done((bf16[128,2048]{1,0:T(8,128)(2,1)}, bf16[128,2048]{1,0:T(8,128)(2,1)S(1)}, u32[]{:S(2)}, u32[]{:S(2)}) %collective-permute-start.11) | collective-permute-done | bytes 524320 | tf_op jit(solution)/shard_map/ppermute | solution.py:305
  428.8 8.0 collective-permute-done.14
  437.7 10.4 collective-permute-done.15
  448.9 7.0 collective-permute-done.16
  459.7 6.3 shard_map.291.w_ref
  483.1 8.3 constant_dynamic-slice_fusion.17
  491.4 8.5 pad_maximum_fusion.dy_ref
  499.9 25.5 %shard_map.292 = (bf16[2048,1024]{1,0:T(8,128)(2,1)S(1)}, bf16[2048,1024]{1,0:T(8,128)(2,1)S(1)}, bf16[2048,1024]{1,0:T(8,128)(2,1)}) custom-call(bf16[2048,2048]{1,0:T(8,128)(2,1)} %constant_dynamic-update-slice_fusion.26.x_ref, bf16[2048,2048]{1,0:T(8,128)(2,1)} %shard_map.291.w_ref), custom_call_target="tpu_custom_call" | custom-call | flops 17179869184 | bytes 29360128 | tf_op jit(solution)/shard_map/pallas_call | solution.py:136
  525.4 10.9 convolution_convert_fusion.2
  536.3 14.7 %shard_map.293 = bf16[2048,2048]{1,0:T(8,128)(2,1)} custom-call(bf16[2048,2048]{1,0:T(8,128)(2,1)} %pad_maximum_fusion.dy_ref, bf16[1024,2048]{1,0:T(8,128)(2,1)S(1)} %copy-done, bf16[2048,1024]{1,0:T(8,128)(2,1)S(1)} %get-tuple-element.81.act_ref, bf16[2048,1024]{1,0:T(8,128)(2,1)} %get-tuple-element.82.slope_ref), custom_call_target="tpu_custom_call" | custom-call | flops 8589934592 | bytes 29360128 | tf_op jit(solution)/shard_map/pallas_call | solution.py:168
  551.1 12.0 %fusion.25 = bf16[1024,2048]{1,0:T(8,128)(2,1)} fusion(bf16[2048,2048]{1,0:T(8,128)(2,1)S(1)} %bitcast.128, bf16[2048,2048]{1,0:T(8,128)(2,1)} %shard_map.293), kind=kOutput, calls=%fused_computation.63 | convolution fusion | flops 8592031744 | bytes 16777216 | tf_op jit(solution)/shard_map/dot_general | solution.py:19
  564.9 13.9 %fusion.19 = bf16[1024,2048]{1,0:T(8,128)(2,1)S(1)} fusion(bf16[2048,2048]{1,0:T(8,128)(2,1)} %shard_map.291.w_ref, bf16[2048,2048]{1,0:T(8,128)(2,1)} %shard_map.293), kind=kOutput, calls=%fused_computation.61 | convolution fusion | flops 8592031744 | bytes 16777216 | tf_op jit(solution)/shard_map/dot_general | solution.py:19
  587.6 11.6 %fusion.22 = bf16[2048,1024]{1,0:T(8,128)(2,1)S(1)} fusion(bf16[2048,2048]{1,0:T(8,128)(2,1)} %constant_dynamic-update-slice_fusion.26.x_ref, bf16[2048,2048]{1,0:T(8,128)(2,1)S(1)} %bitcast.166), kind=kOutput, calls=%fused_computation.62 | convolution fusion | flops 8592031744 | bytes 16777216 | tf_op jit(solution)/shard_map/dot_general | solution.py:19
  604.2 6.0 convolution_convert_fusion.1
  614.1 6.0 add_convert_fusion.3
  620.1 6.2 convolution_convert_fusion
  638.3 23.4 %collective-permute-done.29 = bf16[2048,512]{1,0:T(8,128)(2,1)} collective-permute-done((bf16[2048,512]{1,0:T(8,128)(2,1)}, bf16[2048,512]{1,0:T(8,128)(2,1)}, u32[]{:S(2)}, u32[]{:S(2)}) %collective-permute-start.29) | collective-permute-done | bytes 2097184 | tf_op jit(solution)/shard_map/ppermute | solution.py:308
  661.8 10.6 add_convert_fusion.2
  672.3 9.7 collective-permute-done.26
  686.9 8.2 convert_multiply_fusion.5
  703.3 6.0 multiply_convert_fusion
  730.8 26.3 %collective-permute-done.32 = bf16[512,512]{1,0:T(8,128)(2,1)S(1)} collective-permute-done((bf16[512,512]{1,0:T(8,128)(2,1)S(1)}, bf16[512,512]{1,0:T(8,128)(2,1)S(1)}, u32[]{:S(2)}, u32[]{:S(2)}) %collective-permute-start.32) | collective-permute-done | bytes 524320 | tf_op jit(solution)/shard_map/ppermute | solution.py:305
  761.5 15.8 %collective-permute-done.33 = bf16[128,512]{1,0:T(8,128)(2,1)S(1)} collective-permute-done((bf16[128,512]{1,0:T(8,128)(2,1)S(1)}, bf16[128,512]{1,0:T(8,128)(2,1)S(1)}, u32[]{:S(2)}, u32[]{:S(2)}) %collective-permute-start.33) | collective-permute-done | bytes 131104 | tf_op jit(solution)/shard_map/ppermute | solution.py:305
  777.3 7.2 collective-permute-done.35
  784.5 48.4 %collective-permute-done.34 = bf16[128,512]{1,0:T(8,128)(2,1)S(1)} collective-permute-done((bf16[128,512]{1,0:T(8,128)(2,1)S(1)}, bf16[128,512]{1,0:T(8,128)(2,1)S(1)}, u32[]{:S(2)}, u32[]{:S(2)}) %collective-permute-start.34) | collective-permute-done | bytes 131104 | tf_op jit(solution)/shard_map/ppermute | solution.py:305
  841.1 9.2 add_convert_fusion.1
  850.3 40.7 %collective-permute-done.41.other = bf16[512,2304]{1,0:T(8,128)(2,1)} collective-permute-done((bf16[512,2304]{1,0:T(8,128)(2,1)}, bf16[512,2304]{1,0:T(8,128)(2,1)}, u32[]{:S(2)}, u32[]{:S(2)}) %collective-permute-start.41) | collective-permute-done | bytes 2359328 | tf_op jit(solution)/shard_map/ppermute | solution.py:308
  918.3 10.9 collective-permute-done.51
  939.2 41.1 %collective-permute-done.37 = bf16[512,2048]{1,0:T(8,128)(2,1)} collective-permute-done((bf16[512,2048]{1,0:T(8,128)(2,1)}, bf16[512,2048]{1,0:T(8,128)(2,1)}, u32[]{:S(2)}, u32[]{:S(2)}) %collective-permute-start.37) | collective-permute-done | bytes 2097184 | tf_op jit(solution)/shard_map/ppermute | solution.py:305
  980.3 6.9 fusion.49
  1021.5 5.8 collective-permute-done.61
  1044.2 9.5 shard_map.294
  1053.7 6.7 shard_map.295
  1060.3 16.2 %collective-permute-done.64 = bf16[128,512]{0,1:T(8,128)(2,1)} collective-permute-done((bf16[128,512]{0,1:T(8,128)(2,1)}, bf16[128,512]{0,1:T(8,128)(2,1)}, u32[]{:S(2)}, u32[]{:S(2)}) %collective-permute-start.64) | collective-permute-done | bytes 131104 | tf_op jit(solution)/shard_map/ppermute | solution.py:305
  1076.5 15.3 %collective-permute-start.63 = (bf16[128,512]{0,1:T(8,128)(2,1)}, bf16[128,512]{0,1:T(8,128)(2,1)S(1)}, u32[]{:S(2)}, u32[]{:S(2)}) collective-permute-start(bf16[128,512]{0,1:T(8,128)(2,1)} %get-tuple-element.248), channel_id=1, source_target_pairs={{0,8},{1,9},{2,10},{3,11},{4,12},{5,13},{6,14},{7,15},{8,0},{9,1},... | collective-permute-start | bytes 393224 | tf_op jit(solution)/shard_map/ppermute | solution.py:305
  1105.0 6.5 shard_map.296
  1111.6 6.3 fusion.127
  1125.4 12.0 %collective-permute-done.58 = bf16[144,2560]{1,0:T(8,128)(2,1)S(1)} collective-permute-done((bf16[144,2560]{1,0:T(8,128)(2,1)S(1)}, bf16[144,2560]{1,0:T(8,128)(2,1)S(1)}, u32[]{:S(2)}, u32[]{:S(2)}) %collective-permute-start.58) | collective-permute-done | bytes 737312 | tf_op jit(solution)/shard_map/ppermute | solution.py:308
  (544 shorter events, 344.8 us)
Async XLA Ops:
  7.2 153.2 %all-gather.6.cloned.1.call-start = ((), (), s32[]{:S(2)}) async-start(), calls=%async_computation.5 | async-start | bytes 13926400 | tf_op jit(solution)/shard_map/all_gather | solution.py:404
  11.9 303.1 %all-gather.8.cloned.1.call-start = ((), (), s32[]{:S(2)}) async-start(), calls=%async_computation.6 | async-start | bytes 13369344 | tf_op jit(solution)/shard_map/all_gather | solution.py:415
  17.1 152.0 %all-to-all-start = ((bf16[16,144,512]{2,1,0:T(8,128)(2,1)}), bf16[16,144,512]{2,1,0:T(8,128)(2,1)S(1)}, u32[]{:S(2)}, u32[]{:S(2)}) async-start(bf16[16,144,512]{2,1,0:T(8,128)(2,1)} %shard_map.288), calls=%async_computation | async-start | bytes 4718592 | tf_op jit(solution)/shard_map/all_to_all | solution.py:423
  24.5 458.5 %all-gather.10.cloned.1.call-start = ((), (), s32[]{:S(2)}) async-start(), calls=%async_computation.7 | async-start | bytes 8912896 | tf_op jit(solution)/shard_map/all_gather | solution.py:472
  181.7 26.1 %collective-permute-start = (bf16[128,512]{1,0:T(8,128)(2,1)}, bf16[128,512]{1,0:T(8,128)(2,1)}, u32[]{:S(2)}, u32[]{:S(2)}) collective-permute-start(bf16[128,512]{1,0:T(8,128)(2,1)} %get-tuple-element.291), channel_id=1, source_target_pairs={{0,4},{1,5},{2,6},{3,7},{4,0},{5,1},{6,2},{7,3},{8,12},{9,13},{10,... | collective-permute-start | bytes 393224 | tf_op jit(solution)/shard_map/ppermute | solution.py:305
  184.6 28.1 %collective-permute-start.3 = (bf16[128,512]{1,0:T(8,128)(2,1)}, bf16[128,512]{1,0:T(8,128)(2,1)}, u32[]{:S(2)}, u32[]{:S(2)}) collective-permute-start(bf16[128,512]{1,0:T(8,128)(2,1)} %get-tuple-element.291), channel_id=1, source_target_pairs={{0,2},{1,3},{2,0},{3,1},{4,6},{5,7},{6,4},{7,5},{8,10},{9,11},{10,... | collective-permute-start | bytes 393224 | tf_op jit(solution)/shard_map/ppermute | solution.py:305
  218.3 29.1 %collective-permute-start.8 = (bf16[8,144,512]{2,1,0:T(8,128)(2,1)}, bf16[8,144,512]{2,1,0:T(8,128)(2,1)}, u32[]{:S(2)}, u32[]{:S(2)}) collective-permute-start(bf16[8,144,512]{2,1,0:T(8,128)(2,1)} %get-tuple-element.231), channel_id=1, source_target_pairs={{0,16},{16,0},{1,17},{17,1},{2,18},{18,2},{3,19},{19,3},{4,20},{20... | collective-permute-start | bytes 3538952 | tf_op jit(solution)/shard_map/ppermute | solution.py:308
  220.8 51.5 %collective-permute-start.9 = (bf16[8,144,512]{2,1,0:T(8,128)(2,1)}, bf16[8,144,512]{2,1,0:T(8,128)(2,1)}, u32[]{:S(2)}, u32[]{:S(2)}) collective-permute-start(bf16[8,144,512]{2,1,0:T(8,128)(2,1)} %get-tuple-element.230), channel_id=1, source_target_pairs={{0,16},{16,0},{1,17},{17,1},{2,18},{18,2},{3,19},{19,3},{4,20},{20... | collective-permute-start | bytes 3538952 | tf_op jit(solution)/shard_map/ppermute | solution.py:308
  225.4 101.4 %all-to-all-start.1 = ((bf16[16,144,512]{2,1,0:T(8,128)(2,1)}), bf16[16,144,512]{2,1,0:T(8,128)(2,1)}, u32[]{:S(2)}, u32[]{:S(2)}) async-start(bf16[16,144,512]{2,1,0:T(8,128)(2,1)} %shard_map.289), calls=%async_computation.1 | async-start | bytes 4718592 | tf_op jit(solution)/shard_map/all_to_all | solution.py:423
  341.5 82.5 %collective-permute-start.12 = (bf16[128,2048]{1,0:T(8,128)(2,1)}, bf16[128,2048]{1,0:T(8,128)(2,1)S(1)}, u32[]{:S(2)}, u32[]{:S(2)}) collective-permute-start(bf16[128,2048]{1,0:T(8,128)(2,1)} %get-tuple-element.202), channel_id=1, source_target_pairs={{0,12},{1,13},{2,14},{3,15},{4,8},{5,9},{6,10},{7,11},{8,4},{9,5},... | collective-permute-start | bytes 1572872 | tf_op jit(solution)/shard_map/ppermute | solution.py:305
  342.4 79.6 %collective-permute-start.11 = (bf16[128,2048]{1,0:T(8,128)(2,1)}, bf16[128,2048]{1,0:T(8,128)(2,1)S(1)}, u32[]{:S(2)}, u32[]{:S(2)}) collective-permute-start(bf16[128,2048]{1,0:T(8,128)(2,1)} %get-tuple-element.202), channel_id=1, source_target_pairs={{0,8},{1,9},{2,10},{3,11},{4,12},{5,13},{6,14},{7,15},{8,0},{9,1},... | collective-permute-start | bytes 1572872 | tf_op jit(solution)/shard_map/ppermute | solution.py:305
  344.8 80.9 %collective-permute-start.13 = (bf16[128,2048]{1,0:T(8,128)(2,1)}, bf16[128,2048]{1,0:T(8,128)(2,1)}, u32[]{:S(2)}, u32[]{:S(2)}) collective-permute-start(bf16[128,2048]{1,0:T(8,128)(2,1)} %get-tuple-element.202), channel_id=1, source_target_pairs={{0,2},{1,3},{2,0},{3,1},{4,6},{5,7},{6,4},{7,5},{8,10},{9,11},{10,... | collective-permute-start | bytes 1572872 | tf_op jit(solution)/shard_map/ppermute | solution.py:305
  349.1 107.8 %collective-permute-start.18 = (bf16[8,144,512]{2,1,0:T(8,128)(2,1)}, bf16[8,144,512]{2,1,0:T(8,128)(2,1)}, u32[]{:S(2)}, u32[]{:S(2)}) collective-permute-start(bf16[8,144,512]{2,1,0:T(8,128)(2,1)} %get-tuple-element.228), channel_id=1, source_target_pairs={{0,16},{16,0},{1,17},{17,1},{2,18},{18,2},{3,19},{19,3},{4,20},{20... | collective-permute-start | bytes 3538952 | tf_op jit(solution)/shard_map/ppermute | solution.py:308
  359.0 97.7 %collective-permute-start.17 = (bf16[8,144,512]{2,1,0:T(8,128)(2,1)S(1)}, bf16[8,144,512]{2,1,0:T(8,128)(2,1)S(1)}, u32[]{:S(2)}, u32[]{:S(2)}) collective-permute-start(bf16[8,144,512]{2,1,0:T(8,128)(2,1)S(1)} %get-tuple-element.229), channel_id=1, source_target_pairs={{0,16},{16,0},{1,17},{17,1},{2,18},{18,2},{3,19},{19,3},{4,20},{20... | collective-permute-start | bytes 3538952 | tf_op jit(solution)/shard_map/ppermute | solution.py:308
  425.7 30.2 %collective-permute-start.16 = (bf16[128,2048]{1,0:T(8,128)(2,1)S(1)}, bf16[128,2048]{1,0:T(8,128)(2,1)S(1)}, u32[]{:S(2)}, u32[]{:S(2)}) collective-permute-start(bf16[128,2048]{1,0:T(8,128)(2,1)S(1)} %collective-permute-done.12), channel_id=1, source_target_pairs={{0,2},{1,3},{2,0},{3,1},{4,6},{5,7},{6,4},{7,5},{8,10},{9,11},{10,... | collective-permute-start | bytes 1572872 | tf_op jit(solution)/shard_map/ppermute | solution.py:305
  479.3 84.2 %all-to-all-start.2 = ((bf16[16,128,288]{1,2,0:T(8,128)(2,1)}), bf16[16,128,288]{1,2,0:T(8,128)(2,1)S(1)}, u32[]{:S(2)}, u32[]{:S(2)}) async-start(bf16[16,128,288]{1,2,0:T(8,128)(2,1)} %maximum_bitcast_fusion), calls=%async_computation.2 | async-start | bytes 2359296 | tf_op jit(solution)/shard_map/all_to_all | solution.py:556
  483.0 628.6 %all-gather.12.cloned.1.call-start = ((), (), s32[]{:S(2)}) async-start(), calls=%async_computation.8 | async-start | bytes 8912896 | tf_op jit(solution)/shard_map/all_gather | solution.py:590
  563.6 47.9 %collective-permute-start.28 = (bf16[512,2048]{1,0:T(8,128)(2,1)}, bf16[512,2048]{1,0:T(8,128)(2,1)S(1)}, u32[]{:S(2)}, u32[]{:S(2)}) collective-permute-start(bf16[512,2048]{1,0:T(8,128)(2,1)} %convolution_convert_fusion.2), channel_id=1, source_target_pairs={{0,16},{16,0},{1,17},{17,1},{2,18},{18,2},{3,19},{19,3},{4,20},{20... | collective-permute-start | bytes 6291464 | tf_op jit(solution)/shard_map/ppermute | solution.py:308
  583.6 45.2 %collective-permute-start.24 = (bf16[128,2048]{1,0:T(8,128)(2,1)}, bf16[128,2048]{1,0:T(8,128)(2,1)}, u32[]{:S(2)}, u32[]{:S(2)}) collective-permute-start(bf16[128,2048]{1,0:T(8,128)(2,1)} %get-tuple-element.218), channel_id=1, source_target_pairs={{0,2},{1,3},{2,0},{3,1},{4,6},{5,7},{6,4},{7,5},{8,10},{9,11},{10,... | collective-permute-start | bytes 1572872 | tf_op jit(solution)/shard_map/ppermute | solution.py:305
  585.1 44.4 %collective-permute-start.23 = (bf16[128,2048]{1,0:T(8,128)(2,1)}, bf16[128,2048]{1,0:T(8,128)(2,1)}, u32[]{:S(2)}, u32[]{:S(2)}) collective-permute-start(bf16[128,2048]{1,0:T(8,128)(2,1)} %get-tuple-element.219), channel_id=1, source_target_pairs={{0,2},{1,3},{2,0},{3,1},{4,6},{5,7},{6,4},{7,5},{8,10},{9,11},{10,... | collective-permute-start | bytes 1572872 | tf_op jit(solution)/shard_map/ppermute | solution.py:305
  585.6 43.9 %collective-permute-start.22 = (bf16[128,2048]{1,0:T(8,128)(2,1)}, bf16[128,2048]{1,0:T(8,128)(2,1)}, u32[]{:S(2)}, u32[]{:S(2)}) collective-permute-start(bf16[128,2048]{1,0:T(8,128)(2,1)} %get-tuple-element.220), channel_id=1, source_target_pairs={{0,2},{1,3},{2,0},{3,1},{4,6},{5,7},{6,4},{7,5},{8,10},{9,11},{10,... | collective-permute-start | bytes 1572872 | tf_op jit(solution)/shard_map/ppermute | solution.py:305
  587.2 44.0 %collective-permute-start.21 = (bf16[128,2048]{1,0:T(8,128)(2,1)S(1)}, bf16[128,2048]{1,0:T(8,128)(2,1)S(1)}, u32[]{:S(2)}, u32[]{:S(2)}) collective-permute-start(bf16[128,2048]{1,0:T(8,128)(2,1)S(1)} %get-tuple-element.221), channel_id=1, source_target_pairs={{0,2},{1,3},{2,0},{3,1},{4,6},{5,7},{6,4},{7,5},{8,10},{9,11},{10,... | collective-permute-start | bytes 1572872 | tf_op jit(solution)/shard_map/ppermute | solution.py:305
  612.9 48.9 %collective-permute-start.29 = (bf16[2048,512]{1,0:T(8,128)(2,1)}, bf16[2048,512]{1,0:T(8,128)(2,1)}, u32[]{:S(2)}, u32[]{:S(2)}) collective-permute-start(bf16[2048,512]{1,0:T(8,128)(2,1)} %get-tuple-element.225), channel_id=1, source_target_pairs={{0,16},{16,0},{1,17},{17,1},{2,18},{18,2},{3,19},{19,3},{4,20},{20... | collective-permute-start | bytes 6291464 | tf_op jit(solution)/shard_map/ppermute | solution.py:308
  628.7 80.6 %collective-permute-start.30 = (bf16[2048,512]{1,0:T(8,128)(2,1)}, bf16[2048,512]{1,0:T(8,128)(2,1)}, u32[]{:S(2)}, u32[]{:S(2)}) collective-permute-start(bf16[2048,512]{1,0:T(8,128)(2,1)} %get-tuple-element.224), channel_id=1, source_target_pairs={{0,16},{16,0},{1,17},{17,1},{2,18},{18,2},{3,19},{19,3},{4,20},{20... | collective-permute-start | bytes 6291464 | tf_op jit(solution)/shard_map/ppermute | solution.py:308
  633.9 38.5 %collective-permute-start.27 = (bf16[128,2048]{1,0:T(8,128)(2,1)S(1)}, bf16[128,2048]{1,0:T(8,128)(2,1)S(1)}, u32[]{:S(2)}, u32[]{:S(2)}) collective-permute-start(bf16[128,2048]{1,0:T(8,128)(2,1)S(1)} %get-tuple-element.215), channel_id=1, source_target_pairs={{0,12},{1,13},{2,14},{3,15},{4,8},{5,9},{6,10},{7,11},{8,4},{9,5},... | collective-permute-start | bytes 1572872 | tf_op jit(solution)/shard_map/ppermute | solution.py:305
  637.5 44.4 %collective-permute-start.26 = (bf16[128,2048]{1,0:T(8,128)(2,1)S(1)}, bf16[128,2048]{1,0:T(8,128)(2,1)S(1)}, u32[]{:S(2)}, u32[]{:S(2)}) collective-permute-start(bf16[128,2048]{1,0:T(8,128)(2,1)S(1)} %get-tuple-element.216), channel_id=1, source_target_pairs={{0,8},{1,9},{2,10},{3,11},{4,12},{5,13},{6,14},{7,15},{8,0},{9,1},... | collective-permute-start | bytes 1572872 | tf_op jit(solution)/shard_map/ppermute | solution.py:305
  637.6 44.4 %collective-permute-start.25 = (bf16[128,2048]{1,0:T(8,128)(2,1)S(1)}, bf16[128,2048]{1,0:T(8,128)(2,1)S(1)}, u32[]{:S(2)}, u32[]{:S(2)}) collective-permute-start(bf16[128,2048]{1,0:T(8,128)(2,1)S(1)} %get-tuple-element.217), channel_id=1, source_target_pairs={{0,4},{1,5},{2,6},{3,7},{4,0},{5,1},{6,2},{7,3},{8,12},{9,13},{10,... | collective-permute-start | bytes 1572872 | tf_op jit(solution)/shard_map/ppermute | solution.py:305
  713.7 127.3 %all-to-all-start.3 = ((bf16[16,144,512]{2,1,0:T(8,128)(2,1)}), bf16[16,144,512]{2,1,0:T(8,128)(2,1)}, u32[]{:S(2)}, u32[]{:S(2)}) async-start(bf16[16,144,512]{2,1,0:T(8,128)(2,1)} %pad_maximum_fusion.3), calls=%async_computation.3 | async-start | bytes 4718592 | tf_op jit(solution)/shard_map/all_to_all | solution.py:423
  718.5 401.2 %all-gather.14.cloned.1.call-start = ((), (), s32[]{:S(2)}) async-start(), calls=%async_computation.9 | async-start | bytes 8912896 | tf_op jit(solution)/shard_map/all_gather | solution.py:598
  728.8 28.2 %collective-permute-start.32 = (bf16[512,512]{1,0:T(8,128)(2,1)S(1)}, bf16[512,512]{1,0:T(8,128)(2,1)S(1)}, u32[]{:S(2)}, u32[]{:S(2)}) collective-permute-start(bf16[512,512]{1,0:T(8,128)(2,1)S(1)} %slice.478), channel_id=1, source_target_pairs={{0,2},{1,3},{2,0},{3,1},{4,6},{5,7},{6,4},{7,5},{8,10},{9,11},{10,... | collective-permute-start | bytes 1572872 | tf_op jit(solution)/shard_map/ppermute | solution.py:305
  757.4 27.0 %collective-permute-start.35 = (bf16[128,512]{1,0:T(8,128)(2,1)S(1)}, bf16[128,512]{1,0:T(8,128)(2,1)S(1)}, u32[]{:S(2)}, u32[]{:S(2)}) collective-permute-start(bf16[128,512]{1,0:T(8,128)(2,1)S(1)} %get-tuple-element.250), channel_id=1, source_target_pairs={{0,12},{1,13},{2,14},{3,15},{4,8},{5,9},{6,10},{7,11},{8,4},{9,5},... | collective-permute-start | bytes 393224 | tf_op jit(solution)/shard_map/ppermute | solution.py:305
  761.0 71.8 %collective-permute-start.34 = (bf16[128,512]{1,0:T(8,128)(2,1)S(1)}, bf16[128,512]{1,0:T(8,128)(2,1)S(1)}, u32[]{:S(2)}, u32[]{:S(2)}) collective-permute-start(bf16[128,512]{1,0:T(8,128)(2,1)S(1)} %get-tuple-element.251), channel_id=1, source_target_pairs={{0,8},{1,9},{2,10},{3,11},{4,12},{5,13},{6,14},{7,15},{8,0},{9,1},... | collective-permute-start | bytes 393224 | tf_op jit(solution)/shard_map/ppermute | solution.py:305
  832.9 73.6 %collective-permute-start.36 = (bf16[1024,2048]{1,0:T(8,128)(2,1)}, bf16[1024,2048]{1,0:T(8,128)(2,1)}, u32[]{:S(2)}, u32[]{:S(2)}) collective-permute-start(bf16[1024,2048]{1,0:T(8,128)(2,1)} %convolution_convert_fusion), channel_id=1, source_target_pairs={{0,1},{1,0},{2,3},{3,2},{4,5},{5,4},{6,7},{7,6},{8,9},{9,8},{10,11... | collective-permute-start | bytes 12582920 | tf_op jit(solution)/shard_map/ppermute | solution.py:305
  837.2 53.7 %collective-permute-start.41 = (bf16[512,2304]{1,0:T(8,128)(2,1)}, bf16[512,2304]{1,0:T(8,128)(2,1)}, u32[]{:S(2)}, u32[]{:S(2)}) collective-permute-start(bf16[512,2304]{1,0:T(8,128)(2,1)} %pad_maximum_fusion.2.mine), channel_id=1, source_target_pairs={{0,16},{16,0},{1,17},{17,1},{2,18},{18,2},{3,19},{19,3},{4,20},{20... | collective-permute-start | bytes 7077896 | tf_op jit(solution)/shard_map/ppermute | solution.py:308
  892.4 43.5 %collective-permute-start.53 = (bf16[128,512]{1,0:T(8,128)(2,1)}, bf16[128,512]{1,0:T(8,128)(2,1)}, u32[]{:S(2)}, u32[]{:S(2)}) collective-permute-start(bf16[128,512]{1,0:T(8,128)(2,1)} %get-tuple-element.274), channel_id=1, source_target_pairs={{0,2},{1,3},{2,0},{3,1},{4,6},{5,7},{6,4},{7,5},{8,10},{9,11},{10,... | collective-permute-start | bytes 393224 | tf_op jit(solution)/shard_map/ppermute | solution.py:305
  896.3 32.8 %collective-permute-start.51 = (bf16[128,512]{1,0:T(8,128)(2,1)}, bf16[128,512]{1,0:T(8,128)(2,1)}, u32[]{:S(2)}, u32[]{:S(2)}) collective-permute-start(bf16[128,512]{1,0:T(8,128)(2,1)} %get-tuple-element.274), channel_id=1, source_target_pairs={{0,8},{1,9},{2,10},{3,11},{4,12},{5,13},{6,14},{7,15},{8,0},{9,1},... | collective-permute-start | bytes 393224 | tf_op jit(solution)/shard_map/ppermute | solution.py:305
  896.3 34.4 %collective-permute-start.50 = (bf16[128,512]{1,0:T(8,128)(2,1)}, bf16[128,512]{1,0:T(8,128)(2,1)}, u32[]{:S(2)}, u32[]{:S(2)}) collective-permute-start(bf16[128,512]{1,0:T(8,128)(2,1)} %get-tuple-element.274), channel_id=1, source_target_pairs={{0,4},{1,5},{2,6},{3,7},{4,0},{5,1},{6,2},{7,3},{8,12},{9,13},{10,... | collective-permute-start | bytes 393224 | tf_op jit(solution)/shard_map/ppermute | solution.py:305
  901.9 118.9 %all-to-all-start.4 = ((bf16[16,144,512]{2,1,0:T(8,128)(2,1)}), bf16[16,144,512]{2,1,0:T(8,128)(2,1)}, u32[]{:S(2)}, u32[]{:S(2)}) async-start(bf16[16,144,512]{2,1,0:T(8,128)(2,1)} %pad_maximum_fusion.4), calls=%async_computation.4 | async-start | bytes 4718592 | tf_op jit(solution)/shard_map/all_to_all | solution.py:423
  911.2 69.1 %collective-permute-start.37 = (bf16[512,2048]{1,0:T(8,128)(2,1)}, bf16[512,2048]{1,0:T(8,128)(2,1)}, u32[]{:S(2)}, u32[]{:S(2)}) collective-permute-start(bf16[512,2048]{1,0:T(8,128)(2,1)} %pad_maximum_fusion.5), channel_id=1, source_target_pairs={{0,2},{1,3},{2,0},{3,1},{4,6},{5,7},{6,4},{7,5},{8,10},{9,11},{10,... | collective-permute-start | bytes 6291464 | tf_op jit(solution)/shard_map/ppermute | solution.py:305
  917.4 103.3 %collective-permute-start.47 = (bf16[16,144,512]{2,1,0:T(8,128)(2,1)}, bf16[16,144,512]{2,1,0:T(8,128)(2,1)}, u32[]{:S(2)}, u32[]{:S(2)}) collective-permute-start(bf16[16,144,512]{2,1,0:T(8,128)(2,1)} %all-to-all-done.3.mine), channel_id=1, source_target_pairs={{0,16},{16,0},{1,17},{17,1},{2,18},{18,2},{3,19},{19,3},{4,20},{20... | collective-permute-start | bytes 7077896 | tf_op jit(solution)/shard_map/ppermute | solution.py:308
  929.1 71.0 %collective-permute-start.56 = (bf16[128,512]{1,0:T(8,128)(2,1)}, bf16[128,512]{1,0:T(8,128)(2,1)S(1)}, u32[]{:S(2)}, u32[]{:S(2)}) collective-permute-start(bf16[128,512]{1,0:T(8,128)(2,1)} %collective-permute-done.52), channel_id=1, source_target_pairs={{0,2},{1,3},{2,0},{3,1},{4,6},{5,7},{6,4},{7,5},{8,10},{9,11},{10,... | collective-permute-start | bytes 393224 | tf_op jit(solution)/shard_map/ppermute | solution.py:305
  930.7 68.7 %collective-permute-start.55 = (bf16[128,512]{1,0:T(8,128)(2,1)}, bf16[128,512]{1,0:T(8,128)(2,1)S(1)}, u32[]{:S(2)}, u32[]{:S(2)}) collective-permute-start(bf16[128,512]{1,0:T(8,128)(2,1)} %collective-permute-done.51), channel_id=1, source_target_pairs={{0,2},{1,3},{2,0},{3,1},{4,6},{5,7},{6,4},{7,5},{8,10},{9,11},{10,... | collective-permute-start | bytes 393224 | tf_op jit(solution)/shard_map/ppermute | solution.py:305
  936.0 62.7 %collective-permute-start.54 = (bf16[128,512]{1,0:T(8,128)(2,1)}, bf16[128,512]{1,0:T(8,128)(2,1)S(1)}, u32[]{:S(2)}, u32[]{:S(2)}) collective-permute-start(bf16[128,512]{1,0:T(8,128)(2,1)} %collective-permute-done.50), channel_id=1, source_target_pairs={{0,2},{1,3},{2,0},{3,1},{4,6},{5,7},{6,4},{7,5},{8,10},{9,11},{10,... | collective-permute-start | bytes 393224 | tf_op jit(solution)/shard_map/ppermute | solution.py:305
  1020.8 81.8 %collective-permute-start.48 = (bf16[16,144,512]{2,1,0:T(8,128)(2,1)}, bf16[16,144,512]{2,1,0:T(8,128)(2,1)}, u32[]{:S(2)}, u32[]{:S(2)}) collective-permute-start(bf16[16,144,512]{2,1,0:T(8,128)(2,1)} %all-to-all-done.4.mine), channel_id=1, source_target_pairs={{0,16},{16,0},{1,17},{17,1},{2,18},{18,2},{3,19},{19,3},{4,20},{20... | collective-permute-start | bytes 7077896 | tf_op jit(solution)/shard_map/ppermute | solution.py:308
  1036.1 62.3 %collective-permute-start.38 = (bf16[128,2048]{1,0:T(8,128)(2,1)}, bf16[128,2048]{1,0:T(8,128)(2,1)S(1)}, u32[]{:S(2)}, u32[]{:S(2)}) collective-permute-start(bf16[128,2048]{1,0:T(8,128)(2,1)} %get-tuple-element.208), channel_id=1, source_target_pairs={{0,4},{1,5},{2,6},{3,7},{4,0},{5,1},{6,2},{7,3},{8,12},{9,13},{10,... | collective-permute-start | bytes 1572872 | tf_op jit(solution)/shard_map/ppermute | solution.py:305
  1036.6 61.8 %collective-permute-start.40 = (bf16[128,2048]{1,0:T(8,128)(2,1)}, bf16[128,2048]{1,0:T(8,128)(2,1)S(1)}, u32[]{:S(2)}, u32[]{:S(2)}) collective-permute-start(bf16[128,2048]{1,0:T(8,128)(2,1)} %get-tuple-element.209), channel_id=1, source_target_pairs={{0,12},{1,13},{2,14},{3,15},{4,8},{5,9},{6,10},{7,11},{8,4},{9,5},... | collective-permute-start | bytes 1572872 | tf_op jit(solution)/shard_map/ppermute | solution.py:305
  1039.9 58.5 %collective-permute-start.39 = (bf16[128,2048]{1,0:T(8,128)(2,1)S(1)}, bf16[128,2048]{1,0:T(8,128)(2,1)S(1)}, u32[]{:S(2)}, u32[]{:S(2)}) collective-permute-start(bf16[128,2048]{1,0:T(8,128)(2,1)S(1)} %get-tuple-element.210), channel_id=1, source_target_pairs={{0,8},{1,9},{2,10},{3,11},{4,12},{5,13},{6,14},{7,15},{8,0},{9,1},... | collective-permute-start | bytes 1572872 | tf_op jit(solution)/shard_map/ppermute | solution.py:305
  1039.9 36.6 %collective-permute-start.64 = (bf16[128,512]{0,1:T(8,128)(2,1)}, bf16[128,512]{0,1:T(8,128)(2,1)}, u32[]{:S(2)}, u32[]{:S(2)}) collective-permute-start(bf16[128,512]{0,1:T(8,128)(2,1)} %get-tuple-element.247), channel_id=1, source_target_pairs={{0,12},{1,13},{2,14},{3,15},{4,8},{5,9},{6,10},{7,11},{8,4},{9,5},... | collective-permute-start | bytes 393224 | tf_op jit(solution)/shard_map/ppermute | solution.py:305
  (127 other events, 2419.8 us)
Sparse Core Ops, SparseCore 0:
  12.1 148.2 all-gather.5
  163.2 151.7 all-gather.7
  317.2 110.4 all-gather.9
  712.8 129.3 all-gather.11
  844.2 99.3 all-gather.13

commit v4 on v3

--- a/solution.py
+++ b/solution.py
@@ -540,8 +540,13 @@
     g_down_first = mm(down_half, down_second, 1, 1).astype(BF)
     down_rows = jnp.concatenate([down_half, g_down_first], axis=1)
 
-    late_rows = after(all_rows, down_rows, out_near, out_far, *line_sums)
+    out_here, out_there = fold_core(out_near, hop(out_far, 1))
+    out_there = all_after(out_there, *line_sums)
+    out_side = [hop(part, 2) for part in out_there]
+    late_rows = after(all_rows, down_rows, *line_sums, *out_there)
     gate_half = (mm(late_rows, grads[:, :h], 0, 0) + gate_part.astype(F32)).astype(BF)
+    late_rows = after(all_rows, gate_half)
+    up_half = (mm(late_rows, grads[:, h : 2 * h], 0, 0) + up_part.astype(F32)).astype(BF)
 
     pieces = jnp.concatenate(
         [
@@ -555,11 +560,12 @@
     pieces = after(pieces, all_rows)
     inputs = lax.all_to_all(pieces.reshape(seq, 2 * ext), "ctx", 0, 0, tiled=True)
 
-    arrivals = all_after(arrivals, gate_half, inputs)
+    arrivals = all_after(arrivals, up_half, inputs)
     grad_norm_two = sums[0] + sum(part.astype(F32) for part in arrivals)
     feed_gain_rows = jnp.sum(grad_norm_two * mid * inv_two, axis=0, keepdims=True)
     grad_mid = dy.astype(F32) + norm_back(mid, inv_two, feed_gain, grad_norm_two)
     grad_branch = grad_mid.astype(BF)
+    branch_all = lax.all_gather(grad_branch, "ctx", axis=0, tiled=True)
     grad_inner_out = mm(grad_branch, out_second, 1, 1).astype(BF)
     grad_attended = mm(
         jnp.concatenate([grad_branch, grad_inner_out], axis=1), out_full, 1, 1
@@ -572,11 +578,11 @@
     gate_ext = jnp.concatenate(
         [gate_half.reshape(n, w_rows, h), gate_second.reshape(n, r_rows, h)], axis=1
     )
-    gate_got = exchange(gate_ext)
     grad_flat = after(grad_flat, gate_ext)
+    down_back = swap(after(down_rows, up_half))
     grad_probs = mm(grad_flat, v_all, 1, 1)
     grad_scores = (probs.astype(F32) * (grad_probs - delta)).astype(BF)
-    grad_scores = after(grad_scores, up_part)
+    grad_scores = after(grad_scores, down_back, *out_side)
     grad_k = mm(grad_scores, q_flat, 0, 0) * score_scale
     grad_v = mm(probs, grad_flat, 0, 0)
     kv_part = jnp.concatenate([grad_k, grad_v], axis=1).astype(BF)
@@ -588,38 +594,29 @@
         .astype(BF)
     )
     q_all = lax.all_gather(grad_q_rows, "ctx", axis=0, tiled=True)
-    up_half = (
-        mm(after(all_rows, grad_q_rows, gate_got), grads[:, h : 2 * h], 0, 0)
-        + up_part.astype(F32)
-    ).astype(BF)
-    down_back = swap(after(down_rows, up_part))
-    out_here, out_there = fold_core(out_near, hop(after(out_far, grad_kv), 1))
-    out_side = hop(jnp.concatenate(out_there, axis=0), 2)
-    branch_all = lax.all_gather(after(grad_branch, grad_kv), "ctx", axis=0, tiled=True)
-    grad_kv = after(grad_kv, up_half, down_back)
+    out_parts = [out_here[k] + out_side[k].astype(F32) for k in range(lines)]
+    out_lines = [part.astype(BF) for part in out_parts[1:]]
+    out_lines = all_after(out_lines, grad_kv)
+    out_lines = [hop(part, 4 * (k + 1)) for k, part in enumerate(out_lines)]
+    gate_got = exchange(after(gate_ext, grad_kv))
     grad_k_rows = rotate(grad_kv[:, :HD], cosine, -sine_rows)
     grad_kv_rows = jnp.concatenate([grad_k_rows, grad_kv[:, HD:]], axis=1).astype(BF)
     kv_all_grads = gather(grad_kv_rows)
-    up_second = mm(gate_up_first, after(up_half, grad_kv_rows), 0, 0).astype(BF)
+    up_second = mm(gate_up_first, after(up_half, kv_part), 0, 0).astype(BF)
     up_ext = jnp.concatenate(
         [up_half.reshape(n, w_rows, h), up_second.reshape(n, r_rows, h)], axis=1
     )
-    up_ext = after(up_ext, gate_got)
-    up_got = exchange(up_ext)
+    up_got = exchange(after(up_ext, grad_kv))
     grad_qkv = jnp.concatenate([grad_q_rows, grad_kv_rows], axis=1)
     grad_qkv = after(grad_qkv, up_ext)
     grad_inner_qkv = mm(grad_qkv, qkv_second, 1, 1).astype(BF)
     grad_norm_one = mm(
-        after(jnp.concatenate([grad_qkv, grad_inner_qkv], axis=1), out_side), qkv_full, 1, 1
+        jnp.concatenate([grad_qkv, grad_inner_qkv], axis=1), qkv_full, 1, 1
     )
     attn_gain_rows = jnp.sum(grad_norm_one * x * inv_one, axis=0, keepdims=True)
     grad_input = (grad_mid + norm_back(x, inv_one, attn_gain, grad_norm_one)).astype(BF)
     gate_back = swap(after(gate_got, down_back))
-    output = mid + out_here[0] + out_side[:rows].astype(F32)
-    for k in range(1, lines):
-        part = out_here[k] + out_side[k * rows : (k + 1) * rows].astype(F32)
-        output = output + hop(part.astype(BF), 4 * k).astype(F32)
-    output = output.astype(BF)
+    output = (mid + out_parts[0] + sum(part.astype(F32) for part in out_lines)).astype(BF)
 
     def both_planes(own):
         own = own.astype(BF)
@@ -649,14 +646,14 @@
     up_got_other = swap(after(up_got, gate_back))
     gate_up_grads = collect(plane_id, up_got, up_got_other, w_rows, 1, gate_up_grads)
 
-    g_q = mm(inputs[:, :ext], after(q_all, down_grads[0]), 0, 0)
-    g_out = mm(inputs[:, ext:], after(branch_all, g_q), 0, 0).astype(BF)
+    g_out = mm(inputs[:, ext:], after(branch_all, down_grads[0]), 0, 0).astype(BF)
+    g_q = mm(inputs[:, :ext], after(q_all, g_out), 0, 0)
     inputs_rel = reorder(inputs[:, :ext])
     g_kv = mm(inputs_rel, kv_all_grads, 0, 0)
     g_qkv = jnp.concatenate([g_q, g_kv], axis=1).astype(BF)
-    g_out = g_out.astype(F32) + after(swap(g_out), gate_up_grads[0]).astype(F32)
+    g_out = both_planes(after(g_out, gate_back))
     small = both_planes(after(small, gate_back))
-    g_qkv = both_planes(g_qkv)
+    g_qkv = g_qkv.astype(F32) + after(swap(g_qkv), gate_up_grads[0]).astype(F32)
     gain_rows = gain_rows + swap(after(gain_rows, up_got_other))
     g_gu_first = small[:, :rank]
     g_down_second = small[:, rank:].reshape(r_rows, width)

time: 1160 us -> 1160 us (level)
  starting transfers between devices: 113 us -> 143 us
  waiting for transfers between devices: 566 us -> 538 us
    all_to_all x4, waiting for transfers between devices: 0.01 us -> 37.8 us  [exchange(): lax.all_to_all(flat, 'ctx', 0, 0, tiled=True).reshape(n, ext, feed_half)]
    ppermute x52 -> x55, waiting for transfers between devices: 296 us -> 262 us  [hop(): return lax.ppermute(x, 'ctx', [(i, i ^ k) for i in range(n)])]
    ppermute x14, waiting for transfers between devices: 115 us -> 83.2 us  [swap(): return lax.ppermute(x, 'grp', [(0, 1), (1, 0)])]
    ppermute x52 -> x55, starting transfers between devices: 73.3 us -> 89.2 us  [hop(): return lax.ppermute(x, 'ctx', [(i, i ^ k) for i in range(n)])]
    unnamed x232 -> x244, local copies, waits for them, and re-layouts: 53.1 us -> 43.6 us
  transfers between devices with their start and end apart: 76 -> 79, of which waited for: 28 -> 36; matrix products, arithmetic and copies ran while one was open for 30% -> 27% of each run, Pallas kernels for 7% -> 4%
where the time goes in v4:
time: 1160 us; the launch traced here: 1150 us
  waiting for transfers between devices  538 us (46%)
  matrix products  166 us (14%)
  starting transfers between devices  143 us (12%)
  local copies, waits for them, and re-layouts  134 us (12%)
  Pallas kernels  84 us (7%)
  other arithmetic  68.5 us (6%)
  between operations  16.2 us (1%)
    ppermute x55, waiting for transfers between devices, hop(): return lax.ppermute(x, 'ctx', [(i, i ^ k) for i in range(n)])  262 us
    dot_general x35, matrix products, mm(): lax.dot_general(a, b, (((ca,), (cb,)), ((), ())), preferred_element_type=...  166 us
    all_gather x1, waiting for transfers between devices, body(): qkv_got = lax.all_gather(qkv_ext, 'ctx', axis=0, tiled=True)  129 us
    ppermute x55, starting transfers between devices, hop(): return lax.ppermute(x, 'ctx', [(i, i ^ k) for i in range(n)])  89.2 us
    ppermute x14, waiting for transfers between devices, swap(): return lax.ppermute(x, 'grp', [(0, 1), (1, 0)])  83.2 us
    unnamed x244, local copies, waits for them, and re-layouts  43.6 us
    all_to_all x4, waiting for transfers between devices, exchange(): lax.all_to_all(flat, 'ctx', 0, 0, tiled=True).reshape(n, ext, feed_half)  37.8 us
    all_to_all x4, starting transfers between devices, exchange(): lax.all_to_all(flat, 'ctx', 0, 0, tiled=True).reshape(n, ext, feed_half)  32.6 us
  transfers between devices with their start and end apart: 79, of which 36 were waited for; matrix products, arithmetic and copies ran while one was open for 27% of the time, Pallas kernels for 4%

profile of v4, /device:TPU:0, one launch (start us, length us, event | category | flops | bytes accessed | tf_op | source)
XLA Modules:
  0.0 1149.9 jit_solution(11715518381237201345)
XLA Ops:
  17.1 7.4 all-to-all-start
  31.7 128.7 %all-gather.6.cloned.1.call-done = bf16[2048,3200]{1,0:T(8,128)(2,1)} async-done(((bf16[128,3200]{1,0:T(8,128)(2,1)}), bf16[2048,3200]{1,0:T(8,128)(2,1)}) %all-gather.6.cloned.1.call-update) | async-done | bytes 13107216 | tf_op jit(solution)/shard_map/all_gather | solution.py:404
  169.2 6.6 fusion.3
  191.0 13.5 %collective-permute-done.1 = bf16[128,512]{1,0:T(8,128)(2,1)} collective-permute-done((bf16[128,512]{1,0:T(8,128)(2,1)}, bf16[128,512]{1,0:T(8,128)(2,1)}, u32[]{:S(2)}, u32[]{:S(2)}) %collective-permute-start.1) | collective-permute-done | bytes 131104 | tf_op jit(solution)/shard_map/ppermute | solution.py:305
  238.2 9.0 collective-permute-done.8
  248.6 23.5 %collective-permute-done.9 = bf16[8,144,512]{2,1,0:T(8,128)(2,1)} collective-permute-done((bf16[8,144,512]{2,1,0:T(8,128)(2,1)}, bf16[8,144,512]{2,1,0:T(8,128)(2,1)}, u32[]{:S(2)}, u32[]{:S(2)}) %collective-permute-start.9) | collective-permute-done | bytes 1179680 | tf_op jit(solution)/shard_map/ppermute | solution.py:308
  289.3 25.9 %all-gather.8.cloned.1.call-done = bf16[2048,3072]{1,0:T(8,128)(2,1)} async-done(((bf16[128,3072]{1,0:T(8,128)(2,1)}), bf16[2048,3072]{1,0:T(8,128)(2,1)}) %all-gather.8.cloned.1.call-update) | async-done | bytes 12582928 | tf_op jit(solution)/shard_map/all_gather | solution.py:415
  352.2 6.6 shard_map.290.refs_0_
  359.8 62.1 %collective-permute-done.11 = bf16[128,2048]{1,0:T(8,128)(2,1)S(1)} collective-permute-done((bf16[128,2048]{1,0:T(8,128)(2,1)}, bf16[128,2048]{1,0:T(8,128)(2,1)S(1)}, u32[]{:S(2)}, u32[]{:S(2)}) %collective-permute-start.11) | collective-permute-done | bytes 524320 | tf_op jit(solution)/shard_map/ppermute | solution.py:305
  428.8 7.9 collective-permute-done.14
  437.6 10.4 collective-permute-done.15
  448.8 7.1 collective-permute-done.16
  459.7 6.2 shard_map.291.w_ref
  478.3 8.3 constant_dynamic-slice_fusion.17
  486.6 8.3 pad_maximum_fusion.dy_ref
  495.0 25.7 %shard_map.292 = (bf16[2048,1024]{1,0:T(8,128)(2,1)S(1)}, bf16[2048,1024]{1,0:T(8,128)(2,1)S(1)}, bf16[2048,1024]{1,0:T(8,128)(2,1)}) custom-call(bf16[2048,2048]{1,0:T(8,128)(2,1)} %constant_dynamic-update-slice_fusion.26.x_ref, bf16[2048,2048]{1,0:T(8,128)(2,1)} %shard_map.291.w_ref), custom_call_target="tpu_custom_call" | custom-call | flops 17179869184 | bytes 29360128 | tf_op jit(solution)/shard_map/pallas_call | solution.py:136
  520.7 10.9 convolution_convert_fusion.2
  531.6 14.7 %shard_map.293 = bf16[2048,2048]{1,0:T(8,128)(2,1)} custom-call(bf16[2048,2048]{1,0:T(8,128)(2,1)} %pad_maximum_fusion.dy_ref, bf16[1024,2048]{1,0:T(8,128)(2,1)S(1)} %copy-done, bf16[2048,1024]{1,0:T(8,128)(2,1)S(1)} %get-tuple-element.86.act_ref, bf16[2048,1024]{1,0:T(8,128)(2,1)} %get-tuple-element.87.slope_ref), custom_call_target="tpu_custom_call" | custom-call | flops 8589934592 | bytes 29360128 | tf_op jit(solution)/shard_map/pallas_call | solution.py:168
  546.3 12.0 %fusion.25 = bf16[1024,2048]{1,0:T(8,128)(2,1)} fusion(bf16[2048,2048]{1,0:T(8,128)(2,1)S(1)} %bitcast.127, bf16[2048,2048]{1,0:T(8,128)(2,1)} %shard_map.293), kind=kOutput, calls=%fused_computation.63 | convolution fusion | flops 8592031744 | bytes 16777216 | tf_op jit(solution)/shard_map/dot_general | solution.py:19
  567.3 12.7 %fusion.19 = bf16[1024,2048]{1,0:T(8,128)(2,1)S(1)} fusion(bf16[2048,2048]{1,0:T(8,128)(2,1)} %shard_map.291.w_ref, bf16[2048,2048]{1,0:T(8,128)(2,1)} %shard_map.293), kind=kOutput, calls=%fused_computation.61 | convolution fusion | flops 8592031744 | bytes 16777216 | tf_op jit(solution)/shard_map/dot_general | solution.py:19
  584.9 14.1 %fusion.22 = bf16[2048,1024]{1,0:T(8,128)(2,1)} fusion(bf16[2048,2048]{1,0:T(8,128)(2,1)} %constant_dynamic-update-slice_fusion.26.x_ref, bf16[2048,2048]{1,0:T(8,128)(2,1)} %shard_map.293), kind=kOutput, calls=%fused_computation.62 | convolution fusion | flops 8592031744 | bytes 16777216 | tf_op jit(solution)/shard_map/dot_general | solution.py:19
  599.0 6.3 convolution_convert_fusion
  615.4 7.6 add_convert_fusion.3
  633.7 9.4 collective-permute-done.23
  643.1 10.8 collective-permute-done.22
  664.2 10.5 add_convert_fusion.2
  674.8 31.4 %collective-permute-done.35 = bf16[2048,512]{1,0:T(8,128)(2,1)S(1)} collective-permute-done((bf16[2048,512]{1,0:T(8,128)(2,1)}, bf16[2048,512]{1,0:T(8,128)(2,1)S(1)}, u32[]{:S(2)}, u32[]{:S(2)}) %collective-permute-start.35) | collective-permute-done | bytes 2097184 | tf_op jit(solution)/shard_map/ppermute | solution.py:308
  706.2 9.9 add_convert_fusion.1
  728.9 8.1 convert_multiply_fusion.5
  756.9 19.8 %collective-permute-done.28 = bf16[128,2048]{1,0:T(8,128)(2,1)} collective-permute-done((bf16[128,2048]{1,0:T(8,128)(2,1)}, bf16[128,2048]{1,0:T(8,128)(2,1)}, u32[]{:S(2)}, u32[]{:S(2)}) %collective-permute-start.28) | collective-permute-done | bytes 524320 | tf_op jit(solution)/shard_map/ppermute | solution.py:305
  776.7 19.6 %collective-permute-done.29 = bf16[128,2048]{1,0:T(8,128)(2,1)} collective-permute-done((bf16[128,2048]{1,0:T(8,128)(2,1)}, bf16[128,2048]{1,0:T(8,128)(2,1)}, u32[]{:S(2)}, u32[]{:S(2)}) %collective-permute-start.29) | collective-permute-done | bytes 524320 | tf_op jit(solution)/shard_map/ppermute | solution.py:305
  812.9 12.4 %collective-permute-done.38 = bf16[512,512]{1,0:T(8,128)(2,1)S(1)} collective-permute-done((bf16[512,512]{1,0:T(8,128)(2,1)S(1)}, bf16[512,512]{1,0:T(8,128)(2,1)S(1)}, u32[]{:S(2)}, u32[]{:S(2)}) %collective-permute-start.38) | collective-permute-done | bytes 524320 | tf_op jit(solution)/shard_map/ppermute | solution.py:305
  829.2 6.9 collective-permute-done.39
  841.0 12.2 %collective-permute-done.40 = bf16[128,512]{1,0:T(8,128)(2,1)S(1)} collective-permute-done((bf16[128,512]{1,0:T(8,128)(2,1)S(1)}, bf16[128,512]{1,0:T(8,128)(2,1)S(1)}, u32[]{:S(2)}, u32[]{:S(2)}) %collective-permute-start.40) | collective-permute-done | bytes 131104 | tf_op jit(solution)/shard_map/ppermute | solution.py:305
  888.1 9.4 fusion.49
  897.5 37.8 %all-to-all-done.4.mine = bf16[16,144,512]{2,1,0:T(8,128)(2,1)} async-done(((bf16[16,144,512]{2,1,0:T(8,128)(2,1)}), bf16[16,144,512]{2,1,0:T(8,128)(2,1)}, u32[]{:S(2)}, u32[]{:S(2)}) %all-to-all-start.4) | async-done | bytes 2359328 | tf_op jit(solution)/shard_map/all_to_all | solution.py:423
  935.3 15.1 %all-to-all-start.3 = ((bf16[16,144,512]{2,1,0:T(8,128)(2,1)}), bf16[16,144,512]{2,1,0:T(8,128)(2,1)}, u32[]{:S(2)}, u32[]{:S(2)}) async-start(bf16[16,144,512]{2,1,0:T(8,128)(2,1)} %pad_maximum_fusion.4), calls=%async_computation.3 | async-start | bytes 4718592 | tf_op jit(solution)/shard_map/all_to_all | solution.py:423
  974.7 9.5 shard_map.294
  984.1 5.6 collective-permute-done.47
  994.4 17.4 %collective-permute-start.53 = (bf16[128,512]{1,0:T(8,128)(2,1)S(1)}, bf16[128,512]{1,0:T(8,128)(2,1)S(1)}, u32[]{:S(2)}, u32[]{:S(2)}) collective-permute-start(bf16[128,512]{1,0:T(8,128)(2,1)S(1)} %get-tuple-element.284), channel_id=1, source_target_pairs={{0,4},{1,5},{2,6},{3,7},{4,0},{5,1},{6,2},{7,3},{8,12},{9,13},{10,... | collective-permute-start | bytes 393224 | tf_op jit(solution)/shard_map/ppermute | solution.py:305
  1011.8 5.7 collective-permute-done.53
  1039.3 25.0 %collective-permute-done.43 = bf16[128,2048]{1,0:T(8,128)(2,1)} collective-permute-done((bf16[128,2048]{1,0:T(8,128)(2,1)}, bf16[128,2048]{1,0:T(8,128)(2,1)}, u32[]{:S(2)}, u32[]{:S(2)}) %collective-permute-start.43) | collective-permute-done | bytes 524320 | tf_op jit(solution)/shard_map/ppermute | solution.py:305
  1067.7 9.3 collective-permute-start.65
  1090.7 6.5 shard_map.295
  1099.3 6.8 shard_map.296
  1113.1 6.3 convolution_convert_fusion.5
  1120.0 7.8 collective-permute-done.62
  1129.9 10.4 collective-permute-done.61
  (559 shorter events, 374.2 us)
Async XLA Ops:
  7.2 153.2 %all-gather.6.cloned.1.call-start = ((), (), s32[]{:S(2)}) async-start(), calls=%async_computation.5 | async-start | bytes 13926400 | tf_op jit(solution)/shard_map/all_gather | solution.py:404
  11.9 303.2 %all-gather.8.cloned.1.call-start = ((), (), s32[]{:S(2)}) async-start(), calls=%async_computation.6 | async-start | bytes 13369344 | tf_op jit(solution)/shard_map/all_gather | solution.py:415
  17.1 152.0 %all-to-all-start = ((bf16[16,144,512]{2,1,0:T(8,128)(2,1)}), bf16[16,144,512]{2,1,0:T(8,128)(2,1)S(1)}, u32[]{:S(2)}, u32[]{:S(2)}) async-start(bf16[16,144,512]{2,1,0:T(8,128)(2,1)} %shard_map.288), calls=%async_computation | async-start | bytes 4718592 | tf_op jit(solution)/shard_map/all_to_all | solution.py:423
  24.5 453.7 %all-gather.10.cloned.1.call-start = ((), (), s32[]{:S(2)}) async-start(), calls=%async_computation.7 | async-start | bytes 8912896 | tf_op jit(solution)/shard_map/all_gather | solution.py:472
  181.7 26.1 %collective-permute-start = (bf16[128,512]{1,0:T(8,128)(2,1)}, bf16[128,512]{1,0:T(8,128)(2,1)}, u32[]{:S(2)}, u32[]{:S(2)}) collective-permute-start(bf16[128,512]{1,0:T(8,128)(2,1)} %get-tuple-element.301), channel_id=1, source_target_pairs={{0,4},{1,5},{2,6},{3,7},{4,0},{5,1},{6,2},{7,3},{8,12},{9,13},{10,... | collective-permute-start | bytes 393224 | tf_op jit(solution)/shard_map/ppermute | solution.py:305
  184.6 28.1 %collective-permute-start.3 = (bf16[128,512]{1,0:T(8,128)(2,1)}, bf16[128,512]{1,0:T(8,128)(2,1)}, u32[]{:S(2)}, u32[]{:S(2)}) collective-permute-start(bf16[128,512]{1,0:T(8,128)(2,1)} %get-tuple-element.301), channel_id=1, source_target_pairs={{0,2},{1,3},{2,0},{3,1},{4,6},{5,7},{6,4},{7,5},{8,10},{9,11},{10,... | collective-permute-start | bytes 393224 | tf_op jit(solution)/shard_map/ppermute | solution.py:305
  190.4 25.4 %collective-permute-start.6 = (bf16[128,512]{1,0:T(8,128)(2,1)}, bf16[128,512]{1,0:T(8,128)(2,1)S(1)}, u32[]{:S(2)}, u32[]{:S(2)}) collective-permute-start(bf16[128,512]{1,0:T(8,128)(2,1)} %collective-permute-done.2), channel_id=1, source_target_pairs={{0,2},{1,3},{2,0},{3,1},{4,6},{5,7},{6,4},{7,5},{8,10},{9,11},{10,... | collective-permute-start | bytes 393224 | tf_op jit(solution)/shard_map/ppermute | solution.py:305
  218.2 29.1 %collective-permute-start.8 = (bf16[8,144,512]{2,1,0:T(8,128)(2,1)}, bf16[8,144,512]{2,1,0:T(8,128)(2,1)}, u32[]{:S(2)}, u32[]{:S(2)}) collective-permute-start(bf16[8,144,512]{2,1,0:T(8,128)(2,1)} %get-tuple-element.241), channel_id=1, source_target_pairs={{0,16},{16,0},{1,17},{17,1},{2,18},{18,2},{3,19},{19,3},{4,20},{20... | collective-permute-start | bytes 3538952 | tf_op jit(solution)/shard_map/ppermute | solution.py:308
  220.7 51.5 %collective-permute-start.9 = (bf16[8,144,512]{2,1,0:T(8,128)(2,1)}, bf16[8,144,512]{2,1,0:T(8,128)(2,1)}, u32[]{:S(2)}, u32[]{:S(2)}) collective-permute-start(bf16[8,144,512]{2,1,0:T(8,128)(2,1)} %get-tuple-element.240), channel_id=1, source_target_pairs={{0,16},{16,0},{1,17},{17,1},{2,18},{18,2},{3,19},{19,3},{4,20},{20... | collective-permute-start | bytes 3538952 | tf_op jit(solution)/shard_map/ppermute | solution.py:308
  225.2 101.4 %all-to-all-start.1 = ((bf16[16,144,512]{2,1,0:T(8,128)(2,1)}), bf16[16,144,512]{2,1,0:T(8,128)(2,1)}, u32[]{:S(2)}, u32[]{:S(2)}) async-start(bf16[16,144,512]{2,1,0:T(8,128)(2,1)} %shard_map.289), calls=%async_computation.1 | async-start | bytes 4718592 | tf_op jit(solution)/shard_map/all_to_all | solution.py:423
  341.5 82.5 %collective-permute-start.12 = (bf16[128,2048]{1,0:T(8,128)(2,1)}, bf16[128,2048]{1,0:T(8,128)(2,1)S(1)}, u32[]{:S(2)}, u32[]{:S(2)}) collective-permute-start(bf16[128,2048]{1,0:T(8,128)(2,1)} %get-tuple-element.212), channel_id=1, source_target_pairs={{0,12},{1,13},{2,14},{3,15},{4,8},{5,9},{6,10},{7,11},{8,4},{9,5},... | collective-permute-start | bytes 1572872 | tf_op jit(solution)/shard_map/ppermute | solution.py:305
  342.5 79.4 %collective-permute-start.11 = (bf16[128,2048]{1,0:T(8,128)(2,1)}, bf16[128,2048]{1,0:T(8,128)(2,1)S(1)}, u32[]{:S(2)}, u32[]{:S(2)}) collective-permute-start(bf16[128,2048]{1,0:T(8,128)(2,1)} %get-tuple-element.212), channel_id=1, source_target_pairs={{0,8},{1,9},{2,10},{3,11},{4,12},{5,13},{6,14},{7,15},{8,0},{9,1},... | collective-permute-start | bytes 1572872 | tf_op jit(solution)/shard_map/ppermute | solution.py:305
  344.8 80.8 %collective-permute-start.13 = (bf16[128,2048]{1,0:T(8,128)(2,1)}, bf16[128,2048]{1,0:T(8,128)(2,1)}, u32[]{:S(2)}, u32[]{:S(2)}) collective-permute-start(bf16[128,2048]{1,0:T(8,128)(2,1)} %get-tuple-element.212), channel_id=1, source_target_pairs={{0,2},{1,3},{2,0},{3,1},{4,6},{5,7},{6,4},{7,5},{8,10},{9,11},{10,... | collective-permute-start | bytes 1572872 | tf_op jit(solution)/shard_map/ppermute | solution.py:305
  349.1 107.8 %collective-permute-start.18 = (bf16[8,144,512]{2,1,0:T(8,128)(2,1)}, bf16[8,144,512]{2,1,0:T(8,128)(2,1)}, u32[]{:S(2)}, u32[]{:S(2)}) collective-permute-start(bf16[8,144,512]{2,1,0:T(8,128)(2,1)} %get-tuple-element.238), channel_id=1, source_target_pairs={{0,16},{16,0},{1,17},{17,1},{2,18},{18,2},{3,19},{19,3},{4,20},{20... | collective-permute-start | bytes 3538952 | tf_op jit(solution)/shard_map/ppermute | solution.py:308
  358.8 98.0 %collective-permute-start.17 = (bf16[8,144,512]{2,1,0:T(8,128)(2,1)S(1)}, bf16[8,144,512]{2,1,0:T(8,128)(2,1)S(1)}, u32[]{:S(2)}, u32[]{:S(2)}) collective-permute-start(bf16[8,144,512]{2,1,0:T(8,128)(2,1)S(1)} %get-tuple-element.239), channel_id=1, source_target_pairs={{0,16},{16,0},{1,17},{17,1},{2,18},{18,2},{3,19},{19,3},{4,20},{20... | collective-permute-start | bytes 3538952 | tf_op jit(solution)/shard_map/ppermute | solution.py:308
  425.6 30.4 %collective-permute-start.16 = (bf16[128,2048]{1,0:T(8,128)(2,1)S(1)}, bf16[128,2048]{1,0:T(8,128)(2,1)S(1)}, u32[]{:S(2)}, u32[]{:S(2)}) collective-permute-start(bf16[128,2048]{1,0:T(8,128)(2,1)S(1)} %collective-permute-done.12), channel_id=1, source_target_pairs={{0,2},{1,3},{2,0},{3,1},{4,6},{5,7},{6,4},{7,5},{8,10},{9,11},{10,... | collective-permute-start | bytes 1572872 | tf_op jit(solution)/shard_map/ppermute | solution.py:305
  562.3 43.1 %all-to-all-start.2 = ((bf16[16,128,288]{1,2,0:T(8,128)(2,1)}), bf16[16,128,288]{1,2,0:T(8,128)(2,1)S(1)}, u32[]{:S(2)}, u32[]{:S(2)}) async-start(bf16[16,128,288]{1,2,0:T(8,128)(2,1)} %maximum_bitcast_fusion), calls=%async_computation.2 | async-start | bytes 2359296 | tf_op jit(solution)/shard_map/all_to_all | solution.py:561
  566.0 540.7 %all-gather.14.cloned.1.call-start = ((), (), s32[]{:S(2)}) async-start(), calls=%async_computation.9 | async-start | bytes 8912896 | tf_op jit(solution)/shard_map/all_gather | solution.py:568
  566.0 48.2 %collective-permute-start.33 = (bf16[512,2048]{1,0:T(8,128)(2,1)}, bf16[512,2048]{1,0:T(8,128)(2,1)}, u32[]{:S(2)}, u32[]{:S(2)}) collective-permute-start(bf16[512,2048]{1,0:T(8,128)(2,1)} %convolution_convert_fusion.2), channel_id=1, source_target_pairs={{0,16},{16,0},{1,17},{17,1},{2,18},{18,2},{3,19},{19,3},{4,20},{20... | collective-permute-start | bytes 6291464 | tf_op jit(solution)/shard_map/ppermute | solution.py:308
  605.3 54.8 %collective-permute-start.21 = (bf16[1024,2048]{1,0:T(8,128)(2,1)}, bf16[1024,2048]{1,0:T(8,128)(2,1)}, u32[]{:S(2)}, u32[]{:S(2)}) collective-permute-start(bf16[1024,2048]{1,0:T(8,128)(2,1)} %convolution_convert_fusion), channel_id=1, source_target_pairs={{0,1},{1,0},{2,3},{3,2},{4,5},{5,4},{6,7},{7,6},{8,9},{9,8},{10,11... | collective-permute-start | bytes 12582920 | tf_op jit(solution)/shard_map/ppermute | solution.py:305
  607.4 25.1 %collective-permute-start.24 = (bf16[128,2048]{1,0:T(8,128)(2,1)}, bf16[128,2048]{1,0:T(8,128)(2,1)}, u32[]{:S(2)}, u32[]{:S(2)}) collective-permute-start(bf16[128,2048]{1,0:T(8,128)(2,1)} %get-tuple-element.229), channel_id=1, source_target_pairs={{0,2},{1,3},{2,0},{3,1},{4,6},{5,7},{6,4},{7,5},{8,10},{9,11},{10,... | collective-permute-start | bytes 1572872 | tf_op jit(solution)/shard_map/ppermute | solution.py:305
  607.6 35.5 %collective-permute-start.23 = (bf16[128,2048]{1,0:T(8,128)(2,1)}, bf16[128,2048]{1,0:T(8,128)(2,1)}, u32[]{:S(2)}, u32[]{:S(2)}) collective-permute-start(bf16[128,2048]{1,0:T(8,128)(2,1)} %get-tuple-element.230), channel_id=1, source_target_pairs={{0,2},{1,3},{2,0},{3,1},{4,6},{5,7},{6,4},{7,5},{8,10},{9,11},{10,... | collective-permute-start | bytes 1572872 | tf_op jit(solution)/shard_map/ppermute | solution.py:305
  614.2 50.0 %collective-permute-start.34 = (bf16[2048,512]{1,0:T(8,128)(2,1)S(1)}, bf16[2048,512]{1,0:T(8,128)(2,1)}, u32[]{:S(2)}, u32[]{:S(2)}) collective-permute-start(bf16[2048,512]{1,0:T(8,128)(2,1)S(1)} %get-tuple-element.234), channel_id=1, source_target_pairs={{0,16},{16,0},{1,17},{17,1},{2,18},{18,2},{3,19},{19,3},{4,20},{20... | collective-permute-start | bytes 6291464 | tf_op jit(solution)/shard_map/ppermute | solution.py:308
  628.3 25.6 %collective-permute-start.22 = (bf16[128,2048]{1,0:T(8,128)(2,1)S(1)}, bf16[128,2048]{1,0:T(8,128)(2,1)S(1)}, u32[]{:S(2)}, u32[]{:S(2)}) collective-permute-start(bf16[128,2048]{1,0:T(8,128)(2,1)S(1)} %copy-done.65), channel_id=1, source_target_pairs={{0,2},{1,3},{2,0},{3,1},{4,6},{5,7},{6,4},{7,5},{8,10},{9,11},{10,... | collective-permute-start | bytes 1572872 | tf_op jit(solution)/shard_map/ppermute | solution.py:305
  632.5 73.7 %collective-permute-start.35 = (bf16[2048,512]{1,0:T(8,128)(2,1)}, bf16[2048,512]{1,0:T(8,128)(2,1)S(1)}, u32[]{:S(2)}, u32[]{:S(2)}) collective-permute-start(bf16[2048,512]{1,0:T(8,128)(2,1)} %get-tuple-element.235), channel_id=1, source_target_pairs={{0,16},{16,0},{1,17},{17,1},{2,18},{18,2},{3,19},{19,3},{4,20},{20... | collective-permute-start | bytes 6291464 | tf_op jit(solution)/shard_map/ppermute | solution.py:308
  656.4 59.7 %collective-permute-start.32 = (bf16[128,2048]{1,0:T(8,128)(2,1)S(1)}, bf16[128,2048]{1,0:T(8,128)(2,1)S(1)}, u32[]{:S(2)}, u32[]{:S(2)}) collective-permute-start(bf16[128,2048]{1,0:T(8,128)(2,1)S(1)} %get-tuple-element.221), channel_id=1, source_target_pairs={{0,12},{1,13},{2,14},{3,15},{4,8},{5,9},{6,10},{7,11},{8,4},{9,5},... | collective-permute-start | bytes 1572872 | tf_op jit(solution)/shard_map/ppermute | solution.py:305
  660.1 56.1 %collective-permute-start.31 = (bf16[128,2048]{1,0:T(8,128)(2,1)S(1)}, bf16[128,2048]{1,0:T(8,128)(2,1)S(1)}, u32[]{:S(2)}, u32[]{:S(2)}) collective-permute-start(bf16[128,2048]{1,0:T(8,128)(2,1)S(1)} %get-tuple-element.222), channel_id=1, source_target_pairs={{0,8},{1,9},{2,10},{3,11},{4,12},{5,13},{6,14},{7,15},{8,0},{9,1},... | collective-permute-start | bytes 1572872 | tf_op jit(solution)/shard_map/ppermute | solution.py:305
  660.1 56.1 %collective-permute-start.30 = (bf16[128,2048]{1,0:T(8,128)(2,1)S(1)}, bf16[128,2048]{1,0:T(8,128)(2,1)S(1)}, u32[]{:S(2)}, u32[]{:S(2)}) collective-permute-start(bf16[128,2048]{1,0:T(8,128)(2,1)S(1)} %get-tuple-element.223), channel_id=1, source_target_pairs={{0,4},{1,5},{2,6},{3,7},{4,0},{5,1},{6,2},{7,3},{8,12},{9,13},{10,... | collective-permute-start | bytes 1572872 | tf_op jit(solution)/shard_map/ppermute | solution.py:305
  719.8 393.3 %all-gather.12.cloned.1.call-start = ((), (), s32[]{:S(2)}) async-start(), calls=%async_computation.8 | async-start | bytes 8912896 | tf_op jit(solution)/shard_map/all_gather | solution.py:596
  722.0 74.2 %collective-permute-start.36 = (bf16[512,2304]{1,0:T(8,128)(2,1)}, bf16[512,2304]{1,0:T(8,128)(2,1)}, u32[]{:S(2)}, u32[]{:S(2)}) collective-permute-start(bf16[512,2304]{1,0:T(8,128)(2,1)} %pad_maximum_fusion.2.mine), channel_id=1, source_target_pairs={{0,16},{16,0},{1,17},{17,1},{2,18},{18,2},{3,19},{19,3},{4,20},{20... | collective-permute-start | bytes 7077896 | tf_op jit(solution)/shard_map/ppermute | solution.py:308
  724.8 29.0 %collective-permute-start.26 = (bf16[128,2048]{1,0:T(8,128)(2,1)}, bf16[128,2048]{1,0:T(8,128)(2,1)}, u32[]{:S(2)}, u32[]{:S(2)}) collective-permute-start(bf16[128,2048]{1,0:T(8,128)(2,1)} %get-tuple-element.95), channel_id=1, source_target_pairs={{0,2},{1,3},{2,0},{3,1},{4,6},{5,7},{6,4},{7,5},{8,10},{9,11},{10,... | collective-permute-start | bytes 1572872 | tf_op jit(solution)/shard_map/ppermute | solution.py:305
  726.4 30.5 %collective-permute-start.27 = (bf16[128,2048]{1,0:T(8,128)(2,1)}, bf16[128,2048]{1,0:T(8,128)(2,1)}, u32[]{:S(2)}, u32[]{:S(2)}) collective-permute-start(bf16[128,2048]{1,0:T(8,128)(2,1)} %get-tuple-element.96), channel_id=1, source_target_pairs={{0,2},{1,3},{2,0},{3,1},{4,6},{5,7},{6,4},{7,5},{8,10},{9,11},{10,... | collective-permute-start | bytes 1572872 | tf_op jit(solution)/shard_map/ppermute | solution.py:305
  726.9 49.8 %collective-permute-start.28 = (bf16[128,2048]{1,0:T(8,128)(2,1)}, bf16[128,2048]{1,0:T(8,128)(2,1)}, u32[]{:S(2)}, u32[]{:S(2)}) collective-permute-start(bf16[128,2048]{1,0:T(8,128)(2,1)} %get-tuple-element.97), channel_id=1, source_target_pairs={{0,2},{1,3},{2,0},{3,1},{4,6},{5,7},{6,4},{7,5},{8,10},{9,11},{10,... | collective-permute-start | bytes 1572872 | tf_op jit(solution)/shard_map/ppermute | solution.py:305
  728.4 67.8 %collective-permute-start.29 = (bf16[128,2048]{1,0:T(8,128)(2,1)}, bf16[128,2048]{1,0:T(8,128)(2,1)}, u32[]{:S(2)}, u32[]{:S(2)}) collective-permute-start(bf16[128,2048]{1,0:T(8,128)(2,1)} %get-tuple-element.98), channel_id=1, source_target_pairs={{0,2},{1,3},{2,0},{3,1},{4,6},{5,7},{6,4},{7,5},{8,10},{9,11},{10,... | collective-permute-start | bytes 1572872 | tf_op jit(solution)/shard_map/ppermute | solution.py:305
  828.9 24.3 %collective-permute-start.40 = (bf16[128,512]{1,0:T(8,128)(2,1)S(1)}, bf16[128,512]{1,0:T(8,128)(2,1)S(1)}, u32[]{:S(2)}, u32[]{:S(2)}) collective-permute-start(bf16[128,512]{1,0:T(8,128)(2,1)S(1)} %get-tuple-element.261), channel_id=1, source_target_pairs={{0,8},{1,9},{2,10},{3,11},{4,12},{5,13},{6,14},{7,15},{8,0},{9,1},... | collective-permute-start | bytes 393224 | tf_op jit(solution)/shard_map/ppermute | solution.py:305
  854.0 81.3 %all-to-all-start.4 = ((bf16[16,144,512]{2,1,0:T(8,128)(2,1)}), bf16[16,144,512]{2,1,0:T(8,128)(2,1)}, u32[]{:S(2)}, u32[]{:S(2)}) async-start(bf16[16,144,512]{2,1,0:T(8,128)(2,1)} %pad_maximum_fusion.3), calls=%async_computation.4 | async-start | bytes 4718592 | tf_op jit(solution)/shard_map/all_to_all | solution.py:423
  935.3 97.9 %all-to-all-start.3 = ((bf16[16,144,512]{2,1,0:T(8,128)(2,1)}), bf16[16,144,512]{2,1,0:T(8,128)(2,1)}, u32[]{:S(2)}, u32[]{:S(2)}) async-start(bf16[16,144,512]{2,1,0:T(8,128)(2,1)} %pad_maximum_fusion.4), calls=%async_computation.3 | async-start | bytes 4718592 | tf_op jit(solution)/shard_map/all_to_all | solution.py:423
  958.1 72.0 %collective-permute-start.50 = (bf16[16,144,512]{2,1,0:T(8,128)(2,1)}, bf16[16,144,512]{2,1,0:T(8,128)(2,1)}, u32[]{:S(2)}, u32[]{:S(2)}) collective-permute-start(bf16[16,144,512]{2,1,0:T(8,128)(2,1)} %all-to-all-done.4.mine), channel_id=1, source_target_pairs={{0,16},{16,0},{1,17},{17,1},{2,18},{18,2},{3,19},{19,3},{4,20},{20... | collective-permute-start | bytes 7077896 | tf_op jit(solution)/shard_map/ppermute | solution.py:308
  968.7 25.8 %collective-permute-start.49 = (f32[2,128]{1,0:T(2,128)S(1)}, f32[2,128]{1,0:T(2,128)S(1)}, u32[]{:S(2)}, u32[]{:S(2)}) collective-permute-start(f32[2,128]{1,0:T(2,128)S(1)} %get-tuple-element.321), channel_id=1, source_target_pairs={{0,12},{1,13},{2,14},{3,15},{4,8},{5,9},{6,10},{7,11},{8,4},{9,5},... | collective-permute-start | bytes 3080 | tf_op jit(solution)/shard_map/ppermute | solution.py:305
  971.1 40.7 %collective-permute-start.48 = (f32[2,128]{1,0:T(2,128)S(1)}, f32[2,128]{1,0:T(2,128)S(1)}, u32[]{:S(2)}, u32[]{:S(2)}) collective-permute-start(f32[2,128]{1,0:T(2,128)S(1)} %get-tuple-element.322), channel_id=1, source_target_pairs={{0,8},{1,9},{2,10},{3,11},{4,12},{5,13},{6,14},{7,15},{8,0},{9,1},... | collective-permute-start | bytes 3080 | tf_op jit(solution)/shard_map/ppermute | solution.py:305
  971.8 48.6 %collective-permute-start.55 = (bf16[128,512]{1,0:T(8,128)(2,1)S(1)}, bf16[128,512]{1,0:T(8,128)(2,1)S(1)}, u32[]{:S(2)}, u32[]{:S(2)}) collective-permute-start(bf16[128,512]{1,0:T(8,128)(2,1)S(1)} %get-tuple-element.284), channel_id=1, source_target_pairs={{0,12},{1,13},{2,14},{3,15},{4,8},{5,9},{6,10},{7,11},{8,4},{9,5},... | collective-permute-start | bytes 393224 | tf_op jit(solution)/shard_map/ppermute | solution.py:305
  989.7 29.9 %collective-permute-start.54 = (bf16[128,512]{1,0:T(8,128)(2,1)S(1)}, bf16[128,512]{1,0:T(8,128)(2,1)S(1)}, u32[]{:S(2)}, u32[]{:S(2)}) collective-permute-start(bf16[128,512]{1,0:T(8,128)(2,1)S(1)} %get-tuple-element.284), channel_id=1, source_target_pairs={{0,8},{1,9},{2,10},{3,11},{4,12},{5,13},{6,14},{7,15},{8,0},{9,1},... | collective-permute-start | bytes 393224 | tf_op jit(solution)/shard_map/ppermute | solution.py:305
  1011.8 24.1 %collective-permute-start.63 = (bf16[1024,512]{0,1:T(8,128)(2,1)}, bf16[1024,512]{0,1:T(8,128)(2,1)}, u32[]{:S(2)}, u32[]{:S(2)}) collective-permute-start(bf16[1024,512]{0,1:T(8,128)(2,1)} %constant_dynamic-update-slice_fusion.69), channel_id=1, source_target_pairs={{0,1},{1,0},{2,3},{3,2},{4,5},{5,4},{6,7},{7,6},{8,9},{9,8},{10,11... | collective-permute-start | bytes 3145736 | tf_op jit(solution)/shard_map/ppermute | solution.py:305
  1028.9 35.4 %collective-permute-start.43 = (bf16[128,2048]{1,0:T(8,128)(2,1)}, bf16[128,2048]{1,0:T(8,128)(2,1)}, u32[]{:S(2)}, u32[]{:S(2)}) collective-permute-start(bf16[128,2048]{1,0:T(8,128)(2,1)} %get-tuple-element.110), channel_id=1, source_target_pairs={{0,8},{1,9},{2,10},{3,11},{4,12},{5,13},{6,14},{7,15},{8,0},{9,1},... | collective-permute-start | bytes 1572872 | tf_op jit(solution)/shard_map/ppermute | solution.py:305
  1030.1 34.2 %collective-permute-start.44 = (bf16[128,2048]{1,0:T(8,128)(2,1)}, bf16[128,2048]{1,0:T(8,128)(2,1)}, u32[]{:S(2)}, u32[]{:S(2)}) collective-permute-start(bf16[128,2048]{1,0:T(8,128)(2,1)} %get-tuple-element.111), channel_id=1, source_target_pairs={{0,12},{1,13},{2,14},{3,15},{4,8},{5,9},{6,10},{7,11},{8,4},{9,5},... | collective-permute-start | bytes 1572872 | tf_op jit(solution)/shard_map/ppermute | solution.py:305
  1033.2 64.1 %collective-permute-start.51 = (bf16[16,144,512]{2,1,0:T(8,128)(2,1)}, bf16[16,144,512]{2,1,0:T(8,128)(2,1)}, u32[]{:S(2)}, u32[]{:S(2)}) collective-permute-start(bf16[16,144,512]{2,1,0:T(8,128)(2,1)} %all-to-all-done.3.mine), channel_id=1, source_target_pairs={{0,16},{16,0},{1,17},{17,1},{2,18},{18,2},{3,19},{19,3},{4,20},{20... | collective-permute-start | bytes 7077896 | tf_op jit(solution)/shard_map/ppermute | solution.py:308
  1035.9 42.7 %collective-permute-start.60 = (bf16[1024,512]{1,0:T(8,128)(2,1)}, bf16[1024,512]{1,0:T(8,128)(2,1)S(1)}, u32[]{:S(2)}, u32[]{:S(2)}) collective-permute-start(bf16[1024,512]{1,0:T(8,128)(2,1)} %get-tuple-element.268), channel_id=1, source_target_pairs={{0,1},{1,0},{2,3},{3,2},{4,5},{5,4},{6,7},{7,6},{8,9},{9,8},{10,11... | collective-permute-start | bytes 3145736 | tf_op jit(solution)/shard_map/ppermute | solution.py:305
  1038.0 29.5 %collective-permute-start.64 = (bf16[512,512]{0,1:T(8,128)(2,1)S(1)}, bf16[512,512]{0,1:T(8,128)(2,1)S(1)}, u32[]{:S(2)}, u32[]{:S(2)}) collective-permute-start(bf16[512,512]{0,1:T(8,128)(2,1)S(1)} %slice.453), channel_id=1, source_target_pairs={{0,2},{1,3},{2,0},{3,1},{4,6},{5,7},{6,4},{7,5},{8,10},{9,11},{10,... | collective-permute-start | bytes 1572872 | tf_op jit(solution)/shard_map/ppermute | solution.py:305
  (136 other events, 2411.3 us)
Sparse Core Ops, SparseCore 0:
  12.1 148.2 all-gather.5
  163.2 151.9 all-gather.7
  317.4 110.3 all-gather.9
  719.9 95.9 all-gather.13
  817.9 124.8 all-gather.11

commit v5 on v3

--- a/solution.py
+++ b/solution.py
@@ -111,8 +111,9 @@
     )(gate, up, *seconds, first, *held), seconds
 
 
-def forward_kernel(x_ref, w_ref, hidden_ref, act_ref, slope_ref):
-    h = hidden_ref.shape[1] // 2
+def forward_kernel(core_ref, x_ref, w_ref, hidden_ref, act_ref, slope_ref):
+    h = act_ref.shape[1] // 2
+    rows = hidden_ref.shape[1]
     c = 0.7978845608028654
     for k in (0, 1):
         both = mm(x_ref[...], w_ref[:, 2 * k * h : 2 * (k + 1) * h])
@@ -123,64 +124,83 @@
         act = gate * half_up
         slope = half_up + 0.5 * gate * (1.0 - t * t) * (c * (1.0 + 3 * 0.044715 * square))
         part = slice(k * h, (k + 1) * h)
-        hidden_ref[:, part] = (act * up).astype(BF)
+        hidden = (act * up).astype(BF)
+        for j in range(hidden_ref.shape[0]):
+            hidden_ref[j, :, part] = hidden[j * rows : (j + 1) * rows]
         act_ref[:, part] = act.astype(BF)
         slope_ref[:, part] = (slope * up).astype(BF)
 
 
-def forward(x, w):
+def owner(tiles):
+    def place(i, core_ref):
+        mine = i < tiles // 2
+        return (i % (tiles // 2), jnp.where(mine, core_ref[0], 1 - core_ref[0]), 0, 0)
+
+    return place
+
+
+def forward(core, x, w, rows):
     t, d = x.shape
     f = w.shape[1] // 2
-    tile = 256
-    out = pl.BlockSpec((tile, f), lambda i: (i, 0))
+    tile = 2 * rows
+    out = pl.BlockSpec((tile, f), lambda i, _: (i, 0))
+    ordered = pl.BlockSpec((2, None, rows, f), owner(t // tile))
     return pl.pallas_call(
         forward_kernel,
-        out_shape=(jax.ShapeDtypeStruct((t, f), BF),) * 3,
-        grid=(t // tile,),
-        in_specs=[
-            pl.BlockSpec((tile, d), lambda i: (i, 0)),
-            pl.BlockSpec((d, 2 * f), lambda i: (0, 0)),
-        ],
-        out_specs=(out,) * 3,
+        out_shape=(jax.ShapeDtypeStruct((t // tile, 2, rows, f), BF),)
+        + (jax.ShapeDtypeStruct((t, f), BF),) * 2,
+        grid_spec=pltpu.PrefetchScalarGridSpec(
+            num_scalar_prefetch=1,
+            grid=(t // tile,),
+            in_specs=[
+                pl.BlockSpec((tile, d), lambda i, _: (i, 0)),
+                pl.BlockSpec((d, 2 * f), lambda i, _: (0, 0)),
+            ],
+            out_specs=(ordered, out, out),
+        ),
         compiler_params=pltpu.CompilerParams(vmem_limit_bytes=44 * 2**20),
         cost_estimate=pl.CostEstimate(
             flops=4 * t * d * f, transcendentals=t * f, bytes_accessed=2 * (t * d + 2 * d * f + 3 * t * f)
         ),
-    )(x, w)
-
-
-def backward_kernel(dy_ref, w_ref, act_ref, slope_ref, out_ref):
+    )(core, x, w)
+
+
+def backward_kernel(core_ref, dy_ref, w_ref, act_ref, slope_ref, out_ref):
     h = act_ref.shape[1] // 2
+    dy = dy_ref[...].reshape(act_ref.shape[0], dy_ref.shape[2])
     for k in (0, 1):
         part = slice(k * h, (k + 1) * h)
-        grad = mm(dy_ref[...], w_ref[part, :], 1, 1)
+        grad = mm(dy, w_ref[part, :], 1, 1)
         out_ref[:, 2 * k * h : (2 * k + 1) * h] = (grad * slope_ref[:, part].astype(F32)).astype(BF)
         out_ref[:, (2 * k + 1) * h : 2 * (k + 1) * h] = (
             grad * act_ref[:, part].astype(F32)
         ).astype(BF)
 
 
-def backward(dy, w, act, slope):
-    t, d = dy.shape
-    f = w.shape[0]
-    tile = 256
-    given = pl.BlockSpec((tile, f), lambda i: (i, 0))
+def backward(core, dy, w, act, slope, rows):
+    t, f = act.shape
+    d = dy.shape[1]
+    tile = 2 * rows
+    given = pl.BlockSpec((tile, f), lambda i, _: (i, 0))
     return pl.pallas_call(
         backward_kernel,
         out_shape=jax.ShapeDtypeStruct((t, 2 * f), BF),
-        grid=(t // tile,),
-        in_specs=[
-            pl.BlockSpec((tile, d), lambda i: (i, 0)),
-            pl.BlockSpec((f, d), lambda i: (0, 0)),
-            given,
-            given,
-        ],
-        out_specs=pl.BlockSpec((tile, 2 * f), lambda i: (i, 0)),
+        grid_spec=pltpu.PrefetchScalarGridSpec(
+            num_scalar_prefetch=1,
+            grid=(t // tile,),
+            in_specs=[
+                pl.BlockSpec((2, None, rows, d), owner(t // tile)),
+                pl.BlockSpec((f, d), lambda i, _: (0, 0)),
+                given,
+                given,
+            ],
+            out_specs=pl.BlockSpec((tile, 2 * f), lambda i, _: (i, 0)),
+        ),
         compiler_params=pltpu.CompilerParams(vmem_limit_bytes=44 * 2**20),
         cost_estimate=pl.CostEstimate(
             flops=2 * t * d * f, transcendentals=0, bytes_accessed=2 * (t * d + d * f + 4 * t * f)
         ),
-    )(dy, w, act, slope)
+    )(core, dy.reshape(t // tile, 2, rows, d), w, act, slope)
 
 
 def collect_kernel(plane_ref, mine, other, *refs):
@@ -498,24 +518,20 @@
     inv_two = inv_rms(mid)
     norm_two = (mid * inv_two * (1.0 + feed_gain)).astype(BF)
     near_rows = gather_chips(norm_two)
-    dy_pair = dy_got.reshape(n // 2, 2, rows, width)
-    all_dy = jnp.concatenate(
-        [
-            lax.dynamic_index_in_dim(dy_pair, c, 1, False).reshape(n // 2 * rows, width)
-            for c in (core, 1 - core)
-        ],
-        axis=0,
-    )
+    core_id = core.astype(jnp.int32).reshape(1)
     up_other = jnp.concatenate(up_pieces, axis=0)
     w_eff, (gate_b, up_b) = fold(gate_mine, up_mine, gate_up_first, 0, None)
     w_eff, _ = fold(gate_other, up_other, gate_up_first, 1, w_eff)
     near_rows = after(near_rows, w_eff, down_eff)
     all_rows = jnp.concatenate([near_rows, hop(near_rows, 1)], axis=0)
-    hidden, act, slope = forward(after(all_rows, all_dy), w_eff)
+    hidden, act, slope = forward(core_id, all_rows, w_eff, rows)
+    hidden = hidden.reshape(seq, feed_dev)
+    out_part = mm(hidden, down_eff).astype(BF)
+    out_sum = lax.psum_scatter(out_part, "ctx", scatter_dimension=0, tiled=True)
     h = feed_half
     half_seq = seq // 2
-    down_part = mm(hidden[:, h:], all_dy, 0, 0).astype(BF)
-    grads = backward(after(all_dy, down_part), down_eff, act, slope)
+    down_part = mm(after(hidden, out_part)[:, h:], dy_got, 0, 0).astype(BF)
+    grads = backward(core_id, after(dy_got, down_part), down_eff, act, slope, rows)
     down_part = swap(down_part)
     far_part = mm(grads[half_seq:], w_eff, 1, 1).astype(BF)
     near_part = mm(after(grads, far_part)[:half_seq], w_eff, 1, 1).astype(BF)
@@ -531,16 +547,13 @@
     sums = [a + b.astype(F32) for a, b in zip(here, sides)]
     line_sums = [part.astype(BF) for part in sums[1:]]
     arrivals = [hop(part, 4 * (k + 1)) for k, part in enumerate(line_sums)]
-    late_hidden = after(hidden, other_part)
-    out_far = mm(late_hidden[half_seq:], down_eff).astype(BF)
-    out_near = mm(late_hidden[:half_seq], down_eff).astype(BF)
     down_half = (
-        mm(after(hidden, other_part)[:, :h], all_dy, 0, 0) + down_part.astype(F32)
+        mm(after(hidden, other_part)[:, :h], dy_got, 0, 0) + down_part.astype(F32)
     ).astype(BF)
     g_down_first = mm(down_half, down_second, 1, 1).astype(BF)
     down_rows = jnp.concatenate([down_half, g_down_first], axis=1)
 
-    late_rows = after(all_rows, down_rows, out_near, out_far, *line_sums)
+    late_rows = after(all_rows, down_rows, *line_sums)
     gate_half = (mm(late_rows, grads[:, :h], 0, 0) + gate_part.astype(F32)).astype(BF)
 
     pieces = jnp.concatenate(
@@ -560,6 +573,7 @@
     feed_gain_rows = jnp.sum(grad_norm_two * mid * inv_two, axis=0, keepdims=True)
     grad_mid = dy.astype(F32) + norm_back(mid, inv_two, feed_gain, grad_norm_two)
     grad_branch = grad_mid.astype(BF)
+    branch_all = lax.all_gather(grad_branch, "ctx", axis=0, tiled=True)
     grad_inner_out = mm(grad_branch, out_second, 1, 1).astype(BF)
     grad_attended = mm(
         jnp.concatenate([grad_branch, grad_inner_out], axis=1), out_full, 1, 1
@@ -573,7 +587,7 @@
         [gate_half.reshape(n, w_rows, h), gate_second.reshape(n, r_rows, h)], axis=1
     )
     gate_got = exchange(gate_ext)
-    grad_flat = after(grad_flat, gate_ext)
+    grad_flat = after(grad_flat, gate_ext, out_sum)
     grad_probs = mm(grad_flat, v_all, 1, 1)
     grad_scores = (probs.astype(F32) * (grad_probs - delta)).astype(BF)
     grad_scores = after(grad_scores, up_part)
@@ -593,9 +607,6 @@
         + up_part.astype(F32)
     ).astype(BF)
     down_back = swap(after(down_rows, up_part))
-    out_here, out_there = fold_core(out_near, hop(after(out_far, grad_kv), 1))
-    out_side = hop(jnp.concatenate(out_there, axis=0), 2)
-    branch_all = lax.all_gather(after(grad_branch, grad_kv), "ctx", axis=0, tiled=True)
     grad_kv = after(grad_kv, up_half, down_back)
     grad_k_rows = rotate(grad_kv[:, :HD], cosine, -sine_rows)
     grad_kv_rows = jnp.concatenate([grad_k_rows, grad_kv[:, HD:]], axis=1).astype(BF)
@@ -610,16 +621,12 @@
     grad_qkv = after(grad_qkv, up_ext)
     grad_inner_qkv = mm(grad_qkv, qkv_second, 1, 1).astype(BF)
     grad_norm_one = mm(
-        after(jnp.concatenate([grad_qkv, grad_inner_qkv], axis=1), out_side), qkv_full, 1, 1
+        jnp.concatenate([grad_qkv, grad_inner_qkv], axis=1), qkv_full, 1, 1
     )
     attn_gain_rows = jnp.sum(grad_norm_one * x * inv_one, axis=0, keepdims=True)
     grad_input = (grad_mid + norm_back(x, inv_one, attn_gain, grad_norm_one)).astype(BF)
     gate_back = swap(after(gate_got, down_back))
-    output = mid + out_here[0] + out_side[:rows].astype(F32)
-    for k in range(1, lines):
-        part = out_here[k] + out_side[k * rows : (k + 1) * rows].astype(F32)
-        output = output + hop(part.astype(BF), 4 * k).astype(F32)
-    output = output.astype(BF)
+    output = (mid + out_sum.astype(F32)).astype(BF)
 
     def both_planes(own):
         own = own.astype(BF)
@@ -649,14 +656,14 @@
     up_got_other = swap(after(up_got, gate_back))
     gate_up_grads = collect(plane_id, up_got, up_got_other, w_rows, 1, gate_up_grads)
 
-    g_q = mm(inputs[:, :ext], after(q_all, down_grads[0]), 0, 0)
-    g_out = mm(inputs[:, ext:], after(branch_all, g_q), 0, 0).astype(BF)
+    g_out = mm(inputs[:, ext:], after(branch_all, down_grads[0]), 0, 0).astype(BF)
+    g_q = mm(inputs[:, :ext], after(q_all, g_out), 0, 0)
     inputs_rel = reorder(inputs[:, :ext])
     g_kv = mm(inputs_rel, kv_all_grads, 0, 0)
     g_qkv = jnp.concatenate([g_q, g_kv], axis=1).astype(BF)
-    g_out = g_out.astype(F32) + after(swap(g_out), gate_up_grads[0]).astype(F32)
+    g_out = both_planes(after(g_out, gate_back))
     small = both_planes(after(small, gate_back))
-    g_qkv = both_planes(g_qkv)
+    g_qkv = g_qkv.astype(F32) + after(swap(g_qkv), gate_up_grads[0]).astype(F32)
     gain_rows = gain_rows + swap(after(gain_rows, up_got_other))
     g_gu_first = small[:, :rank]
     g_down_second = small[:, rank:].reshape(r_rows, width)

time: 1160 us -> 1070 us (0.922); the launches traced: 1150 us -> 1050 us
  waiting for transfers between devices: 566 us -> 499 us
  other arithmetic: 68.4 us -> 43.1 us
  local copies, waits for them, and re-layouts: 142 us -> 125 us
    ppermute x52 -> x47, waiting for transfers between devices: 296 us -> 234 us  [hop(): return lax.ppermute(x, 'ctx', [(i, i ^ k) for i in range(n)])]
    ppermute x14, waiting for transfers between devices: 115 us -> 91.1 us  [swap(): return lax.ppermute(x, 'grp', [(0, 1), (1, 0)])]
    all_to_all x4, waiting for transfers between devices: 0.01 us -> 19.3 us  [exchange(): lax.all_to_all(flat, 'ctx', 0, 0, tiled=True).reshape(n, ext, feed_half)]
    unnamed x232 -> x212, local copies, waits for them, and re-layouts: 53.1 us -> 44.5 us
    dot_general x35 -> x34, matrix products: 164 us -> 165 us  [mm(): lax.dot_general(a, b, (((ca,), (cb,)), ((), ())), preferred_element_type=...]
    ppermute x52 -> x47, starting transfers between devices: 73.3 us -> 73.5 us  [hop(): return lax.ppermute(x, 'ctx', [(i, i ^ k) for i in range(n)])]
  transfers between devices with their start and end apart: 76 -> 72, of which waited for: 28 -> 31; matrix products, arithmetic and copies ran while one was open for 30% -> 29% of each run, Pallas kernels for 7% -> 8%
where the time goes in v5:
time: 1070 us; the launch traced here: 1050 us
  waiting for transfers between devices  499 us (47%)
  matrix products  165 us (15%)
  local copies, waits for them, and re-layouts  125 us (12%)
  starting transfers between devices  115 us (11%)
  Pallas kernels  85.2 us (8%)
  other arithmetic  43.1 us (4%)
  between operations  16.2 us (2%)
    ppermute x47, waiting for transfers between devices, hop(): return lax.ppermute(x, 'ctx', [(i, i ^ k) for i in range(n)])  234 us
    dot_general x34, matrix products, mm(): lax.dot_general(a, b, (((ca,), (cb,)), ((), ())), preferred_element_type=...  165 us
    all_gather x1, waiting for transfers between devices, body(): qkv_got = lax.all_gather(qkv_ext, 'ctx', axis=0, tiled=True)  129 us
    ppermute x14, waiting for transfers between devices, swap(): return lax.ppermute(x, 'grp', [(0, 1), (1, 0)])  91.1 us
    ppermute x47, starting transfers between devices, hop(): return lax.ppermute(x, 'ctx', [(i, i ^ k) for i in range(n)])  73.5 us
    unnamed x212, local copies, waits for them, and re-layouts  44.5 us
    pallas_call x1, Pallas kernels, forward(): pl.pallas_call(forward_kernel, out_shape=(jax.ShapeDtypeStruct((t // tile...  26.4 us
    all_gather x1, waiting for transfers between devices, body(): out_got = lax.all_gather(out_ext, 'ctx', axis=0, tiled=True)  26.2 us
  transfers between devices with their start and end apart: 72, of which 31 were waited for; matrix products, arithmetic and copies ran while one was open for 29% of the time, Pallas kernels for 8%

profile of v5, /device:TPU:0, one launch (start us, length us, event | category | flops | bytes accessed | tf_op | source)
XLA Modules:
  0.0 1049.5 jit_solution(9205738010307263261)
XLA Ops:
  17.2 7.4 all-to-all-start
  31.6 128.8 %all-gather.6.cloned.1.call-done = bf16[2048,3200]{1,0:T(8,128)(2,1)} async-done(((bf16[128,3200]{1,0:T(8,128)(2,1)}), bf16[2048,3200]{1,0:T(8,128)(2,1)}) %all-gather.6.cloned.1.call-update) | async-done | bytes 13107216 | tf_op jit(solution)/shard_map/all_gather | solution.py:424
  169.2 6.6 fusion.3
  190.7 13.4 %collective-permute-done.1 = bf16[128,512]{1,0:T(8,128)(2,1)S(1)} collective-permute-done((bf16[128,512]{1,0:T(8,128)(2,1)S(1)}, bf16[128,512]{1,0:T(8,128)(2,1)S(1)}, u32[]{:S(2)}, u32[]{:S(2)}) %collective-permute-start.1) | collective-permute-done | bytes 131104 | tf_op jit(solution)/shard_map/ppermute | solution.py:325
  224.6 5.5 all-to-all-start.1
  237.8 8.9 collective-permute-done.8
  248.0 23.4 %collective-permute-done.9 = bf16[8,144,512]{2,1,0:T(8,128)(2,1)} collective-permute-done((bf16[8,144,512]{2,1,0:T(8,128)(2,1)}, bf16[8,144,512]{2,1,0:T(8,128)(2,1)}, u32[]{:S(2)}, u32[]{:S(2)}) %collective-permute-start.9) | collective-permute-done | bytes 1179680 | tf_op jit(solution)/shard_map/ppermute | solution.py:328
  289.1 26.2 %all-gather.8.cloned.1.call-done = bf16[2048,3072]{1,0:T(8,128)(2,1)} async-done(((bf16[128,3072]{1,0:T(8,128)(2,1)}), bf16[2048,3072]{1,0:T(8,128)(2,1)}) %all-gather.8.cloned.1.call-update) | async-done | bytes 12582928 | tf_op jit(solution)/shard_map/all_gather | solution.py:435
  325.2 5.6 fusion.7
  351.4 6.2 shard_map.290.refs_0_
  359.0 62.4 %collective-permute-done.11 = bf16[128,2048]{1,0:T(8,128)(2,1)S(1)} collective-permute-done((bf16[128,2048]{1,0:T(8,128)(2,1)}, bf16[128,2048]{1,0:T(8,128)(2,1)S(1)}, u32[]{:S(2)}, u32[]{:S(2)}) %collective-permute-start.11) | collective-permute-done | bytes 524320 | tf_op jit(solution)/shard_map/ppermute | solution.py:325
  428.5 7.9 collective-permute-done.14
  437.2 10.4 collective-permute-done.15
  448.5 8.5 collective-permute-done.16
  460.7 6.3 shard_map.291.w_ref
  484.1 26.4 %shard_map.292 = (bf16[8,2,128,1024]{3,2,1,0:T(8,128)(2,1)S(1)}, bf16[2048,1024]{1,0:T(8,128)(2,1)S(1)}, bf16[2048,1024]{1,0:T(8,128)(2,1)}) custom-call(s32[1]{0:T(128)} %bitcast.12.core_ref, bf16[2048,2048]{1,0:T(8,128)(2,1)} %constant_dynamic-update-slice_fusion.26.x_ref, bf16[2048,2048]{1,0:T(8,128)(2,1)} %shard_map.291.w_ref), custom_call_target="tpu_custom_call" | custom-call | flops 17179869184 | bytes 29360128 | tf_op jit(solution)/shard_map/pallas_call | solution.py:148
  514.5 10.7 %convolution_convert_fusion = bf16[2048,2048]{1,0:T(8,128)(2,1)} fusion(bf16[2048,1024]{1,0:T(8,128)(2,1)S(1)} %bitcast.124, bf16[1024,2048]{1,0:T(8,128)(2,1)S(1)} %copy-done.2), kind=kOutput, calls=%fused_computation.14 | convolution fusion | flops 8594128896 | bytes 16777216 | tf_op jit(solution)/shard_map/dot_general | solution.py:19
  525.4 10.1 convolution_convert_fusion.1
  535.5 15.5 %shard_map.293 = bf16[2048,2048]{1,0:T(8,128)(2,1)} custom-call(s32[1]{0:T(128)} %bitcast.12.core_ref, bf16[8,2,128,2048]{3,2,1,0:T(8,128)(2,1)} %bitcast.158, bf16[1024,2048]{1,0:T(8,128)(2,1)S(1)} %copy-done.3, bf16[2048,1024]{1,0:T(8,128)(2,1)S(1)} %copy-done.5, bf16[2048,1024]{1,0:T(8,128)(2,1)} %get-tuple-element.80.slope_ref), custom_call_target="tpu_custom_call" | custom-call | flops 8589934592 | bytes 29360128 | tf_op jit(solution)/shard_map/pallas_call | solution.py:185
  551.0 12.0 %fusion.25 = bf16[1024,2048]{1,0:T(8,128)(2,1)} fusion(bf16[2048,2048]{1,0:T(8,128)(2,1)S(1)} %bitcast.128, bf16[2048,2048]{1,0:T(8,128)(2,1)} %shard_map.293), kind=kOutput, calls=%fused_computation.63 | convolution fusion | flops 8592031744 | bytes 16777216 | tf_op jit(solution)/shard_map/dot_general | solution.py:19
  564.1 12.6 %fusion.19 = bf16[1024,2048]{1,0:T(8,128)(2,1)S(1)} fusion(bf16[2048,2048]{1,0:T(8,128)(2,1)} %shard_map.291.w_ref, bf16[2048,2048]{1,0:T(8,128)(2,1)} %shard_map.293), kind=kOutput, calls=%fused_computation.61 | convolution fusion | flops 8592031744 | bytes 16777216 | tf_op jit(solution)/shard_map/dot_general | solution.py:19
  583.4 13.2 %fusion.22 = bf16[2048,1024]{1,0:T(8,128)(2,1)S(1)} fusion(bf16[2048,2048]{1,0:T(8,128)(2,1)} %constant_dynamic-update-slice_fusion.26.x_ref, bf16[2048,2048]{1,0:T(8,128)(2,1)} %shard_map.293), kind=kOutput, calls=%fused_computation.62 | convolution fusion | flops 8592031744 | bytes 16777216 | tf_op jit(solution)/shard_map/dot_general | solution.py:19
  598.3 13.2 %collective-permute-done.28 = bf16[512,2048]{1,0:T(8,128)(2,1)S(1)} collective-permute-done((bf16[512,2048]{1,0:T(8,128)(2,1)}, bf16[512,2048]{1,0:T(8,128)(2,1)S(1)}, u32[]{:S(2)}, u32[]{:S(2)}) %collective-permute-start.28) | collective-permute-done | bytes 2097184 | tf_op jit(solution)/shard_map/ppermute | solution.py:328
  613.2 6.4 add_convert_fusion.3
  622.0 10.2 collective-permute-done.22
  632.2 11.5 %collective-permute-done.21 = bf16[128,2048]{1,0:T(8,128)(2,1)S(1)} collective-permute-done((bf16[128,2048]{1,0:T(8,128)(2,1)S(1)}, bf16[128,2048]{1,0:T(8,128)(2,1)S(1)}, u32[]{:S(2)}, u32[]{:S(2)}) %collective-permute-start.21) | collective-permute-done | bytes 524320 | tf_op jit(solution)/shard_map/ppermute | solution.py:325
  650.4 9.3 collective-permute-done.29
  659.7 10.0 add_convert_fusion.2
  669.7 24.5 %collective-permute-done.26 = bf16[128,2048]{1,0:T(8,128)(2,1)S(1)} collective-permute-done((bf16[128,2048]{1,0:T(8,128)(2,1)S(1)}, bf16[128,2048]{1,0:T(8,128)(2,1)S(1)}, u32[]{:S(2)}, u32[]{:S(2)}) %collective-permute-start.26) | collective-permute-done | bytes 524320 | tf_op jit(solution)/shard_map/ppermute | solution.py:325
  712.9 8.0 convert_multiply_fusion.5
  722.8 6.1 multiply_convert_fusion
  728.9 17.6 %collective-permute-done.30 = bf16[2048,512]{1,0:T(8,128)(2,1)} collective-permute-done((bf16[2048,512]{1,0:T(8,128)(2,1)}, bf16[2048,512]{1,0:T(8,128)(2,1)}, u32[]{:S(2)}, u32[]{:S(2)}) %collective-permute-start.30) | collective-permute-done | bytes 2097184 | tf_op jit(solution)/shard_map/ppermute | solution.py:328
  751.2 6.2 convolution_convert_fusion.3
  772.1 22.0 %collective-permute-done.32 = bf16[512,512]{1,0:T(8,128)(2,1)S(1)} collective-permute-done((bf16[512,512]{1,0:T(8,128)(2,1)S(1)}, bf16[512,512]{1,0:T(8,128)(2,1)S(1)}, u32[]{:S(2)}, u32[]{:S(2)}) %collective-permute-start.32) | collective-permute-done | bytes 524320 | tf_op jit(solution)/shard_map/ppermute | solution.py:325
  799.1 8.3 collective-permute-done.33
  810.0 13.9 %collective-permute-done.34 = bf16[128,512]{1,0:T(8,128)(2,1)S(1)} collective-permute-done((bf16[128,512]{1,0:T(8,128)(2,1)S(1)}, bf16[128,512]{1,0:T(8,128)(2,1)S(1)}, u32[]{:S(2)}, u32[]{:S(2)}) %collective-permute-start.34) | collective-permute-done | bytes 131104 | tf_op jit(solution)/shard_map/ppermute | solution.py:325
  824.0 9.2 add_convert_fusion.1
  850.0 7.0 fusion.47
  890.2 13.5 %collective-permute-done.50 = bf16[128,512]{1,0:T(8,128)(2,1)S(1)} collective-permute-done((bf16[128,512]{1,0:T(8,128)(2,1)}, bf16[128,512]{1,0:T(8,128)(2,1)S(1)}, u32[]{:S(2)}, u32[]{:S(2)}) %collective-permute-start.50) | collective-permute-done | bytes 131104 | tf_op jit(solution)/shard_map/ppermute | solution.py:325
  905.1 19.3 %all-to-all-done.4.mine = bf16[16,144,512]{2,1,0:T(8,128)(2,1)} async-done(((bf16[16,144,512]{2,1,0:T(8,128)(2,1)}), bf16[16,144,512]{2,1,0:T(8,128)(2,1)}, u32[]{:S(2)}, u32[]{:S(2)}) %all-to-all-start.4) | async-done | bytes 2359328 | tf_op jit(solution)/shard_map/all_to_all | solution.py:443
  929.8 12.5 %collective-permute-start.56 = (bf16[512,512]{0,1:T(8,128)(2,1)}, bf16[512,512]{0,1:T(8,128)(2,1)}, u32[]{:S(2)}, u32[]{:S(2)}) collective-permute-start(bf16[512,512]{0,1:T(8,128)(2,1)} %slice.441), channel_id=1, source_target_pairs={{0,2},{1,3},{2,0},{3,1},{4,6},{5,7},{6,4},{7,5},{8,10},{9,11},{10,... | collective-permute-start | bytes 1572872 | tf_op jit(solution)/shard_map/ppermute | solution.py:325
  942.3 12.2 %collective-permute-start.39 = (f32[2,128]{1,0:T(2,128)S(1)}, f32[2,128]{1,0:T(2,128)S(1)}, u32[]{:S(2)}, u32[]{:S(2)}) collective-permute-start(f32[2,128]{1,0:T(2,128)S(1)} %get-tuple-element.298), channel_id=1, source_target_pairs={{0,4},{1,5},{2,6},{3,7},{4,0},{5,1},{6,2},{7,3},{8,12},{9,13},{10,... | collective-permute-start | bytes 3080 | tf_op jit(solution)/shard_map/ppermute | solution.py:325
  960.7 9.5 shard_map.294
  989.0 6.5 shard_map.295
  998.7 6.8 shard_map.296
  1011.4 6.3 convolution_convert_fusion.4
  1019.3 7.8 collective-permute-done.54
  1029.2 11.0 %collective-permute-done.53 = bf16[144,2560]{1,0:T(8,128)(2,1)S(1)} collective-permute-done((bf16[144,2560]{1,0:T(8,128)(2,1)S(1)}, bf16[144,2560]{1,0:T(8,128)(2,1)S(1)}, u32[]{:S(2)}, u32[]{:S(2)}) %collective-permute-start.53) | collective-permute-done | bytes 737312 | tf_op jit(solution)/shard_map/ppermute | solution.py:328
  (509 shorter events, 316.6 us)
Async XLA Ops:
  7.2 153.2 %all-gather.6.cloned.1.call-start = ((), (), s32[]{:S(2)}) async-start(), calls=%async_computation.6 | async-start | bytes 13926400 | tf_op jit(solution)/shard_map/all_gather | solution.py:424
  12.0 303.4 %all-gather.8.cloned.1.call-start = ((), (), s32[]{:S(2)}) async-start(), calls=%async_computation.7 | async-start | bytes 13369344 | tf_op jit(solution)/shard_map/all_gather | solution.py:435
  17.2 152.0 %all-to-all-start = ((bf16[16,144,512]{2,1,0:T(8,128)(2,1)}), bf16[16,144,512]{2,1,0:T(8,128)(2,1)S(1)}, u32[]{:S(2)}, u32[]{:S(2)}) async-start(bf16[16,144,512]{2,1,0:T(8,128)(2,1)} %shard_map.288), calls=%async_computation | async-start | bytes 4718592 | tf_op jit(solution)/shard_map/all_to_all | solution.py:443
  181.7 22.4 %collective-permute-start.1 = (bf16[128,512]{1,0:T(8,128)(2,1)S(1)}, bf16[128,512]{1,0:T(8,128)(2,1)S(1)}, u32[]{:S(2)}, u32[]{:S(2)}) collective-permute-start(bf16[128,512]{1,0:T(8,128)(2,1)S(1)} %get-tuple-element.279), channel_id=1, source_target_pairs={{0,8},{1,9},{2,10},{3,11},{4,12},{5,13},{6,14},{7,15},{8,0},{9,1},... | collective-permute-start | bytes 393224 | tf_op jit(solution)/shard_map/ppermute | solution.py:325
  181.7 25.2 %collective-permute-start = (bf16[128,512]{1,0:T(8,128)(2,1)S(1)}, bf16[128,512]{1,0:T(8,128)(2,1)S(1)}, u32[]{:S(2)}, u32[]{:S(2)}) collective-permute-start(bf16[128,512]{1,0:T(8,128)(2,1)S(1)} %get-tuple-element.279), channel_id=1, source_target_pairs={{0,4},{1,5},{2,6},{3,7},{4,0},{5,1},{6,2},{7,3},{8,12},{9,13},{10,... | collective-permute-start | bytes 393224 | tf_op jit(solution)/shard_map/ppermute | solution.py:325
  184.0 25.1 %collective-permute-start.3 = (bf16[128,512]{1,0:T(8,128)(2,1)S(1)}, bf16[128,512]{1,0:T(8,128)(2,1)S(1)}, u32[]{:S(2)}, u32[]{:S(2)}) collective-permute-start(bf16[128,512]{1,0:T(8,128)(2,1)S(1)} %get-tuple-element.279), channel_id=1, source_target_pairs={{0,2},{1,3},{2,0},{3,1},{4,6},{5,7},{6,4},{7,5},{8,10},{9,11},{10,... | collective-permute-start | bytes 393224 | tf_op jit(solution)/shard_map/ppermute | solution.py:325
  190.0 25.1 %collective-permute-start.6 = (bf16[128,512]{1,0:T(8,128)(2,1)S(1)}, bf16[128,512]{1,0:T(8,128)(2,1)S(1)}, u32[]{:S(2)}, u32[]{:S(2)}) collective-permute-start(bf16[128,512]{1,0:T(8,128)(2,1)S(1)} %collective-permute-done.2), channel_id=1, source_target_pairs={{0,2},{1,3},{2,0},{3,1},{4,6},{5,7},{6,4},{7,5},{8,10},{9,11},{10,... | collective-permute-start | bytes 393224 | tf_op jit(solution)/shard_map/ppermute | solution.py:325
  217.5 29.1 %collective-permute-start.8 = (bf16[8,144,512]{2,1,0:T(8,128)(2,1)}, bf16[8,144,512]{2,1,0:T(8,128)(2,1)}, u32[]{:S(2)}, u32[]{:S(2)}) collective-permute-start(bf16[8,144,512]{2,1,0:T(8,128)(2,1)} %get-tuple-element.218), channel_id=1, source_target_pairs={{0,16},{16,0},{1,17},{17,1},{2,18},{18,2},{3,19},{19,3},{4,20},{20... | collective-permute-start | bytes 3538952 | tf_op jit(solution)/shard_map/ppermute | solution.py:328
  220.0 51.3 %collective-permute-start.9 = (bf16[8,144,512]{2,1,0:T(8,128)(2,1)}, bf16[8,144,512]{2,1,0:T(8,128)(2,1)}, u32[]{:S(2)}, u32[]{:S(2)}) collective-permute-start(bf16[8,144,512]{2,1,0:T(8,128)(2,1)} %get-tuple-element.217), channel_id=1, source_target_pairs={{0,16},{16,0},{1,17},{17,1},{2,18},{18,2},{3,19},{19,3},{4,20},{20... | collective-permute-start | bytes 3538952 | tf_op jit(solution)/shard_map/ppermute | solution.py:328
  224.6 100.6 %all-to-all-start.1 = ((bf16[16,144,512]{2,1,0:T(8,128)(2,1)}), bf16[16,144,512]{2,1,0:T(8,128)(2,1)}, u32[]{:S(2)}, u32[]{:S(2)}) async-start(bf16[16,144,512]{2,1,0:T(8,128)(2,1)} %shard_map.289), calls=%async_computation.1 | async-start | bytes 4718592 | tf_op jit(solution)/shard_map/all_to_all | solution.py:443
  230.1 295.3 %all-gather.10.cloned.1.call-start = ((), (), s32[]{:S(2)}) async-start(), calls=%async_computation.9 | async-start | bytes 8912896 | tf_op jit(solution)/shard_map/all_gather | solution.py:492
  335.7 22.0 %collective-permute-start.10 = (bf16[128,2048]{1,0:T(8,128)(2,1)}, bf16[128,2048]{1,0:T(8,128)(2,1)S(1)}, u32[]{:S(2)}, u32[]{:S(2)}) collective-permute-start(bf16[128,2048]{1,0:T(8,128)(2,1)} %get-tuple-element.198), channel_id=1, source_target_pairs={{0,4},{1,5},{2,6},{3,7},{4,0},{5,1},{6,2},{7,3},{8,12},{9,13},{10,... | collective-permute-start | bytes 1572872 | tf_op jit(solution)/shard_map/ppermute | solution.py:325
  341.2 82.5 %collective-permute-start.12 = (bf16[128,2048]{1,0:T(8,128)(2,1)}, bf16[128,2048]{1,0:T(8,128)(2,1)S(1)}, u32[]{:S(2)}, u32[]{:S(2)}) collective-permute-start(bf16[128,2048]{1,0:T(8,128)(2,1)} %get-tuple-element.198), channel_id=1, source_target_pairs={{0,12},{1,13},{2,14},{3,15},{4,8},{5,9},{6,10},{7,11},{8,4},{9,5},... | collective-permute-start | bytes 1572872 | tf_op jit(solution)/shard_map/ppermute | solution.py:325
  343.0 78.5 %collective-permute-start.11 = (bf16[128,2048]{1,0:T(8,128)(2,1)}, bf16[128,2048]{1,0:T(8,128)(2,1)S(1)}, u32[]{:S(2)}, u32[]{:S(2)}) collective-permute-start(bf16[128,2048]{1,0:T(8,128)(2,1)} %get-tuple-element.198), channel_id=1, source_target_pairs={{0,8},{1,9},{2,10},{3,11},{4,12},{5,13},{6,14},{7,15},{8,0},{9,1},... | collective-permute-start | bytes 1572872 | tf_op jit(solution)/shard_map/ppermute | solution.py:325
  343.8 81.4 %collective-permute-start.13 = (bf16[128,2048]{1,0:T(8,128)(2,1)}, bf16[128,2048]{1,0:T(8,128)(2,1)}, u32[]{:S(2)}, u32[]{:S(2)}) collective-permute-start(bf16[128,2048]{1,0:T(8,128)(2,1)} %get-tuple-element.198), channel_id=1, source_target_pairs={{0,2},{1,3},{2,0},{3,1},{4,6},{5,7},{6,4},{7,5},{8,10},{9,11},{10,... | collective-permute-start | bytes 1572872 | tf_op jit(solution)/shard_map/ppermute | solution.py:325
  348.2 109.6 %collective-permute-start.18 = (bf16[8,144,512]{2,1,0:T(8,128)(2,1)}, bf16[8,144,512]{2,1,0:T(8,128)(2,1)}, u32[]{:S(2)}, u32[]{:S(2)}) collective-permute-start(bf16[8,144,512]{2,1,0:T(8,128)(2,1)} %get-tuple-element.215), channel_id=1, source_target_pairs={{0,16},{16,0},{1,17},{17,1},{2,18},{18,2},{3,19},{19,3},{4,20},{20... | collective-permute-start | bytes 3538952 | tf_op jit(solution)/shard_map/ppermute | solution.py:328
  357.6 100.2 %collective-permute-start.17 = (bf16[8,144,512]{2,1,0:T(8,128)(2,1)S(1)}, bf16[8,144,512]{2,1,0:T(8,128)(2,1)S(1)}, u32[]{:S(2)}, u32[]{:S(2)}) collective-permute-start(bf16[8,144,512]{2,1,0:T(8,128)(2,1)S(1)} %get-tuple-element.216), channel_id=1, source_target_pairs={{0,16},{16,0},{1,17},{17,1},{2,18},{18,2},{3,19},{19,3},{4,20},{20... | collective-permute-start | bytes 3538952 | tf_op jit(solution)/shard_map/ppermute | solution.py:328
  423.7 23.9 %collective-permute-start.15 = (bf16[128,2048]{1,0:T(8,128)(2,1)S(1)}, bf16[128,2048]{1,0:T(8,128)(2,1)S(1)}, u32[]{:S(2)}, u32[]{:S(2)}) collective-permute-start(bf16[128,2048]{1,0:T(8,128)(2,1)S(1)} %collective-permute-done.11), channel_id=1, source_target_pairs={{0,2},{1,3},{2,0},{3,1},{4,6},{5,7},{6,4},{7,5},{8,10},{9,11},{10,... | collective-permute-start | bytes 1572872 | tf_op jit(solution)/shard_map/ppermute | solution.py:325
  425.2 31.7 %collective-permute-start.16 = (bf16[128,2048]{1,0:T(8,128)(2,1)S(1)}, bf16[128,2048]{1,0:T(8,128)(2,1)S(1)}, u32[]{:S(2)}, u32[]{:S(2)}) collective-permute-start(bf16[128,2048]{1,0:T(8,128)(2,1)S(1)} %collective-permute-done.12), channel_id=1, source_target_pairs={{0,2},{1,3},{2,0},{3,1},{4,6},{5,7},{6,4},{7,5},{8,10},{9,11},{10,... | collective-permute-start | bytes 1572872 | tf_op jit(solution)/shard_map/ppermute | solution.py:325
  480.4 83.0 %all-to-all-start.2 = ((bf16[16,128,288]{1,2,0:T(8,128)(2,1)}), bf16[16,128,288]{1,2,0:T(8,128)(2,1)S(1)}, u32[]{:S(2)}, u32[]{:S(2)}) async-start(bf16[16,128,288]{1,2,0:T(8,128)(2,1)} %maximum_bitcast_fusion), calls=%async_computation.3 | async-start | bytes 2359296 | tf_op jit(solution)/shard_map/all_to_all | solution.py:569
  484.1 212.4 %reduce-scatter.2.cloned.1.call-start = ((), (), s32[]{:S(2)}) async-start(), calls=%async_computation.8 | async-start | bytes 8912896 | tf_op jit(solution)/shard_map/reduce_scatter | solution.py:530
  525.3 480.7 %all-gather.14.cloned.1.call-start = ((), (), s32[]{:S(2)}) async-start(), calls=%async_computation.11 | async-start | bytes 8912896 | tf_op jit(solution)/shard_map/all_gather | solution.py:576
  563.5 47.9 %collective-permute-start.28 = (bf16[512,2048]{1,0:T(8,128)(2,1)}, bf16[512,2048]{1,0:T(8,128)(2,1)S(1)}, u32[]{:S(2)}, u32[]{:S(2)}) collective-permute-start(bf16[512,2048]{1,0:T(8,128)(2,1)} %convolution_convert_fusion.1), channel_id=1, source_target_pairs={{0,16},{16,0},{1,17},{17,1},{2,18},{18,2},{3,19},{19,3},{4,20},{20... | collective-permute-start | bytes 6291464 | tf_op jit(solution)/shard_map/ppermute | solution.py:328
  579.2 42.8 %collective-permute-start.24 = (bf16[128,2048]{1,0:T(8,128)(2,1)S(1)}, bf16[128,2048]{1,0:T(8,128)(2,1)S(1)}, u32[]{:S(2)}, u32[]{:S(2)}) collective-permute-start(bf16[128,2048]{1,0:T(8,128)(2,1)S(1)} %get-tuple-element.207), channel_id=1, source_target_pairs={{0,2},{1,3},{2,0},{3,1},{4,6},{5,7},{6,4},{7,5},{8,10},{9,11},{10,... | collective-permute-start | bytes 1572872 | tf_op jit(solution)/shard_map/ppermute | solution.py:325
  580.9 41.2 %collective-permute-start.23 = (bf16[128,2048]{1,0:T(8,128)(2,1)S(1)}, bf16[128,2048]{1,0:T(8,128)(2,1)S(1)}, u32[]{:S(2)}, u32[]{:S(2)}) collective-permute-start(bf16[128,2048]{1,0:T(8,128)(2,1)S(1)} %get-tuple-element.208), channel_id=1, source_target_pairs={{0,2},{1,3},{2,0},{3,1},{4,6},{5,7},{6,4},{7,5},{8,10},{9,11},{10,... | collective-permute-start | bytes 1572872 | tf_op jit(solution)/shard_map/ppermute | solution.py:325
  581.3 50.9 %collective-permute-start.22 = (bf16[128,2048]{1,0:T(8,128)(2,1)S(1)}, bf16[128,2048]{1,0:T(8,128)(2,1)S(1)}, u32[]{:S(2)}, u32[]{:S(2)}) collective-permute-start(bf16[128,2048]{1,0:T(8,128)(2,1)S(1)} %get-tuple-element.209), channel_id=1, source_target_pairs={{0,2},{1,3},{2,0},{3,1},{4,6},{5,7},{6,4},{7,5},{8,10},{9,11},{10,... | collective-permute-start | bytes 1572872 | tf_op jit(solution)/shard_map/ppermute | solution.py:325
  582.9 60.9 %collective-permute-start.21 = (bf16[128,2048]{1,0:T(8,128)(2,1)S(1)}, bf16[128,2048]{1,0:T(8,128)(2,1)S(1)}, u32[]{:S(2)}, u32[]{:S(2)}) collective-permute-start(bf16[128,2048]{1,0:T(8,128)(2,1)S(1)} %get-tuple-element.210), channel_id=1, source_target_pairs={{0,2},{1,3},{2,0},{3,1},{4,6},{5,7},{6,4},{7,5},{8,10},{9,11},{10,... | collective-permute-start | bytes 1572872 | tf_op jit(solution)/shard_map/ppermute | solution.py:325
  612.8 46.9 %collective-permute-start.29 = (bf16[2048,512]{1,0:T(8,128)(2,1)S(1)}, bf16[2048,512]{1,0:T(8,128)(2,1)S(1)}, u32[]{:S(2)}, u32[]{:S(2)}) collective-permute-start(bf16[2048,512]{1,0:T(8,128)(2,1)S(1)} %get-tuple-element.212), channel_id=1, source_target_pairs={{0,16},{16,0},{1,17},{17,1},{2,18},{18,2},{3,19},{19,3},{4,20},{20... | collective-permute-start | bytes 6291464 | tf_op jit(solution)/shard_map/ppermute | solution.py:328
  646.0 23.7 %collective-permute-start.27 = (bf16[128,2048]{1,0:T(8,128)(2,1)S(1)}, bf16[128,2048]{1,0:T(8,128)(2,1)S(1)}, u32[]{:S(2)}, u32[]{:S(2)}) collective-permute-start(bf16[128,2048]{1,0:T(8,128)(2,1)S(1)} %get-tuple-element.204), channel_id=1, source_target_pairs={{0,12},{1,13},{2,14},{3,15},{4,8},{5,9},{6,10},{7,11},{8,4},{9,5},... | collective-permute-start | bytes 1572872 | tf_op jit(solution)/shard_map/ppermute | solution.py:325
  649.6 44.5 %collective-permute-start.26 = (bf16[128,2048]{1,0:T(8,128)(2,1)S(1)}, bf16[128,2048]{1,0:T(8,128)(2,1)S(1)}, u32[]{:S(2)}, u32[]{:S(2)}) collective-permute-start(bf16[128,2048]{1,0:T(8,128)(2,1)S(1)} %get-tuple-element.205), channel_id=1, source_target_pairs={{0,8},{1,9},{2,10},{3,11},{4,12},{5,13},{6,14},{7,15},{8,0},{9,1},... | collective-permute-start | bytes 1572872 | tf_op jit(solution)/shard_map/ppermute | solution.py:325
  649.7 44.5 %collective-permute-start.25 = (bf16[128,2048]{1,0:T(8,128)(2,1)S(1)}, bf16[128,2048]{1,0:T(8,128)(2,1)S(1)}, u32[]{:S(2)}, u32[]{:S(2)}) collective-permute-start(bf16[128,2048]{1,0:T(8,128)(2,1)S(1)} %get-tuple-element.206), channel_id=1, source_target_pairs={{0,4},{1,5},{2,6},{3,7},{4,0},{5,1},{6,2},{7,3},{8,12},{9,13},{10,... | collective-permute-start | bytes 1572872 | tf_op jit(solution)/shard_map/ppermute | solution.py:325
  699.5 47.0 %collective-permute-start.30 = (bf16[2048,512]{1,0:T(8,128)(2,1)}, bf16[2048,512]{1,0:T(8,128)(2,1)}, u32[]{:S(2)}, u32[]{:S(2)}) collective-permute-start(bf16[2048,512]{1,0:T(8,128)(2,1)} %get-tuple-element.211), channel_id=1, source_target_pairs={{0,16},{16,0},{1,17},{17,1},{2,18},{18,2},{3,19},{19,3},{4,20},{20... | collective-permute-start | bytes 6291464 | tf_op jit(solution)/shard_map/ppermute | solution.py:328
  707.3 116.7 %all-to-all-start.3 = ((bf16[16,144,512]{2,1,0:T(8,128)(2,1)}), bf16[16,144,512]{2,1,0:T(8,128)(2,1)}, u32[]{:S(2)}, u32[]{:S(2)}) async-start(bf16[16,144,512]{2,1,0:T(8,128)(2,1)} %pad_maximum_fusion.2), calls=%async_computation.4 | async-start | bytes 4718592 | tf_op jit(solution)/shard_map/all_to_all | solution.py:443
  712.3 298.5 %all-gather.12.cloned.1.call-start = ((), (), s32[]{:S(2)}) async-start(), calls=%async_computation.10 | async-start | bytes 8912896 | tf_op jit(solution)/shard_map/all_gather | solution.py:604
  766.0 28.1 %collective-permute-start.32 = (bf16[512,512]{1,0:T(8,128)(2,1)S(1)}, bf16[512,512]{1,0:T(8,128)(2,1)S(1)}, u32[]{:S(2)}, u32[]{:S(2)}) collective-permute-start(bf16[512,512]{1,0:T(8,128)(2,1)S(1)} %slice.442), channel_id=1, source_target_pairs={{0,2},{1,3},{2,0},{3,1},{4,6},{5,7},{6,4},{7,5},{8,10},{9,11},{10,... | collective-permute-start | bytes 1572872 | tf_op jit(solution)/shard_map/ppermute | solution.py:325
  770.7 62.5 %collective-permute-start.36 = (bf16[512,2304]{1,0:T(8,128)(2,1)}, bf16[512,2304]{1,0:T(8,128)(2,1)}, u32[]{:S(2)}, u32[]{:S(2)}) collective-permute-start(bf16[512,2304]{1,0:T(8,128)(2,1)} %pad_maximum_fusion.1.mine), channel_id=1, source_target_pairs={{0,16},{16,0},{1,17},{17,1},{2,18},{18,2},{3,19},{19,3},{4,20},{20... | collective-permute-start | bytes 7077896 | tf_op jit(solution)/shard_map/ppermute | solution.py:328
  797.6 26.3 %collective-permute-start.34 = (bf16[128,512]{1,0:T(8,128)(2,1)S(1)}, bf16[128,512]{1,0:T(8,128)(2,1)S(1)}, u32[]{:S(2)}, u32[]{:S(2)}) collective-permute-start(bf16[128,512]{1,0:T(8,128)(2,1)S(1)} %get-tuple-element.239), channel_id=1, source_target_pairs={{0,8},{1,9},{2,10},{3,11},{4,12},{5,13},{6,14},{7,15},{8,0},{9,1},... | collective-permute-start | bytes 393224 | tf_op jit(solution)/shard_map/ppermute | solution.py:325
  834.9 42.7 %collective-permute-start.47 = (bf16[128,512]{1,0:T(8,128)(2,1)}, bf16[128,512]{1,0:T(8,128)(2,1)S(1)}, u32[]{:S(2)}, u32[]{:S(2)}) collective-permute-start(bf16[128,512]{1,0:T(8,128)(2,1)} %get-tuple-element.262), channel_id=1, source_target_pairs={{0,12},{1,13},{2,14},{3,15},{4,8},{5,9},{6,10},{7,11},{8,4},{9,5},... | collective-permute-start | bytes 393224 | tf_op jit(solution)/shard_map/ppermute | solution.py:325
  835.9 41.8 %collective-permute-start.46 = (bf16[128,512]{1,0:T(8,128)(2,1)}, bf16[128,512]{1,0:T(8,128)(2,1)}, u32[]{:S(2)}, u32[]{:S(2)}) collective-permute-start(bf16[128,512]{1,0:T(8,128)(2,1)} %get-tuple-element.262), channel_id=1, source_target_pairs={{0,8},{1,9},{2,10},{3,11},{4,12},{5,13},{6,14},{7,15},{8,0},{9,1},... | collective-permute-start | bytes 393224 | tf_op jit(solution)/shard_map/ppermute | solution.py:325
  835.9 38.1 %collective-permute-start.45 = (bf16[128,512]{1,0:T(8,128)(2,1)}, bf16[128,512]{1,0:T(8,128)(2,1)}, u32[]{:S(2)}, u32[]{:S(2)}) collective-permute-start(bf16[128,512]{1,0:T(8,128)(2,1)} %get-tuple-element.262), channel_id=1, source_target_pairs={{0,4},{1,5},{2,6},{3,7},{4,0},{5,1},{6,2},{7,3},{8,12},{9,13},{10,... | collective-permute-start | bytes 393224 | tf_op jit(solution)/shard_map/ppermute | solution.py:325
  839.3 65.7 %collective-permute-start.42 = (bf16[16,144,512]{2,1,0:T(8,128)(2,1)}, bf16[16,144,512]{2,1,0:T(8,128)(2,1)}, u32[]{:S(2)}, u32[]{:S(2)}) collective-permute-start(bf16[16,144,512]{2,1,0:T(8,128)(2,1)} %all-to-all-done.3.mine), channel_id=1, source_target_pairs={{0,16},{16,0},{1,17},{17,1},{2,18},{18,2},{3,19},{19,3},{4,20},{20... | collective-permute-start | bytes 7077896 | tf_op jit(solution)/shard_map/ppermute | solution.py:328
  844.3 80.1 %all-to-all-start.4 = ((bf16[16,144,512]{2,1,0:T(8,128)(2,1)}), bf16[16,144,512]{2,1,0:T(8,128)(2,1)}, u32[]{:S(2)}, u32[]{:S(2)}) async-start(bf16[16,144,512]{2,1,0:T(8,128)(2,1)} %pad_maximum_fusion.3), calls=%async_computation.5 | async-start | bytes 4718592 | tf_op jit(solution)/shard_map/all_to_all | solution.py:443
  874.0 52.0 %collective-permute-start.55 = (bf16[1024,512]{0,1:T(8,128)(2,1)}, bf16[1024,512]{0,1:T(8,128)(2,1)S(1)}, u32[]{:S(2)}, u32[]{:S(2)}) collective-permute-start(bf16[1024,512]{0,1:T(8,128)(2,1)} %constant_dynamic-update-slice_fusion.69), channel_id=1, source_target_pairs={{0,1},{1,0},{2,3},{3,2},{4,5},{5,4},{6,7},{7,6},{8,9},{9,8},{10,11... | collective-permute-start | bytes 3145736 | tf_op jit(solution)/shard_map/ppermute | solution.py:325
  877.7 26.6 %collective-permute-start.51 = (bf16[128,512]{1,0:T(8,128)(2,1)S(1)}, bf16[128,512]{1,0:T(8,128)(2,1)S(1)}, u32[]{:S(2)}, u32[]{:S(2)}) collective-permute-start(bf16[128,512]{1,0:T(8,128)(2,1)S(1)} %collective-permute-done.47), channel_id=1, source_target_pairs={{0,2},{1,3},{2,0},{3,1},{4,6},{5,7},{6,4},{7,5},{8,10},{9,11},{10,... | collective-permute-start | bytes 393224 | tf_op jit(solution)/shard_map/ppermute | solution.py:325
  905.1 70.2 %collective-permute-start.52 = (bf16[1024,512]{1,0:T(8,128)(2,1)}, bf16[1024,512]{1,0:T(8,128)(2,1)}, u32[]{:S(2)}, u32[]{:S(2)}) collective-permute-start(bf16[1024,512]{1,0:T(8,128)(2,1)} %get-tuple-element.246), channel_id=1, source_target_pairs={{0,1},{1,0},{2,3},{3,2},{4,5},{5,4},{6,7},{7,6},{8,9},{9,8},{10,11... | collective-permute-start | bytes 3145736 | tf_op jit(solution)/shard_map/ppermute | solution.py:325
  924.4 71.2 %collective-permute-start.43 = (bf16[16,144,512]{2,1,0:T(8,128)(2,1)}, bf16[16,144,512]{2,1,0:T(8,128)(2,1)}, u32[]{:S(2)}, u32[]{:S(2)}) collective-permute-start(bf16[16,144,512]{2,1,0:T(8,128)(2,1)} %all-to-all-done.4.mine), channel_id=1, source_target_pairs={{0,16},{16,0},{1,17},{17,1},{2,18},{18,2},{3,19},{19,3},{4,20},{20... | collective-permute-start | bytes 7077896 | tf_op jit(solution)/shard_map/ppermute | solution.py:328
  929.8 40.4 %collective-permute-start.56 = (bf16[512,512]{0,1:T(8,128)(2,1)}, bf16[512,512]{0,1:T(8,128)(2,1)}, u32[]{:S(2)}, u32[]{:S(2)}) collective-permute-start(bf16[512,512]{0,1:T(8,128)(2,1)} %slice.441), channel_id=1, source_target_pairs={{0,2},{1,3},{2,0},{3,1},{4,6},{5,7},{6,4},{7,5},{8,10},{9,11},{10,... | collective-permute-start | bytes 1572872 | tf_op jit(solution)/shard_map/ppermute | solution.py:325
  1017.8 22.4 %collective-permute-start.53 = (bf16[144,2560]{1,0:T(8,128)(2,1)S(1)}, bf16[144,2560]{1,0:T(8,128)(2,1)S(1)}, u32[]{:S(2)}, u32[]{:S(2)}) collective-permute-start(bf16[144,2560]{1,0:T(8,128)(2,1)S(1)} %pad_maximum_fusion.4), channel_id=1, source_target_pairs={{0,16},{16,0},{1,17},{17,1},{2,18},{18,2},{3,19},{19,3},{4,20},{20... | collective-permute-start | bytes 2211848 | tf_op jit(solution)/shard_map/ppermute | solution.py:328
  (113 other events, 1916.2 us)
Sparse Core Ops, SparseCore 0:
  12.1 148.2 all-gather.5
  163.3 152.0 all-gather.7
  317.5 110.5 all-gather.9
  525.4 121.0 reduce-scatter.1
  699.6 121.8 all-gather.13
  823.5 127.3 all-gather.11

commit v6 on v5

--- a/solution.py
+++ b/solution.py
@@ -351,8 +351,8 @@
 
     chip, core = me // 2, me % 2
 
-    def gather_chips(x):
-        along = lines_of(x)
+    def gather_chips(along):
+        x = along[0]
         blocks = [(2 * k, b) for k, b in enumerate(along)]
         blocks = blocks + [(k + 1, hop(b, 2)) for k, b in blocks]
         near = jnp.zeros((x.shape[0] * n // 2, x.shape[1]), x.dtype)
@@ -489,7 +489,6 @@
     k_mine = rotate(qkv[:, width : width + HD], cosine, sine_rows).astype(BF)
     kv_mine = jnp.concatenate([k_mine, qkv[:, width + HD :].astype(BF)], axis=1)
     kv_all = gather(kv_mine)
-    dy_got = lax.all_gather(after(dy, kv_mine), "ctx", axis=0, tiled=True)
     up_mine = exchange(after(up_sent, kv_all))
     gate_pieces = swap_pieces(gate_mine, 2)
     kv_all = after(kv_all, gate_pieces[0])
@@ -517,7 +516,9 @@
 
     inv_two = inv_rms(mid)
     norm_two = (mid * inv_two * (1.0 + feed_gain)).astype(BF)
-    near_rows = gather_chips(norm_two)
+    along = lines_of(norm_two)
+    near_rows = gather_chips(along)
+    dy_got = lax.all_gather(after(dy, *along), "ctx", axis=0, tiled=True)
     core_id = core.astype(jnp.int32).reshape(1)
     up_other = jnp.concatenate(up_pieces, axis=0)
     w_eff, (gate_b, up_b) = fold(gate_mine, up_mine, gate_up_first, 0, None)
@@ -649,22 +650,24 @@
     gain_rows = gain_rows.reshape(2, n, w_rows).transpose(1, 0, 2).reshape(2 * n, w_rows)
     gain_rows = scatter_whole(reorder(gain_rows))
 
-    down_grads = stack(plane_id, down_rows, after(down_back, grad_input), width)
+    g_out = mm(inputs[:, ext:], after(branch_all, grad_input), 0, 0).astype(BF)
+    g_out_other = swap(g_out)
+    down_grads = stack(plane_id, down_rows, after(down_back, g_out), width)
     gate_up_grads = collect(
-        plane_id, gate_got, after(gate_back, grad_input), w_rows, 0, None
+        plane_id, gate_got, after(gate_back, g_out_other), w_rows, 0, None
     )
     up_got_other = swap(after(up_got, gate_back))
-    gate_up_grads = collect(plane_id, up_got, up_got_other, w_rows, 1, gate_up_grads)
-
-    g_out = mm(inputs[:, ext:], after(branch_all, down_grads[0]), 0, 0).astype(BF)
-    g_q = mm(inputs[:, :ext], after(q_all, g_out), 0, 0)
+    g_q = mm(inputs[:, :ext], q_all, 0, 0)
     inputs_rel = reorder(inputs[:, :ext])
     g_kv = mm(inputs_rel, kv_all_grads, 0, 0)
     g_qkv = jnp.concatenate([g_q, g_kv], axis=1).astype(BF)
-    g_out = both_planes(after(g_out, gate_back))
+    gate_up_grads = collect(
+        plane_id, up_got, after(up_got_other, g_qkv), w_rows, 1, gate_up_grads
+    )
+    g_out = g_out.astype(F32) + g_out_other.astype(F32)
     small = both_planes(after(small, gate_back))
     g_qkv = g_qkv.astype(F32) + after(swap(g_qkv), gate_up_grads[0]).astype(F32)
-    gain_rows = gain_rows + swap(after(gain_rows, up_got_other))
+    gain_rows = gain_rows + swap(after(gain_rows, gate_back))
     g_gu_first = small[:, :rank]
     g_down_second = small[:, rank:].reshape(r_rows, width)
     g_out_first = mm(g_out[:w_rows].astype(BF), out_second, 1, 1)

time: 1070 us -> 1090 us (1.019)
  waiting for transfers between devices: 499 us -> 542 us
  starting transfers between devices: 115 us -> 96.7 us
    ppermute x47, waiting for transfers between devices: 234 us -> 268 us  [hop(): return lax.ppermute(x, 'ctx', [(i, i ^ k) for i in range(n)])]
    all_gather x1, waiting for transfers between devices: 26.2 us -> 47.7 us  [body(): out_got = lax.all_gather(out_ext, 'ctx', axis=0, tiled=True)]
    all_to_all x4, waiting for transfers between devices: 19.3 us -> 0.01 us  [exchange(): lax.all_to_all(flat, 'ctx', 0, 0, tiled=True).reshape(n, ext, feed_half)]
    ppermute x47, starting transfers between devices: 73.5 us -> 54.9 us  [hop(): return lax.ppermute(x, 'ctx', [(i, i ^ k) for i in range(n)])]
    unnamed x212 -> x222, local copies, waits for them, and re-layouts: 44.5 us -> 38.9 us
  transfers between devices with their start and end apart: 72 -> 72, of which waited for: 31 -> 29; matrix products, arithmetic and copies ran while one was open for 29% -> 28% of each run, Pallas kernels for 8% -> 8%
where the time goes in v6:
time: 1090 us; the launch traced here: 1080 us
  waiting for transfers between devices  542 us (50%)
  matrix products  168 us (15%)
  local copies, waits for them, and re-layouts  119 us (11%)
  starting transfers between devices  96.7 us (9%)
  Pallas kernels  84.6 us (8%)
  other arithmetic  51.7 us (5%)
  between operations  16.5 us (2%)
    ppermute x47, waiting for transfers between devices, hop(): return lax.ppermute(x, 'ctx', [(i, i ^ k) for i in range(n)])  268 us
    dot_general x34, matrix products, mm(): lax.dot_general(a, b, (((ca,), (cb,)), ((), ())), preferred_element_type=...  168 us
    all_gather x1, waiting for transfers between devices, body(): qkv_got = lax.all_gather(qkv_ext, 'ctx', axis=0, tiled=True)  130 us
    ppermute x14, waiting for transfers between devices, swap(): return lax.ppermute(x, 'grp', [(0, 1), (1, 0)])  96 us
    ppermute x47, starting transfers between devices, hop(): return lax.ppermute(x, 'ctx', [(i, i ^ k) for i in range(n)])  54.9 us
    all_gather x1, waiting for transfers between devices, body(): out_got = lax.all_gather(out_ext, 'ctx', axis=0, tiled=True)  47.7 us
    unnamed x222, local copies, waits for them, and re-layouts  38.9 us
    pallas_call x1, Pallas kernels, forward(): pl.pallas_call(forward_kernel, out_shape=(jax.ShapeDtypeStruct((t // tile...  26 us
  transfers between devices with their start and end apart: 72, of which 29 were waited for; matrix products, arithmetic and copies ran while one was open for 28% of the time, Pallas kernels for 8%

profile of v6, /device:TPU:0, one launch (start us, length us, event | category | flops | bytes accessed | tf_op | source)
XLA Modules:
  0.0 1078.0 jit_solution(10529740523669283066)
XLA Ops:
  17.2 7.4 all-to-all-start
  30.3 130.1 %all-gather.6.cloned.1.call-done = bf16[2048,3200]{1,0:T(8,128)(2,1)} async-done(((bf16[128,3200]{1,0:T(8,128)(2,1)}), bf16[2048,3200]{1,0:T(8,128)(2,1)}) %all-gather.6.cloned.1.call-update) | async-done | bytes 13107216 | tf_op jit(solution)/shard_map/all_gather | solution.py:424
  169.2 6.8 fusion.3
  184.3 5.9 collective-permute-done.2
  190.8 13.6 %collective-permute-done.1 = bf16[128,512]{1,0:T(8,128)(2,1)S(1)} collective-permute-done((bf16[128,512]{1,0:T(8,128)(2,1)S(1)}, bf16[128,512]{1,0:T(8,128)(2,1)S(1)}, u32[]{:S(2)}, u32[]{:S(2)}) %collective-permute-start.1) | collective-permute-done | bytes 131104 | tf_op jit(solution)/shard_map/ppermute | solution.py:325
  222.4 5.5 all-to-all-start.1
  230.4 18.5 %collective-permute-done.8 = bf16[8,144,512]{2,1,0:T(8,128)(2,1)} collective-permute-done((bf16[8,144,512]{2,1,0:T(8,128)(2,1)}, bf16[8,144,512]{2,1,0:T(8,128)(2,1)}, u32[]{:S(2)}, u32[]{:S(2)}) %collective-permute-start.8) | collective-permute-done | bytes 1179680 | tf_op jit(solution)/shard_map/ppermute | solution.py:328
  251.5 6.0 fusion.143
  268.3 47.7 %all-gather.8.cloned.1.call-done = bf16[2048,3072]{1,0:T(8,128)(2,1)} async-done(((bf16[128,3072]{1,0:T(8,128)(2,1)}), bf16[2048,3072]{1,0:T(8,128)(2,1)}) %all-gather.8.cloned.1.call-update) | async-done | bytes 12582928 | tf_op jit(solution)/shard_map/all_gather | solution.py:435
  326.1 5.6 fusion.7
  340.7 12.6 %collective-permute-done.12 = bf16[128,2048]{1,0:T(8,128)(2,1)} collective-permute-done((bf16[128,2048]{1,0:T(8,128)(2,1)}, bf16[128,2048]{1,0:T(8,128)(2,1)}, u32[]{:S(2)}, u32[]{:S(2)}) %collective-permute-start.12) | collective-permute-done | bytes 524320 | tf_op jit(solution)/shard_map/ppermute | solution.py:325
  353.4 26.7 %collective-permute-done.11 = bf16[128,2048]{1,0:T(8,128)(2,1)} collective-permute-done((bf16[128,2048]{1,0:T(8,128)(2,1)}, bf16[128,2048]{1,0:T(8,128)(2,1)}, u32[]{:S(2)}, u32[]{:S(2)}) %collective-permute-start.11) | collective-permute-done | bytes 524320 | tf_op jit(solution)/shard_map/ppermute | solution.py:325
  407.0 6.2 shard_map.290.refs_0_
  422.6 38.9 %collective-permute-done.14 = bf16[128,2048]{1,0:T(8,128)(2,1)S(1)} collective-permute-done((bf16[128,2048]{1,0:T(8,128)(2,1)}, bf16[128,2048]{1,0:T(8,128)(2,1)S(1)}, u32[]{:S(2)}, u32[]{:S(2)}) %collective-permute-start.14) | collective-permute-done | bytes 524320 | tf_op jit(solution)/shard_map/ppermute | solution.py:325
  463.2 7.7 collective-permute-done.16
  474.8 6.4 shard_map.291.w_ref
  498.3 26.0 %shard_map.292 = (bf16[8,2,128,1024]{3,2,1,0:T(8,128)(2,1)S(1)}, bf16[2048,1024]{1,0:T(8,128)(2,1)S(1)}, bf16[2048,1024]{1,0:T(8,128)(2,1)}) custom-call(s32[1]{0:T(128)} %bitcast.12.core_ref, bf16[2048,2048]{1,0:T(8,128)(2,1)} %constant_dynamic-update-slice_fusion.26.x_ref, bf16[2048,2048]{1,0:T(8,128)(2,1)} %shard_map.291.w_ref), custom_call_target="tpu_custom_call" | custom-call | flops 17179869184 | bytes 29360128 | tf_op jit(solution)/shard_map/pallas_call | solution.py:148
  528.2 10.8 convolution_convert_fusion
  539.1 10.0 convolution_convert_fusion.1
  549.2 15.6 %shard_map.293 = bf16[2048,2048]{1,0:T(8,128)(2,1)} custom-call(s32[1]{0:T(128)} %bitcast.12.core_ref, bf16[8,2,128,2048]{3,2,1,0:T(8,128)(2,1)} %bitcast.158, bf16[1024,2048]{1,0:T(8,128)(2,1)S(1)} %copy-done.3, bf16[2048,1024]{1,0:T(8,128)(2,1)S(1)} %copy-done.5, bf16[2048,1024]{1,0:T(8,128)(2,1)} %get-tuple-element.79.slope_ref), custom_call_target="tpu_custom_call" | custom-call | flops 8589934592 | bytes 29360128 | tf_op jit(solution)/shard_map/pallas_call | solution.py:185
  564.8 12.0 %fusion.25 = bf16[1024,2048]{1,0:T(8,128)(2,1)} fusion(bf16[2048,2048]{1,0:T(8,128)(2,1)S(1)} %bitcast.128, bf16[2048,2048]{1,0:T(8,128)(2,1)} %shard_map.293), kind=kOutput, calls=%fused_computation.63 | convolution fusion | flops 8592031744 | bytes 16777216 | tf_op jit(solution)/shard_map/dot_general | solution.py:19
  579.0 12.6 %fusion.19 = bf16[1024,2048]{1,0:T(8,128)(2,1)S(1)} fusion(bf16[2048,2048]{1,0:T(8,128)(2,1)} %shard_map.291.w_ref, bf16[2048,2048]{1,0:T(8,128)(2,1)} %shard_map.293), kind=kOutput, calls=%fused_computation.61 | convolution fusion | flops 8592031744 | bytes 16777216 | tf_op jit(solution)/shard_map/dot_general | solution.py:19
  598.3 13.2 %fusion.22 = bf16[2048,1024]{1,0:T(8,128)(2,1)S(1)} fusion(bf16[2048,2048]{1,0:T(8,128)(2,1)} %constant_dynamic-update-slice_fusion.26.x_ref, bf16[2048,2048]{1,0:T(8,128)(2,1)} %shard_map.293), kind=kOutput, calls=%fused_computation.62 | convolution fusion | flops 8592031744 | bytes 16777216 | tf_op jit(solution)/shard_map/dot_general | solution.py:19
  613.2 12.1 %collective-permute-done.28 = bf16[512,2048]{1,0:T(8,128)(2,1)S(1)} collective-permute-done((bf16[512,2048]{1,0:T(8,128)(2,1)}, bf16[512,2048]{1,0:T(8,128)(2,1)S(1)}, u32[]{:S(2)}, u32[]{:S(2)}) %collective-permute-start.28) | collective-permute-done | bytes 2097184 | tf_op jit(solution)/shard_map/ppermute | solution.py:328
  628.3 6.4 add_convert_fusion.3
  637.2 10.2 collective-permute-done.22
  647.3 11.2 %collective-permute-done.21 = bf16[128,2048]{1,0:T(8,128)(2,1)S(1)} collective-permute-done((bf16[128,2048]{1,0:T(8,128)(2,1)S(1)}, bf16[128,2048]{1,0:T(8,128)(2,1)S(1)}, u32[]{:S(2)}, u32[]{:S(2)}) %collective-permute-start.21) | collective-permute-done | bytes 524320 | tf_op jit(solution)/shard_map/ppermute | solution.py:325
  665.3 8.4 collective-permute-done.29
  673.6 10.0 add_convert_fusion.2
  683.6 25.2 %collective-permute-done.26 = bf16[128,2048]{1,0:T(8,128)(2,1)S(1)} collective-permute-done((bf16[128,2048]{1,0:T(8,128)(2,1)S(1)}, bf16[128,2048]{1,0:T(8,128)(2,1)S(1)}, u32[]{:S(2)}, u32[]{:S(2)}) %collective-permute-start.26) | collective-permute-done | bytes 524320 | tf_op jit(solution)/shard_map/ppermute | solution.py:325
  719.5 8.3 convert_multiply_fusion.5
  746.3 15.6 %collective-permute-done.30 = bf16[2048,512]{1,0:T(8,128)(2,1)} collective-permute-done((bf16[2048,512]{1,0:T(8,128)(2,1)}, bf16[2048,512]{1,0:T(8,128)(2,1)}, u32[]{:S(2)}, u32[]{:S(2)}) %collective-permute-start.30) | collective-permute-done | bytes 2097184 | tf_op jit(solution)/shard_map/ppermute | solution.py:328
  782.9 16.3 %collective-permute-done.32 = bf16[512,512]{1,0:T(8,128)(2,1)S(1)} collective-permute-done((bf16[512,512]{1,0:T(8,128)(2,1)S(1)}, bf16[512,512]{1,0:T(8,128)(2,1)S(1)}, u32[]{:S(2)}, u32[]{:S(2)}) %collective-permute-start.32) | collective-permute-done | bytes 524320 | tf_op jit(solution)/shard_map/ppermute | solution.py:325
  803.1 13.0 %collective-permute-done.33 = bf16[128,512]{1,0:T(8,128)(2,1)S(1)} collective-permute-done((bf16[128,512]{1,0:T(8,128)(2,1)S(1)}, bf16[128,512]{1,0:T(8,128)(2,1)S(1)}, u32[]{:S(2)}, u32[]{:S(2)}) %collective-permute-start.33) | collective-permute-done | bytes 131104 | tf_op jit(solution)/shard_map/ppermute | solution.py:325
  816.1 7.1 collective-permute-done.35
  823.1 16.8 %collective-permute-done.34 = bf16[128,512]{1,0:T(8,128)(2,1)S(1)} collective-permute-done((bf16[128,512]{1,0:T(8,128)(2,1)S(1)}, bf16[128,512]{1,0:T(8,128)(2,1)S(1)}, u32[]{:S(2)}, u32[]{:S(2)}) %collective-permute-start.34) | collective-permute-done | bytes 131104 | tf_op jit(solution)/shard_map/ppermute | solution.py:325
  840.1 9.9 add_convert_fusion.1
  869.4 7.1 fusion.44
  900.0 6.7 collective-permute-done.48
  908.5 6.0 collective-permute-done.49
  931.5 29.5 %collective-permute-done.40 = f32[2,128]{1,0:T(2,128)S(1)} collective-permute-done((f32[2,128]{1,0:T(2,128)S(1)}, f32[2,128]{1,0:T(2,128)S(1)}, u32[]{:S(2)}, u32[]{:S(2)}) %collective-permute-start.40) | collective-permute-done | bytes 1056 | tf_op jit(solution)/shard_map/ppermute | solution.py:325
  971.7 6.3 collective-permute-done.58
  981.2 41.4 %collective-permute-done.60 = bf16[128,512]{0,1:T(8,128)(2,1)S(1)} collective-permute-done((bf16[128,512]{0,1:T(8,128)(2,1)S(1)}, bf16[128,512]{0,1:T(8,128)(2,1)S(1)}, u32[]{:S(2)}, u32[]{:S(2)}) %collective-permute-start.60) | collective-permute-done | bytes 131104 | tf_op jit(solution)/shard_map/ppermute | solution.py:328
  1024.3 5.8 convolution_convert_fusion.4
  1031.2 6.5 convolution_convert_fusion.5
  1039.5 9.5 shard_map.296
  1052.1 6.5 shard_map.294
  1058.6 6.5 shard_map.295
  (519 shorter events, 313.6 us)
Async XLA Ops:
  7.2 153.2 %all-gather.6.cloned.1.call-start = ((), (), s32[]{:S(2)}) async-start(), calls=%async_computation.6 | async-start | bytes 13926400 | tf_op jit(solution)/shard_map/all_gather | solution.py:424
  12.0 304.1 %all-gather.8.cloned.1.call-start = ((), (), s32[]{:S(2)}) async-start(), calls=%async_computation.7 | async-start | bytes 13369344 | tf_op jit(solution)/shard_map/all_gather | solution.py:435
  17.2 152.0 %all-to-all-start = ((bf16[16,144,512]{2,1,0:T(8,128)(2,1)}), bf16[16,144,512]{2,1,0:T(8,128)(2,1)S(1)}, u32[]{:S(2)}, u32[]{:S(2)}) async-start(bf16[16,144,512]{2,1,0:T(8,128)(2,1)} %shard_map.288), calls=%async_computation | async-start | bytes 4718592 | tf_op jit(solution)/shard_map/all_to_all | solution.py:443
  181.8 25.9 %collective-permute-start = (bf16[128,512]{1,0:T(8,128)(2,1)S(1)}, bf16[128,512]{1,0:T(8,128)(2,1)S(1)}, u32[]{:S(2)}, u32[]{:S(2)}) collective-permute-start(bf16[128,512]{1,0:T(8,128)(2,1)S(1)} %get-tuple-element.277), channel_id=1, source_target_pairs={{0,4},{1,5},{2,6},{3,7},{4,0},{5,1},{6,2},{7,3},{8,12},{9,13},{10,... | collective-permute-start | bytes 393224 | tf_op jit(solution)/shard_map/ppermute | solution.py:325
  183.6 26.4 %collective-permute-start.3 = (bf16[128,512]{1,0:T(8,128)(2,1)S(1)}, bf16[128,512]{1,0:T(8,128)(2,1)S(1)}, u32[]{:S(2)}, u32[]{:S(2)}) collective-permute-start(bf16[128,512]{1,0:T(8,128)(2,1)S(1)} %get-tuple-element.277), channel_id=1, source_target_pairs={{0,2},{1,3},{2,0},{3,1},{4,6},{5,7},{6,4},{7,5},{8,10},{9,11},{10,... | collective-permute-start | bytes 393224 | tf_op jit(solution)/shard_map/ppermute | solution.py:325
  190.2 24.8 %collective-permute-start.6 = (bf16[128,512]{1,0:T(8,128)(2,1)S(1)}, bf16[128,512]{1,0:T(8,128)(2,1)S(1)}, u32[]{:S(2)}, u32[]{:S(2)}) collective-permute-start(bf16[128,512]{1,0:T(8,128)(2,1)S(1)} %collective-permute-done.2), channel_id=1, source_target_pairs={{0,2},{1,3},{2,0},{3,1},{4,6},{5,7},{6,4},{7,5},{8,10},{9,11},{10,... | collective-permute-start | bytes 393224 | tf_op jit(solution)/shard_map/ppermute | solution.py:325
  219.9 29.1 %collective-permute-start.8 = (bf16[8,144,512]{2,1,0:T(8,128)(2,1)}, bf16[8,144,512]{2,1,0:T(8,128)(2,1)}, u32[]{:S(2)}, u32[]{:S(2)}) collective-permute-start(bf16[8,144,512]{2,1,0:T(8,128)(2,1)} %get-tuple-element.216), channel_id=1, source_target_pairs={{0,16},{16,0},{1,17},{17,1},{2,18},{18,2},{3,19},{19,3},{4,20},{20... | collective-permute-start | bytes 3538952 | tf_op jit(solution)/shard_map/ppermute | solution.py:328
  222.4 103.6 %all-to-all-start.1 = ((bf16[16,144,512]{2,1,0:T(8,128)(2,1)}), bf16[16,144,512]{2,1,0:T(8,128)(2,1)}, u32[]{:S(2)}, u32[]{:S(2)}) async-start(bf16[16,144,512]{2,1,0:T(8,128)(2,1)} %shard_map.289), calls=%async_computation.1 | async-start | bytes 4718592 | tf_op jit(solution)/shard_map/all_to_all | solution.py:443
  228.0 311.1 %all-gather.10.cloned.1.call-start = ((), (), s32[]{:S(2)}) async-start(), calls=%async_computation.9 | async-start | bytes 8912896 | tf_op jit(solution)/shard_map/all_gather | solution.py:521
  229.1 86.9 %collective-permute-start.9 = (bf16[8,144,512]{2,1,0:T(8,128)(2,1)}, bf16[8,144,512]{2,1,0:T(8,128)(2,1)}, u32[]{:S(2)}, u32[]{:S(2)}) collective-permute-start(bf16[8,144,512]{2,1,0:T(8,128)(2,1)} %get-tuple-element.215), channel_id=1, source_target_pairs={{0,16},{16,0},{1,17},{17,1},{2,18},{18,2},{3,19},{19,3},{4,20},{20... | collective-permute-start | bytes 3538952 | tf_op jit(solution)/shard_map/ppermute | solution.py:328
  337.5 42.6 %collective-permute-start.11 = (bf16[128,2048]{1,0:T(8,128)(2,1)}, bf16[128,2048]{1,0:T(8,128)(2,1)}, u32[]{:S(2)}, u32[]{:S(2)}) collective-permute-start(bf16[128,2048]{1,0:T(8,128)(2,1)} %get-tuple-element.196), channel_id=1, source_target_pairs={{0,8},{1,9},{2,10},{3,11},{4,12},{5,13},{6,14},{7,15},{8,0},{9,1},... | collective-permute-start | bytes 1572872 | tf_op jit(solution)/shard_map/ppermute | solution.py:325
  337.5 42.6 %collective-permute-start.10 = (bf16[128,2048]{1,0:T(8,128)(2,1)}, bf16[128,2048]{1,0:T(8,128)(2,1)}, u32[]{:S(2)}, u32[]{:S(2)}) collective-permute-start(bf16[128,2048]{1,0:T(8,128)(2,1)} %get-tuple-element.196), channel_id=1, source_target_pairs={{0,4},{1,5},{2,6},{3,7},{4,0},{5,1},{6,2},{7,3},{8,12},{9,13},{10,... | collective-permute-start | bytes 1572872 | tf_op jit(solution)/shard_map/ppermute | solution.py:325
  403.3 69.9 %collective-permute-start.18 = (bf16[8,144,512]{2,1,0:T(8,128)(2,1)}, bf16[8,144,512]{2,1,0:T(8,128)(2,1)S(1)}, u32[]{:S(2)}, u32[]{:S(2)}) collective-permute-start(bf16[8,144,512]{2,1,0:T(8,128)(2,1)} %get-tuple-element.213), channel_id=1, source_target_pairs={{0,16},{16,0},{1,17},{17,1},{2,18},{18,2},{3,19},{19,3},{4,20},{20... | collective-permute-start | bytes 3538952 | tf_op jit(solution)/shard_map/ppermute | solution.py:328
  405.3 66.4 %collective-permute-start.17 = (bf16[8,144,512]{2,1,0:T(8,128)(2,1)S(1)}, bf16[8,144,512]{2,1,0:T(8,128)(2,1)}, u32[]{:S(2)}, u32[]{:S(2)}) collective-permute-start(bf16[8,144,512]{2,1,0:T(8,128)(2,1)S(1)} %get-tuple-element.214), channel_id=1, source_target_pairs={{0,16},{16,0},{1,17},{17,1},{2,18},{18,2},{3,19},{19,3},{4,20},{20... | collective-permute-start | bytes 3538952 | tf_op jit(solution)/shard_map/ppermute | solution.py:328
  413.2 49.1 %collective-permute-start.15 = (bf16[128,2048]{1,0:T(8,128)(2,1)}, bf16[128,2048]{1,0:T(8,128)(2,1)S(1)}, u32[]{:S(2)}, u32[]{:S(2)}) collective-permute-start(bf16[128,2048]{1,0:T(8,128)(2,1)} %collective-permute-done.11), channel_id=1, source_target_pairs={{0,2},{1,3},{2,0},{3,1},{4,6},{5,7},{6,4},{7,5},{8,10},{9,11},{10,... | collective-permute-start | bytes 1572872 | tf_op jit(solution)/shard_map/ppermute | solution.py:325
  413.9 47.6 %collective-permute-start.14 = (bf16[128,2048]{1,0:T(8,128)(2,1)}, bf16[128,2048]{1,0:T(8,128)(2,1)S(1)}, u32[]{:S(2)}, u32[]{:S(2)}) collective-permute-start(bf16[128,2048]{1,0:T(8,128)(2,1)} %collective-permute-done.10), channel_id=1, source_target_pairs={{0,2},{1,3},{2,0},{3,1},{4,6},{5,7},{6,4},{7,5},{8,10},{9,11},{10,... | collective-permute-start | bytes 1572872 | tf_op jit(solution)/shard_map/ppermute | solution.py:325
  421.0 49.9 %collective-permute-start.16 = (bf16[128,2048]{1,0:T(8,128)(2,1)}, bf16[128,2048]{1,0:T(8,128)(2,1)S(1)}, u32[]{:S(2)}, u32[]{:S(2)}) collective-permute-start(bf16[128,2048]{1,0:T(8,128)(2,1)} %collective-permute-done.12), channel_id=1, source_target_pairs={{0,2},{1,3},{2,0},{3,1},{4,6},{5,7},{6,4},{7,5},{8,10},{9,11},{10,... | collective-permute-start | bytes 1572872 | tf_op jit(solution)/shard_map/ppermute | solution.py:325
  494.5 82.6 %all-to-all-start.2 = ((bf16[16,128,288]{1,2,0:T(8,128)(2,1)}), bf16[16,128,288]{1,2,0:T(8,128)(2,1)S(1)}, u32[]{:S(2)}, u32[]{:S(2)}) async-start(bf16[16,128,288]{1,2,0:T(8,128)(2,1)} %maximum_bitcast_fusion), calls=%async_computation.3 | async-start | bytes 2359296 | tf_op jit(solution)/shard_map/all_to_all | solution.py:570
  498.2 213.2 %reduce-scatter.2.cloned.1.call-start = ((), (), s32[]{:S(2)}) async-start(), calls=%async_computation.8 | async-start | bytes 8912896 | tf_op jit(solution)/shard_map/reduce_scatter | solution.py:531
  539.0 485.3 %all-gather.14.cloned.1.call-start = ((), (), s32[]{:S(2)}) async-start(), calls=%async_computation.11 | async-start | bytes 8912896 | tf_op jit(solution)/shard_map/all_gather | solution.py:577
  577.3 48.0 %collective-permute-start.28 = (bf16[512,2048]{1,0:T(8,128)(2,1)}, bf16[512,2048]{1,0:T(8,128)(2,1)S(1)}, u32[]{:S(2)}, u32[]{:S(2)}) collective-permute-start(bf16[512,2048]{1,0:T(8,128)(2,1)} %convolution_convert_fusion.1), channel_id=1, source_target_pairs={{0,16},{16,0},{1,17},{17,1},{2,18},{18,2},{3,19},{19,3},{4,20},{20... | collective-permute-start | bytes 6291464 | tf_op jit(solution)/shard_map/ppermute | solution.py:328
  594.1 43.0 %collective-permute-start.24 = (bf16[128,2048]{1,0:T(8,128)(2,1)S(1)}, bf16[128,2048]{1,0:T(8,128)(2,1)S(1)}, u32[]{:S(2)}, u32[]{:S(2)}) collective-permute-start(bf16[128,2048]{1,0:T(8,128)(2,1)S(1)} %get-tuple-element.205), channel_id=1, source_target_pairs={{0,2},{1,3},{2,0},{3,1},{4,6},{5,7},{6,4},{7,5},{8,10},{9,11},{10,... | collective-permute-start | bytes 1572872 | tf_op jit(solution)/shard_map/ppermute | solution.py:325
  595.8 41.4 %collective-permute-start.23 = (bf16[128,2048]{1,0:T(8,128)(2,1)S(1)}, bf16[128,2048]{1,0:T(8,128)(2,1)S(1)}, u32[]{:S(2)}, u32[]{:S(2)}) collective-permute-start(bf16[128,2048]{1,0:T(8,128)(2,1)S(1)} %get-tuple-element.206), channel_id=1, source_target_pairs={{0,2},{1,3},{2,0},{3,1},{4,6},{5,7},{6,4},{7,5},{8,10},{9,11},{10,... | collective-permute-start | bytes 1572872 | tf_op jit(solution)/shard_map/ppermute | solution.py:325
  596.2 51.1 %collective-permute-start.22 = (bf16[128,2048]{1,0:T(8,128)(2,1)S(1)}, bf16[128,2048]{1,0:T(8,128)(2,1)S(1)}, u32[]{:S(2)}, u32[]{:S(2)}) collective-permute-start(bf16[128,2048]{1,0:T(8,128)(2,1)S(1)} %get-tuple-element.207), channel_id=1, source_target_pairs={{0,2},{1,3},{2,0},{3,1},{4,6},{5,7},{6,4},{7,5},{8,10},{9,11},{10,... | collective-permute-start | bytes 1572872 | tf_op jit(solution)/shard_map/ppermute | solution.py:325
  597.8 60.7 %collective-permute-start.21 = (bf16[128,2048]{1,0:T(8,128)(2,1)S(1)}, bf16[128,2048]{1,0:T(8,128)(2,1)S(1)}, u32[]{:S(2)}, u32[]{:S(2)}) collective-permute-start(bf16[128,2048]{1,0:T(8,128)(2,1)S(1)} %get-tuple-element.208), channel_id=1, source_target_pairs={{0,2},{1,3},{2,0},{3,1},{4,6},{5,7},{6,4},{7,5},{8,10},{9,11},{10,... | collective-permute-start | bytes 1572872 | tf_op jit(solution)/shard_map/ppermute | solution.py:325
  626.6 47.0 %collective-permute-start.29 = (bf16[2048,512]{1,0:T(8,128)(2,1)S(1)}, bf16[2048,512]{1,0:T(8,128)(2,1)S(1)}, u32[]{:S(2)}, u32[]{:S(2)}) collective-permute-start(bf16[2048,512]{1,0:T(8,128)(2,1)S(1)} %get-tuple-element.210), channel_id=1, source_target_pairs={{0,16},{16,0},{1,17},{17,1},{2,18},{18,2},{3,19},{19,3},{4,20},{20... | collective-permute-start | bytes 6291464 | tf_op jit(solution)/shard_map/ppermute | solution.py:328
  664.5 44.3 %collective-permute-start.26 = (bf16[128,2048]{1,0:T(8,128)(2,1)S(1)}, bf16[128,2048]{1,0:T(8,128)(2,1)S(1)}, u32[]{:S(2)}, u32[]{:S(2)}) collective-permute-start(bf16[128,2048]{1,0:T(8,128)(2,1)S(1)} %get-tuple-element.203), channel_id=1, source_target_pairs={{0,8},{1,9},{2,10},{3,11},{4,12},{5,13},{6,14},{7,15},{8,0},{9,1},... | collective-permute-start | bytes 1572872 | tf_op jit(solution)/shard_map/ppermute | solution.py:325
  664.5 44.3 %collective-permute-start.25 = (bf16[128,2048]{1,0:T(8,128)(2,1)S(1)}, bf16[128,2048]{1,0:T(8,128)(2,1)S(1)}, u32[]{:S(2)}, u32[]{:S(2)}) collective-permute-start(bf16[128,2048]{1,0:T(8,128)(2,1)S(1)} %get-tuple-element.204), channel_id=1, source_target_pairs={{0,4},{1,5},{2,6},{3,7},{4,0},{5,1},{6,2},{7,3},{8,12},{9,13},{10,... | collective-permute-start | bytes 1572872 | tf_op jit(solution)/shard_map/ppermute | solution.py:325
  714.8 47.1 %collective-permute-start.30 = (bf16[2048,512]{1,0:T(8,128)(2,1)}, bf16[2048,512]{1,0:T(8,128)(2,1)}, u32[]{:S(2)}, u32[]{:S(2)}) collective-permute-start(bf16[2048,512]{1,0:T(8,128)(2,1)} %get-tuple-element.209), channel_id=1, source_target_pairs={{0,16},{16,0},{1,17},{17,1},{2,18},{18,2},{3,19},{19,3},{4,20},{20... | collective-permute-start | bytes 6291464 | tf_op jit(solution)/shard_map/ppermute | solution.py:328
  735.8 104.2 %all-to-all-start.3 = ((bf16[16,144,512]{2,1,0:T(8,128)(2,1)}), bf16[16,144,512]{2,1,0:T(8,128)(2,1)}, u32[]{:S(2)}, u32[]{:S(2)}) async-start(bf16[16,144,512]{2,1,0:T(8,128)(2,1)} %pad_maximum_fusion.2), calls=%async_computation.4 | async-start | bytes 4718592 | tf_op jit(solution)/shard_map/all_to_all | solution.py:443
  740.4 290.8 %all-gather.12.cloned.1.call-start = ((), (), s32[]{:S(2)}) async-start(), calls=%async_computation.10 | async-start | bytes 8912896 | tf_op jit(solution)/shard_map/all_gather | solution.py:605
  781.8 68.2 %collective-permute-start.36 = (bf16[512,2304]{1,0:T(8,128)(2,1)}, bf16[512,2304]{1,0:T(8,128)(2,1)}, u32[]{:S(2)}, u32[]{:S(2)}) collective-permute-start(bf16[512,2304]{1,0:T(8,128)(2,1)} %pad_maximum_fusion.1.mine), channel_id=1, source_target_pairs={{0,16},{16,0},{1,17},{17,1},{2,18},{18,2},{3,19},{19,3},{4,20},{20... | collective-permute-start | bytes 7077896 | tf_op jit(solution)/shard_map/ppermute | solution.py:328
  799.5 23.6 %collective-permute-start.35 = (bf16[128,512]{1,0:T(8,128)(2,1)S(1)}, bf16[128,512]{1,0:T(8,128)(2,1)S(1)}, u32[]{:S(2)}, u32[]{:S(2)}) collective-permute-start(bf16[128,512]{1,0:T(8,128)(2,1)S(1)} %get-tuple-element.236), channel_id=1, source_target_pairs={{0,12},{1,13},{2,14},{3,15},{4,8},{5,9},{6,10},{7,11},{8,4},{9,5},... | collective-permute-start | bytes 393224 | tf_op jit(solution)/shard_map/ppermute | solution.py:325
  803.0 36.9 %collective-permute-start.34 = (bf16[128,512]{1,0:T(8,128)(2,1)S(1)}, bf16[128,512]{1,0:T(8,128)(2,1)S(1)}, u32[]{:S(2)}, u32[]{:S(2)}) collective-permute-start(bf16[128,512]{1,0:T(8,128)(2,1)S(1)} %get-tuple-element.237), channel_id=1, source_target_pairs={{0,8},{1,9},{2,10},{3,11},{4,12},{5,13},{6,14},{7,15},{8,0},{9,1},... | collective-permute-start | bytes 393224 | tf_op jit(solution)/shard_map/ppermute | solution.py:325
  853.5 43.1 %collective-permute-start.47 = (bf16[128,512]{1,0:T(8,128)(2,1)}, bf16[128,512]{1,0:T(8,128)(2,1)}, u32[]{:S(2)}, u32[]{:S(2)}) collective-permute-start(bf16[128,512]{1,0:T(8,128)(2,1)} %get-tuple-element.260), channel_id=1, source_target_pairs={{0,2},{1,3},{2,0},{3,1},{4,6},{5,7},{6,4},{7,5},{8,10},{9,11},{10,... | collective-permute-start | bytes 393224 | tf_op jit(solution)/shard_map/ppermute | solution.py:325
  855.1 39.7 %collective-permute-start.46 = (bf16[128,512]{1,0:T(8,128)(2,1)}, bf16[128,512]{1,0:T(8,128)(2,1)}, u32[]{:S(2)}, u32[]{:S(2)}) collective-permute-start(bf16[128,512]{1,0:T(8,128)(2,1)} %get-tuple-element.260), channel_id=1, source_target_pairs={{0,12},{1,13},{2,14},{3,15},{4,8},{5,9},{6,10},{7,11},{8,4},{9,5},... | collective-permute-start | bytes 393224 | tf_op jit(solution)/shard_map/ppermute | solution.py:325
  856.2 35.1 %collective-permute-start.45 = (bf16[128,512]{1,0:T(8,128)(2,1)}, bf16[128,512]{1,0:T(8,128)(2,1)}, u32[]{:S(2)}, u32[]{:S(2)}) collective-permute-start(bf16[128,512]{1,0:T(8,128)(2,1)} %get-tuple-element.260), channel_id=1, source_target_pairs={{0,8},{1,9},{2,10},{3,11},{4,12},{5,13},{6,14},{7,15},{8,0},{9,1},... | collective-permute-start | bytes 393224 | tf_op jit(solution)/shard_map/ppermute | solution.py:325
  856.3 33.4 %collective-permute-start.44 = (bf16[128,512]{1,0:T(8,128)(2,1)}, bf16[128,512]{1,0:T(8,128)(2,1)}, u32[]{:S(2)}, u32[]{:S(2)}) collective-permute-start(bf16[128,512]{1,0:T(8,128)(2,1)} %get-tuple-element.260), channel_id=1, source_target_pairs={{0,4},{1,5},{2,6},{3,7},{4,0},{5,1},{6,2},{7,3},{8,12},{9,13},{10,... | collective-permute-start | bytes 393224 | tf_op jit(solution)/shard_map/ppermute | solution.py:325
  863.0 104.9 %all-to-all-start.4 = ((bf16[16,144,512]{2,1,0:T(8,128)(2,1)}), bf16[16,144,512]{2,1,0:T(8,128)(2,1)}, u32[]{:S(2)}, u32[]{:S(2)}) async-start(bf16[16,144,512]{2,1,0:T(8,128)(2,1)} %pad_maximum_fusion.3), calls=%async_computation.5 | async-start | bytes 4718592 | tf_op jit(solution)/shard_map/all_to_all | solution.py:443
  888.7 77.8 %collective-permute-start.42 = (bf16[16,144,512]{2,1,0:T(8,128)(2,1)}, bf16[16,144,512]{2,1,0:T(8,128)(2,1)}, u32[]{:S(2)}, u32[]{:S(2)}) collective-permute-start(bf16[16,144,512]{2,1,0:T(8,128)(2,1)} %all-to-all-done.3.mine), channel_id=1, source_target_pairs={{0,16},{16,0},{1,17},{17,1},{2,18},{18,2},{3,19},{19,3},{4,20},{20... | collective-permute-start | bytes 7077896 | tf_op jit(solution)/shard_map/ppermute | solution.py:328
  889.6 33.7 %collective-permute-start.55 = (bf16[1024,512]{0,1:T(8,128)(2,1)}, bf16[1024,512]{0,1:T(8,128)(2,1)S(1)}, u32[]{:S(2)}, u32[]{:S(2)}) collective-permute-start(bf16[1024,512]{0,1:T(8,128)(2,1)} %copy-done.72), channel_id=1, source_target_pairs={{0,1},{1,0},{2,3},{3,2},{4,5},{5,4},{6,7},{7,6},{8,9},{9,8},{10,11... | collective-permute-start | bytes 3145736 | tf_op jit(solution)/shard_map/ppermute | solution.py:325
  891.3 29.9 %collective-permute-start.38 = (f32[8,128]{1,0:T(8,128)S(1)}, f32[8,128]{1,0:T(8,128)S(1)}, u32[]{:S(2)}, u32[]{:S(2)}) collective-permute-start(f32[8,128]{1,0:T(8,128)S(1)} %slice.333), channel_id=1, source_target_pairs={{0,2},{1,3},{2,0},{3,1},{4,6},{5,7},{6,4},{7,5},{8,10},{9,11},{10,... | collective-permute-start | bytes 12296 | tf_op jit(solution)/shard_map/ppermute | solution.py:325
  921.2 40.3 %collective-permute-start.51 = (bf16[1024,512]{1,0:T(8,128)(2,1)}, bf16[1024,512]{1,0:T(8,128)(2,1)S(1)}, u32[]{:S(2)}, u32[]{:S(2)}) collective-permute-start(bf16[1024,512]{1,0:T(8,128)(2,1)} %get-tuple-element.244), channel_id=1, source_target_pairs={{0,1},{1,0},{2,3},{3,2},{4,5},{5,4},{6,7},{7,6},{8,9},{9,8},{10,11... | collective-permute-start | bytes 3145736 | tf_op jit(solution)/shard_map/ppermute | solution.py:325
  923.8 37.8 %collective-permute-start.56 = (bf16[512,512]{0,1:T(8,128)(2,1)S(1)}, bf16[512,512]{0,1:T(8,128)(2,1)S(1)}, u32[]{:S(2)}, u32[]{:S(2)}) collective-permute-start(bf16[512,512]{0,1:T(8,128)(2,1)S(1)} %slice.439), channel_id=1, source_target_pairs={{0,2},{1,3},{2,0},{3,1},{4,6},{5,7},{6,4},{7,5},{8,10},{9,11},{10,... | collective-permute-start | bytes 1572872 | tf_op jit(solution)/shard_map/ppermute | solution.py:325
  928.8 32.2 %collective-permute-start.40 = (f32[2,128]{1,0:T(2,128)S(1)}, f32[2,128]{1,0:T(2,128)S(1)}, u32[]{:S(2)}, u32[]{:S(2)}) collective-permute-start(f32[2,128]{1,0:T(2,128)S(1)} %get-tuple-element.298), channel_id=1, source_target_pairs={{0,8},{1,9},{2,10},{3,11},{4,12},{5,13},{6,14},{7,15},{8,0},{9,1},... | collective-permute-start | bytes 3080 | tf_op jit(solution)/shard_map/ppermute | solution.py:325
  968.0 71.5 %collective-permute-start.53 = (bf16[16,144,512]{2,1,0:T(8,128)(2,1)}, bf16[16,144,512]{2,1,0:T(8,128)(2,1)}, u32[]{:S(2)}, u32[]{:S(2)}) collective-permute-start(bf16[16,144,512]{2,1,0:T(8,128)(2,1)} %all-to-all-done.4.mine), channel_id=1, source_target_pairs={{0,16},{16,0},{1,17},{17,1},{2,18},{18,2},{3,19},{19,3},{4,20},{20... | collective-permute-start | bytes 7077896 | tf_op jit(solution)/shard_map/ppermute | solution.py:328
  979.1 43.6 %collective-permute-start.60 = (bf16[128,512]{0,1:T(8,128)(2,1)S(1)}, bf16[128,512]{0,1:T(8,128)(2,1)S(1)}, u32[]{:S(2)}, u32[]{:S(2)}) collective-permute-start(bf16[128,512]{0,1:T(8,128)(2,1)S(1)} %fusion.77), channel_id=1, source_target_pairs={{0,16},{16,0},{1,17},{17,1},{2,18},{18,2},{3,19},{19,3},{4,20},{20... | collective-permute-start | bytes 393224 | tf_op jit(solution)/shard_map/ppermute | solution.py:328
  1038.6 28.8 %collective-permute-start.52 = (bf16[144,2560]{1,0:T(8,128)(2,1)}, bf16[144,2560]{1,0:T(8,128)(2,1)}, u32[]{:S(2)}, u32[]{:S(2)}) collective-permute-start(bf16[144,2560]{1,0:T(8,128)(2,1)} %pad_maximum_fusion.4), channel_id=1, source_target_pairs={{0,16},{16,0},{1,17},{17,1},{2,18},{18,2},{3,19},{19,3},{4,20},{20... | collective-permute-start | bytes 2211848 | tf_op jit(solution)/shard_map/ppermute | solution.py:328
  (118 other events, 2005.5 us)
Sparse Core Ops, SparseCore 0:
  12.1 148.2 all-gather.5
  163.3 152.7 all-gather.7
  380.2 98.3 all-gather.9
  539.1 122.1 reduce-scatter.1
  714.9 113.8 all-gather.13
  830.8 130.8 all-gather.11

commit v7 on v5

--- a/solution.py
+++ b/solution.py
@@ -603,7 +603,7 @@
     )
     q_all = lax.all_gather(grad_q_rows, "ctx", axis=0, tiled=True)
     up_half = (
-        mm(after(all_rows, grad_q_rows, gate_got), grads[:, h : 2 * h], 0, 0)
+        mm(after(all_rows, grad_q_rows), grads[:, h : 2 * h], 0, 0)
         + up_part.astype(F32)
     ).astype(BF)
     down_back = swap(after(down_rows, up_part))

time: 1070 us -> 1080 us (level)
  waiting for transfers between devices: 499 us -> 523 us
  starting transfers between devices: 115 us -> 103 us
    ppermute x47, waiting for transfers between devices: 234 us -> 260 us  [hop(): return lax.ppermute(x, 'ctx', [(i, i ^ k) for i in range(n)])]
    all_to_all x4, waiting for transfers between devices: 19.3 us -> 2.8 us  [exchange(): lax.all_to_all(flat, 'ctx', 0, 0, tiled=True).reshape(n, ext, feed_half)]
    ppermute x47, starting transfers between devices: 73.5 us -> 59.4 us  [hop(): return lax.ppermute(x, 'ctx', [(i, i ^ k) for i in range(n)])]
    ppermute x14, waiting for transfers between devices: 91.1 us -> 104 us  [swap(): return lax.ppermute(x, 'grp', [(0, 1), (1, 0)])]
    unnamed x212 -> x226, local copies, waits for them, and re-layouts: 44.5 us -> 46 us
  transfers between devices with their start and end apart: 72 -> 72, of which waited for: 31 -> 33; matrix products, arithmetic and copies ran while one was open for 29% -> 29% of each run, Pallas kernels for 8% -> 8%
where the time goes in v7:
time: 1080 us; the launch traced here: 1060 us
  waiting for transfers between devices  523 us (48%)
  matrix products  165 us (15%)
  local copies, waits for them, and re-layouts  125 us (12%)
  starting transfers between devices  103 us (10%)
  Pallas kernels  85.3 us (8%)
  other arithmetic  46 us (4%)
  between operations  16.4 us (2%)
    ppermute x47, waiting for transfers between devices, hop(): return lax.ppermute(x, 'ctx', [(i, i ^ k) for i in range(n)])  260 us
    dot_general x34, matrix products, mm(): lax.dot_general(a, b, (((ca,), (cb,)), ((), ())), preferred_element_type=...  165 us
    all_gather x1, waiting for transfers between devices, body(): qkv_got = lax.all_gather(qkv_ext, 'ctx', axis=0, tiled=True)  129 us
    ppermute x14, waiting for transfers between devices, swap(): return lax.ppermute(x, 'grp', [(0, 1), (1, 0)])  104 us
    ppermute x47, starting transfers between devices, hop(): return lax.ppermute(x, 'ctx', [(i, i ^ k) for i in range(n)])  59.4 us
    unnamed x226, local copies, waits for them, and re-layouts  46 us
    pallas_call x1, Pallas kernels, forward(): pl.pallas_call(forward_kernel, out_shape=(jax.ShapeDtypeStruct((t // tile...  26.5 us
    all_gather x1, waiting for transfers between devices, body(): out_got = lax.all_gather(out_ext, 'ctx', axis=0, tiled=True)  26.4 us
  transfers between devices with their start and end apart: 72, of which 33 were waited for; matrix products, arithmetic and copies ran while one was open for 29% of the time, Pallas kernels for 8%

profile of v7, /device:TPU:0, one launch (start us, length us, event | category | flops | bytes accessed | tf_op | source)
XLA Modules:
  0.0 1063.5 jit_solution(11369785924643271291)
XLA Ops:
  17.2 7.4 all-to-all-start
  31.0 129.4 %all-gather.6.cloned.1.call-done = bf16[2048,3200]{1,0:T(8,128)(2,1)} async-done(((bf16[128,3200]{1,0:T(8,128)(2,1)}), bf16[2048,3200]{1,0:T(8,128)(2,1)}) %all-gather.6.cloned.1.call-update) | async-done | bytes 13107216 | tf_op jit(solution)/shard_map/all_gather | solution.py:424
  169.2 6.8 fusion.3
  184.9 5.3 collective-permute-done.2
  190.8 13.6 %collective-permute-done.1 = bf16[128,512]{1,0:T(8,128)(2,1)S(1)} collective-permute-done((bf16[128,512]{1,0:T(8,128)(2,1)S(1)}, bf16[128,512]{1,0:T(8,128)(2,1)S(1)}, u32[]{:S(2)}, u32[]{:S(2)}) %collective-permute-start.1) | collective-permute-done | bytes 131104 | tf_op jit(solution)/shard_map/ppermute | solution.py:325
  223.3 5.5 all-to-all-start.1
  229.9 4.9 dynamic-slice_bitcast_fusion.1
  235.5 11.2 %collective-permute-done.8 = bf16[8,144,512]{2,1,0:T(8,128)(2,1)} collective-permute-done((bf16[8,144,512]{2,1,0:T(8,128)(2,1)}, bf16[8,144,512]{2,1,0:T(8,128)(2,1)}, u32[]{:S(2)}, u32[]{:S(2)}) %collective-permute-start.8) | collective-permute-done | bytes 1179680 | tf_op jit(solution)/shard_map/ppermute | solution.py:328
  248.0 23.4 %collective-permute-done.9 = bf16[8,144,512]{2,1,0:T(8,128)(2,1)} collective-permute-done((bf16[8,144,512]{2,1,0:T(8,128)(2,1)}, bf16[8,144,512]{2,1,0:T(8,128)(2,1)}, u32[]{:S(2)}, u32[]{:S(2)}) %collective-permute-start.9) | collective-permute-done | bytes 1179680 | tf_op jit(solution)/shard_map/ppermute | solution.py:328
  289.1 26.4 %all-gather.8.cloned.1.call-done = bf16[2048,3072]{1,0:T(8,128)(2,1)} async-done(((bf16[128,3072]{1,0:T(8,128)(2,1)}), bf16[2048,3072]{1,0:T(8,128)(2,1)}) %all-gather.8.cloned.1.call-update) | async-done | bytes 12582928 | tf_op jit(solution)/shard_map/all_gather | solution.py:435
  324.8 5.6 fusion.7
  350.8 6.2 shard_map.290.refs_0_
  358.7 63.1 %collective-permute-done.11 = bf16[128,2048]{1,0:T(8,128)(2,1)S(1)} collective-permute-done((bf16[128,2048]{1,0:T(8,128)(2,1)}, bf16[128,2048]{1,0:T(8,128)(2,1)S(1)}, u32[]{:S(2)}, u32[]{:S(2)}) %collective-permute-start.11) | collective-permute-done | bytes 524320 | tf_op jit(solution)/shard_map/ppermute | solution.py:325
  428.6 8.1 collective-permute-done.14
  437.5 10.4 collective-permute-done.15
  448.8 8.9 collective-permute-done.16
  461.6 6.3 shard_map.291.w_ref
  484.9 26.5 %shard_map.292 = (bf16[8,2,128,1024]{3,2,1,0:T(8,128)(2,1)S(1)}, bf16[2048,1024]{1,0:T(8,128)(2,1)S(1)}, bf16[2048,1024]{1,0:T(8,128)(2,1)}) custom-call(s32[1]{0:T(128)} %bitcast.12.core_ref, bf16[2048,2048]{1,0:T(8,128)(2,1)} %constant_dynamic-update-slice_fusion.26.x_ref, bf16[2048,2048]{1,0:T(8,128)(2,1)} %shard_map.291.w_ref), custom_call_target="tpu_custom_call" | custom-call | flops 17179869184 | bytes 29360128 | tf_op jit(solution)/shard_map/pallas_call | solution.py:148
  515.4 10.8 %convolution_convert_fusion = bf16[2048,2048]{1,0:T(8,128)(2,1)} fusion(bf16[2048,1024]{1,0:T(8,128)(2,1)S(1)} %bitcast.124, bf16[1024,2048]{1,0:T(8,128)(2,1)S(1)} %copy-done.2), kind=kOutput, calls=%fused_computation.14 | convolution fusion | flops 8594128896 | bytes 16777216 | tf_op jit(solution)/shard_map/dot_general | solution.py:19
  526.3 10.1 convolution_convert_fusion.1
  536.4 15.6 %shard_map.293 = bf16[2048,2048]{1,0:T(8,128)(2,1)} custom-call(s32[1]{0:T(128)} %bitcast.12.core_ref, bf16[8,2,128,2048]{3,2,1,0:T(8,128)(2,1)} %bitcast.158, bf16[1024,2048]{1,0:T(8,128)(2,1)S(1)} %copy-done.3, bf16[2048,1024]{1,0:T(8,128)(2,1)S(1)} %copy-done.5, bf16[2048,1024]{1,0:T(8,128)(2,1)} %get-tuple-element.80.slope_ref), custom_call_target="tpu_custom_call" | custom-call | flops 8589934592 | bytes 29360128 | tf_op jit(solution)/shard_map/pallas_call | solution.py:185
  551.9 12.0 %fusion.25 = bf16[1024,2048]{1,0:T(8,128)(2,1)} fusion(bf16[2048,2048]{1,0:T(8,128)(2,1)S(1)} %bitcast.128, bf16[2048,2048]{1,0:T(8,128)(2,1)} %shard_map.293), kind=kOutput, calls=%fused_computation.63 | convolution fusion | flops 8592031744 | bytes 16777216 | tf_op jit(solution)/shard_map/dot_general | solution.py:19
  565.2 12.6 %fusion.19 = bf16[1024,2048]{1,0:T(8,128)(2,1)S(1)} fusion(bf16[2048,2048]{1,0:T(8,128)(2,1)} %shard_map.291.w_ref, bf16[2048,2048]{1,0:T(8,128)(2,1)} %shard_map.293), kind=kOutput, calls=%fused_computation.61 | convolution fusion | flops 8592031744 | bytes 16777216 | tf_op jit(solution)/shard_map/dot_general | solution.py:19
  584.4 13.2 %fusion.22 = bf16[2048,1024]{1,0:T(8,128)(2,1)S(1)} fusion(bf16[2048,2048]{1,0:T(8,128)(2,1)} %constant_dynamic-update-slice_fusion.26.x_ref, bf16[2048,2048]{1,0:T(8,128)(2,1)} %shard_map.293), kind=kOutput, calls=%fused_computation.62 | convolution fusion | flops 8592031744 | bytes 16777216 | tf_op jit(solution)/shard_map/dot_general | solution.py:19
  599.3 13.1 %collective-permute-done.28 = bf16[512,2048]{1,0:T(8,128)(2,1)S(1)} collective-permute-done((bf16[512,2048]{1,0:T(8,128)(2,1)}, bf16[512,2048]{1,0:T(8,128)(2,1)S(1)}, u32[]{:S(2)}, u32[]{:S(2)}) %collective-permute-start.28) | collective-permute-done | bytes 2097184 | tf_op jit(solution)/shard_map/ppermute | solution.py:328
  614.5 6.3 add_convert_fusion.3
  623.2 10.4 collective-permute-done.22
  633.6 11.2 %collective-permute-done.21 = bf16[128,2048]{1,0:T(8,128)(2,1)S(1)} collective-permute-done((bf16[128,2048]{1,0:T(8,128)(2,1)S(1)}, bf16[128,2048]{1,0:T(8,128)(2,1)S(1)}, u32[]{:S(2)}, u32[]{:S(2)}) %collective-permute-start.21) | collective-permute-done | bytes 524320 | tf_op jit(solution)/shard_map/ppermute | solution.py:325
  651.4 9.2 collective-permute-done.29
  660.7 9.9 add_convert_fusion.2
  670.6 24.4 %collective-permute-done.26 = bf16[128,2048]{1,0:T(8,128)(2,1)S(1)} collective-permute-done((bf16[128,2048]{1,0:T(8,128)(2,1)S(1)}, bf16[128,2048]{1,0:T(8,128)(2,1)S(1)}, u32[]{:S(2)}, u32[]{:S(2)}) %collective-permute-start.26) | collective-permute-done | bytes 524320 | tf_op jit(solution)/shard_map/ppermute | solution.py:325
  712.1 7.6 convert_multiply_fusion.5
  721.4 6.3 multiply_convert_fusion
  727.8 24.0 %collective-permute-done.30 = bf16[2048,512]{1,0:T(8,128)(2,1)} collective-permute-done((bf16[2048,512]{1,0:T(8,128)(2,1)}, bf16[2048,512]{1,0:T(8,128)(2,1)}, u32[]{:S(2)}, u32[]{:S(2)}) %collective-permute-start.30) | collective-permute-done | bytes 2097184 | tf_op jit(solution)/shard_map/ppermute | solution.py:328
  780.2 9.6 add_convert_fusion.1
  791.2 22.8 %collective-permute-done.32 = bf16[512,512]{1,0:T(8,128)(2,1)S(1)} collective-permute-done((bf16[512,512]{1,0:T(8,128)(2,1)S(1)}, bf16[512,512]{1,0:T(8,128)(2,1)S(1)}, u32[]{:S(2)}, u32[]{:S(2)}) %collective-permute-start.32) | collective-permute-done | bytes 524320 | tf_op jit(solution)/shard_map/ppermute | solution.py:325
  819.0 14.0 %collective-permute-done.33 = bf16[128,512]{1,0:T(8,128)(2,1)S(1)} collective-permute-done((bf16[128,512]{1,0:T(8,128)(2,1)S(1)}, bf16[128,512]{1,0:T(8,128)(2,1)S(1)}, u32[]{:S(2)}, u32[]{:S(2)}) %collective-permute-start.33) | collective-permute-done | bytes 131104 | tf_op jit(solution)/shard_map/ppermute | solution.py:325
  832.9 8.3 collective-permute-done.35
  841.2 37.3 %collective-permute-done.34 = bf16[128,512]{1,0:T(8,128)(2,1)S(1)} collective-permute-done((bf16[128,512]{1,0:T(8,128)(2,1)S(1)}, bf16[128,512]{1,0:T(8,128)(2,1)S(1)}, u32[]{:S(2)}, u32[]{:S(2)}) %collective-permute-start.34) | collective-permute-done | bytes 131104 | tf_op jit(solution)/shard_map/ppermute | solution.py:325
  900.1 6.4 all-to-all-start.4
  909.3 7.6 fusion.47
  960.3 6.9 collective-permute-start.39
  971.9 9.5 shard_map.294
  1001.9 6.5 shard_map.295
  1011.4 6.8 shard_map.296
  1025.0 6.3 convolution_convert_fusion.4
  1032.0 7.8 collective-permute-done.54
  1041.9 12.3 %collective-permute-done.53 = bf16[144,2560]{1,0:T(8,128)(2,1)S(1)} collective-permute-done((bf16[144,2560]{1,0:T(8,128)(2,1)S(1)}, bf16[144,2560]{1,0:T(8,128)(2,1)S(1)}, u32[]{:S(2)}, u32[]{:S(2)}) %collective-permute-start.53) | collective-permute-done | bytes 737312 | tf_op jit(solution)/shard_map/ppermute | solution.py:328
  (523 shorter events, 319.7 us)
Async XLA Ops:
  7.2 153.2 %all-gather.6.cloned.1.call-start = ((), (), s32[]{:S(2)}) async-start(), calls=%async_computation.6 | async-start | bytes 13926400 | tf_op jit(solution)/shard_map/all_gather | solution.py:424
  12.0 303.5 %all-gather.8.cloned.1.call-start = ((), (), s32[]{:S(2)}) async-start(), calls=%async_computation.7 | async-start | bytes 13369344 | tf_op jit(solution)/shard_map/all_gather | solution.py:435
  17.2 152.0 %all-to-all-start = ((bf16[16,144,512]{2,1,0:T(8,128)(2,1)}), bf16[16,144,512]{2,1,0:T(8,128)(2,1)S(1)}, u32[]{:S(2)}, u32[]{:S(2)}) async-start(bf16[16,144,512]{2,1,0:T(8,128)(2,1)} %shard_map.288), calls=%async_computation | async-start | bytes 4718592 | tf_op jit(solution)/shard_map/all_to_all | solution.py:443
  181.8 22.6 %collective-permute-start.1 = (bf16[128,512]{1,0:T(8,128)(2,1)S(1)}, bf16[128,512]{1,0:T(8,128)(2,1)S(1)}, u32[]{:S(2)}, u32[]{:S(2)}) collective-permute-start(bf16[128,512]{1,0:T(8,128)(2,1)S(1)} %get-tuple-element.279), channel_id=1, source_target_pairs={{0,8},{1,9},{2,10},{3,11},{4,12},{5,13},{6,14},{7,15},{8,0},{9,1},... | collective-permute-start | bytes 393224 | tf_op jit(solution)/shard_map/ppermute | solution.py:325
  181.8 25.9 %collective-permute-start = (bf16[128,512]{1,0:T(8,128)(2,1)S(1)}, bf16[128,512]{1,0:T(8,128)(2,1)S(1)}, u32[]{:S(2)}, u32[]{:S(2)}) collective-permute-start(bf16[128,512]{1,0:T(8,128)(2,1)S(1)} %get-tuple-element.279), channel_id=1, source_target_pairs={{0,4},{1,5},{2,6},{3,7},{4,0},{5,1},{6,2},{7,3},{8,12},{9,13},{10,... | collective-permute-start | bytes 393224 | tf_op jit(solution)/shard_map/ppermute | solution.py:325
  184.2 25.8 %collective-permute-start.3 = (bf16[128,512]{1,0:T(8,128)(2,1)S(1)}, bf16[128,512]{1,0:T(8,128)(2,1)S(1)}, u32[]{:S(2)}, u32[]{:S(2)}) collective-permute-start(bf16[128,512]{1,0:T(8,128)(2,1)S(1)} %get-tuple-element.279), channel_id=1, source_target_pairs={{0,2},{1,3},{2,0},{3,1},{4,6},{5,7},{6,4},{7,5},{8,10},{9,11},{10,... | collective-permute-start | bytes 393224 | tf_op jit(solution)/shard_map/ppermute | solution.py:325
  190.2 24.9 %collective-permute-start.6 = (bf16[128,512]{1,0:T(8,128)(2,1)S(1)}, bf16[128,512]{1,0:T(8,128)(2,1)S(1)}, u32[]{:S(2)}, u32[]{:S(2)}) collective-permute-start(bf16[128,512]{1,0:T(8,128)(2,1)S(1)} %collective-permute-done.2), channel_id=1, source_target_pairs={{0,2},{1,3},{2,0},{3,1},{4,6},{5,7},{6,4},{7,5},{8,10},{9,11},{10,... | collective-permute-start | bytes 393224 | tf_op jit(solution)/shard_map/ppermute | solution.py:325
  217.6 29.1 %collective-permute-start.8 = (bf16[8,144,512]{2,1,0:T(8,128)(2,1)}, bf16[8,144,512]{2,1,0:T(8,128)(2,1)}, u32[]{:S(2)}, u32[]{:S(2)}) collective-permute-start(bf16[8,144,512]{2,1,0:T(8,128)(2,1)} %get-tuple-element.218), channel_id=1, source_target_pairs={{0,16},{16,0},{1,17},{17,1},{2,18},{18,2},{3,19},{19,3},{4,20},{20... | collective-permute-start | bytes 3538952 | tf_op jit(solution)/shard_map/ppermute | solution.py:328
  219.4 52.0 %collective-permute-start.9 = (bf16[8,144,512]{2,1,0:T(8,128)(2,1)}, bf16[8,144,512]{2,1,0:T(8,128)(2,1)}, u32[]{:S(2)}, u32[]{:S(2)}) collective-permute-start(bf16[8,144,512]{2,1,0:T(8,128)(2,1)} %get-tuple-element.217), channel_id=1, source_target_pairs={{0,16},{16,0},{1,17},{17,1},{2,18},{18,2},{3,19},{19,3},{4,20},{20... | collective-permute-start | bytes 3538952 | tf_op jit(solution)/shard_map/ppermute | solution.py:328
  223.3 101.5 %all-to-all-start.1 = ((bf16[16,144,512]{2,1,0:T(8,128)(2,1)}), bf16[16,144,512]{2,1,0:T(8,128)(2,1)}, u32[]{:S(2)}, u32[]{:S(2)}) async-start(bf16[16,144,512]{2,1,0:T(8,128)(2,1)} %shard_map.289), calls=%async_computation.1 | async-start | bytes 4718592 | tf_op jit(solution)/shard_map/all_to_all | solution.py:443
  228.8 297.4 %all-gather.10.cloned.1.call-start = ((), (), s32[]{:S(2)}) async-start(), calls=%async_computation.9 | async-start | bytes 8912896 | tf_op jit(solution)/shard_map/all_gather | solution.py:492
  340.8 83.1 %collective-permute-start.12 = (bf16[128,2048]{1,0:T(8,128)(2,1)}, bf16[128,2048]{1,0:T(8,128)(2,1)S(1)}, u32[]{:S(2)}, u32[]{:S(2)}) collective-permute-start(bf16[128,2048]{1,0:T(8,128)(2,1)} %get-tuple-element.198), channel_id=1, source_target_pairs={{0,12},{1,13},{2,14},{3,15},{4,8},{5,9},{6,10},{7,11},{8,4},{9,5},... | collective-permute-start | bytes 1572872 | tf_op jit(solution)/shard_map/ppermute | solution.py:325
  342.7 79.1 %collective-permute-start.11 = (bf16[128,2048]{1,0:T(8,128)(2,1)}, bf16[128,2048]{1,0:T(8,128)(2,1)S(1)}, u32[]{:S(2)}, u32[]{:S(2)}) collective-permute-start(bf16[128,2048]{1,0:T(8,128)(2,1)} %get-tuple-element.198), channel_id=1, source_target_pairs={{0,8},{1,9},{2,10},{3,11},{4,12},{5,13},{6,14},{7,15},{8,0},{9,1},... | collective-permute-start | bytes 1572872 | tf_op jit(solution)/shard_map/ppermute | solution.py:325
  343.4 82.1 %collective-permute-start.13 = (bf16[128,2048]{1,0:T(8,128)(2,1)}, bf16[128,2048]{1,0:T(8,128)(2,1)}, u32[]{:S(2)}, u32[]{:S(2)}) collective-permute-start(bf16[128,2048]{1,0:T(8,128)(2,1)} %get-tuple-element.198), channel_id=1, source_target_pairs={{0,2},{1,3},{2,0},{3,1},{4,6},{5,7},{6,4},{7,5},{8,10},{9,11},{10,... | collective-permute-start | bytes 1572872 | tf_op jit(solution)/shard_map/ppermute | solution.py:325
  347.8 110.9 %collective-permute-start.18 = (bf16[8,144,512]{2,1,0:T(8,128)(2,1)}, bf16[8,144,512]{2,1,0:T(8,128)(2,1)}, u32[]{:S(2)}, u32[]{:S(2)}) collective-permute-start(bf16[8,144,512]{2,1,0:T(8,128)(2,1)} %get-tuple-element.215), channel_id=1, source_target_pairs={{0,16},{16,0},{1,17},{17,1},{2,18},{18,2},{3,19},{19,3},{4,20},{20... | collective-permute-start | bytes 3538952 | tf_op jit(solution)/shard_map/ppermute | solution.py:328
  357.1 101.5 %collective-permute-start.17 = (bf16[8,144,512]{2,1,0:T(8,128)(2,1)S(1)}, bf16[8,144,512]{2,1,0:T(8,128)(2,1)S(1)}, u32[]{:S(2)}, u32[]{:S(2)}) collective-permute-start(bf16[8,144,512]{2,1,0:T(8,128)(2,1)S(1)} %get-tuple-element.216), channel_id=1, source_target_pairs={{0,16},{16,0},{1,17},{17,1},{2,18},{18,2},{3,19},{19,3},{4,20},{20... | collective-permute-start | bytes 3538952 | tf_op jit(solution)/shard_map/ppermute | solution.py:328
  423.9 24.0 %collective-permute-start.15 = (bf16[128,2048]{1,0:T(8,128)(2,1)S(1)}, bf16[128,2048]{1,0:T(8,128)(2,1)S(1)}, u32[]{:S(2)}, u32[]{:S(2)}) collective-permute-start(bf16[128,2048]{1,0:T(8,128)(2,1)S(1)} %collective-permute-done.11), channel_id=1, source_target_pairs={{0,2},{1,3},{2,0},{3,1},{4,6},{5,7},{6,4},{7,5},{8,10},{9,11},{10,... | collective-permute-start | bytes 1572872 | tf_op jit(solution)/shard_map/ppermute | solution.py:325
  425.5 32.2 %collective-permute-start.16 = (bf16[128,2048]{1,0:T(8,128)(2,1)S(1)}, bf16[128,2048]{1,0:T(8,128)(2,1)S(1)}, u32[]{:S(2)}, u32[]{:S(2)}) collective-permute-start(bf16[128,2048]{1,0:T(8,128)(2,1)S(1)} %collective-permute-done.12), channel_id=1, source_target_pairs={{0,2},{1,3},{2,0},{3,1},{4,6},{5,7},{6,4},{7,5},{8,10},{9,11},{10,... | collective-permute-start | bytes 1572872 | tf_op jit(solution)/shard_map/ppermute | solution.py:325
  481.2 83.1 %all-to-all-start.2 = ((bf16[16,128,288]{1,2,0:T(8,128)(2,1)}), bf16[16,128,288]{1,2,0:T(8,128)(2,1)S(1)}, u32[]{:S(2)}, u32[]{:S(2)}) async-start(bf16[16,128,288]{1,2,0:T(8,128)(2,1)} %maximum_bitcast_fusion), calls=%async_computation.3 | async-start | bytes 2359296 | tf_op jit(solution)/shard_map/all_to_all | solution.py:569
  484.9 212.4 %reduce-scatter.2.cloned.1.call-start = ((), (), s32[]{:S(2)}) async-start(), calls=%async_computation.8 | async-start | bytes 8912896 | tf_op jit(solution)/shard_map/reduce_scatter | solution.py:530
  526.2 492.5 %all-gather.14.cloned.1.call-start = ((), (), s32[]{:S(2)}) async-start(), calls=%async_computation.11 | async-start | bytes 8912896 | tf_op jit(solution)/shard_map/all_gather | solution.py:576
  564.4 47.9 %collective-permute-start.28 = (bf16[512,2048]{1,0:T(8,128)(2,1)}, bf16[512,2048]{1,0:T(8,128)(2,1)S(1)}, u32[]{:S(2)}, u32[]{:S(2)}) collective-permute-start(bf16[512,2048]{1,0:T(8,128)(2,1)} %convolution_convert_fusion.1), channel_id=1, source_target_pairs={{0,16},{16,0},{1,17},{17,1},{2,18},{18,2},{3,19},{19,3},{4,20},{20... | collective-permute-start | bytes 6291464 | tf_op jit(solution)/shard_map/ppermute | solution.py:328
  580.3 42.9 %collective-permute-start.24 = (bf16[128,2048]{1,0:T(8,128)(2,1)S(1)}, bf16[128,2048]{1,0:T(8,128)(2,1)S(1)}, u32[]{:S(2)}, u32[]{:S(2)}) collective-permute-start(bf16[128,2048]{1,0:T(8,128)(2,1)S(1)} %get-tuple-element.207), channel_id=1, source_target_pairs={{0,2},{1,3},{2,0},{3,1},{4,6},{5,7},{6,4},{7,5},{8,10},{9,11},{10,... | collective-permute-start | bytes 1572872 | tf_op jit(solution)/shard_map/ppermute | solution.py:325
  582.0 41.2 %collective-permute-start.23 = (bf16[128,2048]{1,0:T(8,128)(2,1)S(1)}, bf16[128,2048]{1,0:T(8,128)(2,1)S(1)}, u32[]{:S(2)}, u32[]{:S(2)}) collective-permute-start(bf16[128,2048]{1,0:T(8,128)(2,1)S(1)} %get-tuple-element.208), channel_id=1, source_target_pairs={{0,2},{1,3},{2,0},{3,1},{4,6},{5,7},{6,4},{7,5},{8,10},{9,11},{10,... | collective-permute-start | bytes 1572872 | tf_op jit(solution)/shard_map/ppermute | solution.py:325
  582.4 51.2 %collective-permute-start.22 = (bf16[128,2048]{1,0:T(8,128)(2,1)S(1)}, bf16[128,2048]{1,0:T(8,128)(2,1)S(1)}, u32[]{:S(2)}, u32[]{:S(2)}) collective-permute-start(bf16[128,2048]{1,0:T(8,128)(2,1)S(1)} %get-tuple-element.209), channel_id=1, source_target_pairs={{0,2},{1,3},{2,0},{3,1},{4,6},{5,7},{6,4},{7,5},{8,10},{9,11},{10,... | collective-permute-start | bytes 1572872 | tf_op jit(solution)/shard_map/ppermute | solution.py:325
  584.0 60.7 %collective-permute-start.21 = (bf16[128,2048]{1,0:T(8,128)(2,1)S(1)}, bf16[128,2048]{1,0:T(8,128)(2,1)S(1)}, u32[]{:S(2)}, u32[]{:S(2)}) collective-permute-start(bf16[128,2048]{1,0:T(8,128)(2,1)S(1)} %get-tuple-element.210), channel_id=1, source_target_pairs={{0,2},{1,3},{2,0},{3,1},{4,6},{5,7},{6,4},{7,5},{8,10},{9,11},{10,... | collective-permute-start | bytes 1572872 | tf_op jit(solution)/shard_map/ppermute | solution.py:325
  613.7 46.9 %collective-permute-start.29 = (bf16[2048,512]{1,0:T(8,128)(2,1)S(1)}, bf16[2048,512]{1,0:T(8,128)(2,1)S(1)}, u32[]{:S(2)}, u32[]{:S(2)}) collective-permute-start(bf16[2048,512]{1,0:T(8,128)(2,1)S(1)} %get-tuple-element.212), channel_id=1, source_target_pairs={{0,16},{16,0},{1,17},{17,1},{2,18},{18,2},{3,19},{19,3},{4,20},{20... | collective-permute-start | bytes 6291464 | tf_op jit(solution)/shard_map/ppermute | solution.py:328
  647.0 23.6 %collective-permute-start.27 = (bf16[128,2048]{1,0:T(8,128)(2,1)S(1)}, bf16[128,2048]{1,0:T(8,128)(2,1)S(1)}, u32[]{:S(2)}, u32[]{:S(2)}) collective-permute-start(bf16[128,2048]{1,0:T(8,128)(2,1)S(1)} %get-tuple-element.204), channel_id=1, source_target_pairs={{0,12},{1,13},{2,14},{3,15},{4,8},{5,9},{6,10},{7,11},{8,4},{9,5},... | collective-permute-start | bytes 1572872 | tf_op jit(solution)/shard_map/ppermute | solution.py:325
  650.7 44.3 %collective-permute-start.26 = (bf16[128,2048]{1,0:T(8,128)(2,1)S(1)}, bf16[128,2048]{1,0:T(8,128)(2,1)S(1)}, u32[]{:S(2)}, u32[]{:S(2)}) collective-permute-start(bf16[128,2048]{1,0:T(8,128)(2,1)S(1)} %get-tuple-element.205), channel_id=1, source_target_pairs={{0,8},{1,9},{2,10},{3,11},{4,12},{5,13},{6,14},{7,15},{8,0},{9,1},... | collective-permute-start | bytes 1572872 | tf_op jit(solution)/shard_map/ppermute | solution.py:325
  650.7 44.3 %collective-permute-start.25 = (bf16[128,2048]{1,0:T(8,128)(2,1)S(1)}, bf16[128,2048]{1,0:T(8,128)(2,1)S(1)}, u32[]{:S(2)}, u32[]{:S(2)}) collective-permute-start(bf16[128,2048]{1,0:T(8,128)(2,1)S(1)} %get-tuple-element.206), channel_id=1, source_target_pairs={{0,4},{1,5},{2,6},{3,7},{4,0},{5,1},{6,2},{7,3},{8,12},{9,13},{10,... | collective-permute-start | bytes 1572872 | tf_op jit(solution)/shard_map/ppermute | solution.py:325
  700.4 323.1 %all-gather.12.cloned.1.call-start = ((), (), s32[]{:S(2)}) async-start(), calls=%async_computation.10 | async-start | bytes 8912896 | tf_op jit(solution)/shard_map/all_gather | solution.py:604
  704.8 47.0 %collective-permute-start.30 = (bf16[2048,512]{1,0:T(8,128)(2,1)}, bf16[2048,512]{1,0:T(8,128)(2,1)}, u32[]{:S(2)}, u32[]{:S(2)}) collective-permute-start(bf16[2048,512]{1,0:T(8,128)(2,1)} %get-tuple-element.211), channel_id=1, source_target_pairs={{0,16},{16,0},{1,17},{17,1},{2,18},{18,2},{3,19},{19,3},{4,20},{20... | collective-permute-start | bytes 6291464 | tf_op jit(solution)/shard_map/ppermute | solution.py:328
  770.6 127.9 %all-to-all-start.3 = ((bf16[16,144,512]{2,1,0:T(8,128)(2,1)}), bf16[16,144,512]{2,1,0:T(8,128)(2,1)}, u32[]{:S(2)}, u32[]{:S(2)}) async-start(bf16[16,144,512]{2,1,0:T(8,128)(2,1)} %pad_maximum_fusion.2), calls=%async_computation.4 | async-start | bytes 4718592 | tf_op jit(solution)/shard_map/all_to_all | solution.py:443
  775.2 103.4 %collective-permute-start.36 = (bf16[512,2304]{1,0:T(8,128)(2,1)}, bf16[512,2304]{1,0:T(8,128)(2,1)}, u32[]{:S(2)}, u32[]{:S(2)}) collective-permute-start(bf16[512,2304]{1,0:T(8,128)(2,1)} %pad_maximum_fusion.1.mine), channel_id=1, source_target_pairs={{0,16},{16,0},{1,17},{17,1},{2,18},{18,2},{3,19},{19,3},{4,20},{20... | collective-permute-start | bytes 7077896 | tf_op jit(solution)/shard_map/ppermute | solution.py:328
  778.3 35.7 %collective-permute-start.32 = (bf16[512,512]{1,0:T(8,128)(2,1)S(1)}, bf16[512,512]{1,0:T(8,128)(2,1)S(1)}, u32[]{:S(2)}, u32[]{:S(2)}) collective-permute-start(bf16[512,512]{1,0:T(8,128)(2,1)S(1)} %slice.442), channel_id=1, source_target_pairs={{0,2},{1,3},{2,0},{3,1},{4,6},{5,7},{6,4},{7,5},{8,10},{9,11},{10,... | collective-permute-start | bytes 1572872 | tf_op jit(solution)/shard_map/ppermute | solution.py:325
  814.3 26.9 %collective-permute-start.35 = (bf16[128,512]{1,0:T(8,128)(2,1)S(1)}, bf16[128,512]{1,0:T(8,128)(2,1)S(1)}, u32[]{:S(2)}, u32[]{:S(2)}) collective-permute-start(bf16[128,512]{1,0:T(8,128)(2,1)S(1)} %get-tuple-element.238), channel_id=1, source_target_pairs={{0,12},{1,13},{2,14},{3,15},{4,8},{5,9},{6,10},{7,11},{8,4},{9,5},... | collective-permute-start | bytes 393224 | tf_op jit(solution)/shard_map/ppermute | solution.py:325
  817.7 60.7 %collective-permute-start.34 = (bf16[128,512]{1,0:T(8,128)(2,1)S(1)}, bf16[128,512]{1,0:T(8,128)(2,1)S(1)}, u32[]{:S(2)}, u32[]{:S(2)}) collective-permute-start(bf16[128,512]{1,0:T(8,128)(2,1)S(1)} %get-tuple-element.239), channel_id=1, source_target_pairs={{0,8},{1,9},{2,10},{3,11},{4,12},{5,13},{6,14},{7,15},{8,0},{9,1},... | collective-permute-start | bytes 393224 | tf_op jit(solution)/shard_map/ppermute | solution.py:325
  880.1 52.0 %collective-permute-start.48 = (bf16[128,512]{1,0:T(8,128)(2,1)}, bf16[128,512]{1,0:T(8,128)(2,1)}, u32[]{:S(2)}, u32[]{:S(2)}) collective-permute-start(bf16[128,512]{1,0:T(8,128)(2,1)} %get-tuple-element.262), channel_id=1, source_target_pairs={{0,2},{1,3},{2,0},{3,1},{4,6},{5,7},{6,4},{7,5},{8,10},{9,11},{10,... | collective-permute-start | bytes 393224 | tf_op jit(solution)/shard_map/ppermute | solution.py:325
  882.8 45.6 %collective-permute-start.46 = (bf16[128,512]{1,0:T(8,128)(2,1)}, bf16[128,512]{1,0:T(8,128)(2,1)}, u32[]{:S(2)}, u32[]{:S(2)}) collective-permute-start(bf16[128,512]{1,0:T(8,128)(2,1)} %get-tuple-element.262), channel_id=1, source_target_pairs={{0,8},{1,9},{2,10},{3,11},{4,12},{5,13},{6,14},{7,15},{8,0},{9,1},... | collective-permute-start | bytes 393224 | tf_op jit(solution)/shard_map/ppermute | solution.py:325
  892.9 52.4 %collective-permute-start.51 = (bf16[128,512]{1,0:T(8,128)(2,1)}, bf16[128,512]{1,0:T(8,128)(2,1)}, u32[]{:S(2)}, u32[]{:S(2)}) collective-permute-start(bf16[128,512]{1,0:T(8,128)(2,1)} %collective-permute-done.47), channel_id=1, source_target_pairs={{0,2},{1,3},{2,0},{3,1},{4,6},{5,7},{6,4},{7,5},{8,10},{9,11},{10,... | collective-permute-start | bytes 393224 | tf_op jit(solution)/shard_map/ppermute | solution.py:325
  896.5 38.9 %collective-permute-start.49 = (bf16[128,512]{1,0:T(8,128)(2,1)}, bf16[128,512]{1,0:T(8,128)(2,1)}, u32[]{:S(2)}, u32[]{:S(2)}) collective-permute-start(bf16[128,512]{1,0:T(8,128)(2,1)} %collective-permute-done.45), channel_id=1, source_target_pairs={{0,2},{1,3},{2,0},{3,1},{4,6},{5,7},{6,4},{7,5},{8,10},{9,11},{10,... | collective-permute-start | bytes 393224 | tf_op jit(solution)/shard_map/ppermute | solution.py:325
  898.4 51.1 %collective-permute-start.42 = (bf16[16,144,512]{2,1,0:T(8,128)(2,1)}, bf16[16,144,512]{2,1,0:T(8,128)(2,1)}, u32[]{:S(2)}, u32[]{:S(2)}) collective-permute-start(bf16[16,144,512]{2,1,0:T(8,128)(2,1)} %all-to-all-done.3.mine), channel_id=1, source_target_pairs={{0,16},{16,0},{1,17},{17,1},{2,18},{18,2},{3,19},{19,3},{4,20},{20... | collective-permute-start | bytes 7077896 | tf_op jit(solution)/shard_map/ppermute | solution.py:328
  900.1 52.1 %all-to-all-start.4 = ((bf16[16,144,512]{2,1,0:T(8,128)(2,1)}), bf16[16,144,512]{2,1,0:T(8,128)(2,1)}, u32[]{:S(2)}, u32[]{:S(2)}) async-start(bf16[16,144,512]{2,1,0:T(8,128)(2,1)} %pad_maximum_fusion.3), calls=%async_computation.5 | async-start | bytes 4718592 | tf_op jit(solution)/shard_map/all_to_all | solution.py:443
  928.4 24.4 %collective-permute-start.55 = (bf16[1024,512]{0,1:T(8,128)(2,1)}, bf16[1024,512]{0,1:T(8,128)(2,1)S(1)}, u32[]{:S(2)}, u32[]{:S(2)}) collective-permute-start(bf16[1024,512]{0,1:T(8,128)(2,1)} %constant_dynamic-update-slice_fusion.69), channel_id=1, source_target_pairs={{0,1},{1,0},{2,3},{3,2},{4,5},{5,4},{6,7},{7,6},{8,9},{9,8},{10,11... | collective-permute-start | bytes 3145736 | tf_op jit(solution)/shard_map/ppermute | solution.py:325
  946.8 39.9 %collective-permute-start.52 = (bf16[1024,512]{1,0:T(8,128)(2,1)}, bf16[1024,512]{1,0:T(8,128)(2,1)}, u32[]{:S(2)}, u32[]{:S(2)}) collective-permute-start(bf16[1024,512]{1,0:T(8,128)(2,1)} %get-tuple-element.246), channel_id=1, source_target_pairs={{0,1},{1,0},{2,3},{3,2},{4,5},{5,4},{6,7},{7,6},{8,9},{9,8},{10,11... | collective-permute-start | bytes 3145736 | tf_op jit(solution)/shard_map/ppermute | solution.py:325
  952.3 56.9 %collective-permute-start.43 = (bf16[16,144,512]{2,1,0:T(8,128)(2,1)}, bf16[16,144,512]{2,1,0:T(8,128)(2,1)}, u32[]{:S(2)}, u32[]{:S(2)}) collective-permute-start(bf16[16,144,512]{2,1,0:T(8,128)(2,1)} %all-to-all-done.4.mine), channel_id=1, source_target_pairs={{0,16},{16,0},{1,17},{17,1},{2,18},{18,2},{3,19},{19,3},{4,20},{20... | collective-permute-start | bytes 7077896 | tf_op jit(solution)/shard_map/ppermute | solution.py:328
  956.6 24.8 %collective-permute-start.56 = (bf16[512,512]{0,1:T(8,128)(2,1)}, bf16[512,512]{0,1:T(8,128)(2,1)}, u32[]{:S(2)}, u32[]{:S(2)}) collective-permute-start(bf16[512,512]{0,1:T(8,128)(2,1)} %slice.441), channel_id=1, source_target_pairs={{0,2},{1,3},{2,0},{3,1},{4,6},{5,7},{6,4},{7,5},{8,10},{9,11},{10,... | collective-permute-start | bytes 1572872 | tf_op jit(solution)/shard_map/ppermute | solution.py:325
  1031.4 22.8 %collective-permute-start.53 = (bf16[144,2560]{1,0:T(8,128)(2,1)S(1)}, bf16[144,2560]{1,0:T(8,128)(2,1)S(1)}, u32[]{:S(2)}, u32[]{:S(2)}) collective-permute-start(bf16[144,2560]{1,0:T(8,128)(2,1)S(1)} %pad_maximum_fusion.4), channel_id=1, source_target_pairs={{0,16},{16,0},{1,17},{17,1},{2,18},{18,2},{3,19},{19,3},{4,20},{20... | collective-permute-start | bytes 2211848 | tf_op jit(solution)/shard_map/ppermute | solution.py:328
  (120 other events, 2235.7 us)
Sparse Core Ops, SparseCore 0:
  12.1 148.2 all-gather.5
  163.3 152.2 all-gather.7
  317.7 110.7 all-gather.9
  526.3 121.0 reduce-scatter.1
  700.5 74.6 all-gather.13
  777.2 128.8 all-gather.11
